TPU v7x, 32 devices: a whole 2x2x4 slice. The times are simulated.
32 devices in a mesh: ex: 8 (over y, x, core), feat: 4 (over z).
Axes of the slice: x: 2, y: 2, z: 4, core: 2. Of those that a mesh axis runs over, the one named last changes fastest.
Arguments:
- activations: bfloat16 [512, 64, 4096], P('ex', None, 'feat'), may hold values from -6 to 6
- output_gradient_rows: bfloat16 [512, 64, 4096], P('ex', None, 'feat'), may hold values from -6 to 6
- adapter_down_matrix: bfloat16 [4096, 128], P('feat'), may hold values from -0.09375 to 0.09375
- rank_side_sketch: bfloat16 [128, 64], replicated, may hold values from -0.5 to 0.5
- output_side_sketch: bfloat16 [4096, 128], P('feat'), may hold values from -0.09375 to 0.09375
- heldout_gradient_features: float32 [256, 8192], P('ex', 'feat'), may hold values from -6 to 6
- heldout_language_permutation: int32 [256], P('ex'), may hold values from 0 to 255, each once
Outputs:
- scores: float32 [512, 64], P('ex')
Inputs may be any that keep to these rules, and one draw needn't show every extreme that they name: `heldout_language_permutation`: every value of 0 to 255 appears once, so every language has 4 validation examples.
All inputs are finite; a program needn't handle non-finite values.
Results may differ from a plain program's by a relative error of at most 0.0029.
Values sent between devices are 32-bit elements; how exact they have to be, the bound alone decides.
No kernel may reach another device: no remote copies, remote signals or barrier semaphores. Data moves between devices by JAX's collectives and lax.ppermute only.
A program may use at most 64 MiB of HBM per device.

v0:
```python
import jax
import jax.numpy as jnp
from jax import lax
from jax.sharding import PartitionSpec as P

KF = 8192
LANGS = 64


def shards(
    activations,
    output_gradient_rows,
    adapter_down_matrix,
    rank_side_sketch,
    output_side_sketch,
    heldout_gradient_features,
    heldout_language_permutation,
):
    highest = lax.Precision.HIGHEST
    ex_dev = activations.shape[0]
    down_projection_name = jnp.dot(
        adapter_down_matrix, rank_side_sketch, preferred_element_type=jnp.float32
    ).astype(jnp.bfloat16)
    rank_part = jnp.einsum(
        "esd,dr->esr", activations, down_projection_name, preferred_element_type=jnp.float32
    )
    rank_side = lax.psum(rank_part, "feat")
    out_part = jnp.einsum(
        "esd,dk->esk", output_gradient_rows, output_side_sketch, preferred_element_type=jnp.float32
    )
    out_side = lax.psum_scatter(out_part, "feat", scatter_dimension=2, tiled=True)
    grad_feat = jnp.einsum("esk,esr->ekr", out_side, rank_side, precision=highest).reshape(
        ex_dev, -1
    )
    val_square = lax.psum(
        jnp.sum(heldout_gradient_features * heldout_gradient_features, axis=1), "feat"
    )
    val_unit = heldout_gradient_features * lax.rsqrt(val_square + 1e-06)[:, None]
    lang = heldout_language_permutation % LANGS
    onehot = (lang[:, None] == jnp.arange(LANGS, dtype=jnp.int32)[None, :]).astype(jnp.float32)
    lang_part = jnp.dot(onehot.T, val_unit, precision=highest)
    lang_mean = lax.psum(lang_part, "ex") / (
        heldout_language_permutation.shape[0] * lax.axis_size("ex") // LANGS
    )
    inner_part = jnp.dot(grad_feat, lang_mean.T, precision=highest)
    square_part = jnp.sum(grad_feat * grad_feat, axis=1)
    inner, squares = lax.psum((inner_part, square_part), "feat")
    per_lang = heldout_language_permutation.shape[0] * lax.axis_size("ex") // LANGS
    scale = jnp.sqrt(jnp.float32(KF * per_lang))
    return scale * inner * lax.rsqrt(squares + 1e-06)[:, None]


def solution(mesh):
    placed = (
        P("ex", None, "feat"),
        P("ex", None, "feat"),
        P("feat", None),
        P(),
        P("feat", None),
        P("ex", "feat"),
        P("ex"),
    )
    return jax.shard_map(
        shards, mesh=mesh, in_specs=placed, out_specs=P("ex", None), check_vma=False
    )
```

profile of v0, /device:TPU:0, one launch (start us, length us, event | category | flops | bytes accessed | tf_op | source)
XLA Modules:
  0.0 268.0 jit_solution(1419638174889042181)
XLA Ops:
  6.5 0.0 copy-start
  6.5 0.0 all-reduce.4.cloned.1.call-start
  6.5 7.4 %convolution_bitcast_fusion = f32[64,64,64]{2,1,0:T(8,128)} fusion(bf16[64,64,1024]{2,1,0:T(8,128)(2,1)} %param.7, bf16[1024,128]{1,0:T(8,128)(2,1)} %param.9, bf16[128,64]{0,1:T(8,128)(2,1)} %param.10), kind=kOutput, calls=%fused_computation | convolution fusion | flops 553713664 | bytes 9715712 | tf_op jit(solution)/shard_map/esd,dr->esr/dot_general | solution.py:24
  14.0 0.0 all-reduce.4.cloned.1.call-update
  14.0 0.0 copy-start.1
  14.0 0.0 copy-start.2
  14.0 0.0 reduce-scatter.2.cloned.1.call-start
  14.1 0.0 copy-done
  14.1 9.5 %fusion.3 = f32[64,64,128]{1,2,0:T(8,128)} fusion(bf16[64,64,1024]{2,1,0:T(8,128)(2,1)} %param.8, bf16[1024,128]{1,0:T(8,128)(2,1)S(1)} %copy-done), kind=kOutput, calls=%fused_computation.6 | convolution fusion | flops 1073741824 | bytes 10747904 | tf_op jit(solution)/shard_map/esd,dk->esk/dot_general | solution.py:28
  23.5 0.0 reduce-scatter.2.cloned.1.call-update
  23.6 0.0 all-reduce.6.cloned.1.call-start
  23.6 0.0 copy-done.1
  23.6 0.1 multiply_reduce_fusion.1
  23.7 14.1 %psum.36 = f32[32]{0:T(128)S(1)} all-reduce(f32[32]{0:T(128)S(1)} %multiply_reduce_fusion.1), channel_id=1, replica_groups=mesh['ex'=8,'feat'=4] {'feat'}, use_global_device_ids=true, to_apply=%region_3.0 | all-reduce | flops 32 | bytes 256 | tf_op jit(solution)/shard_map/psum | solution.py:35
  37.8 1.3 fusion.6
  39.1 0.0 all-reduce.6.cloned.1.call-update
  39.1 64.1 %all-reduce.4.cloned.1.call-done = f32[64,64,64]{2,1,0:T(8,128)} async-done(((f32[64,64,64]{2,1,0:T(8,128)}), f32[64,64,64]{2,1,0:T(8,128)}) %all-reduce.4.cloned.1.call-update) | async-done | bytes 1048592 | tf_op jit(solution)/shard_map/psum | solution.py:27
  103.3 78.1 %reduce-scatter.2.cloned.1.call-done = f32[64,64,32]{1,2,0:T(8,128)} async-done(((f32[64,64,128]{1,2,0:T(8,128)}), f32[64,64,32]{1,2,0:T(8,128)}) %reduce-scatter.2.cloned.1.call-update) | async-done | bytes 524304 | tf_op jit(solution)/shard_map/reduce_scatter | solution.py:31
  181.4 4.2 %multiply_reduce_fusion = (f32[64]{0:T(128)S(1)}, f32[64,32,64]{2,1,0:T(8,128)S(1)}) fusion(f32[64,64,32]{1,2,0:T(8,128)} %reduce-scatter.2.cloned.1.call-done, f32[64,64,64]{2,1,0:T(8,128)} %all-reduce.4.cloned.1.call-done), kind=kOutput, calls=%fused_computation.3 | convolution fusion | flops 100925376 | bytes 2097408 | tf_op jit(solution)/shard_map/esk,esr->ekr/dot_general | solution.py:32
  185.6 0.4 reshape.6
  186.0 53.9 %all-reduce.6.cloned.1.call-done = f32[64,2048]{1,0:T(8,128)} async-done(((f32[64,2048]{1,0:T(8,128)}), f32[64,2048]{1,0:T(8,128)}) %all-reduce.6.cloned.1.call-update) | async-done | bytes 524304 | tf_op jit(solution)/shard_map/psum | solution.py:42
  239.9 1.6 fusion.1
  241.5 19.3 %all-reduce = (f32[64,64]{1,0:T(8,128)S(1)}, f32[64]{0:T(128)S(1)}) all-reduce(f32[64,64]{1,0:T(8,128)S(1)} %fusion.1, f32[64]{0:T(128)S(1)} %get-tuple-element.7), channel_id=1, replica_groups=mesh['ex'=8,'feat'=4] {'feat'}, use_global_device_ids=true, to_apply=%region_5.6 | all-reduce | flops 4160 | bytes 33280 | tf_op jit(solution)/shard_map/psum | solution.py:47
  260.8 0.7 broadcast_multiply_fusion
  (4 shorter events, 0.0 us)
Async XLA Ops:
  6.5 7.5 %copy-start = (bf16[1024,128]{1,0:T(8,128)(2,1)S(1)}, bf16[1024,128]{1,0:T(8,128)(2,1)}, u32[]{:S(2)}) copy-start(bf16[1024,128]{1,0:T(8,128)(2,1)} %param.11) | copy-start | bytes 786436
  6.5 96.7 %all-reduce.4.cloned.1.call-start = ((), (), s32[]{:S(2)}) async-start(), calls=%async_computation.2 | async-start | bytes 4194304 | tf_op jit(solution)/shard_map/psum | solution.py:27
  14.0 9.6 %copy-start.1 = (f32[32,2048]{1,0:T(8,128)S(1)}, f32[32,2048]{1,0:T(8,128)}, u32[]{:S(2)}) copy-start(f32[32,2048]{1,0:T(8,128)} %param.12) | copy-start | bytes 786436
  14.0 23.8 %copy-start.2 = (s32[32]{0:T(128)S(1)}, s32[32]{0:T(128)}, u32[]{:S(2)}) copy-start(s32[32]{0:T(128)} %param.13) | copy-start | bytes 388
  14.0 167.4 %reduce-scatter.2.cloned.1.call-start = ((), (), s32[]{:S(2)}) async-start(), calls=%async_computation.1 | async-start | bytes 5242880 | tf_op jit(solution)/shard_map/reduce_scatter | solution.py:31
  23.6 216.3 %all-reduce.6.cloned.1.call-start = ((), (), s32[]{:S(2)}) async-start(), calls=%async_computation.3 | async-start | bytes 1048576 | tf_op jit(solution)/shard_map/psum | solution.py:42
Sparse Core Ops, SparseCore 0:
  14.1 89.1 all-reduce.3
  105.6 75.8 reduce-scatter.1
  184.5 55.3 all-reduce.5
where the time goes:
time: 268 us
  waiting for transfers between devices  196 us (73%)
  blocking collectives  33.3 us (12%)
  matrix products  23.9 us (9%)
  between operations  13.2 us (5%)
    reduce_scatter x1, waiting for transfers between devices, shards(): lax.psum_scatter(out_part, 'feat', scatter_dimension=2, tiled=True)  78.1 us
    psum x1, waiting for transfers between devices, shards(): rank_side = lax.psum(rank_part, 'feat')  64.1 us
    psum x1, waiting for transfers between devices, shards(): lax.psum(lang_part, 'ex')  53.9 us
    psum x1, blocking collectives, shards(): inner, squares = lax.psum((inner_part, square_part), 'feat')  19.3 us
    psum x1, blocking collectives, shards(): lax.psum(jnp.sum(heldout_gradient_features * heldout_gradient_features, a...  14.1 us
    dot_general x1, matrix products, shards(): jnp.einsum('esd,dk->esk', output_gradient_rows, output_side_sketch, prefe...  9.45 us
    dot_general x1, matrix products, shards(): jnp.einsum('esd,dr->esr', activations, down_projection_name, preferred_el...  7.42 us
  transfers between devices with their start and end apart: 3, of which 3 were waited for; matrix products, arithmetic and copies ran while one was open for 6% of the time, Pallas kernels for 0%

commit v1 on v0

v1 whole, which is shorter than its diff:
```python
import functools

import jax
import jax.numpy as jnp
from jax import lax
from jax.experimental import pallas as pl
from jax.experimental.pallas import tpu as pltpu
from jax.sharding import PartitionSpec as P


KF = 8192
LANGS = 64
UNIT = 4
PIECE = 2
HIGHEST = lax.Precision.HIGHEST
SMALL = 24 * 1024 * 1024
VMEM = pl.BlockSpec(memory_space=pltpu.VMEM)
SMEM = pl.BlockSpec(memory_space=pltpu.SMEM)


def project_piece(act, grad, down, sketch, o_ref):
    rows = act.shape[0] // PIECE
    half = rows // 2
    out = jnp.dot(grad, sketch, preferred_element_type=jnp.float32)
    rank = jnp.dot(act, down, preferred_element_type=jnp.float32)
    low = lax.broadcasted_iota(jnp.int32, (half, down.shape[1]), 1) < down.shape[1] // 2
    for unit in range(PIECE):
        start = unit * rows
        o_ref[unit, :rows, :] = out[start : start + rows]
        o_ref[unit, rows:, :] = jnp.where(low, rank[start : start + half], rank[start + half : start + rows])


def first_kernel(order, act_ref, grad_ref, adapter_ref, rank_ref, sketch_ref, held_ref, *o_refs):
    del order
    *piece_refs, down_ref, square_ref = o_refs
    step = pl.program_id(0)

    @pl.when(step == 0)
    def _():
        down = lax.dot_general(
            adapter_ref[...], rank_ref[...], (((1,), (1,)), ((), ())), preferred_element_type=jnp.float32
        )
        down_ref[...] = jnp.concatenate([down, down], axis=1).astype(jnp.bfloat16)
        held = held_ref[...]
        square_ref[...] = jnp.sum(held * held, axis=1, keepdims=True)

    for index, ref in enumerate(piece_refs):

        @pl.when(step == index)
        def _(ref=ref):
            project_piece(act_ref[...], grad_ref[...], down_ref[...], sketch_ref[...], ref)


def more_kernel(order, act_ref, grad_ref, down_ref, sketch_ref, *piece_refs):
    del order
    step = pl.program_id(0)
    for index, ref in enumerate(piece_refs):

        @pl.when(step == index)
        def _(ref=ref):
            project_piece(act_ref[...], grad_ref[...], down_ref[...], sketch_ref[...], ref)


def whole(shape):
    return pl.BlockSpec(shape, lambda i, order: (0,) * len(shape))


def project(kernel, order, first, count, acts, grads, operands, extra):
    ko = operands[-1 if kernel is more_kernel else 2].shape[1]
    width = acts.shape[1]
    rows = acts.shape[0] // order.shape[0]
    piece = (PIECE, rows // PIECE * 3 // 2, ko)
    block = pl.BlockSpec((rows, width), lambda i, order: (order[first + i], 0))
    return pl.pallas_call(
        kernel,
        out_shape=[jax.ShapeDtypeStruct(piece, jnp.float32)] * count + extra,
        grid_spec=pltpu.PrefetchScalarGridSpec(
            num_scalar_prefetch=1,
            grid=(count,),
            in_specs=[block, block] + [whole(x.shape) for x in operands],
            out_specs=[whole(piece)] * count + [whole(x.shape) for x in extra],
        ),
        cost_estimate=pl.CostEstimate(
            flops=count * rows * width * ko * 4,
            bytes_accessed=count * rows * (width * 4 + ko * 6),
            transcendentals=0,
        ),
        name="project",
    )(order, acts, grads, *operands)


def lang_kernel(me_ref, held_ref, lang_ref, *refs):
    *square_refs, other_ref = refs[:5]
    own_refs = refs[5:]
    count = len(own_refs)
    rows, width = held_ref.shape
    piece = width // (2 * count)
    hit = lang_ref[...] == lax.broadcasted_iota(jnp.int32, (LANGS, rows), 0)
    hit = jnp.where(hit, 1.0, 0.0)
    inverse = lax.rsqrt(sum(ref[...] for ref in square_refs) + 1e-06)

    def sums(part):
        columns = pl.ds(pl.multiple_of(part * piece, piece), piece)
        return jnp.dot(
            hit, held_ref[:, columns] * inverse, precision=HIGHEST, preferred_element_type=jnp.float32
        )

    for index in range(count):
        other_ref[index] = sums(me_ref[0] ^ 1 ^ (2 * index))
        own_refs[index][...] = sums(me_ref[0] ^ (2 * index))


def lang_parts(me, held, squares, lang, n_ex):
    rows, width = held.shape
    piece = width // n_ex
    half = n_ex // 2
    return pl.pallas_call(
        lang_kernel,
        out_shape=[jax.ShapeDtypeStruct((half, LANGS, piece), jnp.float32)]
        + [jax.ShapeDtypeStruct((LANGS, piece), jnp.float32)] * half,
        in_specs=[SMEM] + [VMEM] * 6,
        out_specs=[VMEM] * (1 + half),
        compiler_params=pltpu.CompilerParams(vmem_limit_bytes=SMALL),
        name="lang_parts",
    )(me, held, lang.reshape(1, rows), *squares)


def product_kernel(middle_ref, *refs):
    *part_refs, o_ref, square_ref, own_ref, one_ref, two_ref, grad_ref, sem = refs
    own = pltpu.make_async_copy(part_refs[0], own_ref, sem.at[0])
    own.start()

    def fetch(one, two):
        copies = [
            pltpu.make_async_copy(one, one_ref, sem.at[1]),
            pltpu.make_async_copy(two, two_ref, sem.at[2]),
        ]
        for copy in copies:
            copy.start()
        for copy in copies:
            copy.wait()

    @pl.when(middle_ref[0] == 1)
    def _():
        fetch(part_refs[1], part_refs[2])

    @pl.when(middle_ref[0] != 1)
    def _():
        fetch(part_refs[3], part_refs[4])

    own.wait()
    rows = own_ref.shape[1] * 2 // 3
    seq = rows // UNIT
    wide = own_ref.shape[2]
    low = lax.broadcasted_iota(jnp.int32, (seq, wide), 1) < wide // 2

    def split(x, order):
        high = x.astype(jnp.bfloat16)
        rest = (x - high.astype(jnp.float32)).astype(jnp.bfloat16)
        return jnp.concatenate([high, rest, high] if order else [high, high, rest], axis=0)

    def total(unit, start):
        block = (unit, pl.ds(start, seq), slice(None))
        return own_ref[block] + one_ref[block] + two_ref[block]

    for unit in range(PIECE):
        for pair in range(UNIT // 2):
            both = total(unit, rows + pair * seq)
            turned = pltpu.roll(both, wide // 2, 1)
            for side in range(2):
                example = pair + side * (UNIT // 2)
                rank = jnp.where(low, turned, both) if side else jnp.where(low, both, turned)
                grad_ref[unit * UNIT + example] = lax.dot_general(
                    split(total(unit, example * seq), True),
                    split(rank, False),
                    (((0,), (0,)), ((), ())),
                    preferred_element_type=jnp.float32,
                )
    count = PIECE * UNIT
    low = lax.broadcasted_iota(jnp.int32, (count, wide), 1) < wide // 2
    square = jnp.zeros((count, 2 * wide), jnp.float32)
    for index in range(o_ref.shape[0]):
        rows_of = [grad_ref[:, 4 * index + j, :] for j in range(4)]
        part = jnp.concatenate(
            [jnp.where(low, rows_of[0], rows_of[1]), jnp.where(low, rows_of[2], rows_of[3])], axis=1
        )
        square += part * part
        rest = part - part.astype(jnp.bfloat16).astype(jnp.float32)
        o_ref[index] = jnp.concatenate([part, rest], axis=0).astype(jnp.bfloat16)
    square_ref[...] = jnp.sum(square, axis=1, keepdims=True)


def product(middle, parts):
    count, wide = PIECE * UNIT, parts[0].shape[2]
    return pl.pallas_call(
        product_kernel,
        out_shape=[
            jax.ShapeDtypeStruct((wide // 4, 2 * count, 2 * wide), jnp.bfloat16),
            jax.ShapeDtypeStruct((count, 1), jnp.float32),
        ],
        in_specs=[SMEM] + [pl.BlockSpec(memory_space=pl.ANY)] * len(parts),
        out_specs=[VMEM] * 2,
        scratch_shapes=[pltpu.VMEM(parts[0].shape, jnp.float32)] * 3
        + [pltpu.VMEM((count, wide, wide), jnp.float32), pltpu.SemaphoreType.DMA((3,))],
        compiler_params=pltpu.CompilerParams(vmem_limit_bytes=SMALL),
        name="product",
    )(middle, *parts)


def score_kernel(places_ref, *refs, scale, n_lang):
    lang_refs, grad_refs, square_refs, o_ref = refs[:n_lang], refs[n_lang:-1:2], refs[n_lang + 1 : -1 : 2], refs[-1]
    zs = lang_refs[0].shape[0]
    total = None
    for j, ref in enumerate(lang_refs):
        for m in range(zs):
            index = places_ref[n_lang + m] * n_lang + places_ref[j]
            lang = ref[m]
            rest = lang - lang.astype(jnp.bfloat16).astype(jnp.float32)
            lang = jnp.concatenate([lang, rest], axis=0).astype(jnp.bfloat16)
            grad = jnp.concatenate([g[index] for g in grad_refs], axis=0)
            term = lax.dot_general(
                grad, lang, (((1,), (1,)), ((), ())), preferred_element_type=jnp.float32
            )
            total = term if total is None else total + term
    total = total + pltpu.roll(total, LANGS, 1)
    count = square_refs[0].shape[0]
    for index, square_ref in enumerate(square_refs):
        start = 2 * count * index
        inner = total[start : start + count, :LANGS] + total[start + count : start + 2 * count, :LANGS]
        o_ref[index * count : (index + 1) * count] = inner * (lax.rsqrt(square_ref[...] + 1e-06) * scale)


def score(places, langs, products, scale):
    flat = [x for pair in products for x in pair]
    mine = sum(square.shape[0] for _, square in products)
    return pl.pallas_call(
        functools.partial(score_kernel, scale=scale, n_lang=len(langs)),
        out_shape=jax.ShapeDtypeStruct((mine, LANGS), jnp.float32),
        in_specs=[SMEM] + [VMEM] * (len(langs) + len(flat)),
        out_specs=VMEM,
        compiler_params=pltpu.CompilerParams(vmem_limit_bytes=SMALL),
        name="score",
    )(places, *langs, *flat)


def place_kernel(me_ref, *refs):
    *parts, o_ref = refs
    rows = parts[0].shape[0]
    for mask, ref in enumerate(parts):
        o_ref[pl.ds(pl.multiple_of((me_ref[0] ^ mask) * rows, rows), rows), :] = ref[...]


def place(me, parts):
    rows, columns = parts[0].shape
    return pl.pallas_call(
        place_kernel,
        out_shape=jax.ShapeDtypeStruct((rows * len(parts), columns), jnp.float32),
        in_specs=[SMEM] + [VMEM] * len(parts),
        out_specs=VMEM,
        compiler_params=pltpu.CompilerParams(vmem_limit_bytes=SMALL),
        name="place",
    )(me, *parts)


def swap(x, axis, mask):
    return lax.ppermute(x, axis, [(i, i ^ mask) for i in range(lax.axis_size(axis))])


def after(x, *others):
    return lax.optimization_barrier((x, *others))[0]


def fast(*args):
    return ordered(*args)


def ordered(acts, grads, adapter, rank_sketch, out_sketch, held, perm):
    feat, ex = lax.axis_index("feat"), lax.axis_index("ex")
    n_ex = lax.axis_size("ex")
    _, _, width = acts.shape
    middle = (feat == 1) | (feat == 2)
    left = feat < 2
    me_ex = ex.astype(jnp.int32).reshape(1)
    me_feat = feat.astype(jnp.int32).reshape(1)

    base = jnp.array([3, 2, 1, 0, 0, 3, 2, 1, 3, 0, 1, 2, 0, 1, 2, 3], jnp.int32).reshape(4, 4)
    chunks = lax.dynamic_index_in_dim(base, feat, 0, keepdims=False)
    order = (chunks[:, None] * 2 + jnp.arange(2, dtype=jnp.int32)).reshape(-1)
    acts2, grads2 = acts.reshape(-1, width), grads.reshape(-1, width)
    down_like = jax.ShapeDtypeStruct((width, 2 * rank_sketch.shape[1]), jnp.bfloat16)
    square_like = jax.ShapeDtypeStruct((held.shape[0], 1), jnp.float32)
    ends_in = [(0, 1), (3, 2)]
    far_pairs = [(1, 3), (2, 0)]
    near_pairs = [(1, 2), (2, 1)]
    cross = [
        [(i, i ^ (2 if i % 2 == 0 else 4)) for i in range(n_ex)],
        [(i, i ^ (4 if i % 2 == 0 else 2)) for i in range(n_ex)],
        [(i, i ^ 1) for i in range(n_ex)],
    ]

    *raw0, down, own_square = project(
        first_kernel, order, 0, 2, acts2, grads2, [adapter, rank_sketch.T, out_sketch, held], [down_like, square_like]
    )
    squares = [own_square] + [swap(own_square, "feat", mask) for mask in (1, 2, 3)]
    got0 = [swap(x, "feat", 1) for x in raw0]

    other, *parts = lang_parts(me_ex, held, squares, perm % LANGS, n_ex)
    other = swap(other, "ex", 1)
    parts = [x + other[i] for i, x in enumerate(parts)]
    scattered = [swap(parts[i], "ex", 2 * i) for i in range(1, n_ex // 2)]

    raw1 = project(more_kernel, order, 2, 2, acts2, grads2, [after(down, *parts), out_sketch], [])
    sums = [got0[0] + raw1[0]]
    far = [lax.ppermute(sums[0], "feat", far_pairs)]
    lang = after(parts[0], sums[0]) + sum(scattered)
    pair = swap(lang, "feat", 1)
    raw1 = [after(x, lang) for x in raw1]
    got1 = [lax.ppermute(x, "feat", ends_in) for x in raw1]
    sums.append(got0[1] + raw1[1])
    far.append(lax.ppermute(sums[1], "feat", far_pairs))
    *raw2, own_a, own_b = project(
        more_kernel, order, 4, 4, acts2, grads2, [after(down, sums[1]), out_sketch], []
    )
    own = [own_a, own_b]
    got2 = [lax.ppermute(x, "feat", ends_in) for x in raw2]
    pair = jnp.stack([after(lang, own_a), pair])
    far_pair = [lax.ppermute(pair, "feat", far_pairs), lax.ppermute(pair, "feat", near_pairs)]
    sums.append(got1[0] + after(raw2[0], pair))
    near = [lax.ppermute(sums[2], "feat", near_pairs)]
    langs = [jnp.concatenate([after(pair, sums[2]), far_pair[0] + far_pair[1]])]
    langs = langs + [lax.ppermute(x, "ex", cross[0]) for x in langs]
    sums.append(got1[1] + after(raw2[1], langs[0]))
    near.append(lax.ppermute(sums[3], "feat", near_pairs))
    langs[1] = after(langs[1], sums[3])
    langs = langs + [lax.ppermute(x, "ex", cross[1]) for x in langs]
    is_middle = middle.astype(jnp.int32).reshape(1)
    products = [product(is_middle, [after(own[0], langs[1]), got2[0], near[0], got0[0], far[0]])]
    langs[2:] = [after(x, products[0][1]) for x in langs[2:]]
    langs = langs + [lax.ppermute(x, "ex", cross[2]) for x in langs]
    products.append(product(is_middle, [after(own[1], products[0][1]), got2[1], near[1], got0[1], far[1]]))
    one = jnp.where(ex % 2 == 0, 2, 4)
    two = 6 - one
    masks = [0, one, two, 6, 1, 1 ^ two, 1 ^ one, 7]
    second = jnp.where(left, 2, 1)
    places = jnp.stack(
        [jnp.asarray(x, jnp.int32) for x in [ex ^ m for m in masks] + [feat, feat ^ 1, second, second ^ 1]]
    )
    per_lang = perm.shape[0] * n_ex // LANGS
    scale = (KF * per_lang) ** 0.5 / per_lang
    mine = score(places, langs, products, scale)
    return place(me_feat, [mine] + [swap(mine, "feat", mask) for mask in (1, 2, 3)])


def general(acts, grads, adapter, rank_sketch, out_sketch, held, perm):
    ex_dev = acts.shape[0]
    down = jnp.dot(adapter, rank_sketch, preferred_element_type=jnp.float32).astype(jnp.bfloat16)
    rank_part = jnp.einsum("esd,dr->esr", acts, down, preferred_element_type=jnp.float32)
    rank_side = lax.psum(rank_part, "feat")
    out_part = jnp.einsum("esd,dk->esk", grads, out_sketch, preferred_element_type=jnp.float32)
    out_side = lax.psum_scatter(out_part, "feat", scatter_dimension=2, tiled=True)
    grad = jnp.einsum("esk,esr->ekr", out_side, rank_side, precision=HIGHEST).reshape(ex_dev, -1)
    squares = lax.psum(jnp.sum(held * held, axis=1), "feat")
    unit = held * lax.rsqrt(squares + 1e-06)[:, None]
    onehot = ((perm % LANGS)[:, None] == jnp.arange(LANGS, dtype=jnp.int32)[None, :]).astype(jnp.float32)
    per_lang = perm.shape[0] * lax.axis_size("ex") // LANGS
    lang_mean = lax.psum(jnp.dot(onehot.T, unit, precision=HIGHEST), "ex") / per_lang
    inner, norm = lax.psum(
        (jnp.dot(grad, lang_mean.T, precision=HIGHEST), jnp.sum(grad * grad, axis=1)), "feat"
    )
    scale = jnp.sqrt(jnp.float32(KF * per_lang))
    return scale * inner * lax.rsqrt(norm + 1e-06)[:, None]


def solution(mesh):
    placed = (
        P("ex", None, "feat"),
        P("ex", None, "feat"),
        P("feat", None),
        P(),
        P("feat", None),
        P("ex", "feat"),
        P("ex"),
    )
    is_fast = mesh.shape["feat"] == 4 and mesh.shape["ex"] == 8
    body = fast if is_fast else general
    return jax.shard_map(body, mesh=mesh, in_specs=placed, out_specs=P("ex", None), check_vma=False)
```

time: 268 us -> 110 us (0.41)
  waiting for transfers between devices: 196 us -> 27.2 us
  starting transfers between devices: 0.09 us -> 46.4 us
  blocking collectives: 33.3 us -> 0 us
  Pallas kernels: 0 us -> 24 us
  matrix products: 23.9 us -> 0 us
  between operations: 13.2 us -> 0.34 us
  other arithmetic: 0.84 us -> 6.54 us
  local copies, waits for them, and re-layouts: 0.38 us -> 5.01 us
    psum x2 -> x0, waiting for transfers between devices: 118 us -> none  [the longest x1 64.1 us: shards(): rank_side = lax.psum(rank_part, 'feat')]
    reduce_scatter x1 -> x0, waiting for transfers between devices: 78.1 us -> none  [shards(): lax.psum_scatter(out_part, 'feat', scatter_dimension=2, tiled=True)]
    ppermute x0 -> x30, starting transfers between devices: none -> 46.4 us  [the longest x13 21.5 us: swap(): lax.ppermute(x, axis, [(i, i ^ mask) for i in range(lax.axis_size(axis))])]
    psum x2 -> x0, blocking collectives: 33.3 us -> none  [the longest x1 19.3 us: shards(): inner, squares = lax.psum((inner_part, square_part), 'feat')]
    ppermute x0 -> x30, waiting for transfers between devices: none -> 27.2 us  [the longest x13 16.9 us: swap(): lax.ppermute(x, axis, [(i, i ^ mask) for i in range(lax.axis_size(axis))])]
    pallas_call x0 -> x8, Pallas kernels: none -> 24 us  [the longest x3 17.9 us: project(): pl.pallas_call(kernel, out_shape=[jax.ShapeDtypeStruct(piece, jnp.float32...]
    dot_general x5 -> x0, matrix products: 23.9 us -> none  [the longest x1 9.45 us: shards(): jnp.einsum('esd,dk->esk', output_gradient_rows, output_side_sketch, prefe...]
    add x0 -> x8, other arithmetic: none -> 5.82 us  [the longest x1 1.82 us: ordered(): sums.append(got1[1] + after(raw2[1], langs[0]))]
  transfers between devices with their start and end apart: 3 -> 30, of which waited for: 3 -> 11; matrix products, arithmetic and copies ran while one was open for 6% -> 5% of each run, Pallas kernels for 0% -> 14%
where the time goes in v1:
time: 110 us
  starting transfers between devices  46.4 us (42%)
  waiting for transfers between devices  27.2 us (25%)
  Pallas kernels  24 us (22%)
  other arithmetic  6.54 us (6%)
  local copies, waits for them, and re-layouts  5.01 us (5%)
    ppermute x13, starting transfers between devices, swap(): lax.ppermute(x, axis, [(i, i ^ mask) for i in range(lax.axis_size(axis))])  21.5 us
    pallas_call x3, Pallas kernels, project(): pl.pallas_call(kernel, out_shape=[jax.ShapeDtypeStruct(piece, jnp.float32...  17.9 us
    ppermute x13, waiting for transfers between devices, swap(): lax.ppermute(x, axis, [(i, i ^ mask) for i in range(lax.axis_size(axis))])  16.9 us
    ppermute x2, starting transfers between devices, ordered(): got2 = [lax.ppermute(x, 'feat', ends_in) for x in raw2]  9.72 us
    ppermute x2, starting transfers between devices, ordered(): got1 = [lax.ppermute(x, 'feat', ends_in) for x in raw1]  5.22 us
    unnamed x16, local copies, waits for them, and re-layouts  4.33 us
    ppermute x1, waiting for transfers between devices, ordered(): far.append(lax.ppermute(sums[1], 'feat', far_pairs))  3.97 us
    ppermute x2, waiting for transfers between devices, ordered(): langs = langs + [lax.ppermute(x, 'ex', cross[1]) for x in langs]  3.44 us
  transfers between devices with their start and end apart: 30, of which 11 were waited for; matrix products, arithmetic and copies ran while one was open for 5% of the time, Pallas kernels for 14%

profile of v1, /device:TPU:0, one launch (start us, length us, event | category | flops | bytes accessed | tf_op | source)
XLA Modules:
  0.0 109.5 jit_solution(620880410653043431)
XLA Ops:
  1.4 5.7 %project.3 = (f32[2,384,128]{2,1,0:T(8,128)}, f32[2,384,128]{2,1,0:T(8,128)}, bf16[1024,128]{1,0:T(8,128)(2,1)}, f32[32,1]{1,0:T(8,128)}) custom-call(s32[8]{0:T(128)} %add.73.order, bf16[4096,1024]{1,0:T(8,128)(2,1)} %bitcast.38, bf16[4096,1024]{1,0:T(8,128)(2,1)} %bitcast.41, bf16[1024,128]{1,0:T(8,128)(2,1)} %adapter_ref.1, bf16[64,128]{1,0:T(8,128)(2,1)} %bitcast.46, ...), custom_call_target="tpu_custom_call" | custom-call | flops 536870912 | bytes 4980736 | tf_op jit(solution)/shard_map/project/pallas_call | solution.py:74
  7.0 3.1 %collective-permute-start = (f32[32,1]{1,0:T(8,128)}, f32[32,1]{1,0:T(8,128)S(1)}, u32[]{:S(2)}, u32[]{:S(2)}) collective-permute-start(f32[32,1]{1,0:T(8,128)} %get-tuple-element.38.refs_0_), channel_id=1, source_target_pairs={{0,1},{1,0},{2,3},{3,2},{4,5},{5,4},{6,7},{7,6},{8,9},{9,8},{10,11... | collective-permute-start | bytes 392 | tf_op jit(solution)/shard_map/ppermute | solution.py:266
  10.1 2.6 %collective-permute-start.1 = (f32[32,1]{1,0:T(8,128)}, f32[32,1]{1,0:T(8,128)S(1)}, u32[]{:S(2)}, u32[]{:S(2)}) collective-permute-start(f32[32,1]{1,0:T(8,128)} %get-tuple-element.38.refs_0_), channel_id=1, source_target_pairs={{0,2},{1,3},{2,0},{3,1},{4,6},{5,7},{6,4},{7,5},{8,10},{9,11},{10,... | collective-permute-start | bytes 392 | tf_op jit(solution)/shard_map/ppermute | solution.py:266
  12.7 2.3 %collective-permute-done.1.refs_2_ = f32[32,1]{1,0:T(8,128)S(1)} collective-permute-done((f32[32,1]{1,0:T(8,128)}, f32[32,1]{1,0:T(8,128)S(1)}, u32[]{:S(2)}, u32[]{:S(2)}) %collective-permute-start.1) | collective-permute-done | bytes 160 | tf_op jit(solution)/shard_map/ppermute | solution.py:266
  15.0 3.4 %collective-permute-done.2.refs_3_ = f32[32,1]{1,0:T(8,128)S(1)} collective-permute-done((f32[32,1]{1,0:T(8,128)}, f32[32,1]{1,0:T(8,128)S(1)}, u32[]{:S(2)}, u32[]{:S(2)}) %collective-permute-start.2) | collective-permute-done | bytes 160 | tf_op jit(solution)/shard_map/ppermute | solution.py:266
  20.0 2.0 %collective-permute-start.8 = (f32[2,384,128]{2,1,0:T(8,128)}, f32[2,384,128]{2,1,0:T(8,128)S(1)}, u32[]{:S(2)}, u32[]{:S(2)}) collective-permute-start(f32[2,384,128]{2,1,0:T(8,128)} %get-tuple-element.49), channel_id=1, source_target_pairs={{0,1},{1,0},{2,3},{3,2},{4,5},{5,4},{6,7},{7,6},{8,9},{9,8},{10,11... | collective-permute-start | bytes 1179656 | tf_op jit(solution)/shard_map/ppermute | solution.py:266
  25.6 4.7 %project.4 = (f32[2,384,128]{2,1,0:T(8,128)}, f32[2,384,128]{2,1,0:T(8,128)}) custom-call(s32[8]{0:T(128)} %add.73.order, bf16[4096,1024]{1,0:T(8,128)(2,1)} %bitcast.39, bf16[4096,1024]{1,0:T(8,128)(2,1)} %bitcast.42, bf16[1024,128]{1,0:T(8,128)(2,1)} %get-tuple-element.52.down_ref, bf16[1024,128]{1,0:T(8,128)(2,1)} %sketch_ref.5), custom_call_target="tpu_custom_call" | custom-call | flops 536870912 | bytes 4980736 | tf_op jit(solution)/shard_map/project/pallas_call | solution.py:74
  30.3 1.8 %collective-permute-done.4.refs_3_ = f32[2,384,128]{2,1,0:T(8,128)S(1)} collective-permute-done((f32[2,384,128]{2,1,0:T(8,128)}, f32[2,384,128]{2,1,0:T(8,128)S(1)}, u32[]{:S(2)}, u32[]{:S(2)}) %collective-permute-start.4) | collective-permute-done | bytes 393248 | tf_op jit(solution)/shard_map/ppermute | solution.py:266
  33.2 1.9 %collective-permute-start.10 = (f32[2,384,128]{2,1,0:T(8,128)}, f32[2,384,128]{2,1,0:T(8,128)S(1)}, u32[]{:S(2)}, u32[]{:S(2)}) collective-permute-start(f32[2,384,128]{2,1,0:T(8,128)} %get-tuple-element.55), channel_id=1, source_target_pairs={{0,1},{3,2},{4,5},{7,6},{8,9},{11,10},{12,13},{15,14},{16,17},{19,... | collective-permute-start | bytes 1179656 | tf_op jit(solution)/shard_map/ppermute | solution.py:318
  35.3 5.3 %collective-permute-done.8.refs_3_ = f32[2,384,128]{2,1,0:T(8,128)S(1)} collective-permute-done((f32[2,384,128]{2,1,0:T(8,128)}, f32[2,384,128]{2,1,0:T(8,128)S(1)}, u32[]{:S(2)}, u32[]{:S(2)}) %collective-permute-start.8) | collective-permute-done | bytes 393248 | tf_op jit(solution)/shard_map/ppermute | solution.py:266
  40.6 1.8 %add.82 = f32[2,384,128]{2,1,0:T(8,128)} add(f32[2,384,128]{2,1,0:T(8,128)S(1)} %collective-permute-done.8.refs_3_, f32[2,384,128]{2,1,0:T(8,128)} %get-tuple-element.51) | non-fusion elementwise | flops 98304 | bytes 1179648 | tf_op jit(solution)/shard_map/add | solution.py:319
  42.3 7.5 %project.5 = (f32[2,384,128]{2,1,0:T(8,128)}, f32[2,384,128]{2,1,0:T(8,128)}, f32[2,384,128]{2,1,0:T(8,128)}, f32[2,384,128]{2,1,0:T(8,128)}) custom-call(s32[8]{0:T(128)} %add.73.order, bf16[4096,1024]{1,0:T(8,128)(2,1)} %bitcast.40, bf16[4096,1024]{1,0:T(8,128)(2,1)} %bitcast.43, bf16[1024,128]{1,0:T(8,128)(2,1)} %get-tuple-element.52.down_ref, ...), custom_call_target="tpu_custom_call" | custom-call | flops 1073741824 | bytes 9961472 | tf_op jit(solution)/shard_map/project/pallas_call | solution.py:74
  51.2 3.3 %collective-permute-start.14 = (f32[2,384,128]{2,1,0:T(8,128)S(1)}, f32[2,384,128]{2,1,0:T(8,128)S(1)}, u32[]{:S(2)}, u32[]{:S(2)}) collective-permute-start(f32[2,384,128]{2,1,0:T(8,128)S(1)} %copy-done.6), channel_id=1, source_target_pairs={{0,1},{3,2},{4,5},{7,6},{8,9},{11,10},{12,13},{15,14},{16,17},{19,... | collective-permute-start | bytes 1179656 | tf_op jit(solution)/shard_map/ppermute | solution.py:318
  60.1 1.6 %collective-permute-start.13 = (f32[4,64,256]{2,1,0:T(8,128)S(1)}, f32[4,64,256]{2,1,0:T(8,128)}, u32[]{:S(2)}, u32[]{:S(2)}) collective-permute-start(f32[4,64,256]{2,1,0:T(8,128)S(1)} %pad_maximum_fusion.refs_0_), channel_id=1, source_target_pairs={{0,8},{4,20},{8,0},{12,28},{16,24},{20,4},{24,16},{28,12},{1,9},{5... | collective-permute-start | bytes 786440 | tf_op jit(solution)/shard_map/ppermute | solution.py:331
  62.3 1.7 %collective-permute-done.14 = f32[2,384,128]{2,1,0:T(8,128)S(1)} collective-permute-done((f32[2,384,128]{2,1,0:T(8,128)S(1)}, f32[2,384,128]{2,1,0:T(8,128)S(1)}, u32[]{:S(2)}, u32[]{:S(2)}) %collective-permute-start.14) | collective-permute-done | bytes 393248 | tf_op jit(solution)/shard_map/ppermute | solution.py:318
  64.0 8.4 %collective-permute-start.24 = (f32[2,384,128]{2,1,0:T(8,128)}, f32[2,384,128]{2,1,0:T(8,128)S(1)}, u32[]{:S(2)}, u32[]{:S(2)}) collective-permute-start(f32[2,384,128]{2,1,0:T(8,128)} %get-tuple-element.60), channel_id=1, source_target_pairs={{0,1},{3,2},{4,5},{7,6},{8,9},{11,10},{12,13},{15,14},{16,17},{19,... | collective-permute-start | bytes 1179656 | tf_op jit(solution)/shard_map/ppermute | solution.py:325
  73.7 1.8 %add.85 = f32[2,384,128]{2,1,0:T(8,128)} add(f32[2,384,128]{2,1,0:T(8,128)S(1)} %collective-permute-done.14, f32[2,384,128]{2,1,0:T(8,128)} %get-tuple-element.60) | non-fusion elementwise | flops 98304 | bytes 1179648 | tf_op jit(solution)/shard_map/add | solution.py:332
  75.5 1.6 %collective-permute-start.15 = (f32[4,64,256]{2,1,0:T(8,128)S(1)}, f32[4,64,256]{2,1,0:T(8,128)}, u32[]{:S(2)}, u32[]{:S(2)}) collective-permute-start(f32[4,64,256]{2,1,0:T(8,128)S(1)} %pad_maximum_fusion.refs_0_), channel_id=1, source_target_pairs={{0,16},{4,12},{8,24},{12,4},{16,0},{20,28},{24,8},{28,20},{1,17},{... | collective-permute-start | bytes 786440 | tf_op jit(solution)/shard_map/ppermute | solution.py:335
  82.0 2.8 %collective-permute-done.19.refs_3_ = f32[4,64,256]{2,1,0:T(8,128)} collective-permute-done((f32[4,64,256]{2,1,0:T(8,128)}, f32[4,64,256]{2,1,0:T(8,128)}, u32[]{:S(2)}, u32[]{:S(2)}) %collective-permute-start.19) | collective-permute-done | bytes 262176 | tf_op jit(solution)/shard_map/ppermute | solution.py:335
  85.3 4.0 %collective-permute-done.26.refs_4_ = f32[2,384,128]{2,1,0:T(8,128)S(1)} collective-permute-done((f32[2,384,128]{2,1,0:T(8,128)}, f32[2,384,128]{2,1,0:T(8,128)S(1)}, u32[]{:S(2)}, u32[]{:S(2)}) %collective-permute-start.26) | collective-permute-done | bytes 393248 | tf_op jit(solution)/shard_map/ppermute | solution.py:320
  92.8 2.0 %score.1.refs_0_ = f32[16,64]{1,0:T(8,128)S(1)} custom-call(s32[12]{0:T(128)S(1)} %stack.57.places_ref, f32[4,64,256]{2,1,0:T(8,128)S(1)} %pad_maximum_fusion.refs_0_, f32[4,64,256]{2,1,0:T(8,128)} %collective-permute-done.13.refs_1_, f32[4,64,256]{2,1,0:T(8,128)} %collective-permute-done.15.refs_2_, f32[4,64,256]{2,1,0:T(8,128)} %collective-permute-done.19.refs_3_, ...), custom_call_target="tpu_custom_call" | custom-call | tf_op jit(solution)/shard_map/score/pallas_call | solution.py:236
  94.8 7.2 %collective-permute-start.27 = (f32[16,64]{1,0:T(8,128)S(1)}, f32[16,64]{1,0:T(8,128)S(1)}, u32[]{:S(2)}, u32[]{:S(2)}) collective-permute-start(f32[16,64]{1,0:T(8,128)S(1)} %score.1.refs_0_), channel_id=1, source_target_pairs={{0,1},{1,0},{2,3},{3,2},{4,5},{5,4},{6,7},{7,6},{8,9},{9,8},{10,11... | collective-permute-start | bytes 12296 | tf_op jit(solution)/shard_map/ppermute | solution.py:266
  104.9 1.6 %collective-permute-done.28.refs_2_ = f32[16,64]{1,0:T(8,128)S(1)} collective-permute-done((f32[16,64]{1,0:T(8,128)S(1)}, f32[16,64]{1,0:T(8,128)S(1)}, u32[]{:S(2)}, u32[]{:S(2)}) %collective-permute-start.28) | collective-permute-done | bytes 4128 | tf_op jit(solution)/shard_map/ppermute | solution.py:266
  106.5 2.4 %collective-permute-done.29.refs_3_ = f32[16,64]{1,0:T(8,128)S(1)} collective-permute-done((f32[16,64]{1,0:T(8,128)S(1)}, f32[16,64]{1,0:T(8,128)S(1)}, u32[]{:S(2)}, u32[]{:S(2)}) %collective-permute-start.29) | collective-permute-done | bytes 4128 | tf_op jit(solution)/shard_map/ppermute | solution.py:266
  (74 shorter events, 28.7 us)
Async XLA Ops:
  7.0 5.7 %collective-permute-start = (f32[32,1]{1,0:T(8,128)}, f32[32,1]{1,0:T(8,128)S(1)}, u32[]{:S(2)}, u32[]{:S(2)}) collective-permute-start(f32[32,1]{1,0:T(8,128)} %get-tuple-element.38.refs_0_), channel_id=1, source_target_pairs={{0,1},{1,0},{2,3},{3,2},{4,5},{5,4},{6,7},{7,6},{8,9},{9,8},{10,11... | collective-permute-start | bytes 392 | tf_op jit(solution)/shard_map/ppermute | solution.py:266
  12.7 5.7 %collective-permute-start.2 = (f32[32,1]{1,0:T(8,128)}, f32[32,1]{1,0:T(8,128)S(1)}, u32[]{:S(2)}, u32[]{:S(2)}) collective-permute-start(f32[32,1]{1,0:T(8,128)} %get-tuple-element.38.refs_0_), channel_id=1, source_target_pairs={{0,3},{1,2},{2,1},{3,0},{4,7},{5,6},{6,5},{7,4},{8,11},{9,10},{10,... | collective-permute-start | bytes 392 | tf_op jit(solution)/shard_map/ppermute | solution.py:266
  19.9 12.3 %collective-permute-start.4 = (f32[2,384,128]{2,1,0:T(8,128)}, f32[2,384,128]{2,1,0:T(8,128)S(1)}, u32[]{:S(2)}, u32[]{:S(2)}) collective-permute-start(f32[2,384,128]{2,1,0:T(8,128)} %get-tuple-element.41), channel_id=1, source_target_pairs={{0,1},{1,0},{2,3},{3,2},{4,5},{5,4},{6,7},{7,6},{8,9},{9,8},{10,11... | collective-permute-start | bytes 1179656 | tf_op jit(solution)/shard_map/ppermute | solution.py:266
  20.0 20.6 %collective-permute-start.8 = (f32[2,384,128]{2,1,0:T(8,128)}, f32[2,384,128]{2,1,0:T(8,128)S(1)}, u32[]{:S(2)}, u32[]{:S(2)}) collective-permute-start(f32[2,384,128]{2,1,0:T(8,128)} %get-tuple-element.49), channel_id=1, source_target_pairs={{0,1},{1,0},{2,3},{3,2},{4,5},{5,4},{6,7},{7,6},{8,9},{9,8},{10,11... | collective-permute-start | bytes 1179656 | tf_op jit(solution)/shard_map/ppermute | solution.py:266
  22.0 11.2 %collective-permute-start.5 = (f32[64,256]{1,0:T(8,128)S(1)}, f32[64,256]{1,0:T(8,128)S(1)}, u32[]{:S(2)}, u32[]{:S(2)}) collective-permute-start(f32[64,256]{1,0:T(8,128)S(1)} %get-tuple-element.73), channel_id=1, source_target_pairs={{0,8},{4,12},{8,0},{12,4},{16,24},{20,28},{24,16},{28,20},{1,9},{5... | collective-permute-start | bytes 196616 | tf_op jit(solution)/shard_map/ppermute | solution.py:266
  23.6 9.6 %collective-permute-start.6 = (f32[64,256]{1,0:T(8,128)S(1)}, f32[64,256]{1,0:T(8,128)S(1)}, u32[]{:S(2)}, u32[]{:S(2)}) collective-permute-start(f32[64,256]{1,0:T(8,128)S(1)} %get-tuple-element.72), channel_id=1, source_target_pairs={{0,16},{4,20},{8,24},{12,28},{16,0},{20,4},{24,8},{28,12},{1,17},{... | collective-permute-start | bytes 196616 | tf_op jit(solution)/shard_map/ppermute | solution.py:266
  25.1 8.1 %collective-permute-start.7 = (f32[64,256]{1,0:T(8,128)S(1)}, f32[64,256]{1,0:T(8,128)S(1)}, u32[]{:S(2)}, u32[]{:S(2)}) collective-permute-start(f32[64,256]{1,0:T(8,128)S(1)} %get-tuple-element.71), channel_id=1, source_target_pairs={{0,24},{4,28},{8,16},{12,20},{16,8},{20,12},{24,0},{28,4},{1,25},{... | collective-permute-start | bytes 196616 | tf_op jit(solution)/shard_map/ppermute | solution.py:266
  33.2 25.7 %collective-permute-start.10 = (f32[2,384,128]{2,1,0:T(8,128)}, f32[2,384,128]{2,1,0:T(8,128)S(1)}, u32[]{:S(2)}, u32[]{:S(2)}) collective-permute-start(f32[2,384,128]{2,1,0:T(8,128)} %get-tuple-element.55), channel_id=1, source_target_pairs={{0,1},{3,2},{4,5},{7,6},{8,9},{11,10},{12,13},{15,14},{16,17},{19,... | collective-permute-start | bytes 1179656 | tf_op jit(solution)/shard_map/ppermute | solution.py:318
  35.2 14.7 %collective-permute-start.9 = (f32[64,256]{1,0:T(8,128)S(1)}, f32[64,256]{1,0:T(8,128)S(1)}, u32[]{:S(2)}, u32[]{:S(2)}) collective-permute-start(f32[64,256]{1,0:T(8,128)S(1)} %add_add_fusion), channel_id=1, source_target_pairs={{0,1},{1,0},{2,3},{3,2},{4,5},{5,4},{6,7},{7,6},{8,9},{9,8},{10,11... | collective-permute-start | bytes 196616 | tf_op jit(solution)/shard_map/ppermute | solution.py:266
  49.9 7.8 %collective-permute-start.11 = (f32[2,64,256]{2,1,0:T(8,128)S(1)}, f32[2,64,256]{2,1,0:T(8,128)S(1)}, u32[]{:S(2)}, u32[]{:S(2)}) collective-permute-start(f32[2,64,256]{2,1,0:T(8,128)S(1)} %pad_maximum_fusion.1), channel_id=1, source_target_pairs={{1,3},{2,0},{5,7},{6,4},{9,11},{10,8},{13,15},{14,12},{17,19},{18,... | collective-permute-start | bytes 393224 | tf_op jit(solution)/shard_map/ppermute | solution.py:327
  51.2 12.8 %collective-permute-start.14 = (f32[2,384,128]{2,1,0:T(8,128)S(1)}, f32[2,384,128]{2,1,0:T(8,128)S(1)}, u32[]{:S(2)}, u32[]{:S(2)}) collective-permute-start(f32[2,384,128]{2,1,0:T(8,128)S(1)} %copy-done.6), channel_id=1, source_target_pairs={{0,1},{3,2},{4,5},{7,6},{8,9},{11,10},{12,13},{15,14},{16,17},{19,... | collective-permute-start | bytes 1179656 | tf_op jit(solution)/shard_map/ppermute | solution.py:318
  54.5 17.9 %collective-permute-start.16 = (f32[2,384,128]{2,1,0:T(8,128)}, f32[2,384,128]{2,1,0:T(8,128)S(1)}, u32[]{:S(2)}, u32[]{:S(2)}) collective-permute-start(f32[2,384,128]{2,1,0:T(8,128)} %get-tuple-element.57), channel_id=1, source_target_pairs={{0,1},{3,2},{4,5},{7,6},{8,9},{11,10},{12,13},{15,14},{16,17},{19,... | collective-permute-start | bytes 1179656 | tf_op jit(solution)/shard_map/ppermute | solution.py:325
  57.7 19.5 %collective-permute-start.18 = (f32[2,384,128]{2,1,0:T(8,128)S(1)}, f32[2,384,128]{2,1,0:T(8,128)S(1)}, u32[]{:S(2)}, u32[]{:S(2)}) collective-permute-start(f32[2,384,128]{2,1,0:T(8,128)S(1)} %add.78), channel_id=1, source_target_pairs={{1,3},{2,0},{5,7},{6,4},{9,11},{10,8},{13,15},{14,12},{17,19},{18,... | collective-permute-start | bytes 1179656 | tf_op jit(solution)/shard_map/ppermute | solution.py:314
  60.1 15.4 %collective-permute-start.13 = (f32[4,64,256]{2,1,0:T(8,128)S(1)}, f32[4,64,256]{2,1,0:T(8,128)}, u32[]{:S(2)}, u32[]{:S(2)}) collective-permute-start(f32[4,64,256]{2,1,0:T(8,128)S(1)} %pad_maximum_fusion.refs_0_), channel_id=1, source_target_pairs={{0,8},{4,20},{8,0},{12,28},{16,24},{20,4},{24,16},{28,12},{1,9},{5... | collective-permute-start | bytes 786440 | tf_op jit(solution)/shard_map/ppermute | solution.py:331
  61.6 15.9 %collective-permute-start.17 = (f32[2,384,128]{2,1,0:T(8,128)S(1)}, f32[2,384,128]{2,1,0:T(8,128)S(1)}, u32[]{:S(2)}, u32[]{:S(2)}) collective-permute-start(f32[2,384,128]{2,1,0:T(8,128)S(1)} %add.83), channel_id=1, source_target_pairs={{1,2},{2,1},{5,6},{6,5},{9,10},{10,9},{13,14},{14,13},{17,18},{18,... | collective-permute-start | bytes 1179656 | tf_op jit(solution)/shard_map/ppermute | solution.py:329
  64.0 20.8 %collective-permute-start.24 = (f32[2,384,128]{2,1,0:T(8,128)}, f32[2,384,128]{2,1,0:T(8,128)S(1)}, u32[]{:S(2)}, u32[]{:S(2)}) collective-permute-start(f32[2,384,128]{2,1,0:T(8,128)} %get-tuple-element.60), channel_id=1, source_target_pairs={{0,1},{3,2},{4,5},{7,6},{8,9},{11,10},{12,13},{15,14},{16,17},{19,... | collective-permute-start | bytes 1179656 | tf_op jit(solution)/shard_map/ppermute | solution.py:325
  72.4 16.9 %collective-permute-start.26 = (f32[2,384,128]{2,1,0:T(8,128)}, f32[2,384,128]{2,1,0:T(8,128)S(1)}, u32[]{:S(2)}, u32[]{:S(2)}) collective-permute-start(f32[2,384,128]{2,1,0:T(8,128)} %add.82), channel_id=1, source_target_pairs={{1,3},{2,0},{5,7},{6,4},{9,11},{10,8},{13,15},{14,12},{17,19},{18,... | collective-permute-start | bytes 1179656 | tf_op jit(solution)/shard_map/ppermute | solution.py:320
  75.5 6.5 %collective-permute-start.15 = (f32[4,64,256]{2,1,0:T(8,128)S(1)}, f32[4,64,256]{2,1,0:T(8,128)}, u32[]{:S(2)}, u32[]{:S(2)}) collective-permute-start(f32[4,64,256]{2,1,0:T(8,128)S(1)} %pad_maximum_fusion.refs_0_), channel_id=1, source_target_pairs={{0,16},{4,12},{8,24},{12,4},{16,0},{20,28},{24,8},{28,20},{1,17},{... | collective-permute-start | bytes 786440 | tf_op jit(solution)/shard_map/ppermute | solution.py:335
  77.2 7.6 %collective-permute-start.19 = (f32[4,64,256]{2,1,0:T(8,128)}, f32[4,64,256]{2,1,0:T(8,128)}, u32[]{:S(2)}, u32[]{:S(2)}) collective-permute-start(f32[4,64,256]{2,1,0:T(8,128)} %collective-permute-done.13.refs_1_), channel_id=1, source_target_pairs={{0,16},{4,12},{8,24},{12,4},{16,0},{20,28},{24,8},{28,20},{1,17},{... | collective-permute-start | bytes 786440 | tf_op jit(solution)/shard_map/ppermute | solution.py:335
  77.5 11.8 %collective-permute-start.25 = (f32[2,384,128]{2,1,0:T(8,128)}, f32[2,384,128]{2,1,0:T(8,128)S(1)}, u32[]{:S(2)}, u32[]{:S(2)}) collective-permute-start(f32[2,384,128]{2,1,0:T(8,128)} %add.85), channel_id=1, source_target_pairs={{1,2},{2,1},{5,6},{6,5},{9,10},{10,9},{13,14},{14,13},{17,18},{18,... | collective-permute-start | bytes 1179656 | tf_op jit(solution)/shard_map/ppermute | solution.py:333
  82.0 9.8 %collective-permute-start.20 = (f32[4,64,256]{2,1,0:T(8,128)S(1)}, f32[4,64,256]{2,1,0:T(8,128)S(1)}, u32[]{:S(2)}, u32[]{:S(2)}) collective-permute-start(f32[4,64,256]{2,1,0:T(8,128)S(1)} %pad_maximum_fusion.refs_0_), channel_id=1, source_target_pairs={{0,4},{4,0},{8,12},{12,8},{16,20},{20,16},{24,28},{28,24},{1,5},{5... | collective-permute-start | bytes 786440 | tf_op jit(solution)/shard_map/ppermute | solution.py:339
  84.8 7.0 %collective-permute-start.21 = (f32[4,64,256]{2,1,0:T(8,128)}, f32[4,64,256]{2,1,0:T(8,128)S(1)}, u32[]{:S(2)}, u32[]{:S(2)}) collective-permute-start(f32[4,64,256]{2,1,0:T(8,128)} %collective-permute-done.13.refs_1_), channel_id=1, source_target_pairs={{0,4},{4,0},{8,12},{12,8},{16,20},{20,16},{24,28},{28,24},{1,5},{5... | collective-permute-start | bytes 786440 | tf_op jit(solution)/shard_map/ppermute | solution.py:339
  84.8 7.0 %collective-permute-start.22 = (f32[4,64,256]{2,1,0:T(8,128)}, f32[4,64,256]{2,1,0:T(8,128)S(1)}, u32[]{:S(2)}, u32[]{:S(2)}) collective-permute-start(f32[4,64,256]{2,1,0:T(8,128)} %collective-permute-done.15.refs_2_), channel_id=1, source_target_pairs={{0,4},{4,0},{8,12},{12,8},{16,20},{20,16},{24,28},{28,24},{1,5},{5... | collective-permute-start | bytes 786440 | tf_op jit(solution)/shard_map/ppermute | solution.py:339
  94.8 10.1 %collective-permute-start.27 = (f32[16,64]{1,0:T(8,128)S(1)}, f32[16,64]{1,0:T(8,128)S(1)}, u32[]{:S(2)}, u32[]{:S(2)}) collective-permute-start(f32[16,64]{1,0:T(8,128)S(1)} %score.1.refs_0_), channel_id=1, source_target_pairs={{0,1},{1,0},{2,3},{3,2},{4,5},{5,4},{6,7},{7,6},{8,9},{9,8},{10,11... | collective-permute-start | bytes 12296 | tf_op jit(solution)/shard_map/ppermute | solution.py:266
  (14 other events, 64.4 us)

commit v2 on v1

--- a/solution.py
+++ b/solution.py
@@ -85,6 +85,7 @@
             bytes_accessed=count * rows * (width * 4 + ko * 6),
             transcendentals=0,
         ),
+        compiler_params=pltpu.CompilerParams(vmem_limit_bytes=SMALL),
         name="project",
     )(order, acts, grads, *operands)
 
@@ -125,30 +126,8 @@
     )(me, held, lang.reshape(1, rows), *squares)
 
 
-def product_kernel(middle_ref, *refs):
-    *part_refs, o_ref, square_ref, own_ref, one_ref, two_ref, grad_ref, sem = refs
-    own = pltpu.make_async_copy(part_refs[0], own_ref, sem.at[0])
-    own.start()
-
-    def fetch(one, two):
-        copies = [
-            pltpu.make_async_copy(one, one_ref, sem.at[1]),
-            pltpu.make_async_copy(two, two_ref, sem.at[2]),
-        ]
-        for copy in copies:
-            copy.start()
-        for copy in copies:
-            copy.wait()
-
-    @pl.when(middle_ref[0] == 1)
-    def _():
-        fetch(part_refs[1], part_refs[2])
-
-    @pl.when(middle_ref[0] != 1)
-    def _():
-        fetch(part_refs[3], part_refs[4])
-
-    own.wait()
+def product_kernel(middle_ref, own_ref, r1_ref, r2_ref, r3_ref, r4_ref, o_ref, square_ref, grad_ref):
+    middle = middle_ref[0] == 1
     rows = own_ref.shape[1] * 2 // 3
     seq = rows // UNIT
     wide = own_ref.shape[2]
@@ -161,7 +140,7 @@
 
     def total(unit, start):
         block = (unit, pl.ds(start, seq), slice(None))
-        return own_ref[block] + one_ref[block] + two_ref[block]
+        return own_ref[block] + jnp.where(middle, r3_ref[block] + r4_ref[block], r1_ref[block] + r2_ref[block])
 
     for unit in range(PIECE):
         for pair in range(UNIT // 2):
@@ -198,10 +177,9 @@
             jax.ShapeDtypeStruct((wide // 4, 2 * count, 2 * wide), jnp.bfloat16),
             jax.ShapeDtypeStruct((count, 1), jnp.float32),
         ],
-        in_specs=[SMEM] + [pl.BlockSpec(memory_space=pl.ANY)] * len(parts),
+        in_specs=[SMEM] + [VMEM] * len(parts),
         out_specs=[VMEM] * 2,
-        scratch_shapes=[pltpu.VMEM(parts[0].shape, jnp.float32)] * 3
-        + [pltpu.VMEM((count, wide, wide), jnp.float32), pltpu.SemaphoreType.DMA((3,))],
+        scratch_shapes=[pltpu.VMEM((count, wide, wide), jnp.float32)],
         compiler_params=pltpu.CompilerParams(vmem_limit_bytes=SMALL),
         name="product",
     )(middle, *parts)
@@ -279,7 +257,6 @@
     n_ex = lax.axis_size("ex")
     _, _, width = acts.shape
     middle = (feat == 1) | (feat == 2)
-    left = feat < 2
     me_ex = ex.astype(jnp.int32).reshape(1)
     me_feat = feat.astype(jnp.int32).reshape(1)
 
@@ -287,63 +264,66 @@
     chunks = lax.dynamic_index_in_dim(base, feat, 0, keepdims=False)
     order = (chunks[:, None] * 2 + jnp.arange(2, dtype=jnp.int32)).reshape(-1)
     acts2, grads2 = acts.reshape(-1, width), grads.reshape(-1, width)
-    down_like = jax.ShapeDtypeStruct((width, 2 * rank_sketch.shape[1]), jnp.bfloat16)
+    adapter, rank_sketch, out_sketch, held, acts2, grads2 = (
+        pltpu.with_memory_space_constraint(x, pltpu.HBM)
+        for x in (adapter, rank_sketch.T, out_sketch, held, acts2, grads2)
+    )
+    down_like = jax.ShapeDtypeStruct((width, 2 * rank_sketch.shape[0]), jnp.bfloat16)
     square_like = jax.ShapeDtypeStruct((held.shape[0], 1), jnp.float32)
-    ends_in = [(0, 1), (3, 2)]
-    far_pairs = [(1, 3), (2, 0)]
-    near_pairs = [(1, 2), (2, 1)]
+    round_pairs = [(0, 1), (1, 3), (3, 2), (2, 0)]
+    inner_pairs = [(1, 2), (2, 1), (0, 0), (3, 3)]
     cross = [
         [(i, i ^ (2 if i % 2 == 0 else 4)) for i in range(n_ex)],
         [(i, i ^ (4 if i % 2 == 0 else 2)) for i in range(n_ex)],
         [(i, i ^ 1) for i in range(n_ex)],
     ]
 
+    def onward(raw, got):
+        return raw + jnp.where(middle, got, 0.0)
+
     *raw0, down, own_square = project(
-        first_kernel, order, 0, 2, acts2, grads2, [adapter, rank_sketch.T, out_sketch, held], [down_like, square_like]
+        first_kernel, order, 0, 2, acts2, grads2, [adapter, rank_sketch, out_sketch, held], [down_like, square_like]
     )
     squares = [own_square] + [swap(own_square, "feat", mask) for mask in (1, 2, 3)]
-    got0 = [swap(x, "feat", 1) for x in raw0]
-
-    other, *parts = lang_parts(me_ex, held, squares, perm % LANGS, n_ex)
+    got1 = [swap(x, "feat", 1) for x in raw0]
+    raw1 = project(more_kernel, order, 2, 2, acts2, grads2, [down, out_sketch], [])
+
+    other, *parts = lang_parts(me_ex, held, [squares[0]] + [after(x, raw1[0]) for x in squares[1:]], perm % LANGS, n_ex)
     other = swap(other, "ex", 1)
     parts = [x + other[i] for i, x in enumerate(parts)]
     scattered = [swap(parts[i], "ex", 2 * i) for i in range(1, n_ex // 2)]
-
-    raw1 = project(more_kernel, order, 2, 2, acts2, grads2, [after(down, *parts), out_sketch], [])
-    sums = [got0[0] + raw1[0]]
-    far = [lax.ppermute(sums[0], "feat", far_pairs)]
-    lang = after(parts[0], sums[0]) + sum(scattered)
+    sent2 = [onward(after(raw1[0], parts[1]), got1[0])]
+    lang = after(parts[0], sent2[0]) + sum(scattered)
     pair = swap(lang, "feat", 1)
-    raw1 = [after(x, lang) for x in raw1]
-    got1 = [lax.ppermute(x, "feat", ends_in) for x in raw1]
-    sums.append(got0[1] + raw1[1])
-    far.append(lax.ppermute(sums[1], "feat", far_pairs))
+    got2 = [lax.ppermute(after(sent2[0], lang), "feat", round_pairs)]
+    pair = jnp.stack([lang, pair])
+    far_pair = swap(pair, "feat", 2)
+    sent2.append(onward(after(raw1[1], pair), got1[1]))
+    got2.append(lax.ppermute(sent2[1], "feat", round_pairs))
     *raw2, own_a, own_b = project(
-        more_kernel, order, 4, 4, acts2, grads2, [after(down, sums[1]), out_sketch], []
+        more_kernel, order, 4, 4, acts2, grads2, [after(down, sent2[1]), out_sketch], []
     )
     own = [own_a, own_b]
-    got2 = [lax.ppermute(x, "feat", ends_in) for x in raw2]
-    pair = jnp.stack([after(lang, own_a), pair])
-    far_pair = [lax.ppermute(pair, "feat", far_pairs), lax.ppermute(pair, "feat", near_pairs)]
-    sums.append(got1[0] + after(raw2[0], pair))
-    near = [lax.ppermute(sums[2], "feat", near_pairs)]
-    langs = [jnp.concatenate([after(pair, sums[2]), far_pair[0] + far_pair[1]])]
+    sent3 = [onward(raw2[0], got2[0])]
+    got3 = [swap(sent3[0], "feat", 1)]
+    got4 = [lax.ppermute(sent3[0], "feat", inner_pairs)]
+    langs = [jnp.concatenate([after(pair, sent3[0]), far_pair])]
     langs = langs + [lax.ppermute(x, "ex", cross[0]) for x in langs]
-    sums.append(got1[1] + after(raw2[1], langs[0]))
-    near.append(lax.ppermute(sums[3], "feat", near_pairs))
-    langs[1] = after(langs[1], sums[3])
+    sent3.append(onward(after(raw2[1], langs[0]), got2[1]))
+    got3.append(swap(sent3[1], "feat", 1))
+    got4.append(lax.ppermute(sent3[1], "feat", inner_pairs))
+    langs[1] = after(langs[1], sent3[1])
     langs = langs + [lax.ppermute(x, "ex", cross[1]) for x in langs]
     is_middle = middle.astype(jnp.int32).reshape(1)
-    products = [product(is_middle, [after(own[0], langs[1]), got2[0], near[0], got0[0], far[0]])]
+    products = [product(is_middle, [after(own[0], langs[1]), got1[0], got2[0], got3[0], got4[0]])]
     langs[2:] = [after(x, products[0][1]) for x in langs[2:]]
     langs = langs + [lax.ppermute(x, "ex", cross[2]) for x in langs]
-    products.append(product(is_middle, [after(own[1], products[0][1]), got2[1], near[1], got0[1], far[1]]))
+    products.append(product(is_middle, [after(own[1], products[0][1]), got1[1], got2[1], got3[1], got4[1]]))
     one = jnp.where(ex % 2 == 0, 2, 4)
     two = 6 - one
     masks = [0, one, two, 6, 1, 1 ^ two, 1 ^ one, 7]
-    second = jnp.where(left, 2, 1)
     places = jnp.stack(
-        [jnp.asarray(x, jnp.int32) for x in [ex ^ m for m in masks] + [feat, feat ^ 1, second, second ^ 1]]
+        [jnp.asarray(x, jnp.int32) for x in [ex ^ m for m in masks] + [feat, feat ^ 1, feat ^ 2, feat ^ 3]]
     )
     per_lang = perm.shape[0] * n_ex // LANGS
     scale = (KF * per_lang) ** 0.5 / per_lang

time: 110 us -> 96.9 us (0.88)
  starting transfers between devices: 46.4 us -> 35.8 us
  waiting for transfers between devices: 27.2 us -> 33.5 us
  other arithmetic: 6.54 us -> 2.53 us
  Pallas kernels: 24 us -> 20.7 us
  local copies, waits for them, and re-layouts: 5.01 us -> 3.61 us
    ppermute x10 -> x4, starting transfers between devices: 20.8 us -> 9.6 us  [the longest x1 4.49 us: ordered(): got4 = [lax.ppermute(sent3[0], 'feat', inner_pairs)]]
    ppermute x13 -> x16, waiting for transfers between devices: 16.9 us -> 28 us  [swap(): lax.ppermute(x, axis, [(i, i ^ mask) for i in range(lax.axis_size(axis))])]
    ppermute x10 -> x4, waiting for transfers between devices: 6.81 us -> 0.94 us  [the longest x1 0.93 us: ordered(): got2.append(lax.ppermute(sent2[1], 'feat', round_pairs))]
    pallas_call x3, Pallas kernels: 17.9 us -> 13.7 us  [project(): pl.pallas_call(kernel, out_shape=[jax.ShapeDtypeStruct(piece, jnp.float32...]
    add x6 -> x5, other arithmetic: 5.7 us -> 1.72 us  [the longest x4 1.7 us: onward(): return raw + jnp.where(middle, got, 0.0)]
    ppermute x1, waiting for transfers between devices: 0.01 us -> 3.81 us  [ordered(): langs = langs + [lax.ppermute(x, 'ex', cross[0]) for x in langs]]
    ppermute x2, waiting for transfers between devices: 3.44 us -> 0.01 us  [ordered(): langs = langs + [lax.ppermute(x, 'ex', cross[1]) for x in langs]]
    unnamed x16 -> x11, local copies, waits for them, and re-layouts: 4.33 us -> 3.43 us
  transfers between devices with their start and end apart: 30 -> 27, of which waited for: 11 -> 9; matrix products, arithmetic and copies ran while one was open for 5% -> 2% of each run, Pallas kernels for 14% -> 13%
where the time goes in v2:
time: 96.9 us; the launch traced here: 96.3 us
  starting transfers between devices  35.8 us (37%)
  waiting for transfers between devices  33.5 us (35%)
  Pallas kernels  20.7 us (21%)
  local copies, waits for them, and re-layouts  3.61 us (4%)
  other arithmetic  2.53 us (3%)
    ppermute x16, waiting for transfers between devices, swap(): lax.ppermute(x, axis, [(i, i ^ mask) for i in range(lax.axis_size(axis))])  28 us
    ppermute x16, starting transfers between devices, swap(): lax.ppermute(x, axis, [(i, i ^ mask) for i in range(lax.axis_size(axis))])  21 us
    pallas_call x3, Pallas kernels, project(): pl.pallas_call(kernel, out_shape=[jax.ShapeDtypeStruct(piece, jnp.float32...  13.7 us
    ppermute x1, starting transfers between devices, ordered(): got4 = [lax.ppermute(sent3[0], 'feat', inner_pairs)]  4.49 us
    ppermute x1, waiting for transfers between devices, ordered(): langs = langs + [lax.ppermute(x, 'ex', cross[0]) for x in langs]  3.81 us
    unnamed x11, local copies, waits for them, and re-layouts  3.43 us
    ppermute x2, starting transfers between devices, ordered(): langs = langs + [lax.ppermute(x, 'ex', cross[1]) for x in langs]  3.07 us
    pallas_call x2, Pallas kernels, product(): pl.pallas_call(product_kernel, out_shape=[jax.ShapeDtypeStruct((wide // 4...  2.66 us
  transfers between devices with their start and end apart: 27, of which 9 were waited for; matrix products, arithmetic and copies ran while one was open for 2% of the time, Pallas kernels for 13%

profile of v2, /device:TPU:0, one launch (start us, length us, event | category | flops | bytes accessed | tf_op | source)
XLA Modules:
  0.0 96.3 jit_solution(9736883823203350820)
XLA Ops:
  0.8 4.0 %project.3 = (f32[2,384,128]{2,1,0:T(8,128)S(1)}, f32[2,384,128]{2,1,0:T(8,128)S(1)}, bf16[1024,128]{1,0:T(8,128)(2,1)S(1)}, f32[32,1]{1,0:T(8,128)S(1)}) custom-call(s32[8]{0:T(128)S(1)} %add.70.order, bf16[4096,1024]{1,0:T(8,128)(2,1)} %bitcast.38, bf16[4096,1024]{1,0:T(8,128)(2,1)} %bitcast.41, bf16[1024,128]{1,0:T(8,128)(2,1)} %adapter_ref.1, ...), custom_call_target="tpu_custom_call" | custom-call | flops 536870912 | bytes 4980736 | tf_op jit(solution)/shard_map/project/pallas_call | solution.py:74
  4.9 5.1 %collective-permute-start.2 = (f32[32,1]{1,0:T(8,128)S(1)}, f32[32,1]{1,0:T(8,128)S(1)}, u32[]{:S(2)}, u32[]{:S(2)}) collective-permute-start(f32[32,1]{1,0:T(8,128)S(1)} %get-tuple-element.39.refs_0_), channel_id=1, source_target_pairs={{0,3},{1,2},{2,1},{3,0},{4,7},{5,6},{6,5},{7,4},{8,11},{9,10},{10,... | collective-permute-start | bytes 392 | tf_op jit(solution)/shard_map/ppermute | solution.py:244
  10.7 3.6 %project.4 = (f32[2,384,128]{2,1,0:T(8,128)S(1)}, f32[2,384,128]{2,1,0:T(8,128)S(1)}) custom-call(s32[8]{0:T(128)S(1)} %add.70.order, bf16[4096,1024]{1,0:T(8,128)(2,1)} %bitcast.39, bf16[4096,1024]{1,0:T(8,128)(2,1)} %bitcast.42, bf16[1024,128]{1,0:T(8,128)(2,1)S(1)} %get-tuple-element.56.down_ref, bf16[1024,128]{1,0:T(8,128)(2,1)} %sketch_ref.5), custom_call_target="tpu_custom_call" | custom-call | flops 536870912 | bytes 4980736 | tf_op jit(solution)/shard_map/project/pallas_call | solution.py:74
  14.7 1.6 %lang_parts.1 = (f32[4,64,256]{2,1,0:T(8,128)S(1)}, f32[64,256]{1,0:T(8,128)S(1)}, f32[64,256]{1,0:T(8,128)S(1)}, f32[64,256]{1,0:T(8,128)S(1)}, f32[64,256]{1,0:T(8,128)S(1)}) custom-call(s32[1]{0:T(128)} %bitcast.1.me_ref, f32[32,2048]{1,0:T(8,128)} %held_ref.3, s32[1,32]{1,0:T(1,128)S(1)} %fusion.4.lang_ref, f32[32,1]{1,0:T(8,128)S(1)} %get-tuple-element.39.refs_0_, ...), custom_call_target="tpu_custom_call" | custom-call | tf_op jit(solution)/shard_map/lang_parts/pallas_call | solution.py:118
  18.5 1.6 %collective-permute-start.5 = (f32[64,256]{1,0:T(8,128)S(1)}, f32[64,256]{1,0:T(8,128)S(1)}, u32[]{:S(2)}, u32[]{:S(2)}) collective-permute-start(f32[64,256]{1,0:T(8,128)S(1)} %get-tuple-element.75), channel_id=1, source_target_pairs={{0,8},{4,12},{8,0},{12,4},{16,24},{20,28},{24,16},{28,20},{1,9},{5... | collective-permute-start | bytes 196616 | tf_op jit(solution)/shard_map/ppermute | solution.py:244
  20.0 1.5 %collective-permute-start.6 = (f32[64,256]{1,0:T(8,128)S(1)}, f32[64,256]{1,0:T(8,128)S(1)}, u32[]{:S(2)}, u32[]{:S(2)}) collective-permute-start(f32[64,256]{1,0:T(8,128)S(1)} %get-tuple-element.73), channel_id=1, source_target_pairs={{0,16},{4,20},{8,24},{12,28},{16,0},{20,4},{24,8},{28,12},{1,17},{... | collective-permute-start | bytes 196616 | tf_op jit(solution)/shard_map/ppermute | solution.py:244
  22.0 6.4 %collective-permute-done.4.r1_ref = f32[2,384,128]{2,1,0:T(8,128)S(1)} collective-permute-done((f32[2,384,128]{2,1,0:T(8,128)S(1)}, f32[2,384,128]{2,1,0:T(8,128)S(1)}, u32[]{:S(2)}, u32[]{:S(2)}) %collective-permute-start.4) | collective-permute-done | bytes 393248 | tf_op jit(solution)/shard_map/ppermute | solution.py:244
  30.6 15.5 %collective-permute-done.8 = f32[64,256]{1,0:T(8,128)S(1)} collective-permute-done((f32[64,256]{1,0:T(8,128)S(1)}, f32[64,256]{1,0:T(8,128)S(1)}, u32[]{:S(2)}, u32[]{:S(2)}) %collective-permute-start.8) | collective-permute-done | bytes 65568 | tf_op jit(solution)/shard_map/ppermute | solution.py:244
  46.1 1.6 %collective-permute-start.11 = (f32[2,64,256]{2,1,0:T(8,128)S(1)}, f32[2,64,256]{2,1,0:T(8,128)S(1)}, u32[]{:S(2)}, u32[]{:S(2)}) collective-permute-start(f32[2,64,256]{2,1,0:T(8,128)S(1)} %pad_maximum_fusion), channel_id=1, source_target_pairs={{0,2},{1,3},{2,0},{3,1},{4,6},{5,7},{6,4},{7,5},{8,10},{9,11},{10,... | collective-permute-start | bytes 393224 | tf_op jit(solution)/shard_map/ppermute | solution.py:244
  47.8 2.5 %collective-permute-start.13 = (f32[2,384,128]{2,1,0:T(8,128)S(1)}, f32[2,384,128]{2,1,0:T(8,128)S(1)}, u32[]{:S(2)}, u32[]{:S(2)}) collective-permute-start(f32[2,384,128]{2,1,0:T(8,128)S(1)} %select_add_fusion.2), channel_id=1, source_target_pairs={{0,1},{1,3},{3,2},{2,0},{4,5},{5,7},{7,6},{6,4},{8,9},{9,11},{11,1... | collective-permute-start | bytes 1179656 | tf_op jit(solution)/shard_map/ppermute | solution.py:302
  50.3 6.1 %project.5 = (f32[2,384,128]{2,1,0:T(8,128)S(1)}, f32[2,384,128]{2,1,0:T(8,128)S(1)}, f32[2,384,128]{2,1,0:T(8,128)S(1)}, f32[2,384,128]{2,1,0:T(8,128)S(1)}) custom-call(s32[8]{0:T(128)S(1)} %add.70.order, bf16[4096,1024]{1,0:T(8,128)(2,1)} %bitcast.40, bf16[4096,1024]{1,0:T(8,128)(2,1)} %bitcast.43, bf16[1024,128]{1,0:T(8,128)(2,1)S(1)} %get-tuple-element.56.down_ref, ...), custom_call_target="tpu_custom_call" | custom-call | flops 1073741824 | bytes 9961472 | tf_op jit(solution)/shard_map/project/pallas_call | solution.py:74
  57.2 4.5 %collective-permute-start.16 = (f32[2,384,128]{2,1,0:T(8,128)}, f32[2,384,128]{2,1,0:T(8,128)}, u32[]{:S(2)}, u32[]{:S(2)}) collective-permute-start(f32[2,384,128]{2,1,0:T(8,128)} %select_add_fusion.1), channel_id=1, source_target_pairs={{1,2},{2,1},{0,0},{3,3},{5,6},{6,5},{4,4},{7,7},{9,10},{10,9},{8,8... | collective-permute-start | bytes 1179656 | tf_op jit(solution)/shard_map/ppermute | solution.py:309
  61.8 1.6 %collective-permute-start.12 = (f32[4,64,256]{2,1,0:T(8,128)S(1)}, f32[4,64,256]{2,1,0:T(8,128)}, u32[]{:S(2)}, u32[]{:S(2)}) collective-permute-start(f32[4,64,256]{2,1,0:T(8,128)S(1)} %constant_dynamic-update-slice_fusion.refs_0_), channel_id=1, source_target_pairs={{0,8},{4,20},{8,0},{12,28},{16,24},{20,4},{24,16},{28,12},{1,9},{5... | collective-permute-start | bytes 786440 | tf_op jit(solution)/shard_map/ppermute | solution.py:311
  65.1 1.5 %collective-permute-start.14 = (f32[4,64,256]{2,1,0:T(8,128)S(1)}, f32[4,64,256]{2,1,0:T(8,128)}, u32[]{:S(2)}, u32[]{:S(2)}) collective-permute-start(f32[4,64,256]{2,1,0:T(8,128)S(1)} %constant_dynamic-update-slice_fusion.refs_0_), channel_id=1, source_target_pairs={{0,16},{4,12},{8,24},{12,4},{16,0},{20,28},{24,8},{28,20},{1,17},{... | collective-permute-start | bytes 786440 | tf_op jit(solution)/shard_map/ppermute | solution.py:316
  66.6 3.8 %collective-permute-done.12.refs_1_ = f32[4,64,256]{2,1,0:T(8,128)} collective-permute-done((f32[4,64,256]{2,1,0:T(8,128)S(1)}, f32[4,64,256]{2,1,0:T(8,128)}, u32[]{:S(2)}, u32[]{:S(2)}) %collective-permute-start.12) | collective-permute-done | bytes 262176 | tf_op jit(solution)/shard_map/ppermute | solution.py:311
  70.4 1.5 %collective-permute-start.17 = (f32[4,64,256]{2,1,0:T(8,128)}, f32[4,64,256]{2,1,0:T(8,128)}, u32[]{:S(2)}, u32[]{:S(2)}) collective-permute-start(f32[4,64,256]{2,1,0:T(8,128)} %collective-permute-done.12.refs_1_), channel_id=1, source_target_pairs={{0,16},{4,12},{8,24},{12,4},{16,0},{20,28},{24,8},{28,20},{1,17},{... | collective-permute-start | bytes 786440 | tf_op jit(solution)/shard_map/ppermute | solution.py:316
  72.7 1.6 %collective-permute-start.23 = (f32[2,384,128]{2,1,0:T(8,128)}, f32[2,384,128]{2,1,0:T(8,128)S(1)}, u32[]{:S(2)}, u32[]{:S(2)}) collective-permute-start(f32[2,384,128]{2,1,0:T(8,128)} %select_add_fusion), channel_id=1, source_target_pairs={{1,2},{2,1},{0,0},{3,3},{5,6},{6,5},{4,4},{7,7},{9,10},{10,9},{8,8... | collective-permute-start | bytes 1179656 | tf_op jit(solution)/shard_map/ppermute | solution.py:314
  75.3 1.8 %product.2 = (bf16[32,16,256]{2,1,0:T(8,128)(2,1)S(1)}, f32[8,1]{1,0:T(8,128)S(1)}) custom-call(s32[1]{0:T(128)} %bitcast.23.middle_ref, f32[2,384,128]{2,1,0:T(8,128)S(1)} %get-tuple-element.64.own_ref, f32[2,384,128]{2,1,0:T(8,128)S(1)} %collective-permute-done.4.r1_ref, f32[2,384,128]{2,1,0:T(8,128)S(1)} %collective-permute-done.10.r2_ref, ...), custom_call_target="tpu_custom_call" | custom-call | tf_op jit(solution)/shard_map/product/pallas_call | solution.py:174
  78.5 1.7 %collective-permute-done.22.r3_ref = f32[2,384,128]{2,1,0:T(8,128)S(1)} collective-permute-done((f32[2,384,128]{2,1,0:T(8,128)}, f32[2,384,128]{2,1,0:T(8,128)S(1)}, u32[]{:S(2)}, u32[]{:S(2)}) %collective-permute-start.22) | collective-permute-done | bytes 393248 | tf_op jit(solution)/shard_map/ppermute | solution.py:244
  82.9 2.1 %score.1.refs_0_ = f32[16,64]{1,0:T(8,128)S(1)} custom-call(s32[12]{0:T(128)S(1)} %stack.57.places_ref, f32[4,64,256]{2,1,0:T(8,128)S(1)} %constant_dynamic-update-slice_fusion.refs_0_, f32[4,64,256]{2,1,0:T(8,128)} %collective-permute-done.12.refs_1_, f32[4,64,256]{2,1,0:T(8,128)} %collective-permute-done.14.refs_2_, ...), custom_call_target="tpu_custom_call" | custom-call | tf_op jit(solution)/shard_map/score/pallas_call | solution.py:214
  84.9 4.3 %collective-permute-start.24 = (f32[16,64]{1,0:T(8,128)S(1)}, f32[16,64]{1,0:T(8,128)S(1)}, u32[]{:S(2)}, u32[]{:S(2)}) collective-permute-start(f32[16,64]{1,0:T(8,128)S(1)} %score.1.refs_0_), channel_id=1, source_target_pairs={{0,1},{1,0},{2,3},{3,2},{4,5},{5,4},{6,7},{7,6},{8,9},{9,8},{10,11... | collective-permute-start | bytes 12296 | tf_op jit(solution)/shard_map/ppermute | solution.py:244
  90.3 1.4 %collective-permute-start.26 = (f32[16,64]{1,0:T(8,128)S(1)}, f32[16,64]{1,0:T(8,128)S(1)}, u32[]{:S(2)}, u32[]{:S(2)}) collective-permute-start(f32[16,64]{1,0:T(8,128)S(1)} %score.1.refs_0_), channel_id=1, source_target_pairs={{0,3},{1,2},{2,1},{3,0},{4,7},{5,6},{6,5},{7,4},{8,11},{9,10},{10,... | collective-permute-start | bytes 12296 | tf_op jit(solution)/shard_map/ppermute | solution.py:244
  91.7 2.1 %collective-permute-done.25.refs_2_ = f32[16,64]{1,0:T(8,128)S(1)} collective-permute-done((f32[16,64]{1,0:T(8,128)S(1)}, f32[16,64]{1,0:T(8,128)S(1)}, u32[]{:S(2)}, u32[]{:S(2)}) %collective-permute-start.25) | collective-permute-done | bytes 4128 | tf_op jit(solution)/shard_map/ppermute | solution.py:244
  93.8 1.9 %collective-permute-done.26.refs_3_ = f32[16,64]{1,0:T(8,128)S(1)} collective-permute-done((f32[16,64]{1,0:T(8,128)S(1)}, f32[16,64]{1,0:T(8,128)S(1)}, u32[]{:S(2)}, u32[]{:S(2)}) %collective-permute-start.26) | collective-permute-done | bytes 4128 | tf_op jit(solution)/shard_map/ppermute | solution.py:244
  (62 shorter events, 16.7 us)
Async XLA Ops:
  4.9 9.5 %collective-permute-start.2 = (f32[32,1]{1,0:T(8,128)S(1)}, f32[32,1]{1,0:T(8,128)S(1)}, u32[]{:S(2)}, u32[]{:S(2)}) collective-permute-start(f32[32,1]{1,0:T(8,128)S(1)} %get-tuple-element.39.refs_0_), channel_id=1, source_target_pairs={{0,3},{1,2},{2,1},{3,0},{4,7},{5,6},{6,5},{7,4},{8,11},{9,10},{10,... | collective-permute-start | bytes 392 | tf_op jit(solution)/shard_map/ppermute | solution.py:244
  10.0 4.6 %collective-permute-start.1 = (f32[32,1]{1,0:T(8,128)S(1)}, f32[32,1]{1,0:T(8,128)S(1)}, u32[]{:S(2)}, u32[]{:S(2)}) collective-permute-start(f32[32,1]{1,0:T(8,128)S(1)} %get-tuple-element.39.refs_0_), channel_id=1, source_target_pairs={{0,2},{1,3},{2,0},{3,1},{4,6},{5,7},{6,4},{7,5},{8,10},{9,11},{10,... | collective-permute-start | bytes 392 | tf_op jit(solution)/shard_map/ppermute | solution.py:244
  10.0 4.6 %collective-permute-start = (f32[32,1]{1,0:T(8,128)S(1)}, f32[32,1]{1,0:T(8,128)S(1)}, u32[]{:S(2)}, u32[]{:S(2)}) collective-permute-start(f32[32,1]{1,0:T(8,128)S(1)} %get-tuple-element.39.refs_0_), channel_id=1, source_target_pairs={{0,1},{1,0},{2,3},{3,2},{4,5},{5,4},{6,7},{7,6},{8,9},{9,8},{10,11... | collective-permute-start | bytes 392 | tf_op jit(solution)/shard_map/ppermute | solution.py:244
  16.3 12.1 %collective-permute-start.4 = (f32[2,384,128]{2,1,0:T(8,128)S(1)}, f32[2,384,128]{2,1,0:T(8,128)S(1)}, u32[]{:S(2)}, u32[]{:S(2)}) collective-permute-start(f32[2,384,128]{2,1,0:T(8,128)S(1)} %get-tuple-element.49), channel_id=1, source_target_pairs={{0,1},{1,0},{2,3},{3,2},{4,5},{5,4},{6,7},{7,6},{8,9},{9,8},{10,11... | collective-permute-start | bytes 1179656 | tf_op jit(solution)/shard_map/ppermute | solution.py:244
  17.5 30.2 %collective-permute-start.9 = (f32[2,384,128]{2,1,0:T(8,128)S(1)}, f32[2,384,128]{2,1,0:T(8,128)S(1)}, u32[]{:S(2)}, u32[]{:S(2)}) collective-permute-start(f32[2,384,128]{2,1,0:T(8,128)S(1)} %get-tuple-element.55), channel_id=1, source_target_pairs={{0,1},{1,0},{2,3},{3,2},{4,5},{5,4},{6,7},{7,6},{8,9},{9,8},{10,11... | collective-permute-start | bytes 1179656 | tf_op jit(solution)/shard_map/ppermute | solution.py:244
  18.5 10.0 %collective-permute-start.5 = (f32[64,256]{1,0:T(8,128)S(1)}, f32[64,256]{1,0:T(8,128)S(1)}, u32[]{:S(2)}, u32[]{:S(2)}) collective-permute-start(f32[64,256]{1,0:T(8,128)S(1)} %get-tuple-element.75), channel_id=1, source_target_pairs={{0,8},{4,12},{8,0},{12,4},{16,24},{20,28},{24,16},{28,20},{1,9},{5... | collective-permute-start | bytes 196616 | tf_op jit(solution)/shard_map/ppermute | solution.py:244
  20.0 8.4 %collective-permute-start.6 = (f32[64,256]{1,0:T(8,128)S(1)}, f32[64,256]{1,0:T(8,128)S(1)}, u32[]{:S(2)}, u32[]{:S(2)}) collective-permute-start(f32[64,256]{1,0:T(8,128)S(1)} %get-tuple-element.73), channel_id=1, source_target_pairs={{0,16},{4,20},{8,24},{12,28},{16,0},{20,4},{24,8},{28,12},{1,17},{... | collective-permute-start | bytes 196616 | tf_op jit(solution)/shard_map/ppermute | solution.py:244
  21.6 6.9 %collective-permute-start.7 = (f32[64,256]{1,0:T(8,128)S(1)}, f32[64,256]{1,0:T(8,128)S(1)}, u32[]{:S(2)}, u32[]{:S(2)}) collective-permute-start(f32[64,256]{1,0:T(8,128)S(1)} %get-tuple-element.74), channel_id=1, source_target_pairs={{0,24},{4,28},{8,16},{12,20},{16,8},{20,12},{24,0},{28,4},{1,25},{... | collective-permute-start | bytes 196616 | tf_op jit(solution)/shard_map/ppermute | solution.py:244
  28.5 17.6 %collective-permute-start.8 = (f32[64,256]{1,0:T(8,128)S(1)}, f32[64,256]{1,0:T(8,128)S(1)}, u32[]{:S(2)}, u32[]{:S(2)}) collective-permute-start(f32[64,256]{1,0:T(8,128)S(1)} %add_add_fusion), channel_id=1, source_target_pairs={{0,1},{1,0},{2,3},{3,2},{4,5},{5,4},{6,7},{7,6},{8,9},{9,8},{10,11... | collective-permute-start | bytes 196616 | tf_op jit(solution)/shard_map/ppermute | solution.py:244
  29.7 26.7 %collective-permute-start.10 = (f32[2,384,128]{2,1,0:T(8,128)S(1)}, f32[2,384,128]{2,1,0:T(8,128)S(1)}, u32[]{:S(2)}, u32[]{:S(2)}) collective-permute-start(f32[2,384,128]{2,1,0:T(8,128)S(1)} %select_add_fusion.3), channel_id=1, source_target_pairs={{0,1},{1,3},{3,2},{2,0},{4,5},{5,7},{7,6},{6,4},{8,9},{9,11},{11,1... | collective-permute-start | bytes 1179656 | tf_op jit(solution)/shard_map/ppermute | solution.py:298
  46.1 15.6 %collective-permute-start.11 = (f32[2,64,256]{2,1,0:T(8,128)S(1)}, f32[2,64,256]{2,1,0:T(8,128)S(1)}, u32[]{:S(2)}, u32[]{:S(2)}) collective-permute-start(f32[2,64,256]{2,1,0:T(8,128)S(1)} %pad_maximum_fusion), channel_id=1, source_target_pairs={{0,2},{1,3},{2,0},{3,1},{4,6},{5,7},{6,4},{7,5},{8,10},{9,11},{10,... | collective-permute-start | bytes 393224 | tf_op jit(solution)/shard_map/ppermute | solution.py:244
  47.8 16.5 %collective-permute-start.13 = (f32[2,384,128]{2,1,0:T(8,128)S(1)}, f32[2,384,128]{2,1,0:T(8,128)S(1)}, u32[]{:S(2)}, u32[]{:S(2)}) collective-permute-start(f32[2,384,128]{2,1,0:T(8,128)S(1)} %select_add_fusion.2), channel_id=1, source_target_pairs={{0,1},{1,3},{3,2},{2,0},{4,5},{5,7},{7,6},{6,4},{8,9},{9,11},{11,1... | collective-permute-start | bytes 1179656 | tf_op jit(solution)/shard_map/ppermute | solution.py:302
  57.2 14.7 %collective-permute-start.15 = (f32[2,384,128]{2,1,0:T(8,128)}, f32[2,384,128]{2,1,0:T(8,128)S(1)}, u32[]{:S(2)}, u32[]{:S(2)}) collective-permute-start(f32[2,384,128]{2,1,0:T(8,128)} %select_add_fusion.1), channel_id=1, source_target_pairs={{0,1},{1,0},{2,3},{3,2},{4,5},{5,4},{6,7},{7,6},{8,9},{9,8},{10,11... | collective-permute-start | bytes 1179656 | tf_op jit(solution)/shard_map/ppermute | solution.py:244
  57.2 17.1 %collective-permute-start.16 = (f32[2,384,128]{2,1,0:T(8,128)}, f32[2,384,128]{2,1,0:T(8,128)}, u32[]{:S(2)}, u32[]{:S(2)}) collective-permute-start(f32[2,384,128]{2,1,0:T(8,128)} %select_add_fusion.1), channel_id=1, source_target_pairs={{1,2},{2,1},{0,0},{3,3},{5,6},{6,5},{4,4},{7,7},{9,10},{10,9},{8,8... | collective-permute-start | bytes 1179656 | tf_op jit(solution)/shard_map/ppermute | solution.py:309
  61.8 8.6 %collective-permute-start.12 = (f32[4,64,256]{2,1,0:T(8,128)S(1)}, f32[4,64,256]{2,1,0:T(8,128)}, u32[]{:S(2)}, u32[]{:S(2)}) collective-permute-start(f32[4,64,256]{2,1,0:T(8,128)S(1)} %constant_dynamic-update-slice_fusion.refs_0_), channel_id=1, source_target_pairs={{0,8},{4,20},{8,0},{12,28},{16,24},{20,4},{24,16},{28,12},{1,9},{5... | collective-permute-start | bytes 786440 | tf_op jit(solution)/shard_map/ppermute | solution.py:311
  65.1 15.1 %collective-permute-start.22 = (f32[2,384,128]{2,1,0:T(8,128)}, f32[2,384,128]{2,1,0:T(8,128)S(1)}, u32[]{:S(2)}, u32[]{:S(2)}) collective-permute-start(f32[2,384,128]{2,1,0:T(8,128)} %select_add_fusion), channel_id=1, source_target_pairs={{0,1},{1,0},{2,3},{3,2},{4,5},{5,4},{6,7},{7,6},{8,9},{9,8},{10,11... | collective-permute-start | bytes 1179656 | tf_op jit(solution)/shard_map/ppermute | solution.py:244
  65.1 12.8 %collective-permute-start.14 = (f32[4,64,256]{2,1,0:T(8,128)S(1)}, f32[4,64,256]{2,1,0:T(8,128)}, u32[]{:S(2)}, u32[]{:S(2)}) collective-permute-start(f32[4,64,256]{2,1,0:T(8,128)S(1)} %constant_dynamic-update-slice_fusion.refs_0_), channel_id=1, source_target_pairs={{0,16},{4,12},{8,24},{12,4},{16,0},{20,28},{24,8},{28,20},{1,17},{... | collective-permute-start | bytes 786440 | tf_op jit(solution)/shard_map/ppermute | solution.py:316
  70.4 8.0 %collective-permute-start.17 = (f32[4,64,256]{2,1,0:T(8,128)}, f32[4,64,256]{2,1,0:T(8,128)}, u32[]{:S(2)}, u32[]{:S(2)}) collective-permute-start(f32[4,64,256]{2,1,0:T(8,128)} %collective-permute-done.12.refs_1_), channel_id=1, source_target_pairs={{0,16},{4,12},{8,24},{12,4},{16,0},{20,28},{24,8},{28,20},{1,17},{... | collective-permute-start | bytes 786440 | tf_op jit(solution)/shard_map/ppermute | solution.py:316
  72.7 7.6 %collective-permute-start.23 = (f32[2,384,128]{2,1,0:T(8,128)}, f32[2,384,128]{2,1,0:T(8,128)S(1)}, u32[]{:S(2)}, u32[]{:S(2)}) collective-permute-start(f32[2,384,128]{2,1,0:T(8,128)} %select_add_fusion), channel_id=1, source_target_pairs={{1,2},{2,1},{0,0},{3,3},{5,6},{6,5},{4,4},{7,7},{9,10},{10,9},{8,8... | collective-permute-start | bytes 1179656 | tf_op jit(solution)/shard_map/ppermute | solution.py:314
  74.3 6.8 %collective-permute-start.18 = (f32[4,64,256]{2,1,0:T(8,128)S(1)}, f32[4,64,256]{2,1,0:T(8,128)}, u32[]{:S(2)}, u32[]{:S(2)}) collective-permute-start(f32[4,64,256]{2,1,0:T(8,128)S(1)} %constant_dynamic-update-slice_fusion.refs_0_), channel_id=1, source_target_pairs={{0,4},{4,0},{8,12},{12,8},{16,20},{20,16},{24,28},{28,24},{1,5},{5... | collective-permute-start | bytes 786440 | tf_op jit(solution)/shard_map/ppermute | solution.py:320
  77.9 3.2 %collective-permute-start.19 = (f32[4,64,256]{2,1,0:T(8,128)}, f32[4,64,256]{2,1,0:T(8,128)S(1)}, u32[]{:S(2)}, u32[]{:S(2)}) collective-permute-start(f32[4,64,256]{2,1,0:T(8,128)} %collective-permute-done.12.refs_1_), channel_id=1, source_target_pairs={{0,4},{4,0},{8,12},{12,8},{16,20},{20,16},{24,28},{28,24},{1,5},{5... | collective-permute-start | bytes 786440 | tf_op jit(solution)/shard_map/ppermute | solution.py:320
  84.9 6.7 %collective-permute-start.24 = (f32[16,64]{1,0:T(8,128)S(1)}, f32[16,64]{1,0:T(8,128)S(1)}, u32[]{:S(2)}, u32[]{:S(2)}) collective-permute-start(f32[16,64]{1,0:T(8,128)S(1)} %score.1.refs_0_), channel_id=1, source_target_pairs={{0,1},{1,0},{2,3},{3,2},{4,5},{5,4},{6,7},{7,6},{8,9},{9,8},{10,11... | collective-permute-start | bytes 12296 | tf_op jit(solution)/shard_map/ppermute | solution.py:244
  89.2 4.5 %collective-permute-start.25 = (f32[16,64]{1,0:T(8,128)S(1)}, f32[16,64]{1,0:T(8,128)S(1)}, u32[]{:S(2)}, u32[]{:S(2)}) collective-permute-start(f32[16,64]{1,0:T(8,128)S(1)} %score.1.refs_0_), channel_id=1, source_target_pairs={{0,2},{1,3},{2,0},{3,1},{4,6},{5,7},{6,4},{7,5},{8,10},{9,11},{10,... | collective-permute-start | bytes 12296 | tf_op jit(solution)/shard_map/ppermute | solution.py:244
  90.3 5.4 %collective-permute-start.26 = (f32[16,64]{1,0:T(8,128)S(1)}, f32[16,64]{1,0:T(8,128)S(1)}, u32[]{:S(2)}, u32[]{:S(2)}) collective-permute-start(f32[16,64]{1,0:T(8,128)S(1)} %score.1.refs_0_), channel_id=1, source_target_pairs={{0,3},{1,2},{2,1},{3,0},{4,7},{5,6},{6,5},{7,4},{8,11},{9,10},{10,... | collective-permute-start | bytes 12296 | tf_op jit(solution)/shard_map/ppermute | solution.py:244
  (8 other events, 13.7 us)

commit v3 on v2

--- a/solution.py
+++ b/solution.py
@@ -185,13 +185,18 @@
     )(middle, *parts)
 
 
-def score_kernel(places_ref, *refs, scale, n_lang):
+def score_kernel(feat_ref, ex_ref, *refs, scale, n_lang):
     lang_refs, grad_refs, square_refs, o_ref = refs[:n_lang], refs[n_lang:-1:2], refs[n_lang + 1 : -1 : 2], refs[-1]
     zs = lang_refs[0].shape[0]
     total = None
+    feat, ex = feat_ref[0], ex_ref[0]
+    middle = (feat == 1) | (feat == 2)
+    second = feat ^ jnp.where(middle, 3, 2)
+    rows_from = [feat, feat ^ 1, second, second ^ 1]
+    masks = [*range(0, n_lang, 2), *range(1, n_lang, 2)]
     for j, ref in enumerate(lang_refs):
         for m in range(zs):
-            index = places_ref[n_lang + m] * n_lang + places_ref[j]
+            index = rows_from[m] * n_lang + (ex ^ masks[j])
             lang = ref[m]
             rest = lang - lang.astype(jnp.bfloat16).astype(jnp.float32)
             lang = jnp.concatenate([lang, rest], axis=0).astype(jnp.bfloat16)
@@ -208,17 +213,42 @@
         o_ref[index * count : (index + 1) * count] = inner * (lax.rsqrt(square_ref[...] + 1e-06) * scale)
 
 
-def score(places, langs, products, scale):
+def score(feat, ex, langs, products, scale):
     flat = [x for pair in products for x in pair]
     mine = sum(square.shape[0] for _, square in products)
     return pl.pallas_call(
         functools.partial(score_kernel, scale=scale, n_lang=len(langs)),
         out_shape=jax.ShapeDtypeStruct((mine, LANGS), jnp.float32),
-        in_specs=[SMEM] + [VMEM] * (len(langs) + len(flat)),
+        in_specs=[SMEM] * 2 + [VMEM] * (len(langs) + len(flat)),
         out_specs=VMEM,
         compiler_params=pltpu.CompilerParams(vmem_limit_bytes=SMALL),
         name="score",
-    )(places, *langs, *flat)
+    )(feat, ex, *langs, *flat)
+
+
+def small(kernel, shape, middle, operands):
+    return pl.pallas_call(
+        kernel,
+        out_shape=jax.ShapeDtypeStruct(shape, jnp.float32),
+        in_specs=[SMEM] + [VMEM] * len(operands),
+        out_specs=VMEM,
+        compiler_params=pltpu.CompilerParams(vmem_limit_bytes=SMALL),
+    )(middle, *operands)
+
+
+def onward_kernel(middle_ref, raw_ref, got_ref, o_ref):
+    o_ref[...] = raw_ref[...] + jnp.where(middle_ref[0] == 1, got_ref[...], 0.0)
+
+
+def stack_kernel(middle_ref, one_ref, two_ref, o_ref):
+    del middle_ref
+    o_ref[0] = one_ref[...]
+    o_ref[1] = two_ref[...]
+
+
+def join_kernel(middle_ref, pair_ref, inner_ref, outer_ref, o_ref):
+    o_ref[:2] = pair_ref[...]
+    o_ref[2:] = jnp.where(middle_ref[0] == 1, inner_ref[...], outer_ref[...])
 
 
 def place_kernel(me_ref, *refs):
@@ -272,32 +302,28 @@
     square_like = jax.ShapeDtypeStruct((held.shape[0], 1), jnp.float32)
     round_pairs = [(0, 1), (1, 3), (3, 2), (2, 0)]
     inner_pairs = [(1, 2), (2, 1), (0, 0), (3, 3)]
-    cross = [
-        [(i, i ^ (2 if i % 2 == 0 else 4)) for i in range(n_ex)],
-        [(i, i ^ (4 if i % 2 == 0 else 2)) for i in range(n_ex)],
-        [(i, i ^ 1) for i in range(n_ex)],
-    ]
+
+    is_middle = middle.astype(jnp.int32).reshape(1)
 
     def onward(raw, got):
-        return raw + jnp.where(middle, got, 0.0)
+        return small(onward_kernel, raw.shape, is_middle, [raw, got])
 
     *raw0, down, own_square = project(
         first_kernel, order, 0, 2, acts2, grads2, [adapter, rank_sketch, out_sketch, held], [down_like, square_like]
     )
     squares = [own_square] + [swap(own_square, "feat", mask) for mask in (1, 2, 3)]
     got1 = [swap(x, "feat", 1) for x in raw0]
-    raw1 = project(more_kernel, order, 2, 2, acts2, grads2, [down, out_sketch], [])
-
-    other, *parts = lang_parts(me_ex, held, [squares[0]] + [after(x, raw1[0]) for x in squares[1:]], perm % LANGS, n_ex)
+    other, *parts = lang_parts(me_ex, held, squares, perm % LANGS, n_ex)
     other = swap(other, "ex", 1)
     parts = [x + other[i] for i, x in enumerate(parts)]
     scattered = [swap(parts[i], "ex", 2 * i) for i in range(1, n_ex // 2)]
-    sent2 = [onward(after(raw1[0], parts[1]), got1[0])]
-    lang = after(parts[0], sent2[0]) + sum(scattered)
+    raw1 = project(more_kernel, order, 2, 2, acts2, grads2, [after(down, *parts), out_sketch], [])
+    lang = after(parts[0], raw1[0]) + sum(scattered)
     pair = swap(lang, "feat", 1)
-    got2 = [lax.ppermute(after(sent2[0], lang), "feat", round_pairs)]
-    pair = jnp.stack([lang, pair])
-    far_pair = swap(pair, "feat", 2)
+    sent2 = [onward(after(raw1[0], pair), got1[0])]
+    got2 = [lax.ppermute(sent2[0], "feat", round_pairs)]
+    pair = small(stack_kernel, (2, *lang.shape), is_middle, [lang, pair])
+    far_pair = [lax.ppermute(pair, "feat", pairs) for pairs in (inner_pairs, [(1, 3), (2, 0)])]
     sent2.append(onward(after(raw1[1], pair), got1[1]))
     got2.append(lax.ppermute(sent2[1], "feat", round_pairs))
     *raw2, own_a, own_b = project(
@@ -307,27 +333,22 @@
     sent3 = [onward(raw2[0], got2[0])]
     got3 = [swap(sent3[0], "feat", 1)]
     got4 = [lax.ppermute(sent3[0], "feat", inner_pairs)]
-    langs = [jnp.concatenate([after(pair, sent3[0]), far_pair])]
-    langs = langs + [lax.ppermute(x, "ex", cross[0]) for x in langs]
+    pair = after(pair, sent3[0])
+    langs = [small(join_kernel, (4, *lang.shape), is_middle, [pair, *far_pair])]
+    langs = langs + [swap(langs[0], "ex", mask) for mask in range(2, n_ex, 2)]
     sent3.append(onward(after(raw2[1], langs[0]), got2[1]))
     got3.append(swap(sent3[1], "feat", 1))
     got4.append(lax.ppermute(sent3[1], "feat", inner_pairs))
-    langs[1] = after(langs[1], sent3[1])
-    langs = langs + [lax.ppermute(x, "ex", cross[1]) for x in langs]
-    is_middle = middle.astype(jnp.int32).reshape(1)
-    products = [product(is_middle, [after(own[0], langs[1]), got1[0], got2[0], got3[0], got4[0]])]
-    langs[2:] = [after(x, products[0][1]) for x in langs[2:]]
-    langs = langs + [lax.ppermute(x, "ex", cross[2]) for x in langs]
-    products.append(product(is_middle, [after(own[1], products[0][1]), got1[1], got2[1], got3[1], got4[1]]))
-    one = jnp.where(ex % 2 == 0, 2, 4)
-    two = 6 - one
-    masks = [0, one, two, 6, 1, 1 ^ two, 1 ^ one, 7]
-    places = jnp.stack(
-        [jnp.asarray(x, jnp.int32) for x in [ex ^ m for m in masks] + [feat, feat ^ 1, feat ^ 2, feat ^ 3]]
-    )
+    grad_a, square_a = product(is_middle, [after(own[0], sent3[1]), got1[0], got2[0], got3[0], got4[0]])
+    grad_a = pltpu.with_memory_space_constraint(grad_a, pltpu.VMEM)
+    langs[1:] = [after(x, square_a) for x in langs[1:]]
+    langs = langs + [swap(x, "ex", 1) for x in langs]
+    grad_b, square_b = product(is_middle, [after(own[1], square_a), got1[1], got2[1], got3[1], got4[1]])
+    grad_b = pltpu.with_memory_space_constraint(grad_b, pltpu.VMEM)
+    products = [(grad_a, square_a), (grad_b, square_b)]
     per_lang = perm.shape[0] * n_ex // LANGS
     scale = (KF * per_lang) ** 0.5 / per_lang
-    mine = score(places, langs, products, scale)
+    mine = score(me_feat, me_ex, langs, products, scale)
     return place(me_feat, [mine] + [swap(mine, "feat", mask) for mask in (1, 2, 3)])
 
 

time: 96.9 us -> 93.6 us (0.966)
  waiting for transfers between devices: 33.5 us -> 45.6 us
  starting transfers between devices: 35.8 us -> 27.8 us
  local copies, waits for them, and re-layouts: 3.61 us -> 0.09 us
  Pallas kernels: 20.7 us -> 18.8 us
  other arithmetic: 2.53 us -> 0.83 us
    ppermute x8 -> x3, waiting for transfers between devices: 4.61 us -> 17.2 us  [the longest x2 11.3 us: ordered(): lax.ppermute(pair, 'feat', pairs)]
    ppermute x8 -> x3, starting transfers between devices: 6.16 us -> 2.3 us  [the longest x2 1.96 us: ordered(): lax.ppermute(pair, 'feat', pairs)]
    ppermute x1, starting transfers between devices: 4.49 us -> 0.69 us  [ordered(): got4 = [lax.ppermute(sent3[0], 'feat', inner_pairs)]]
    unnamed x11 -> x2, local copies, waits for them, and re-layouts: 3.43 us -> 0.01 us
    ppermute x16 -> x22, starting transfers between devices: 21 us -> 23.6 us  [swap(): lax.ppermute(x, axis, [(i, i ^ mask) for i in range(lax.axis_size(axis))])]
    ppermute x1, starting transfers between devices: 2.53 us -> 0.51 us  [ordered(): got2.append(lax.ppermute(sent2[1], 'feat', round_pairs))]
    add x5 -> x1, other arithmetic: 1.72 us -> 0.02 us  [ordered(): lang = after(parts[0], raw1[0]) + sum(scattered)]
    pallas_call x1, Pallas kernels: 2.07 us -> 0.88 us  [score(): pl.pallas_call(functools.partial(score_kernel, scale=scale, n_lang=len(la...]
  transfers between devices with their start and end apart: 27 -> 28, of which waited for: 9 -> 15; matrix products, arithmetic and copies ran while one was open for 2% -> 0% of each run, Pallas kernels for 13% -> 12%
where the time goes in v3:
time: 93.6 us; the launch traced here: 93.3 us
  waiting for transfers between devices  45.6 us (49%)
  starting transfers between devices  27.8 us (30%)
  Pallas kernels  18.8 us (20%)
    ppermute x22, waiting for transfers between devices, swap(): lax.ppermute(x, axis, [(i, i ^ mask) for i in range(lax.axis_size(axis))])  28.4 us
    ppermute x22, starting transfers between devices, swap(): lax.ppermute(x, axis, [(i, i ^ mask) for i in range(lax.axis_size(axis))])  23.6 us
    pallas_call x3, Pallas kernels, project(): pl.pallas_call(kernel, out_shape=[jax.ShapeDtypeStruct(piece, jnp.float32...  13.7 us
    ppermute x2, waiting for transfers between devices, ordered(): lax.ppermute(pair, 'feat', pairs)  11.3 us
    ppermute x1, waiting for transfers between devices, ordered(): got2 = [lax.ppermute(sent2[0], 'feat', round_pairs)]  5.93 us
    ppermute x2, starting transfers between devices, ordered(): lax.ppermute(pair, 'feat', pairs)  1.96 us
  transfers between devices with their start and end apart: 28, of which 15 were waited for; matrix products, arithmetic and copies ran while one was open for 0% of the time, Pallas kernels for 12%

profile of v3, /device:TPU:0, one launch (start us, length us, event | category | flops | bytes accessed | tf_op | source)
XLA Modules:
  0.0 93.3 jit_solution(1369893965247737415)
XLA Ops:
  0.8 4.0 %project.3 = (f32[2,384,128]{2,1,0:T(8,128)S(1)}, f32[2,384,128]{2,1,0:T(8,128)S(1)}, bf16[1024,128]{1,0:T(8,128)(2,1)S(1)}, f32[32,1]{1,0:T(8,128)S(1)}) custom-call(s32[8]{0:T(128)S(1)} %add.53.order, bf16[4096,1024]{1,0:T(8,128)(2,1)} %bitcast.26, bf16[4096,1024]{1,0:T(8,128)(2,1)} %bitcast.29, bf16[1024,128]{1,0:T(8,128)(2,1)} %adapter_ref.1, ...), custom_call_target="tpu_custom_call" | custom-call | flops 536870912 | bytes 4980736 | tf_op jit(solution)/shard_map/project/pallas_call | solution.py:74
  4.9 3.1 %collective-permute-start = (f32[32,1]{1,0:T(8,128)S(1)}, f32[32,1]{1,0:T(8,128)S(1)}, u32[]{:S(2)}, u32[]{:S(2)}) collective-permute-start(f32[32,1]{1,0:T(8,128)S(1)} %get-tuple-element.36.refs_0_), channel_id=1, source_target_pairs={{0,1},{1,0},{2,3},{3,2},{4,5},{5,4},{6,7},{7,6},{8,9},{9,8},{10,11... | collective-permute-start | bytes 392 | tf_op jit(solution)/shard_map/ppermute | solution.py:274
  8.0 2.6 %collective-permute-start.1 = (f32[32,1]{1,0:T(8,128)S(1)}, f32[32,1]{1,0:T(8,128)S(1)}, u32[]{:S(2)}, u32[]{:S(2)}) collective-permute-start(f32[32,1]{1,0:T(8,128)S(1)} %get-tuple-element.36.refs_0_), channel_id=1, source_target_pairs={{0,2},{1,3},{2,0},{3,1},{4,6},{5,7},{6,4},{7,5},{8,10},{9,11},{10,... | collective-permute-start | bytes 392 | tf_op jit(solution)/shard_map/ppermute | solution.py:274
  10.6 2.1 %collective-permute-done.1.refs_2_ = f32[32,1]{1,0:T(8,128)S(1)} collective-permute-done((f32[32,1]{1,0:T(8,128)S(1)}, f32[32,1]{1,0:T(8,128)S(1)}, u32[]{:S(2)}, u32[]{:S(2)}) %collective-permute-start.1) | collective-permute-done | bytes 160 | tf_op jit(solution)/shard_map/ppermute | solution.py:274
  12.7 3.4 %collective-permute-done.2.refs_3_ = f32[32,1]{1,0:T(8,128)S(1)} collective-permute-done((f32[32,1]{1,0:T(8,128)S(1)}, f32[32,1]{1,0:T(8,128)S(1)}, u32[]{:S(2)}, u32[]{:S(2)}) %collective-permute-start.2) | collective-permute-done | bytes 160 | tf_op jit(solution)/shard_map/ppermute | solution.py:274
  16.1 1.6 %lang_parts.1 = (f32[4,64,256]{2,1,0:T(8,128)S(1)}, f32[64,256]{1,0:T(8,128)S(1)}, f32[64,256]{1,0:T(8,128)S(1)}, f32[64,256]{1,0:T(8,128)S(1)}, f32[64,256]{1,0:T(8,128)S(1)}) custom-call(s32[1]{0:T(128)} %bitcast.1.me_ref.ex_ref, f32[32,2048]{1,0:T(8,128)} %held_ref.3, s32[1,32]{1,0:T(1,128)S(1)} %fusion.4.lang_ref, ...), custom_call_target="tpu_custom_call" | custom-call | tf_op jit(solution)/shard_map/lang_parts/pallas_call | solution.py:118
  17.9 1.4 %collective-permute-done.3 = f32[4,64,256]{2,1,0:T(8,128)S(1)} collective-permute-done((f32[4,64,256]{2,1,0:T(8,128)S(1)}, f32[4,64,256]{2,1,0:T(8,128)S(1)}, u32[]{:S(2)}, u32[]{:S(2)}) %collective-permute-start.3) | collective-permute-done | bytes 262176 | tf_op jit(solution)/shard_map/ppermute | solution.py:274
  19.4 1.6 %collective-permute-start.4 = (f32[64,256]{1,0:T(8,128)S(1)}, f32[64,256]{1,0:T(8,128)S(1)}, u32[]{:S(2)}, u32[]{:S(2)}) collective-permute-start(f32[64,256]{1,0:T(8,128)S(1)} %get-tuple-element.69), channel_id=1, source_target_pairs={{0,8},{4,12},{8,0},{12,4},{16,24},{20,28},{24,16},{28,20},{1,9},{5... | collective-permute-start | bytes 196616 | tf_op jit(solution)/shard_map/ppermute | solution.py:274
  20.9 1.5 %collective-permute-start.5 = (f32[64,256]{1,0:T(8,128)S(1)}, f32[64,256]{1,0:T(8,128)S(1)}, u32[]{:S(2)}, u32[]{:S(2)}) collective-permute-start(f32[64,256]{1,0:T(8,128)S(1)} %get-tuple-element.68), channel_id=1, source_target_pairs={{0,16},{4,20},{8,24},{12,28},{16,0},{20,4},{24,8},{28,12},{1,17},{... | collective-permute-start | bytes 196616 | tf_op jit(solution)/shard_map/ppermute | solution.py:274
  23.5 3.6 %project.4 = (f32[2,384,128]{2,1,0:T(8,128)S(1)}, f32[2,384,128]{2,1,0:T(8,128)S(1)}) custom-call(s32[8]{0:T(128)S(1)} %add.53.order, bf16[4096,1024]{1,0:T(8,128)(2,1)} %bitcast.27, bf16[4096,1024]{1,0:T(8,128)(2,1)} %bitcast.30, bf16[1024,128]{1,0:T(8,128)(2,1)S(1)} %get-tuple-element.49.down_ref, bf16[1024,128]{1,0:T(8,128)(2,1)} %sketch_ref.5), custom_call_target="tpu_custom_call" | custom-call | flops 536870912 | bytes 4980736 | tf_op jit(solution)/shard_map/project/pallas_call | solution.py:74
  27.6 1.1 %collective-permute-start.7 = (f32[64,256]{1,0:T(8,128)S(1)}, f32[64,256]{1,0:T(8,128)S(1)}, u32[]{:S(2)}, u32[]{:S(2)}) collective-permute-start(f32[64,256]{1,0:T(8,128)S(1)} %add_add_fusion.one_ref), channel_id=1, source_target_pairs={{0,1},{1,0},{2,3},{3,2},{4,5},{5,4},{6,7},{7,6},{8,9},{9,8},{10,11... | collective-permute-start | bytes 196616 | tf_op jit(solution)/shard_map/ppermute | solution.py:274
  28.7 10.4 %collective-permute-done.7.two_ref = f32[64,256]{1,0:T(8,128)S(1)} collective-permute-done((f32[64,256]{1,0:T(8,128)S(1)}, f32[64,256]{1,0:T(8,128)S(1)}, u32[]{:S(2)}, u32[]{:S(2)}) %collective-permute-start.7) | collective-permute-done | bytes 65568 | tf_op jit(solution)/shard_map/ppermute | solution.py:274
  40.1 6.1 %project.5 = (f32[2,384,128]{2,1,0:T(8,128)S(1)}, f32[2,384,128]{2,1,0:T(8,128)S(1)}, f32[2,384,128]{2,1,0:T(8,128)S(1)}, f32[2,384,128]{2,1,0:T(8,128)S(1)}) custom-call(s32[8]{0:T(128)S(1)} %add.53.order, bf16[4096,1024]{1,0:T(8,128)(2,1)} %bitcast.28, bf16[4096,1024]{1,0:T(8,128)(2,1)} %bitcast.31, bf16[1024,128]{1,0:T(8,128)(2,1)S(1)} %get-tuple-element.49.down_ref, ...), custom_call_target="tpu_custom_call" | custom-call | flops 1073741824 | bytes 9961472 | tf_op jit(solution)/shard_map/project/pallas_call | solution.py:74
  46.2 5.9 %collective-permute-done.10.got_ref.r2_ref = f32[2,384,128]{2,1,0:T(8,128)S(1)} collective-permute-done((f32[2,384,128]{2,1,0:T(8,128)S(1)}, f32[2,384,128]{2,1,0:T(8,128)S(1)}, u32[]{:S(2)}, u32[]{:S(2)}) %collective-permute-start.10) | collective-permute-done | bytes 393248 | tf_op jit(solution)/shard_map/ppermute | solution.py:324
  53.0 1.3 %collective-permute-start.12 = (f32[2,64,256]{2,1,0:T(8,128)S(1)}, f32[2,64,256]{2,1,0:T(8,128)S(1)}, u32[]{:S(2)}, u32[]{:S(2)}) collective-permute-start(f32[2,64,256]{2,1,0:T(8,128)S(1)} %shard_map.82.pair_ref), channel_id=1, source_target_pairs={{1,3},{2,0},{5,7},{6,4},{9,11},{10,8},{13,15},{14,12},{17,19},{18,... | collective-permute-start | bytes 393224 | tf_op jit(solution)/shard_map/ppermute | solution.py:326
  55.0 11.3 %collective-permute-done.12.outer_ref = f32[2,64,256]{2,1,0:T(8,128)S(1)} collective-permute-done((f32[2,64,256]{2,1,0:T(8,128)S(1)}, f32[2,64,256]{2,1,0:T(8,128)S(1)}, u32[]{:S(2)}, u32[]{:S(2)}) %collective-permute-start.12) | collective-permute-done | bytes 131104 | tf_op jit(solution)/shard_map/ppermute | solution.py:326
  66.4 2.5 %collective-permute-start.18 = (f32[4,64,256]{2,1,0:T(8,128)S(1)}, f32[4,64,256]{2,1,0:T(8,128)S(1)}, u32[]{:S(2)}, u32[]{:S(2)}) collective-permute-start(f32[4,64,256]{2,1,0:T(8,128)S(1)} %shard_map.86.refs_0_), channel_id=1, source_target_pairs={{0,24},{4,28},{8,16},{12,20},{16,8},{20,12},{24,0},{28,4},{1,25},{... | collective-permute-start | bytes 786440 | tf_op jit(solution)/shard_map/ppermute | solution.py:274
  69.4 1.1 %collective-permute-done.15.r3_ref = f32[2,384,128]{2,1,0:T(8,128)S(1)} collective-permute-done((f32[2,384,128]{2,1,0:T(8,128)S(1)}, f32[2,384,128]{2,1,0:T(8,128)S(1)}, u32[]{:S(2)}, u32[]{:S(2)}) %collective-permute-start.15) | collective-permute-done | bytes 393248 | tf_op jit(solution)/shard_map/ppermute | solution.py:274
  70.5 1.5 %collective-permute-start.13 = (f32[4,64,256]{2,1,0:T(8,128)S(1)}, f32[4,64,256]{2,1,0:T(8,128)S(1)}, u32[]{:S(2)}, u32[]{:S(2)}) collective-permute-start(f32[4,64,256]{2,1,0:T(8,128)S(1)} %shard_map.86.refs_0_), channel_id=1, source_target_pairs={{0,8},{4,12},{8,0},{12,4},{16,24},{20,28},{24,16},{28,20},{1,9},{5... | collective-permute-start | bytes 786440 | tf_op jit(solution)/shard_map/ppermute | solution.py:274
  73.9 4.7 %collective-permute-done.17.refs_2_ = f32[4,64,256]{2,1,0:T(8,128)S(1)} collective-permute-done((f32[4,64,256]{2,1,0:T(8,128)S(1)}, f32[4,64,256]{2,1,0:T(8,128)S(1)}, u32[]{:S(2)}, u32[]{:S(2)}) %collective-permute-start.17) | collective-permute-done | bytes 262176 | tf_op jit(solution)/shard_map/ppermute | solution.py:274
  78.5 0.9 %collective-permute-done.13.refs_1_ = f32[4,64,256]{2,1,0:T(8,128)S(1)} collective-permute-done((f32[4,64,256]{2,1,0:T(8,128)S(1)}, f32[4,64,256]{2,1,0:T(8,128)S(1)}, u32[]{:S(2)}, u32[]{:S(2)}) %collective-permute-start.13) | collective-permute-done | bytes 262176 | tf_op jit(solution)/shard_map/ppermute | solution.py:274
  82.3 5.0 %collective-permute-start.25 = (f32[16,64]{1,0:T(8,128)S(1)}, f32[16,64]{1,0:T(8,128)S(1)}, u32[]{:S(2)}, u32[]{:S(2)}) collective-permute-start(f32[16,64]{1,0:T(8,128)S(1)} %score.1.refs_0_), channel_id=1, source_target_pairs={{0,1},{1,0},{2,3},{3,2},{4,5},{5,4},{6,7},{7,6},{8,9},{9,8},{10,11... | collective-permute-start | bytes 12296 | tf_op jit(solution)/shard_map/ppermute | solution.py:274
  87.3 2.4 %collective-permute-start.27 = (f32[16,64]{1,0:T(8,128)S(1)}, f32[16,64]{1,0:T(8,128)S(1)}, u32[]{:S(2)}, u32[]{:S(2)}) collective-permute-start(f32[16,64]{1,0:T(8,128)S(1)} %score.1.refs_0_), channel_id=1, source_target_pairs={{0,3},{1,2},{2,1},{3,0},{4,7},{5,6},{6,5},{7,4},{8,11},{9,10},{10,... | collective-permute-start | bytes 12296 | tf_op jit(solution)/shard_map/ppermute | solution.py:274
  89.7 2.1 %collective-permute-done.26.refs_2_ = f32[16,64]{1,0:T(8,128)S(1)} collective-permute-done((f32[16,64]{1,0:T(8,128)S(1)}, f32[16,64]{1,0:T(8,128)S(1)}, u32[]{:S(2)}, u32[]{:S(2)}) %collective-permute-start.26) | collective-permute-done | bytes 4128 | tf_op jit(solution)/shard_map/ppermute | solution.py:274
  (54 shorter events, 11.9 us)
Async XLA Ops:
  4.9 5.7 %collective-permute-start = (f32[32,1]{1,0:T(8,128)S(1)}, f32[32,1]{1,0:T(8,128)S(1)}, u32[]{:S(2)}, u32[]{:S(2)}) collective-permute-start(f32[32,1]{1,0:T(8,128)S(1)} %get-tuple-element.36.refs_0_), channel_id=1, source_target_pairs={{0,1},{1,0},{2,3},{3,2},{4,5},{5,4},{6,7},{7,6},{8,9},{9,8},{10,11... | collective-permute-start | bytes 392 | tf_op jit(solution)/shard_map/ppermute | solution.py:274
  8.0 4.7 %collective-permute-start.1 = (f32[32,1]{1,0:T(8,128)S(1)}, f32[32,1]{1,0:T(8,128)S(1)}, u32[]{:S(2)}, u32[]{:S(2)}) collective-permute-start(f32[32,1]{1,0:T(8,128)S(1)} %get-tuple-element.36.refs_0_), channel_id=1, source_target_pairs={{0,2},{1,3},{2,0},{3,1},{4,6},{5,7},{6,4},{7,5},{8,10},{9,11},{10,... | collective-permute-start | bytes 392 | tf_op jit(solution)/shard_map/ppermute | solution.py:274
  10.6 5.5 %collective-permute-start.2 = (f32[32,1]{1,0:T(8,128)S(1)}, f32[32,1]{1,0:T(8,128)S(1)}, u32[]{:S(2)}, u32[]{:S(2)}) collective-permute-start(f32[32,1]{1,0:T(8,128)S(1)} %get-tuple-element.36.refs_0_), channel_id=1, source_target_pairs={{0,3},{1,2},{2,1},{3,0},{4,7},{5,6},{6,5},{7,4},{8,11},{9,10},{10,... | collective-permute-start | bytes 392 | tf_op jit(solution)/shard_map/ppermute | solution.py:274
  17.8 21.4 %collective-permute-start.9 = (f32[2,384,128]{2,1,0:T(8,128)S(1)}, f32[2,384,128]{2,1,0:T(8,128)S(1)}, u32[]{:S(2)}, u32[]{:S(2)}) collective-permute-start(f32[2,384,128]{2,1,0:T(8,128)S(1)} %get-tuple-element.52), channel_id=1, source_target_pairs={{0,1},{1,0},{2,3},{3,2},{4,5},{5,4},{6,7},{7,6},{8,9},{9,8},{10,11... | collective-permute-start | bytes 1179656 | tf_op jit(solution)/shard_map/ppermute | solution.py:274
  19.4 7.8 %collective-permute-start.4 = (f32[64,256]{1,0:T(8,128)S(1)}, f32[64,256]{1,0:T(8,128)S(1)}, u32[]{:S(2)}, u32[]{:S(2)}) collective-permute-start(f32[64,256]{1,0:T(8,128)S(1)} %get-tuple-element.69), channel_id=1, source_target_pairs={{0,8},{4,12},{8,0},{12,4},{16,24},{20,28},{24,16},{28,20},{1,9},{5... | collective-permute-start | bytes 196616 | tf_op jit(solution)/shard_map/ppermute | solution.py:274
  20.9 6.2 %collective-permute-start.5 = (f32[64,256]{1,0:T(8,128)S(1)}, f32[64,256]{1,0:T(8,128)S(1)}, u32[]{:S(2)}, u32[]{:S(2)}) collective-permute-start(f32[64,256]{1,0:T(8,128)S(1)} %get-tuple-element.68), channel_id=1, source_target_pairs={{0,16},{4,20},{8,24},{12,28},{16,0},{20,4},{24,8},{28,12},{1,17},{... | collective-permute-start | bytes 196616 | tf_op jit(solution)/shard_map/ppermute | solution.py:274
  22.5 5.2 %collective-permute-start.6 = (f32[64,256]{1,0:T(8,128)S(1)}, f32[64,256]{1,0:T(8,128)S(1)}, u32[]{:S(2)}, u32[]{:S(2)}) collective-permute-start(f32[64,256]{1,0:T(8,128)S(1)} %get-tuple-element.67), channel_id=1, source_target_pairs={{0,24},{4,28},{8,16},{12,20},{16,8},{20,12},{24,0},{28,4},{1,25},{... | collective-permute-start | bytes 196616 | tf_op jit(solution)/shard_map/ppermute | solution.py:274
  22.9 16.6 %collective-permute-start.8 = (f32[2,384,128]{2,1,0:T(8,128)S(1)}, f32[2,384,128]{2,1,0:T(8,128)S(1)}, u32[]{:S(2)}, u32[]{:S(2)}) collective-permute-start(f32[2,384,128]{2,1,0:T(8,128)S(1)} %get-tuple-element.48), channel_id=1, source_target_pairs={{0,1},{1,0},{2,3},{3,2},{4,5},{5,4},{6,7},{7,6},{8,9},{9,8},{10,11... | collective-permute-start | bytes 1179656 | tf_op jit(solution)/shard_map/ppermute | solution.py:274
  27.6 11.5 %collective-permute-start.7 = (f32[64,256]{1,0:T(8,128)S(1)}, f32[64,256]{1,0:T(8,128)S(1)}, u32[]{:S(2)}, u32[]{:S(2)}) collective-permute-start(f32[64,256]{1,0:T(8,128)S(1)} %add_add_fusion.one_ref), channel_id=1, source_target_pairs={{0,1},{1,0},{2,3},{3,2},{4,5},{5,4},{6,7},{7,6},{8,9},{9,8},{10,11... | collective-permute-start | bytes 196616 | tf_op jit(solution)/shard_map/ppermute | solution.py:274
  39.2 12.9 %collective-permute-start.10 = (f32[2,384,128]{2,1,0:T(8,128)S(1)}, f32[2,384,128]{2,1,0:T(8,128)S(1)}, u32[]{:S(2)}, u32[]{:S(2)}) collective-permute-start(f32[2,384,128]{2,1,0:T(8,128)S(1)} %shard_map.84), channel_id=1, source_target_pairs={{0,1},{1,3},{3,2},{2,0},{4,5},{5,7},{7,6},{6,4},{8,9},{9,11},{11,1... | collective-permute-start | bytes 1179656 | tf_op jit(solution)/shard_map/ppermute | solution.py:324
  39.6 26.6 %collective-permute-start.14 = (f32[2,384,128]{2,1,0:T(8,128)S(1)}, f32[2,384,128]{2,1,0:T(8,128)S(1)}, u32[]{:S(2)}, u32[]{:S(2)}) collective-permute-start(f32[2,384,128]{2,1,0:T(8,128)S(1)} %shard_map.83), channel_id=1, source_target_pairs={{0,1},{1,3},{3,2},{2,0},{4,5},{5,7},{7,6},{6,4},{8,9},{9,11},{11,1... | collective-permute-start | bytes 1179656 | tf_op jit(solution)/shard_map/ppermute | solution.py:328
  52.2 18.3 %collective-permute-start.15 = (f32[2,384,128]{2,1,0:T(8,128)S(1)}, f32[2,384,128]{2,1,0:T(8,128)S(1)}, u32[]{:S(2)}, u32[]{:S(2)}) collective-permute-start(f32[2,384,128]{2,1,0:T(8,128)S(1)} %shard_map.85), channel_id=1, source_target_pairs={{0,1},{1,0},{2,3},{3,2},{4,5},{5,4},{6,7},{7,6},{8,9},{9,8},{10,11... | collective-permute-start | bytes 1179656 | tf_op jit(solution)/shard_map/ppermute | solution.py:274
  52.3 2.7 %collective-permute-start.11 = (f32[2,64,256]{2,1,0:T(8,128)S(1)}, f32[2,64,256]{2,1,0:T(8,128)S(1)}, u32[]{:S(2)}, u32[]{:S(2)}) collective-permute-start(f32[2,64,256]{2,1,0:T(8,128)S(1)} %shard_map.82.pair_ref), channel_id=1, source_target_pairs={{1,2},{2,1},{0,0},{3,3},{5,6},{6,5},{4,4},{7,7},{9,10},{10,9},{8,8... | collective-permute-start | bytes 393224 | tf_op jit(solution)/shard_map/ppermute | solution.py:326
  53.0 13.3 %collective-permute-start.12 = (f32[2,64,256]{2,1,0:T(8,128)S(1)}, f32[2,64,256]{2,1,0:T(8,128)S(1)}, u32[]{:S(2)}, u32[]{:S(2)}) collective-permute-start(f32[2,64,256]{2,1,0:T(8,128)S(1)} %shard_map.82.pair_ref), channel_id=1, source_target_pairs={{1,3},{2,0},{5,7},{6,4},{9,11},{10,8},{13,15},{14,12},{17,19},{18,... | collective-permute-start | bytes 393224 | tf_op jit(solution)/shard_map/ppermute | solution.py:326
  54.3 17.7 %collective-permute-start.16 = (f32[2,384,128]{2,1,0:T(8,128)S(1)}, f32[2,384,128]{2,1,0:T(8,128)S(1)}, u32[]{:S(2)}, u32[]{:S(2)}) collective-permute-start(f32[2,384,128]{2,1,0:T(8,128)S(1)} %shard_map.85), channel_id=1, source_target_pairs={{1,2},{2,1},{0,0},{3,3},{5,6},{6,5},{4,4},{7,7},{9,10},{10,9},{8,8... | collective-permute-start | bytes 1179656 | tf_op jit(solution)/shard_map/ppermute | solution.py:335
  66.3 13.1 %collective-permute-start.23 = (f32[2,384,128]{2,1,0:T(8,128)S(1)}, f32[2,384,128]{2,1,0:T(8,128)S(1)}, u32[]{:S(2)}, u32[]{:S(2)}) collective-permute-start(f32[2,384,128]{2,1,0:T(8,128)S(1)} %shard_map.87), channel_id=1, source_target_pairs={{0,1},{1,0},{2,3},{3,2},{4,5},{5,4},{6,7},{7,6},{8,9},{9,8},{10,11... | collective-permute-start | bytes 1179656 | tf_op jit(solution)/shard_map/ppermute | solution.py:274
  66.4 7.4 %collective-permute-start.18 = (f32[4,64,256]{2,1,0:T(8,128)S(1)}, f32[4,64,256]{2,1,0:T(8,128)S(1)}, u32[]{:S(2)}, u32[]{:S(2)}) collective-permute-start(f32[4,64,256]{2,1,0:T(8,128)S(1)} %shard_map.86.refs_0_), channel_id=1, source_target_pairs={{0,24},{4,28},{8,16},{12,20},{16,8},{20,12},{24,0},{28,4},{1,25},{... | collective-permute-start | bytes 786440 | tf_op jit(solution)/shard_map/ppermute | solution.py:274
  68.9 9.6 %collective-permute-start.17 = (f32[4,64,256]{2,1,0:T(8,128)S(1)}, f32[4,64,256]{2,1,0:T(8,128)S(1)}, u32[]{:S(2)}, u32[]{:S(2)}) collective-permute-start(f32[4,64,256]{2,1,0:T(8,128)S(1)} %shard_map.86.refs_0_), channel_id=1, source_target_pairs={{0,16},{4,20},{8,24},{12,28},{16,0},{20,4},{24,8},{28,12},{1,17},{... | collective-permute-start | bytes 786440 | tf_op jit(solution)/shard_map/ppermute | solution.py:274
  70.5 9.0 %collective-permute-start.13 = (f32[4,64,256]{2,1,0:T(8,128)S(1)}, f32[4,64,256]{2,1,0:T(8,128)S(1)}, u32[]{:S(2)}, u32[]{:S(2)}) collective-permute-start(f32[4,64,256]{2,1,0:T(8,128)S(1)} %shard_map.86.refs_0_), channel_id=1, source_target_pairs={{0,8},{4,12},{8,0},{12,4},{16,24},{20,28},{24,16},{28,20},{1,9},{5... | collective-permute-start | bytes 786440 | tf_op jit(solution)/shard_map/ppermute | solution.py:274
  72.0 8.0 %collective-permute-start.24 = (f32[2,384,128]{2,1,0:T(8,128)S(1)}, f32[2,384,128]{2,1,0:T(8,128)S(1)}, u32[]{:S(2)}, u32[]{:S(2)}) collective-permute-start(f32[2,384,128]{2,1,0:T(8,128)S(1)} %shard_map.87), channel_id=1, source_target_pairs={{1,2},{2,1},{0,0},{3,3},{5,6},{6,5},{4,4},{7,7},{9,10},{10,9},{8,8... | collective-permute-start | bytes 1179656 | tf_op jit(solution)/shard_map/ppermute | solution.py:341
  73.9 7.0 %collective-permute-start.19 = (f32[4,64,256]{2,1,0:T(8,128)S(1)}, f32[4,64,256]{2,1,0:T(8,128)S(1)}, u32[]{:S(2)}, u32[]{:S(2)}) collective-permute-start(f32[4,64,256]{2,1,0:T(8,128)S(1)} %shard_map.86.refs_0_), channel_id=1, source_target_pairs={{0,4},{4,0},{8,12},{12,8},{16,20},{20,16},{24,28},{28,24},{1,5},{5... | collective-permute-start | bytes 786440 | tf_op jit(solution)/shard_map/ppermute | solution.py:274
  82.3 7.4 %collective-permute-start.25 = (f32[16,64]{1,0:T(8,128)S(1)}, f32[16,64]{1,0:T(8,128)S(1)}, u32[]{:S(2)}, u32[]{:S(2)}) collective-permute-start(f32[16,64]{1,0:T(8,128)S(1)} %score.1.refs_0_), channel_id=1, source_target_pairs={{0,1},{1,0},{2,3},{3,2},{4,5},{5,4},{6,7},{7,6},{8,9},{9,8},{10,11... | collective-permute-start | bytes 12296 | tf_op jit(solution)/shard_map/ppermute | solution.py:274
  87.3 4.5 %collective-permute-start.26 = (f32[16,64]{1,0:T(8,128)S(1)}, f32[16,64]{1,0:T(8,128)S(1)}, u32[]{:S(2)}, u32[]{:S(2)}) collective-permute-start(f32[16,64]{1,0:T(8,128)S(1)} %score.1.refs_0_), channel_id=1, source_target_pairs={{0,2},{1,3},{2,0},{3,1},{4,6},{5,7},{6,4},{7,5},{8,10},{9,11},{10,... | collective-permute-start | bytes 12296 | tf_op jit(solution)/shard_map/ppermute | solution.py:274
  87.3 5.4 %collective-permute-start.27 = (f32[16,64]{1,0:T(8,128)S(1)}, f32[16,64]{1,0:T(8,128)S(1)}, u32[]{:S(2)}, u32[]{:S(2)}) collective-permute-start(f32[16,64]{1,0:T(8,128)S(1)} %score.1.refs_0_), channel_id=1, source_target_pairs={{0,3},{1,2},{2,1},{3,0},{4,7},{5,6},{6,5},{7,4},{8,11},{9,10},{10,... | collective-permute-start | bytes 12296 | tf_op jit(solution)/shard_map/ppermute | solution.py:274
  (5 other events, 17.1 us)

commit v4 on v3

--- a/solution.py
+++ b/solution.py
@@ -12,6 +12,7 @@
 LANGS = 64
 UNIT = 4
 PIECE = 2
+PIECES = 8
 HIGHEST = lax.Precision.HIGHEST
 SMALL = 24 * 1024 * 1024
 VMEM = pl.BlockSpec(memory_space=pltpu.VMEM)
@@ -30,8 +31,8 @@
         o_ref[unit, rows:, :] = jnp.where(low, rank[start : start + half], rank[start + half : start + rows])
 
 
-def first_kernel(order, act_ref, grad_ref, adapter_ref, rank_ref, sketch_ref, held_ref, *o_refs):
-    del order
+def first_kernel(feat, act_ref, grad_ref, adapter_ref, rank_ref, sketch_ref, held_ref, *o_refs):
+    del feat
     *piece_refs, down_ref, square_ref = o_refs
     step = pl.program_id(0)
 
@@ -51,8 +52,8 @@
             project_piece(act_ref[...], grad_ref[...], down_ref[...], sketch_ref[...], ref)
 
 
-def more_kernel(order, act_ref, grad_ref, down_ref, sketch_ref, *piece_refs):
-    del order
+def more_kernel(feat, act_ref, grad_ref, down_ref, sketch_ref, *piece_refs):
+    del feat
     step = pl.program_id(0)
     for index, ref in enumerate(piece_refs):
 
@@ -62,15 +63,21 @@
 
 
 def whole(shape):
-    return pl.BlockSpec(shape, lambda i, order: (0,) * len(shape))
-
-
-def project(kernel, order, first, count, acts, grads, operands, extra):
+    return pl.BlockSpec(shape, lambda i, feat: (0,) * len(shape))
+
+
+def chunk_of(turn, feat):
+    left = feat < 2
+    far, near = jnp.where(left, 3, 0), jnp.where(left, 2, 1)
+    return jnp.where(turn == 0, far, jnp.where(turn == 1, near, jnp.where(turn == 2, feat ^ 1, feat)))
+
+
+def project(kernel, feat, first, count, acts, grads, operands, extra):
     ko = operands[-1 if kernel is more_kernel else 2].shape[1]
     width = acts.shape[1]
-    rows = acts.shape[0] // order.shape[0]
+    rows = acts.shape[0] // PIECES
     piece = (PIECE, rows // PIECE * 3 // 2, ko)
-    block = pl.BlockSpec((rows, width), lambda i, order: (order[first + i], 0))
+    block = pl.BlockSpec((rows, width), lambda i, feat: (chunk_of((first + i) // 2, feat[0]) * 2 + (first + i) % 2, 0))
     return pl.pallas_call(
         kernel,
         out_shape=[jax.ShapeDtypeStruct(piece, jnp.float32)] * count + extra,
@@ -87,7 +94,7 @@
         ),
         compiler_params=pltpu.CompilerParams(vmem_limit_bytes=SMALL),
         name="project",
-    )(order, acts, grads, *operands)
+    )(feat, acts, grads, *operands)
 
 
 def lang_kernel(me_ref, held_ref, lang_ref, *refs):
@@ -126,7 +133,7 @@
     )(me, held, lang.reshape(1, rows), *squares)
 
 
-def product_kernel(middle_ref, own_ref, r1_ref, r2_ref, r3_ref, r4_ref, o_ref, square_ref, grad_ref):
+def product_kernel(middle_ref, own_ref, raw_ref, far_ref, near_ref, o_ref, square_ref, grad_ref):
     middle = middle_ref[0] == 1
     rows = own_ref.shape[1] * 2 // 3
     seq = rows // UNIT
@@ -140,7 +147,7 @@
 
     def total(unit, start):
         block = (unit, pl.ds(start, seq), slice(None))
-        return own_ref[block] + jnp.where(middle, r3_ref[block] + r4_ref[block], r1_ref[block] + r2_ref[block])
+        return own_ref[block] + raw_ref[block] + jnp.where(middle, near_ref[block], far_ref[block])
 
     for unit in range(PIECE):
         for pair in range(UNIT // 2):
@@ -187,16 +194,16 @@
 
 def score_kernel(feat_ref, ex_ref, *refs, scale, n_lang):
     lang_refs, grad_refs, square_refs, o_ref = refs[:n_lang], refs[n_lang:-1:2], refs[n_lang + 1 : -1 : 2], refs[-1]
-    zs = lang_refs[0].shape[0]
     total = None
     feat, ex = feat_ref[0], ex_ref[0]
     middle = (feat == 1) | (feat == 2)
     second = feat ^ jnp.where(middle, 3, 2)
     rows_from = [feat, feat ^ 1, second, second ^ 1]
-    masks = [*range(0, n_lang, 2), *range(1, n_lang, 2)]
+    n_ex = n_lang // 2
+    masks = [*range(0, n_ex, 2), *range(1, n_ex, 2)]
     for j, ref in enumerate(lang_refs):
-        for m in range(zs):
-            index = rows_from[m] * n_lang + (ex ^ masks[j])
+        for m in range(2):
+            index = rows_from[j // n_ex * 2 + m] * n_ex + (ex ^ masks[j % n_ex])
             lang = ref[m]
             rest = lang - lang.astype(jnp.bfloat16).astype(jnp.float32)
             lang = jnp.concatenate([lang, rest], axis=0).astype(jnp.bfloat16)
@@ -246,9 +253,8 @@
     o_ref[1] = two_ref[...]
 
 
-def join_kernel(middle_ref, pair_ref, inner_ref, outer_ref, o_ref):
-    o_ref[:2] = pair_ref[...]
-    o_ref[2:] = jnp.where(middle_ref[0] == 1, inner_ref[...], outer_ref[...])
+def choose_kernel(middle_ref, inner_ref, outer_ref, o_ref):
+    o_ref[...] = jnp.where(middle_ref[0] == 1, inner_ref[...], outer_ref[...])
 
 
 def place_kernel(me_ref, *refs):
@@ -289,10 +295,6 @@
     middle = (feat == 1) | (feat == 2)
     me_ex = ex.astype(jnp.int32).reshape(1)
     me_feat = feat.astype(jnp.int32).reshape(1)
-
-    base = jnp.array([3, 2, 1, 0, 0, 3, 2, 1, 3, 0, 1, 2, 0, 1, 2, 3], jnp.int32).reshape(4, 4)
-    chunks = lax.dynamic_index_in_dim(base, feat, 0, keepdims=False)
-    order = (chunks[:, None] * 2 + jnp.arange(2, dtype=jnp.int32)).reshape(-1)
     acts2, grads2 = acts.reshape(-1, width), grads.reshape(-1, width)
     adapter, rank_sketch, out_sketch, held, acts2, grads2 = (
         pltpu.with_memory_space_constraint(x, pltpu.HBM)
@@ -300,51 +302,56 @@
     )
     down_like = jax.ShapeDtypeStruct((width, 2 * rank_sketch.shape[0]), jnp.bfloat16)
     square_like = jax.ShapeDtypeStruct((held.shape[0], 1), jnp.float32)
-    round_pairs = [(0, 1), (1, 3), (3, 2), (2, 0)]
-    inner_pairs = [(1, 2), (2, 1), (0, 0), (3, 3)]
-
+    inward = [(0, 1), (3, 2)]
+    far_pairs = [(1, 3), (2, 0)]
+    near_pairs = [(1, 2), (2, 1), (0, 0), (3, 3)]
     is_middle = middle.astype(jnp.int32).reshape(1)
 
     def onward(raw, got):
         return small(onward_kernel, raw.shape, is_middle, [raw, got])
 
     *raw0, down, own_square = project(
-        first_kernel, order, 0, 2, acts2, grads2, [adapter, rank_sketch, out_sketch, held], [down_like, square_like]
+        first_kernel, me_feat, 0, 2, acts2, grads2, [adapter, rank_sketch, out_sketch, held], [down_like, square_like]
     )
     squares = [own_square] + [swap(own_square, "feat", mask) for mask in (1, 2, 3)]
-    got1 = [swap(x, "feat", 1) for x in raw0]
+    got1 = [lax.ppermute(x, "feat", inward) for x in raw0]
+    raw1 = project(more_kernel, me_feat, 2, 2, acts2, grads2, [down, out_sketch], [])
+
+    squares[1:] = [after(x, raw1[0]) for x in squares[1:]]
     other, *parts = lang_parts(me_ex, held, squares, perm % LANGS, n_ex)
     other = swap(other, "ex", 1)
     parts = [x + other[i] for i, x in enumerate(parts)]
+    sent1 = [onward(after(raw0[0], parts[0]), got1[0])]
+    far = [lax.ppermute(sent1[0], "feat", far_pairs)]
     scattered = [swap(parts[i], "ex", 2 * i) for i in range(1, n_ex // 2)]
-    raw1 = project(more_kernel, order, 2, 2, acts2, grads2, [after(down, *parts), out_sketch], [])
-    lang = after(parts[0], raw1[0]) + sum(scattered)
-    pair = swap(lang, "feat", 1)
-    sent2 = [onward(after(raw1[0], pair), got1[0])]
-    got2 = [lax.ppermute(sent2[0], "feat", round_pairs)]
-    pair = small(stack_kernel, (2, *lang.shape), is_middle, [lang, pair])
-    far_pair = [lax.ppermute(pair, "feat", pairs) for pairs in (inner_pairs, [(1, 3), (2, 0)])]
-    sent2.append(onward(after(raw1[1], pair), got1[1]))
-    got2.append(lax.ppermute(sent2[1], "feat", round_pairs))
+    lang = after(parts[0], sent1[0]) + sum(scattered)
+    other = swap(lang, "feat", 1)
+    raw1 = [after(x, lang) for x in raw1]
+    got2 = [lax.ppermute(raw1[0], "feat", inward)]
+    sent1.append(onward(after(raw0[1], lang), got1[1]))
+    far.append(lax.ppermute(sent1[1], "feat", far_pairs))
+    got2.append(lax.ppermute(after(raw1[1], sent1[1]), "feat", inward))
+    pair = small(stack_kernel, (2, *lang.shape), is_middle, [after(lang, sent1[1]), other])
+    far_pair = [lax.ppermute(pair, "feat", pairs) for pairs in (near_pairs, far_pairs)]
+    near_langs = [pair] + [swap(pair, "ex", mask) for mask in range(2, n_ex, 2)]
     *raw2, own_a, own_b = project(
-        more_kernel, order, 4, 4, acts2, grads2, [after(down, sent2[1]), out_sketch], []
-    )
-    own = [own_a, own_b]
-    sent3 = [onward(raw2[0], got2[0])]
-    got3 = [swap(sent3[0], "feat", 1)]
-    got4 = [lax.ppermute(sent3[0], "feat", inner_pairs)]
-    pair = after(pair, sent3[0])
-    langs = [small(join_kernel, (4, *lang.shape), is_middle, [pair, *far_pair])]
-    langs = langs + [swap(langs[0], "ex", mask) for mask in range(2, n_ex, 2)]
-    sent3.append(onward(after(raw2[1], langs[0]), got2[1]))
-    got3.append(swap(sent3[1], "feat", 1))
-    got4.append(lax.ppermute(sent3[1], "feat", inner_pairs))
-    grad_a, square_a = product(is_middle, [after(own[0], sent3[1]), got1[0], got2[0], got3[0], got4[0]])
-    grad_a = pltpu.with_memory_space_constraint(grad_a, pltpu.VMEM)
-    langs[1:] = [after(x, square_a) for x in langs[1:]]
-    langs = langs + [swap(x, "ex", 1) for x in langs]
-    grad_b, square_b = product(is_middle, [after(own[1], square_a), got1[1], got2[1], got3[1], got4[1]])
-    grad_b = pltpu.with_memory_space_constraint(grad_b, pltpu.VMEM)
+        more_kernel, me_feat, 4, 4, acts2, grads2, [after(down, pair), out_sketch], []
+    )
+    got3 = [swap(x, "feat", 1) for x in raw2]
+    sent2 = [onward(after(raw1[0], own_a), got2[0])]
+    near = [lax.ppermute(sent2[0], "feat", near_pairs)]
+    far_pair = [after(x, sent2[0]) for x in far_pair]
+    pair = small(choose_kernel, pair.shape, is_middle, far_pair)
+    far_langs = [pair] + [swap(pair, "ex", mask) for mask in range(2, n_ex, 2)]
+    sent2.append(onward(after(raw1[1], pair), got2[1]))
+    near.append(lax.ppermute(sent2[1], "feat", near_pairs))
+    near_langs[1:] = [after(x, sent2[1]) for x in near_langs[1:]]
+    near_langs = near_langs + [swap(x, "ex", 1) for x in near_langs]
+    grad_a, square_a = product(is_middle, [after(own_a, sent2[1]), got3[0], far[0], near[0]])
+    far_langs[1:] = [after(x, square_a) for x in far_langs[1:]]
+    far_langs = far_langs + [swap(x, "ex", 1) for x in far_langs]
+    grad_b, square_b = product(is_middle, [after(own_b, square_a), got3[1], far[1], near[1]])
+    langs = near_langs + far_langs
     products = [(grad_a, square_a), (grad_b, square_b)]
     per_lang = perm.shape[0] * n_ex // LANGS
     scale = (KF * per_lang) ** 0.5 / per_lang

time: 93.6 us -> 112 us (1.20)
  starting transfers between devices: 27.8 us -> 48.1 us
  Pallas kernels: 18.8 us -> 17.2 us
    ppermute x4 -> x8, starting transfers between devices: 2.21 us -> 20 us  [the longest x1 7.66 us: ordered(): got2.append(lax.ppermute(after(raw1[1], sent1[1]), 'feat', inward))]
    ppermute x2, waiting for transfers between devices: 11.3 us -> 0.01 us  [ordered(): lax.ppermute(pair, 'feat', pairs)]
    ppermute x22 -> x27, waiting for transfers between devices: 28.4 us -> 36.6 us  [swap(): lax.ppermute(x, axis, [(i, i ^ mask) for i in range(lax.axis_size(axis))])]
    ppermute x4 -> x8, waiting for transfers between devices: 5.93 us -> 9.85 us  [the longest x2 8.16 us: ordered(): got1 = [lax.ppermute(x, 'feat', inward) for x in raw0]]
    ppermute x22 -> x27, starting transfers between devices: 23.6 us -> 26.2 us  [swap(): lax.ppermute(x, axis, [(i, i ^ mask) for i in range(lax.axis_size(axis))])]
    pallas_call x3, Pallas kernels: 13.7 us -> 12.2 us  [project(): pl.pallas_call(kernel, out_shape=[jax.ShapeDtypeStruct(piece, jnp.float32...]
  transfers between devices with their start and end apart: 28 -> 37, of which waited for: 15 -> 14; matrix products, arithmetic and copies ran while one was open for 0% -> 0% of each run, Pallas kernels for 12% -> 9%
where the time goes in v4:
time: 112 us
  starting transfers between devices  48.1 us (43%)
  waiting for transfers between devices  46.4 us (41%)
  Pallas kernels  17.2 us (15%)
    ppermute x27, waiting for transfers between devices, swap(): lax.ppermute(x, axis, [(i, i ^ mask) for i in range(lax.axis_size(axis))])  36.6 us
    ppermute x27, starting transfers between devices, swap(): lax.ppermute(x, axis, [(i, i ^ mask) for i in range(lax.axis_size(axis))])  26.2 us
    pallas_call x3, Pallas kernels, project(): pl.pallas_call(kernel, out_shape=[jax.ShapeDtypeStruct(piece, jnp.float32...  12.2 us
    ppermute x2, waiting for transfers between devices, ordered(): got1 = [lax.ppermute(x, 'feat', inward) for x in raw0]  8.16 us
    ppermute x1, starting transfers between devices, ordered(): got2.append(lax.ppermute(after(raw1[1], sent1[1]), 'feat', inward))  7.66 us
    ppermute x1, starting transfers between devices, ordered(): got2 = [lax.ppermute(raw1[0], 'feat', inward)]  4.41 us
    ppermute x2, starting transfers between devices, ordered(): got1 = [lax.ppermute(x, 'feat', inward) for x in raw0]  3.98 us
  transfers between devices with their start and end apart: 37, of which 14 were waited for; matrix products, arithmetic and copies ran while one was open for 0% of the time, Pallas kernels for 9%

profile of v4, /device:TPU:0, one launch (start us, length us, event | category | flops | bytes accessed | tf_op | source)
XLA Modules:
  0.0 112.1 jit_solution(13080939516649432265)
XLA Ops:
  0.0 3.5 %project.3 = (f32[2,384,128]{2,1,0:T(8,128)S(1)}, f32[2,384,128]{2,1,0:T(8,128)S(1)}, bf16[1024,128]{1,0:T(8,128)(2,1)S(1)}, f32[32,1]{1,0:T(8,128)S(1)}) custom-call(s32[1]{0:T(128)} %bitcast.feat.feat_ref.me_ref, bf16[4096,1024]{1,0:T(8,128)(2,1)} %bitcast.24, bf16[4096,1024]{1,0:T(8,128)(2,1)} %bitcast.27, bf16[1024,128]{1,0:T(8,128)(2,1)} %adapter_ref.1, ...), custom_call_target="tpu_custom_call" | custom-call | flops 536870912 | bytes 4980736 | tf_op jit(solution)/shard_map/project/pallas_call | solution.py:81
  3.5 5.1 %collective-permute-start.2 = (f32[32,1]{1,0:T(8,128)S(1)}, f32[32,1]{1,0:T(8,128)S(1)}, u32[]{:S(2)}, u32[]{:S(2)}) collective-permute-start(f32[32,1]{1,0:T(8,128)S(1)} %get-tuple-element.47.refs_0_), channel_id=1, source_target_pairs={{0,3},{1,2},{2,1},{3,0},{4,7},{5,6},{6,5},{7,4},{8,11},{9,10},{10,... | collective-permute-start | bytes 392 | tf_op jit(solution)/shard_map/ppermute | solution.py:280
  9.3 3.1 %project.4 = (f32[2,384,128]{2,1,0:T(8,128)S(1)}, f32[2,384,128]{2,1,0:T(8,128)S(1)}) custom-call(s32[1]{0:T(128)} %bitcast.feat.feat_ref.me_ref, bf16[4096,1024]{1,0:T(8,128)(2,1)} %bitcast.25, bf16[4096,1024]{1,0:T(8,128)(2,1)} %bitcast.28, bf16[1024,128]{1,0:T(8,128)(2,1)S(1)} %get-tuple-element.67.down_ref, bf16[1024,128]{1,0:T(8,128)(2,1)} %sketch_ref.5), custom_call_target="tpu_custom_call" | custom-call | flops 536870912 | bytes 4980736 | tf_op jit(solution)/shard_map/project/pallas_call | solution.py:81
  13.3 1.6 %lang_parts.1 = (f32[4,64,256]{2,1,0:T(8,128)S(1)}, f32[64,256]{1,0:T(8,128)S(1)}, f32[64,256]{1,0:T(8,128)S(1)}, f32[64,256]{1,0:T(8,128)S(1)}, f32[64,256]{1,0:T(8,128)S(1)}) custom-call(s32[1]{0:T(128)} %bitcast.1.me_ref.ex_ref, f32[32,2048]{1,0:T(8,128)} %held_ref.3, s32[1,32]{1,0:T(1,128)S(1)} %fusion.4.lang_ref, ...), custom_call_target="tpu_custom_call" | custom-call | tf_op jit(solution)/shard_map/lang_parts/pallas_call | solution.py:125
  14.9 2.5 %collective-permute-start.4 = (f32[2,384,128]{2,1,0:T(8,128)S(1)}, f32[2,384,128]{2,1,0:T(8,128)S(1)}, u32[]{:S(2)}, u32[]{:S(2)}) collective-permute-start(f32[2,384,128]{2,1,0:T(8,128)S(1)} %get-tuple-element.56.raw_ref), channel_id=1, source_target_pairs={{0,1},{3,2},{4,5},{7,6},{8,9},{11,10},{12,13},{15,14},{16,17},{19,... | collective-permute-start | bytes 1179656 | tf_op jit(solution)/shard_map/ppermute | solution.py:317
  17.5 1.6 %collective-permute-start.5 = (f32[64,256]{1,0:T(8,128)S(1)}, f32[64,256]{1,0:T(8,128)S(1)}, u32[]{:S(2)}, u32[]{:S(2)}) collective-permute-start(f32[64,256]{1,0:T(8,128)S(1)} %get-tuple-element.91), channel_id=1, source_target_pairs={{0,8},{4,12},{8,0},{12,4},{16,24},{20,28},{24,16},{28,20},{1,9},{5... | collective-permute-start | bytes 196616 | tf_op jit(solution)/shard_map/ppermute | solution.py:280
  22.6 4.3 %collective-permute-done.4.got_ref = f32[2,384,128]{2,1,0:T(8,128)S(1)} collective-permute-done((f32[2,384,128]{2,1,0:T(8,128)S(1)}, f32[2,384,128]{2,1,0:T(8,128)S(1)}, u32[]{:S(2)}, u32[]{:S(2)}) %collective-permute-start.4) | collective-permute-done | bytes 393248 | tf_op jit(solution)/shard_map/ppermute | solution.py:317
  27.0 4.4 %collective-permute-start.12 = (f32[2,384,128]{2,1,0:T(8,128)S(1)}, f32[2,384,128]{2,1,0:T(8,128)S(1)}, u32[]{:S(2)}, u32[]{:S(2)}) collective-permute-start(f32[2,384,128]{2,1,0:T(8,128)S(1)} %get-tuple-element.69.raw_ref), channel_id=1, source_target_pairs={{0,1},{3,2},{4,5},{7,6},{8,9},{11,10},{12,13},{15,14},{16,17},{19,... | collective-permute-start | bytes 1179656 | tf_op jit(solution)/shard_map/ppermute | solution.py:330
  31.5 3.8 %collective-permute-done.8.got_ref = f32[2,384,128]{2,1,0:T(8,128)S(1)} collective-permute-done((f32[2,384,128]{2,1,0:T(8,128)S(1)}, f32[2,384,128]{2,1,0:T(8,128)S(1)}, u32[]{:S(2)}, u32[]{:S(2)}) %collective-permute-start.8) | collective-permute-done | bytes 393248 | tf_op jit(solution)/shard_map/ppermute | solution.py:317
  35.4 9.3 %collective-permute-done.9.two_ref = f32[64,256]{1,0:T(8,128)S(1)} collective-permute-done((f32[64,256]{1,0:T(8,128)S(1)}, f32[64,256]{1,0:T(8,128)S(1)}, u32[]{:S(2)}, u32[]{:S(2)}) %collective-permute-start.9) | collective-permute-done | bytes 65568 | tf_op jit(solution)/shard_map/ppermute | solution.py:280
  46.7 2.5 %collective-permute-start.16 = (f32[2,64,256]{2,1,0:T(8,128)S(1)}, f32[2,64,256]{2,1,0:T(8,128)S(1)}, u32[]{:S(2)}, u32[]{:S(2)}) collective-permute-start(f32[2,64,256]{2,1,0:T(8,128)S(1)} %shard_map.75.refs_0_), channel_id=1, source_target_pairs={{0,24},{4,28},{8,16},{12,20},{16,8},{20,12},{24,0},{28,4},{1,25},{... | collective-permute-start | bytes 393224 | tf_op jit(solution)/shard_map/ppermute | solution.py:280
  49.2 7.7 %collective-permute-start.14 = (f32[2,384,128]{2,1,0:T(8,128)S(1)}, f32[2,384,128]{2,1,0:T(8,128)S(1)}, u32[]{:S(2)}, u32[]{:S(2)}) collective-permute-start(f32[2,384,128]{2,1,0:T(8,128)S(1)} %get-tuple-element.73.raw_ref), channel_id=1, source_target_pairs={{0,1},{3,2},{4,5},{7,6},{8,9},{11,10},{12,13},{15,14},{16,17},{19,... | collective-permute-start | bytes 1179656 | tf_op jit(solution)/shard_map/ppermute | solution.py:333
  56.9 5.6 %project.5 = (f32[2,384,128]{2,1,0:T(8,128)S(1)}, f32[2,384,128]{2,1,0:T(8,128)S(1)}, f32[2,384,128]{2,1,0:T(8,128)S(1)}, f32[2,384,128]{2,1,0:T(8,128)S(1)}) custom-call(s32[1]{0:T(128)} %bitcast.feat.feat_ref.me_ref, bf16[4096,1024]{1,0:T(8,128)(2,1)} %bitcast.26, bf16[4096,1024]{1,0:T(8,128)(2,1)} %bitcast.29, ...), custom_call_target="tpu_custom_call" | custom-call | flops 1073741824 | bytes 9961472 | tf_op jit(solution)/shard_map/project/pallas_call | solution.py:81
  63.8 3.8 %collective-permute-start.22 = (f32[2,384,128]{2,1,0:T(8,128)S(1)}, f32[2,384,128]{2,1,0:T(8,128)S(1)}, u32[]{:S(2)}, u32[]{:S(2)}) collective-permute-start(f32[2,384,128]{2,1,0:T(8,128)S(1)} %get-tuple-element.78), channel_id=1, source_target_pairs={{0,1},{1,0},{2,3},{3,2},{4,5},{5,4},{6,7},{7,6},{8,9},{9,8},{10,11... | collective-permute-start | bytes 1179656 | tf_op jit(solution)/shard_map/ppermute | solution.py:280
  68.1 4.5 %collective-permute-done.15.refs_2_ = f32[2,64,256]{2,1,0:T(8,128)S(1)} collective-permute-done((f32[2,64,256]{2,1,0:T(8,128)S(1)}, f32[2,64,256]{2,1,0:T(8,128)S(1)}, u32[]{:S(2)}, u32[]{:S(2)}) %collective-permute-start.15) | collective-permute-done | bytes 131104 | tf_op jit(solution)/shard_map/ppermute | solution.py:280
  73.1 4.8 %collective-permute-done.10.refs_1_ = f32[2,64,256]{2,1,0:T(8,128)S(1)} collective-permute-done((f32[2,64,256]{2,1,0:T(8,128)S(1)}, f32[2,64,256]{2,1,0:T(8,128)S(1)}, u32[]{:S(2)}, u32[]{:S(2)}) %collective-permute-start.10) | collective-permute-done | bytes 131104 | tf_op jit(solution)/shard_map/ppermute | solution.py:280
  80.1 2.6 %collective-permute-start.31 = (f32[2,384,128]{2,1,0:T(8,128)S(1)}, f32[2,384,128]{2,1,0:T(8,128)S(1)}, u32[]{:S(2)}, u32[]{:S(2)}) collective-permute-start(f32[2,384,128]{2,1,0:T(8,128)S(1)} %get-tuple-element.86), channel_id=1, source_target_pairs={{0,1},{1,0},{2,3},{3,2},{4,5},{5,4},{6,7},{7,6},{8,9},{9,8},{10,11... | collective-permute-start | bytes 1179656 | tf_op jit(solution)/shard_map/ppermute | solution.py:280
  82.6 3.1 %collective-permute-done.22.raw_ref = f32[2,384,128]{2,1,0:T(8,128)S(1)} collective-permute-done((f32[2,384,128]{2,1,0:T(8,128)S(1)}, f32[2,384,128]{2,1,0:T(8,128)S(1)}, u32[]{:S(2)}, u32[]{:S(2)}) %collective-permute-start.22) | collective-permute-done | bytes 393248 | tf_op jit(solution)/shard_map/ppermute | solution.py:280
  86.7 4.2 %collective-permute-done.25.refs_10_ = f32[2,64,256]{2,1,0:T(8,128)S(1)} collective-permute-done((f32[2,64,256]{2,1,0:T(8,128)S(1)}, f32[2,64,256]{2,1,0:T(8,128)S(1)}, u32[]{:S(2)}, u32[]{:S(2)}) %collective-permute-start.25) | collective-permute-done | bytes 131104 | tf_op jit(solution)/shard_map/ppermute | solution.py:280
  90.9 5.0 %collective-permute-done.21.refs_9_ = f32[2,64,256]{2,1,0:T(8,128)S(1)} collective-permute-done((f32[2,64,256]{2,1,0:T(8,128)S(1)}, f32[2,64,256]{2,1,0:T(8,128)S(1)}, u32[]{:S(2)}, u32[]{:S(2)}) %collective-permute-start.21) | collective-permute-done | bytes 131104 | tf_op jit(solution)/shard_map/ppermute | solution.py:280
  97.2 1.7 %collective-permute-done.32.far_ref = f32[2,384,128]{2,1,0:T(8,128)S(1)} collective-permute-done((f32[2,384,128]{2,1,0:T(8,128)S(1)}, f32[2,384,128]{2,1,0:T(8,128)S(1)}, u32[]{:S(2)}, u32[]{:S(2)}) %collective-permute-start.32) | collective-permute-done | bytes 393248 | tf_op jit(solution)/shard_map/ppermute | solution.py:332
  103.3 2.5 %collective-permute-start.34 = (f32[16,64]{1,0:T(8,128)S(1)}, f32[16,64]{1,0:T(8,128)S(1)}, u32[]{:S(2)}, u32[]{:S(2)}) collective-permute-start(f32[16,64]{1,0:T(8,128)S(1)} %score.1.refs_0_), channel_id=1, source_target_pairs={{0,1},{1,0},{2,3},{3,2},{4,5},{5,4},{6,7},{7,6},{8,9},{9,8},{10,11... | collective-permute-start | bytes 12296 | tf_op jit(solution)/shard_map/ppermute | solution.py:280
  106.0 2.2 %collective-permute-start.36 = (f32[16,64]{1,0:T(8,128)S(1)}, f32[16,64]{1,0:T(8,128)S(1)}, u32[]{:S(2)}, u32[]{:S(2)}) collective-permute-start(f32[16,64]{1,0:T(8,128)S(1)} %score.1.refs_0_), channel_id=1, source_target_pairs={{0,3},{1,2},{2,1},{3,0},{4,7},{5,6},{6,5},{7,4},{8,11},{9,10},{10,... | collective-permute-start | bytes 12296 | tf_op jit(solution)/shard_map/ppermute | solution.py:280
  108.3 2.1 %collective-permute-done.35.refs_2_ = f32[16,64]{1,0:T(8,128)S(1)} collective-permute-done((f32[16,64]{1,0:T(8,128)S(1)}, f32[16,64]{1,0:T(8,128)S(1)}, u32[]{:S(2)}, u32[]{:S(2)}) %collective-permute-start.35) | collective-permute-done | bytes 4128 | tf_op jit(solution)/shard_map/ppermute | solution.py:280
  (69 shorter events, 20.3 us)
Async XLA Ops:
  3.5 8.9 %collective-permute-start.2 = (f32[32,1]{1,0:T(8,128)S(1)}, f32[32,1]{1,0:T(8,128)S(1)}, u32[]{:S(2)}, u32[]{:S(2)}) collective-permute-start(f32[32,1]{1,0:T(8,128)S(1)} %get-tuple-element.47.refs_0_), channel_id=1, source_target_pairs={{0,3},{1,2},{2,1},{3,0},{4,7},{5,6},{6,5},{7,4},{8,11},{9,10},{10,... | collective-permute-start | bytes 392 | tf_op jit(solution)/shard_map/ppermute | solution.py:280
  14.9 12.0 %collective-permute-start.4 = (f32[2,384,128]{2,1,0:T(8,128)S(1)}, f32[2,384,128]{2,1,0:T(8,128)S(1)}, u32[]{:S(2)}, u32[]{:S(2)}) collective-permute-start(f32[2,384,128]{2,1,0:T(8,128)S(1)} %get-tuple-element.56.raw_ref), channel_id=1, source_target_pairs={{0,1},{3,2},{4,5},{7,6},{8,9},{11,10},{12,13},{15,14},{16,17},{19,... | collective-permute-start | bytes 1179656 | tf_op jit(solution)/shard_map/ppermute | solution.py:317
  17.5 9.5 %collective-permute-start.5 = (f32[64,256]{1,0:T(8,128)S(1)}, f32[64,256]{1,0:T(8,128)S(1)}, u32[]{:S(2)}, u32[]{:S(2)}) collective-permute-start(f32[64,256]{1,0:T(8,128)S(1)} %get-tuple-element.91), channel_id=1, source_target_pairs={{0,8},{4,12},{8,0},{12,4},{16,24},{20,28},{24,16},{28,20},{1,9},{5... | collective-permute-start | bytes 196616 | tf_op jit(solution)/shard_map/ppermute | solution.py:280
  19.1 7.9 %collective-permute-start.6 = (f32[64,256]{1,0:T(8,128)S(1)}, f32[64,256]{1,0:T(8,128)S(1)}, u32[]{:S(2)}, u32[]{:S(2)}) collective-permute-start(f32[64,256]{1,0:T(8,128)S(1)} %get-tuple-element.89), channel_id=1, source_target_pairs={{0,16},{4,20},{8,24},{12,28},{16,0},{20,4},{24,8},{28,12},{1,17},{... | collective-permute-start | bytes 196616 | tf_op jit(solution)/shard_map/ppermute | solution.py:280
  20.6 6.4 %collective-permute-start.7 = (f32[64,256]{1,0:T(8,128)S(1)}, f32[64,256]{1,0:T(8,128)S(1)}, u32[]{:S(2)}, u32[]{:S(2)}) collective-permute-start(f32[64,256]{1,0:T(8,128)S(1)} %get-tuple-element.90), channel_id=1, source_target_pairs={{0,24},{4,28},{8,16},{12,20},{16,8},{20,12},{24,0},{28,4},{1,25},{... | collective-permute-start | bytes 196616 | tf_op jit(solution)/shard_map/ppermute | solution.py:280
  21.1 14.3 %collective-permute-start.8 = (f32[2,384,128]{2,1,0:T(8,128)S(1)}, f32[2,384,128]{2,1,0:T(8,128)S(1)}, u32[]{:S(2)}, u32[]{:S(2)}) collective-permute-start(f32[2,384,128]{2,1,0:T(8,128)S(1)} %get-tuple-element.62.raw_ref), channel_id=1, source_target_pairs={{0,1},{3,2},{4,5},{7,6},{8,9},{11,10},{12,13},{15,14},{16,17},{19,... | collective-permute-start | bytes 1179656 | tf_op jit(solution)/shard_map/ppermute | solution.py:317
  27.0 46.1 %collective-permute-start.12 = (f32[2,384,128]{2,1,0:T(8,128)S(1)}, f32[2,384,128]{2,1,0:T(8,128)S(1)}, u32[]{:S(2)}, u32[]{:S(2)}) collective-permute-start(f32[2,384,128]{2,1,0:T(8,128)S(1)} %get-tuple-element.69.raw_ref), channel_id=1, source_target_pairs={{0,1},{3,2},{4,5},{7,6},{8,9},{11,10},{12,13},{15,14},{16,17},{19,... | collective-permute-start | bytes 1179656 | tf_op jit(solution)/shard_map/ppermute | solution.py:330
  31.4 13.2 %collective-permute-start.9 = (f32[64,256]{1,0:T(8,128)S(1)}, f32[64,256]{1,0:T(8,128)S(1)}, u32[]{:S(2)}, u32[]{:S(2)}) collective-permute-start(f32[64,256]{1,0:T(8,128)S(1)} %add_add_fusion.one_ref), channel_id=1, source_target_pairs={{0,1},{1,0},{2,3},{3,2},{4,5},{5,4},{6,7},{7,6},{8,9},{9,8},{10,11... | collective-permute-start | bytes 196616 | tf_op jit(solution)/shard_map/ppermute | solution.py:280
  44.7 17.8 %collective-permute-start.13 = (f32[2,64,256]{2,1,0:T(8,128)S(1)}, f32[2,64,256]{2,1,0:T(8,128)S(1)}, u32[]{:S(2)}, u32[]{:S(2)}) collective-permute-start(f32[2,64,256]{2,1,0:T(8,128)S(1)} %shard_map.75.refs_0_), channel_id=1, source_target_pairs={{1,3},{2,0},{5,7},{6,4},{9,11},{10,8},{13,15},{14,12},{17,19},{18,... | collective-permute-start | bytes 393224 | tf_op jit(solution)/shard_map/ppermute | solution.py:335
  46.0 17.8 %collective-permute-start.11 = (f32[2,64,256]{2,1,0:T(8,128)S(1)}, f32[2,64,256]{2,1,0:T(8,128)S(1)}, u32[]{:S(2)}, u32[]{:S(2)}) collective-permute-start(f32[2,64,256]{2,1,0:T(8,128)S(1)} %shard_map.75.refs_0_), channel_id=1, source_target_pairs={{1,2},{2,1},{0,0},{3,3},{5,6},{6,5},{4,4},{7,7},{9,10},{10,9},{8,8... | collective-permute-start | bytes 393224 | tf_op jit(solution)/shard_map/ppermute | solution.py:335
  46.7 20.9 %collective-permute-start.16 = (f32[2,64,256]{2,1,0:T(8,128)S(1)}, f32[2,64,256]{2,1,0:T(8,128)S(1)}, u32[]{:S(2)}, u32[]{:S(2)}) collective-permute-start(f32[2,64,256]{2,1,0:T(8,128)S(1)} %shard_map.75.refs_0_), channel_id=1, source_target_pairs={{0,24},{4,28},{8,16},{12,20},{16,8},{20,12},{24,0},{28,4},{1,25},{... | collective-permute-start | bytes 393224 | tf_op jit(solution)/shard_map/ppermute | solution.py:280
  49.2 29.6 %collective-permute-start.14 = (f32[2,384,128]{2,1,0:T(8,128)S(1)}, f32[2,384,128]{2,1,0:T(8,128)S(1)}, u32[]{:S(2)}, u32[]{:S(2)}) collective-permute-start(f32[2,384,128]{2,1,0:T(8,128)S(1)} %get-tuple-element.73.raw_ref), channel_id=1, source_target_pairs={{0,1},{3,2},{4,5},{7,6},{8,9},{11,10},{12,13},{15,14},{16,17},{19,... | collective-permute-start | bytes 1179656 | tf_op jit(solution)/shard_map/ppermute | solution.py:333
  62.5 17.6 %collective-permute-start.23 = (f32[2,384,128]{2,1,0:T(8,128)S(1)}, f32[2,384,128]{2,1,0:T(8,128)S(1)}, u32[]{:S(2)}, u32[]{:S(2)}) collective-permute-start(f32[2,384,128]{2,1,0:T(8,128)S(1)} %shard_map.73), channel_id=1, source_target_pairs={{1,3},{2,0},{5,7},{6,4},{9,11},{10,8},{13,15},{14,12},{17,19},{18,... | collective-permute-start | bytes 1179656 | tf_op jit(solution)/shard_map/ppermute | solution.py:325
  63.8 22.0 %collective-permute-start.22 = (f32[2,384,128]{2,1,0:T(8,128)S(1)}, f32[2,384,128]{2,1,0:T(8,128)S(1)}, u32[]{:S(2)}, u32[]{:S(2)}) collective-permute-start(f32[2,384,128]{2,1,0:T(8,128)S(1)} %get-tuple-element.78), channel_id=1, source_target_pairs={{0,1},{1,0},{2,3},{3,2},{4,5},{5,4},{6,7},{7,6},{8,9},{9,8},{10,11... | collective-permute-start | bytes 1179656 | tf_op jit(solution)/shard_map/ppermute | solution.py:280
  72.5 5.4 %collective-permute-start.10 = (f32[2,64,256]{2,1,0:T(8,128)S(1)}, f32[2,64,256]{2,1,0:T(8,128)S(1)}, u32[]{:S(2)}, u32[]{:S(2)}) collective-permute-start(f32[2,64,256]{2,1,0:T(8,128)S(1)} %shard_map.75.refs_0_), channel_id=1, source_target_pairs={{0,8},{4,12},{8,0},{12,4},{16,24},{20,28},{24,16},{28,20},{1,9},{5... | collective-permute-start | bytes 393224 | tf_op jit(solution)/shard_map/ppermute | solution.py:280
  73.1 5.5 %collective-permute-start.17 = (f32[2,64,256]{2,1,0:T(8,128)S(1)}, f32[2,64,256]{2,1,0:T(8,128)S(1)}, u32[]{:S(2)}, u32[]{:S(2)}) collective-permute-start(f32[2,64,256]{2,1,0:T(8,128)S(1)} %shard_map.75.refs_0_), channel_id=1, source_target_pairs={{0,4},{4,0},{8,12},{12,8},{16,20},{20,16},{24,28},{28,24},{1,5},{5... | collective-permute-start | bytes 393224 | tf_op jit(solution)/shard_map/ppermute | solution.py:280
  77.9 18.0 %collective-permute-start.24 = (f32[2,384,128]{2,1,0:T(8,128)S(1)}, f32[2,384,128]{2,1,0:T(8,128)S(1)}, u32[]{:S(2)}, u32[]{:S(2)}) collective-permute-start(f32[2,384,128]{2,1,0:T(8,128)S(1)} %shard_map.76), channel_id=1, source_target_pairs={{1,2},{2,1},{0,0},{3,3},{5,6},{6,5},{4,4},{7,7},{9,10},{10,9},{8,8... | collective-permute-start | bytes 1179656 | tf_op jit(solution)/shard_map/ppermute | solution.py:342
  78.6 7.3 %collective-permute-start.26 = (f32[2,64,256]{2,1,0:T(8,128)S(1)}, f32[2,64,256]{2,1,0:T(8,128)S(1)}, u32[]{:S(2)}, u32[]{:S(2)}) collective-permute-start(f32[2,64,256]{2,1,0:T(8,128)S(1)} %shard_map.77.refs_8_), channel_id=1, source_target_pairs={{0,24},{4,28},{8,16},{12,20},{16,8},{20,12},{24,0},{28,4},{1,25},{... | collective-permute-start | bytes 393224 | tf_op jit(solution)/shard_map/ppermute | solution.py:280
  78.8 20.1 %collective-permute-start.32 = (f32[2,384,128]{2,1,0:T(8,128)S(1)}, f32[2,384,128]{2,1,0:T(8,128)S(1)}, u32[]{:S(2)}, u32[]{:S(2)}) collective-permute-start(f32[2,384,128]{2,1,0:T(8,128)S(1)} %shard_map.74), channel_id=1, source_target_pairs={{1,3},{2,0},{5,7},{6,4},{9,11},{10,8},{13,15},{14,12},{17,19},{18,... | collective-permute-start | bytes 1179656 | tf_op jit(solution)/shard_map/ppermute | solution.py:332
  80.1 20.3 %collective-permute-start.31 = (f32[2,384,128]{2,1,0:T(8,128)S(1)}, f32[2,384,128]{2,1,0:T(8,128)S(1)}, u32[]{:S(2)}, u32[]{:S(2)}) collective-permute-start(f32[2,384,128]{2,1,0:T(8,128)S(1)} %get-tuple-element.86), channel_id=1, source_target_pairs={{0,1},{1,0},{2,3},{3,2},{4,5},{5,4},{6,7},{7,6},{8,9},{9,8},{10,11... | collective-permute-start | bytes 1179656 | tf_op jit(solution)/shard_map/ppermute | solution.py:280
  85.8 5.1 %collective-permute-start.25 = (f32[2,64,256]{2,1,0:T(8,128)S(1)}, f32[2,64,256]{2,1,0:T(8,128)S(1)}, u32[]{:S(2)}, u32[]{:S(2)}) collective-permute-start(f32[2,64,256]{2,1,0:T(8,128)S(1)} %shard_map.77.refs_8_), channel_id=1, source_target_pairs={{0,16},{4,20},{8,24},{12,28},{16,0},{20,4},{24,8},{28,12},{1,17},{... | collective-permute-start | bytes 393224 | tf_op jit(solution)/shard_map/ppermute | solution.py:280
  86.0 15.0 %collective-permute-start.33 = (f32[2,384,128]{2,1,0:T(8,128)S(1)}, f32[2,384,128]{2,1,0:T(8,128)S(1)}, u32[]{:S(2)}, u32[]{:S(2)}) collective-permute-start(f32[2,384,128]{2,1,0:T(8,128)S(1)} %shard_map.78), channel_id=1, source_target_pairs={{1,2},{2,1},{0,0},{3,3},{5,6},{6,5},{4,4},{7,7},{9,10},{10,9},{8,8... | collective-permute-start | bytes 1179656 | tf_op jit(solution)/shard_map/ppermute | solution.py:347
  95.9 5.0 %collective-permute-start.19 = (f32[2,64,256]{2,1,0:T(8,128)S(1)}, f32[2,64,256]{2,1,0:T(8,128)S(1)}, u32[]{:S(2)}, u32[]{:S(2)}) collective-permute-start(f32[2,64,256]{2,1,0:T(8,128)S(1)} %collective-permute-done.15.refs_2_), channel_id=1, source_target_pairs={{0,4},{4,0},{8,12},{12,8},{16,20},{20,16},{24,28},{28,24},{1,5},{5... | collective-permute-start | bytes 393224 | tf_op jit(solution)/shard_map/ppermute | solution.py:280
  106.0 5.4 %collective-permute-start.36 = (f32[16,64]{1,0:T(8,128)S(1)}, f32[16,64]{1,0:T(8,128)S(1)}, u32[]{:S(2)}, u32[]{:S(2)}) collective-permute-start(f32[16,64]{1,0:T(8,128)S(1)} %score.1.refs_0_), channel_id=1, source_target_pairs={{0,3},{1,2},{2,1},{3,0},{4,7},{5,6},{6,5},{7,4},{8,11},{9,10},{10,... | collective-permute-start | bytes 12296 | tf_op jit(solution)/shard_map/ppermute | solution.py:280
  (14 other events, 48.9 us)

commit v5 on v4

--- a/solution.py
+++ b/solution.py
@@ -199,11 +199,10 @@
     middle = (feat == 1) | (feat == 2)
     second = feat ^ jnp.where(middle, 3, 2)
     rows_from = [feat, feat ^ 1, second, second ^ 1]
-    n_ex = n_lang // 2
-    masks = [*range(0, n_ex, 2), *range(1, n_ex, 2)]
+    masks = [*range(0, n_lang, 2), *range(1, n_lang, 2)]
     for j, ref in enumerate(lang_refs):
-        for m in range(2):
-            index = rows_from[j // n_ex * 2 + m] * n_ex + (ex ^ masks[j % n_ex])
+        for m in range(4):
+            index = rows_from[m] * n_lang + (ex ^ masks[j])
             lang = ref[m]
             rest = lang - lang.astype(jnp.bfloat16).astype(jnp.float32)
             lang = jnp.concatenate([lang, rest], axis=0).astype(jnp.bfloat16)
@@ -253,8 +252,13 @@
     o_ref[1] = two_ref[...]
 
 
-def choose_kernel(middle_ref, inner_ref, outer_ref, o_ref):
-    o_ref[...] = jnp.where(middle_ref[0] == 1, inner_ref[...], outer_ref[...])
+def route_kernel(middle_ref, raw_ref, got_ref, end_ref, o_ref):
+    o_ref[...] = jnp.where(middle_ref[0] == 1, raw_ref[...] + got_ref[...], end_ref[...])
+
+
+def join_kernel(middle_ref, pair_ref, inner_ref, outer_ref, o_ref):
+    o_ref[:2] = pair_ref[...]
+    o_ref[2:] = jnp.where(middle_ref[0] == 1, inner_ref[...], outer_ref[...])
 
 
 def place_kernel(me_ref, *refs):
@@ -304,6 +308,7 @@
     square_like = jax.ShapeDtypeStruct((held.shape[0], 1), jnp.float32)
     inward = [(0, 1), (3, 2)]
     far_pairs = [(1, 3), (2, 0)]
+    round_pairs = inward + far_pairs
     near_pairs = [(1, 2), (2, 1), (0, 0), (3, 3)]
     is_middle = middle.astype(jnp.int32).reshape(1)
 
@@ -327,31 +332,26 @@
     lang = after(parts[0], sent1[0]) + sum(scattered)
     other = swap(lang, "feat", 1)
     raw1 = [after(x, lang) for x in raw1]
-    got2 = [lax.ppermute(raw1[0], "feat", inward)]
-    sent1.append(onward(after(raw0[1], lang), got1[1]))
-    far.append(lax.ppermute(sent1[1], "feat", far_pairs))
-    got2.append(lax.ppermute(after(raw1[1], sent1[1]), "feat", inward))
+    sent1.append(small(route_kernel, raw1[0].shape, is_middle, [raw0[1], got1[1], after(raw1[0], other)]))
+    round_a = lax.ppermute(sent1[1], "feat", round_pairs)
     pair = small(stack_kernel, (2, *lang.shape), is_middle, [after(lang, sent1[1]), other])
     far_pair = [lax.ppermute(pair, "feat", pairs) for pairs in (near_pairs, far_pairs)]
-    near_langs = [pair] + [swap(pair, "ex", mask) for mask in range(2, n_ex, 2)]
+    got2 = [round_a, lax.ppermute(after(raw1[1], pair), "feat", inward)]
     *raw2, own_a, own_b = project(
         more_kernel, me_feat, 4, 4, acts2, grads2, [after(down, pair), out_sketch], []
     )
-    got3 = [swap(x, "feat", 1) for x in raw2]
+    got3 = [swap(raw2[0], "feat", 1)]
     sent2 = [onward(after(raw1[0], own_a), got2[0])]
     near = [lax.ppermute(sent2[0], "feat", near_pairs)]
-    far_pair = [after(x, sent2[0]) for x in far_pair]
-    pair = small(choose_kernel, pair.shape, is_middle, far_pair)
-    far_langs = [pair] + [swap(pair, "ex", mask) for mask in range(2, n_ex, 2)]
-    sent2.append(onward(after(raw1[1], pair), got2[1]))
+    langs = [small(join_kernel, (4, *lang.shape), is_middle, [after(pair, sent2[0]), *far_pair])]
+    langs = langs + [swap(langs[0], "ex", mask) for mask in range(2, n_ex, 2)]
+    got3.append(swap(after(raw2[1], sent2[0]), "feat", 1))
+    sent2.append(onward(after(raw1[1], langs[0]), got2[1]))
     near.append(lax.ppermute(sent2[1], "feat", near_pairs))
-    near_langs[1:] = [after(x, sent2[1]) for x in near_langs[1:]]
-    near_langs = near_langs + [swap(x, "ex", 1) for x in near_langs]
     grad_a, square_a = product(is_middle, [after(own_a, sent2[1]), got3[0], far[0], near[0]])
-    far_langs[1:] = [after(x, square_a) for x in far_langs[1:]]
-    far_langs = far_langs + [swap(x, "ex", 1) for x in far_langs]
-    grad_b, square_b = product(is_middle, [after(own_b, square_a), got3[1], far[1], near[1]])
-    langs = near_langs + far_langs
+    langs[1:] = [after(x, square_a) for x in langs[1:]]
+    langs = langs + [swap(x, "ex", 1) for x in langs]
+    grad_b, square_b = product(is_middle, [after(own_b, square_a), got3[1], round_a, near[1]])
     products = [(grad_a, square_a), (grad_b, square_b)]
     per_lang = perm.shape[0] * n_ex // LANGS
     scale = (KF * per_lang) ** 0.5 / per_lang

time: 112 us -> 96.9 us (0.87)
  starting transfers between devices: 48.1 us -> 37.5 us
  waiting for transfers between devices: 46.4 us -> 41.6 us
    ppermute x2, waiting for transfers between devices: 0.01 us -> 17.1 us  [ordered(): lax.ppermute(pair, 'feat', pairs)]
    ppermute x27 -> x20, waiting for transfers between devices: 36.6 us -> 20 us  [swap(): lax.ppermute(x, axis, [(i, i ^ mask) for i in range(lax.axis_size(axis))])]
    ppermute x27 -> x20, starting transfers between devices: 26.2 us -> 20.5 us  [swap(): lax.ppermute(x, axis, [(i, i ^ mask) for i in range(lax.axis_size(axis))])]
    ppermute x3 -> x2, starting transfers between devices: 13.3 us -> 8.58 us  [the longest x1 6.05 us: ordered(): got2 = [round_a, lax.ppermute(after(raw1[1], pair), 'feat', inward)]]
    ppermute x2, waiting for transfers between devices: 8.16 us -> 4.53 us  [ordered(): got1 = [lax.ppermute(x, 'feat', inward) for x in raw0]]
    ppermute x3 -> x2, waiting for transfers between devices: 1.68 us -> 0.01 us  [the longest x1 0.01 us: ordered(): round_a = lax.ppermute(sent1[1], 'feat', round_pairs)]
  transfers between devices with their start and end apart: 37 -> 29, of which waited for: 14 -> 13; matrix products, arithmetic and copies ran while one was open for 0% -> 0% of each run, Pallas kernels for 9% -> 11%
where the time goes in v5:
time: 96.9 us; the launch traced here: 96.6 us
  waiting for transfers between devices  41.6 us (43%)
  starting transfers between devices  37.5 us (39%)
  Pallas kernels  17.2 us (18%)
    ppermute x20, starting transfers between devices, swap(): lax.ppermute(x, axis, [(i, i ^ mask) for i in range(lax.axis_size(axis))])  20.5 us
    ppermute x20, waiting for transfers between devices, swap(): lax.ppermute(x, axis, [(i, i ^ mask) for i in range(lax.axis_size(axis))])  20 us
    ppermute x2, waiting for transfers between devices, ordered(): lax.ppermute(pair, 'feat', pairs)  17.1 us
    pallas_call x3, Pallas kernels, project(): pl.pallas_call(kernel, out_shape=[jax.ShapeDtypeStruct(piece, jnp.float32...  12.2 us
    ppermute x1, starting transfers between devices, ordered(): got2 = [round_a, lax.ppermute(after(raw1[1], pair), 'feat', inward)]  6.05 us
    ppermute x2, waiting for transfers between devices, ordered(): got1 = [lax.ppermute(x, 'feat', inward) for x in raw0]  4.53 us
    ppermute x2, starting transfers between devices, ordered(): got1 = [lax.ppermute(x, 'feat', inward) for x in raw0]  3.81 us
    ppermute x1, starting transfers between devices, ordered(): round_a = lax.ppermute(sent1[1], 'feat', round_pairs)  2.53 us
  transfers between devices with their start and end apart: 29, of which 13 were waited for; matrix products, arithmetic and copies ran while one was open for 0% of the time, Pallas kernels for 11%

profile of v5, /device:TPU:0, one launch (start us, length us, event | category | flops | bytes accessed | tf_op | source)
XLA Modules:
  0.0 96.6 jit_solution(9721983356941600678)
XLA Ops:
  0.0 3.5 %project.3 = (f32[2,384,128]{2,1,0:T(8,128)S(1)}, f32[2,384,128]{2,1,0:T(8,128)S(1)}, bf16[1024,128]{1,0:T(8,128)(2,1)S(1)}, f32[32,1]{1,0:T(8,128)S(1)}) custom-call(s32[1]{0:T(128)} %bitcast.feat.feat_ref.me_ref, bf16[4096,1024]{1,0:T(8,128)(2,1)} %bitcast.24, bf16[4096,1024]{1,0:T(8,128)(2,1)} %bitcast.27, bf16[1024,128]{1,0:T(8,128)(2,1)} %adapter_ref.1, ...), custom_call_target="tpu_custom_call" | custom-call | flops 536870912 | bytes 4980736 | tf_op jit(solution)/shard_map/project/pallas_call | solution.py:81
  3.5 5.1 %collective-permute-start.2 = (f32[32,1]{1,0:T(8,128)S(1)}, f32[32,1]{1,0:T(8,128)S(1)}, u32[]{:S(2)}, u32[]{:S(2)}) collective-permute-start(f32[32,1]{1,0:T(8,128)S(1)} %get-tuple-element.44.refs_0_), channel_id=1, source_target_pairs={{0,3},{1,2},{2,1},{3,0},{4,7},{5,6},{6,5},{7,4},{8,11},{9,10},{10,... | collective-permute-start | bytes 392 | tf_op jit(solution)/shard_map/ppermute | solution.py:284
  9.3 3.1 %project.4 = (f32[2,384,128]{2,1,0:T(8,128)S(1)}, f32[2,384,128]{2,1,0:T(8,128)S(1)}) custom-call(s32[1]{0:T(128)} %bitcast.feat.feat_ref.me_ref, bf16[4096,1024]{1,0:T(8,128)(2,1)} %bitcast.25, bf16[4096,1024]{1,0:T(8,128)(2,1)} %bitcast.28, bf16[1024,128]{1,0:T(8,128)(2,1)S(1)} %get-tuple-element.62.down_ref, bf16[1024,128]{1,0:T(8,128)(2,1)} %sketch_ref.5), custom_call_target="tpu_custom_call" | custom-call | flops 536870912 | bytes 4980736 | tf_op jit(solution)/shard_map/project/pallas_call | solution.py:81
  13.3 1.6 %lang_parts.1 = (f32[4,64,256]{2,1,0:T(8,128)S(1)}, f32[64,256]{1,0:T(8,128)S(1)}, f32[64,256]{1,0:T(8,128)S(1)}, f32[64,256]{1,0:T(8,128)S(1)}, f32[64,256]{1,0:T(8,128)S(1)}) custom-call(s32[1]{0:T(128)} %bitcast.1.me_ref.ex_ref, f32[32,2048]{1,0:T(8,128)} %held_ref.3, s32[1,32]{1,0:T(1,128)S(1)} %fusion.4.lang_ref, ...), custom_call_target="tpu_custom_call" | custom-call | tf_op jit(solution)/shard_map/lang_parts/pallas_call | solution.py:125
  14.9 2.5 %collective-permute-start.4 = (f32[2,384,128]{2,1,0:T(8,128)S(1)}, f32[2,384,128]{2,1,0:T(8,128)S(1)}, u32[]{:S(2)}, u32[]{:S(2)}) collective-permute-start(f32[2,384,128]{2,1,0:T(8,128)S(1)} %get-tuple-element.53.raw_ref), channel_id=1, source_target_pairs={{0,1},{3,2},{4,5},{7,6},{8,9},{11,10},{12,13},{15,14},{16,17},{19,... | collective-permute-start | bytes 1179656 | tf_op jit(solution)/shard_map/ppermute | solution.py:322
  17.5 1.3 %collective-permute-start.8 = (f32[2,384,128]{2,1,0:T(8,128)S(1)}, f32[2,384,128]{2,1,0:T(8,128)S(1)}, u32[]{:S(2)}, u32[]{:S(2)}) collective-permute-start(f32[2,384,128]{2,1,0:T(8,128)S(1)} %get-tuple-element.58.raw_ref), channel_id=1, source_target_pairs={{0,1},{3,2},{4,5},{7,6},{8,9},{11,10},{12,13},{15,14},{16,17},{19,... | collective-permute-start | bytes 1179656 | tf_op jit(solution)/shard_map/ppermute | solution.py:322
  18.8 1.6 %collective-permute-start.5 = (f32[64,256]{1,0:T(8,128)S(1)}, f32[64,256]{1,0:T(8,128)S(1)}, u32[]{:S(2)}, u32[]{:S(2)}) collective-permute-start(f32[64,256]{1,0:T(8,128)S(1)} %get-tuple-element.85), channel_id=1, source_target_pairs={{0,8},{4,12},{8,0},{12,4},{16,24},{20,28},{24,16},{28,20},{1,9},{5... | collective-permute-start | bytes 196616 | tf_op jit(solution)/shard_map/ppermute | solution.py:284
  20.4 1.5 %collective-permute-start.6 = (f32[64,256]{1,0:T(8,128)S(1)}, f32[64,256]{1,0:T(8,128)S(1)}, u32[]{:S(2)}, u32[]{:S(2)}) collective-permute-start(f32[64,256]{1,0:T(8,128)S(1)} %get-tuple-element.83), channel_id=1, source_target_pairs={{0,16},{4,20},{8,24},{12,28},{16,0},{20,4},{24,8},{28,12},{1,17},{... | collective-permute-start | bytes 196616 | tf_op jit(solution)/shard_map/ppermute | solution.py:284
  22.4 4.5 %collective-permute-done.4.got_ref = f32[2,384,128]{2,1,0:T(8,128)S(1)} collective-permute-done((f32[2,384,128]{2,1,0:T(8,128)S(1)}, f32[2,384,128]{2,1,0:T(8,128)S(1)}, u32[]{:S(2)}, u32[]{:S(2)}) %collective-permute-start.4) | collective-permute-done | bytes 393248 | tf_op jit(solution)/shard_map/ppermute | solution.py:322
  27.1 2.5 %collective-permute-start.9 = (f32[64,256]{1,0:T(8,128)S(1)}, f32[64,256]{1,0:T(8,128)S(1)}, u32[]{:S(2)}, u32[]{:S(2)}) collective-permute-start(f32[64,256]{1,0:T(8,128)S(1)} %add_add_fusion.one_ref), channel_id=1, source_target_pairs={{0,1},{1,0},{2,3},{3,2},{4,5},{5,4},{6,7},{7,6},{8,9},{9,8},{10,11... | collective-permute-start | bytes 196616 | tf_op jit(solution)/shard_map/ppermute | solution.py:284
  29.6 6.7 %collective-permute-done.9.two_ref = f32[64,256]{1,0:T(8,128)S(1)} collective-permute-done((f32[64,256]{1,0:T(8,128)S(1)}, f32[64,256]{1,0:T(8,128)S(1)}, u32[]{:S(2)}, u32[]{:S(2)}) %collective-permute-start.9) | collective-permute-done | bytes 65568 | tf_op jit(solution)/shard_map/ppermute | solution.py:284
  36.3 2.5 %collective-permute-start.10 = (f32[2,384,128]{2,1,0:T(8,128)S(1)}, f32[2,384,128]{2,1,0:T(8,128)S(1)}, u32[]{:S(2)}, u32[]{:S(2)}) collective-permute-start(f32[2,384,128]{2,1,0:T(8,128)S(1)} %shard_map.74), channel_id=1, source_target_pairs={{0,1},{3,2},{1,3},{2,0},{4,5},{7,6},{5,7},{6,4},{8,9},{11,10},{9,1... | collective-permute-start | bytes 1179656 | tf_op jit(solution)/shard_map/ppermute | solution.py:336
  38.9 1.3 %collective-permute-start.16 = (f32[2,384,128]{2,1,0:T(8,128)S(1)}, f32[2,384,128]{2,1,0:T(8,128)S(1)}, u32[]{:S(2)}, u32[]{:S(2)}) collective-permute-start(f32[2,384,128]{2,1,0:T(8,128)S(1)} %shard_map.73), channel_id=1, source_target_pairs={{1,3},{2,0},{5,7},{6,4},{9,11},{10,8},{13,15},{14,12},{17,19},{18,... | collective-permute-start | bytes 1179656 | tf_op jit(solution)/shard_map/ppermute | solution.py:330
  40.2 6.0 %collective-permute-start.14 = (f32[2,384,128]{2,1,0:T(8,128)S(1)}, f32[2,384,128]{2,1,0:T(8,128)S(1)}, u32[]{:S(2)}, u32[]{:S(2)}) collective-permute-start(f32[2,384,128]{2,1,0:T(8,128)S(1)} %get-tuple-element.69.raw_ref), channel_id=1, source_target_pairs={{0,1},{3,2},{4,5},{7,6},{8,9},{11,10},{12,13},{15,14},{16,17},{19,... | collective-permute-start | bytes 1179656 | tf_op jit(solution)/shard_map/ppermute | solution.py:339
  46.2 5.6 %project.5 = (f32[2,384,128]{2,1,0:T(8,128)S(1)}, f32[2,384,128]{2,1,0:T(8,128)S(1)}, f32[2,384,128]{2,1,0:T(8,128)S(1)}, f32[2,384,128]{2,1,0:T(8,128)S(1)}) custom-call(s32[1]{0:T(128)} %bitcast.feat.feat_ref.me_ref, bf16[4096,1024]{1,0:T(8,128)(2,1)} %bitcast.26, bf16[4096,1024]{1,0:T(8,128)(2,1)} %bitcast.29, ...), custom_call_target="tpu_custom_call" | custom-call | flops 1073741824 | bytes 9961472 | tf_op jit(solution)/shard_map/project/pallas_call | solution.py:81
  53.4 1.3 %collective-permute-start.12 = (f32[2,64,256]{2,1,0:T(8,128)S(1)}, f32[2,64,256]{2,1,0:T(8,128)S(1)}, u32[]{:S(2)}, u32[]{:S(2)}) collective-permute-start(f32[2,64,256]{2,1,0:T(8,128)S(1)} %shard_map.75.pair_ref), channel_id=1, source_target_pairs={{1,3},{2,0},{5,7},{6,4},{9,11},{10,8},{13,15},{14,12},{17,19},{18,... | collective-permute-start | bytes 393224 | tf_op jit(solution)/shard_map/ppermute | solution.py:338
  54.7 17.1 %collective-permute-done.12.outer_ref = f32[2,64,256]{2,1,0:T(8,128)S(1)} collective-permute-done((f32[2,64,256]{2,1,0:T(8,128)S(1)}, f32[2,64,256]{2,1,0:T(8,128)S(1)}, u32[]{:S(2)}, u32[]{:S(2)}) %collective-permute-start.12) | collective-permute-done | bytes 131104 | tf_op jit(solution)/shard_map/ppermute | solution.py:338
  71.8 2.5 %collective-permute-start.19 = (f32[4,64,256]{2,1,0:T(8,128)S(1)}, f32[4,64,256]{2,1,0:T(8,128)S(1)}, u32[]{:S(2)}, u32[]{:S(2)}) collective-permute-start(f32[4,64,256]{2,1,0:T(8,128)S(1)} %shard_map.77.refs_0_), channel_id=1, source_target_pairs={{0,24},{4,28},{8,16},{12,20},{16,8},{20,12},{24,0},{28,4},{1,25},{... | collective-permute-start | bytes 786440 | tf_op jit(solution)/shard_map/ppermute | solution.py:284
  77.0 5.0 %collective-permute-done.19.refs_3_ = f32[4,64,256]{2,1,0:T(8,128)S(1)} collective-permute-done((f32[4,64,256]{2,1,0:T(8,128)S(1)}, f32[4,64,256]{2,1,0:T(8,128)S(1)}, u32[]{:S(2)}, u32[]{:S(2)}) %collective-permute-start.19) | collective-permute-done | bytes 262176 | tf_op jit(solution)/shard_map/ppermute | solution.py:284
  82.0 3.6 %collective-permute-done.18.refs_2_ = f32[4,64,256]{2,1,0:T(8,128)S(1)} collective-permute-done((f32[4,64,256]{2,1,0:T(8,128)S(1)}, f32[4,64,256]{2,1,0:T(8,128)S(1)}, u32[]{:S(2)}, u32[]{:S(2)}) %collective-permute-start.18) | collective-permute-done | bytes 262176 | tf_op jit(solution)/shard_map/ppermute | solution.py:284
  88.8 1.8 %collective-permute-start.26 = (f32[16,64]{1,0:T(8,128)S(1)}, f32[16,64]{1,0:T(8,128)S(1)}, u32[]{:S(2)}, u32[]{:S(2)}) collective-permute-start(f32[16,64]{1,0:T(8,128)S(1)} %score.1.refs_0_), channel_id=1, source_target_pairs={{0,1},{1,0},{2,3},{3,2},{4,5},{5,4},{6,7},{7,6},{8,9},{9,8},{10,11... | collective-permute-start | bytes 12296 | tf_op jit(solution)/shard_map/ppermute | solution.py:284
  90.5 2.6 %collective-permute-start.28 = (f32[16,64]{1,0:T(8,128)S(1)}, f32[16,64]{1,0:T(8,128)S(1)}, u32[]{:S(2)}, u32[]{:S(2)}) collective-permute-start(f32[16,64]{1,0:T(8,128)S(1)} %score.1.refs_0_), channel_id=1, source_target_pairs={{0,3},{1,2},{2,1},{3,0},{4,7},{5,6},{6,5},{7,4},{8,11},{9,10},{10,... | collective-permute-start | bytes 12296 | tf_op jit(solution)/shard_map/ppermute | solution.py:284
  93.2 1.9 %collective-permute-done.27.refs_2_ = f32[16,64]{1,0:T(8,128)S(1)} collective-permute-done((f32[16,64]{1,0:T(8,128)S(1)}, f32[16,64]{1,0:T(8,128)S(1)}, u32[]{:S(2)}, u32[]{:S(2)}) %collective-permute-start.27) | collective-permute-done | bytes 4128 | tf_op jit(solution)/shard_map/ppermute | solution.py:284
  95.1 0.9 collective-permute-done.28.refs_3_
  (53 shorter events, 10.3 us)
Async XLA Ops:
  3.5 8.9 %collective-permute-start.2 = (f32[32,1]{1,0:T(8,128)S(1)}, f32[32,1]{1,0:T(8,128)S(1)}, u32[]{:S(2)}, u32[]{:S(2)}) collective-permute-start(f32[32,1]{1,0:T(8,128)S(1)} %get-tuple-element.44.refs_0_), channel_id=1, source_target_pairs={{0,3},{1,2},{2,1},{3,0},{4,7},{5,6},{6,5},{7,4},{8,11},{9,10},{10,... | collective-permute-start | bytes 392 | tf_op jit(solution)/shard_map/ppermute | solution.py:284
  8.7 4.6 %collective-permute-start.1 = (f32[32,1]{1,0:T(8,128)S(1)}, f32[32,1]{1,0:T(8,128)S(1)}, u32[]{:S(2)}, u32[]{:S(2)}) collective-permute-start(f32[32,1]{1,0:T(8,128)S(1)} %get-tuple-element.44.refs_0_), channel_id=1, source_target_pairs={{0,2},{1,3},{2,0},{3,1},{4,6},{5,7},{6,4},{7,5},{8,10},{9,11},{10,... | collective-permute-start | bytes 392 | tf_op jit(solution)/shard_map/ppermute | solution.py:284
  8.7 4.6 %collective-permute-start = (f32[32,1]{1,0:T(8,128)S(1)}, f32[32,1]{1,0:T(8,128)S(1)}, u32[]{:S(2)}, u32[]{:S(2)}) collective-permute-start(f32[32,1]{1,0:T(8,128)S(1)} %get-tuple-element.44.refs_0_), channel_id=1, source_target_pairs={{0,1},{1,0},{2,3},{3,2},{4,5},{5,4},{6,7},{7,6},{8,9},{9,8},{10,11... | collective-permute-start | bytes 392 | tf_op jit(solution)/shard_map/ppermute | solution.py:284
  14.9 12.0 %collective-permute-start.4 = (f32[2,384,128]{2,1,0:T(8,128)S(1)}, f32[2,384,128]{2,1,0:T(8,128)S(1)}, u32[]{:S(2)}, u32[]{:S(2)}) collective-permute-start(f32[2,384,128]{2,1,0:T(8,128)S(1)} %get-tuple-element.53.raw_ref), channel_id=1, source_target_pairs={{0,1},{3,2},{4,5},{7,6},{8,9},{11,10},{12,13},{15,14},{16,17},{19,... | collective-permute-start | bytes 1179656 | tf_op jit(solution)/shard_map/ppermute | solution.py:322
  17.5 18.8 %collective-permute-start.8 = (f32[2,384,128]{2,1,0:T(8,128)S(1)}, f32[2,384,128]{2,1,0:T(8,128)S(1)}, u32[]{:S(2)}, u32[]{:S(2)}) collective-permute-start(f32[2,384,128]{2,1,0:T(8,128)S(1)} %get-tuple-element.58.raw_ref), channel_id=1, source_target_pairs={{0,1},{3,2},{4,5},{7,6},{8,9},{11,10},{12,13},{15,14},{16,17},{19,... | collective-permute-start | bytes 1179656 | tf_op jit(solution)/shard_map/ppermute | solution.py:322
  18.8 8.1 %collective-permute-start.5 = (f32[64,256]{1,0:T(8,128)S(1)}, f32[64,256]{1,0:T(8,128)S(1)}, u32[]{:S(2)}, u32[]{:S(2)}) collective-permute-start(f32[64,256]{1,0:T(8,128)S(1)} %get-tuple-element.85), channel_id=1, source_target_pairs={{0,8},{4,12},{8,0},{12,4},{16,24},{20,28},{24,16},{28,20},{1,9},{5... | collective-permute-start | bytes 196616 | tf_op jit(solution)/shard_map/ppermute | solution.py:284
  20.4 6.6 %collective-permute-start.6 = (f32[64,256]{1,0:T(8,128)S(1)}, f32[64,256]{1,0:T(8,128)S(1)}, u32[]{:S(2)}, u32[]{:S(2)}) collective-permute-start(f32[64,256]{1,0:T(8,128)S(1)} %get-tuple-element.83), channel_id=1, source_target_pairs={{0,16},{4,20},{8,24},{12,28},{16,0},{20,4},{24,8},{28,12},{1,17},{... | collective-permute-start | bytes 196616 | tf_op jit(solution)/shard_map/ppermute | solution.py:284
  21.9 5.2 %collective-permute-start.7 = (f32[64,256]{1,0:T(8,128)S(1)}, f32[64,256]{1,0:T(8,128)S(1)}, u32[]{:S(2)}, u32[]{:S(2)}) collective-permute-start(f32[64,256]{1,0:T(8,128)S(1)} %get-tuple-element.84), channel_id=1, source_target_pairs={{0,24},{4,28},{8,16},{12,20},{16,8},{20,12},{24,0},{28,4},{1,25},{... | collective-permute-start | bytes 196616 | tf_op jit(solution)/shard_map/ppermute | solution.py:284
  27.1 9.2 %collective-permute-start.9 = (f32[64,256]{1,0:T(8,128)S(1)}, f32[64,256]{1,0:T(8,128)S(1)}, u32[]{:S(2)}, u32[]{:S(2)}) collective-permute-start(f32[64,256]{1,0:T(8,128)S(1)} %add_add_fusion.one_ref), channel_id=1, source_target_pairs={{0,1},{1,0},{2,3},{3,2},{4,5},{5,4},{6,7},{7,6},{8,9},{9,8},{10,11... | collective-permute-start | bytes 196616 | tf_op jit(solution)/shard_map/ppermute | solution.py:284
  36.3 16.3 %collective-permute-start.10 = (f32[2,384,128]{2,1,0:T(8,128)S(1)}, f32[2,384,128]{2,1,0:T(8,128)S(1)}, u32[]{:S(2)}, u32[]{:S(2)}) collective-permute-start(f32[2,384,128]{2,1,0:T(8,128)S(1)} %shard_map.74), channel_id=1, source_target_pairs={{0,1},{3,2},{1,3},{2,0},{4,5},{7,6},{5,7},{6,4},{8,9},{11,10},{9,1... | collective-permute-start | bytes 1179656 | tf_op jit(solution)/shard_map/ppermute | solution.py:336
  38.9 32.9 %collective-permute-start.16 = (f32[2,384,128]{2,1,0:T(8,128)S(1)}, f32[2,384,128]{2,1,0:T(8,128)S(1)}, u32[]{:S(2)}, u32[]{:S(2)}) collective-permute-start(f32[2,384,128]{2,1,0:T(8,128)S(1)} %shard_map.73), channel_id=1, source_target_pairs={{1,3},{2,0},{5,7},{6,4},{9,11},{10,8},{13,15},{14,12},{17,19},{18,... | collective-permute-start | bytes 1179656 | tf_op jit(solution)/shard_map/ppermute | solution.py:330
  40.2 34.1 %collective-permute-start.14 = (f32[2,384,128]{2,1,0:T(8,128)S(1)}, f32[2,384,128]{2,1,0:T(8,128)S(1)}, u32[]{:S(2)}, u32[]{:S(2)}) collective-permute-start(f32[2,384,128]{2,1,0:T(8,128)S(1)} %get-tuple-element.69.raw_ref), channel_id=1, source_target_pairs={{0,1},{3,2},{4,5},{7,6},{8,9},{11,10},{12,13},{15,14},{16,17},{19,... | collective-permute-start | bytes 1179656 | tf_op jit(solution)/shard_map/ppermute | solution.py:339
  51.8 23.0 %collective-permute-start.15 = (f32[2,384,128]{2,1,0:T(8,128)S(1)}, f32[2,384,128]{2,1,0:T(8,128)S(1)}, u32[]{:S(2)}, u32[]{:S(2)}) collective-permute-start(f32[2,384,128]{2,1,0:T(8,128)S(1)} %get-tuple-element.71), channel_id=1, source_target_pairs={{0,1},{1,0},{2,3},{3,2},{4,5},{5,4},{6,7},{7,6},{8,9},{9,8},{10,11... | collective-permute-start | bytes 1179656 | tf_op jit(solution)/shard_map/ppermute | solution.py:284
  52.7 22.7 %collective-permute-start.17 = (f32[2,384,128]{2,1,0:T(8,128)S(1)}, f32[2,384,128]{2,1,0:T(8,128)S(1)}, u32[]{:S(2)}, u32[]{:S(2)}) collective-permute-start(f32[2,384,128]{2,1,0:T(8,128)S(1)} %shard_map.76), channel_id=1, source_target_pairs={{1,2},{2,1},{0,0},{3,3},{5,6},{6,5},{4,4},{7,7},{9,10},{10,9},{8,8... | collective-permute-start | bytes 1179656 | tf_op jit(solution)/shard_map/ppermute | solution.py:345
  53.4 18.4 %collective-permute-start.12 = (f32[2,64,256]{2,1,0:T(8,128)S(1)}, f32[2,64,256]{2,1,0:T(8,128)S(1)}, u32[]{:S(2)}, u32[]{:S(2)}) collective-permute-start(f32[2,64,256]{2,1,0:T(8,128)S(1)} %shard_map.75.pair_ref), channel_id=1, source_target_pairs={{1,3},{2,0},{5,7},{6,4},{9,11},{10,8},{13,15},{14,12},{17,19},{18,... | collective-permute-start | bytes 393224 | tf_op jit(solution)/shard_map/ppermute | solution.py:338
  71.7 14.4 %collective-permute-start.24 = (f32[2,384,128]{2,1,0:T(8,128)S(1)}, f32[2,384,128]{2,1,0:T(8,128)S(1)}, u32[]{:S(2)}, u32[]{:S(2)}) collective-permute-start(f32[2,384,128]{2,1,0:T(8,128)S(1)} %get-tuple-element.80), channel_id=1, source_target_pairs={{0,1},{1,0},{2,3},{3,2},{4,5},{5,4},{6,7},{7,6},{8,9},{9,8},{10,11... | collective-permute-start | bytes 1179656 | tf_op jit(solution)/shard_map/ppermute | solution.py:284
  71.8 10.2 %collective-permute-start.19 = (f32[4,64,256]{2,1,0:T(8,128)S(1)}, f32[4,64,256]{2,1,0:T(8,128)S(1)}, u32[]{:S(2)}, u32[]{:S(2)}) collective-permute-start(f32[4,64,256]{2,1,0:T(8,128)S(1)} %shard_map.77.refs_0_), channel_id=1, source_target_pairs={{0,24},{4,28},{8,16},{12,20},{16,8},{20,12},{24,0},{28,4},{1,25},{... | collective-permute-start | bytes 786440 | tf_op jit(solution)/shard_map/ppermute | solution.py:284
  74.3 11.3 %collective-permute-start.18 = (f32[4,64,256]{2,1,0:T(8,128)S(1)}, f32[4,64,256]{2,1,0:T(8,128)S(1)}, u32[]{:S(2)}, u32[]{:S(2)}) collective-permute-start(f32[4,64,256]{2,1,0:T(8,128)S(1)} %shard_map.77.refs_0_), channel_id=1, source_target_pairs={{0,16},{4,20},{8,24},{12,28},{16,0},{20,4},{24,8},{28,12},{1,17},{... | collective-permute-start | bytes 786440 | tf_op jit(solution)/shard_map/ppermute | solution.py:284
  74.8 10.9 %collective-permute-start.13 = (f32[4,64,256]{2,1,0:T(8,128)S(1)}, f32[4,64,256]{2,1,0:T(8,128)S(1)}, u32[]{:S(2)}, u32[]{:S(2)}) collective-permute-start(f32[4,64,256]{2,1,0:T(8,128)S(1)} %shard_map.77.refs_0_), channel_id=1, source_target_pairs={{0,8},{4,12},{8,0},{12,4},{16,24},{20,28},{24,16},{28,20},{1,9},{5... | collective-permute-start | bytes 786440 | tf_op jit(solution)/shard_map/ppermute | solution.py:284
  75.4 10.8 %collective-permute-start.25 = (f32[2,384,128]{2,1,0:T(8,128)S(1)}, f32[2,384,128]{2,1,0:T(8,128)S(1)}, u32[]{:S(2)}, u32[]{:S(2)}) collective-permute-start(f32[2,384,128]{2,1,0:T(8,128)S(1)} %shard_map.78), channel_id=1, source_target_pairs={{1,2},{2,1},{0,0},{3,3},{5,6},{6,5},{4,4},{7,7},{9,10},{10,9},{8,8... | collective-permute-start | bytes 1179656 | tf_op jit(solution)/shard_map/ppermute | solution.py:350
  82.0 5.1 %collective-permute-start.20 = (f32[4,64,256]{2,1,0:T(8,128)S(1)}, f32[4,64,256]{2,1,0:T(8,128)S(1)}, u32[]{:S(2)}, u32[]{:S(2)}) collective-permute-start(f32[4,64,256]{2,1,0:T(8,128)S(1)} %shard_map.77.refs_0_), channel_id=1, source_target_pairs={{0,4},{4,0},{8,12},{12,8},{16,20},{20,16},{24,28},{28,24},{1,5},{5... | collective-permute-start | bytes 786440 | tf_op jit(solution)/shard_map/ppermute | solution.py:284
  88.8 4.4 %collective-permute-start.26 = (f32[16,64]{1,0:T(8,128)S(1)}, f32[16,64]{1,0:T(8,128)S(1)}, u32[]{:S(2)}, u32[]{:S(2)}) collective-permute-start(f32[16,64]{1,0:T(8,128)S(1)} %score.1.refs_0_), channel_id=1, source_target_pairs={{0,1},{1,0},{2,3},{3,2},{4,5},{5,4},{6,7},{7,6},{8,9},{9,8},{10,11... | collective-permute-start | bytes 12296 | tf_op jit(solution)/shard_map/ppermute | solution.py:284
  90.5 4.5 %collective-permute-start.27 = (f32[16,64]{1,0:T(8,128)S(1)}, f32[16,64]{1,0:T(8,128)S(1)}, u32[]{:S(2)}, u32[]{:S(2)}) collective-permute-start(f32[16,64]{1,0:T(8,128)S(1)} %score.1.refs_0_), channel_id=1, source_target_pairs={{0,2},{1,3},{2,0},{3,1},{4,6},{5,7},{6,4},{7,5},{8,10},{9,11},{10,... | collective-permute-start | bytes 12296 | tf_op jit(solution)/shard_map/ppermute | solution.py:284
  90.5 5.4 %collective-permute-start.28 = (f32[16,64]{1,0:T(8,128)S(1)}, f32[16,64]{1,0:T(8,128)S(1)}, u32[]{:S(2)}, u32[]{:S(2)}) collective-permute-start(f32[16,64]{1,0:T(8,128)S(1)} %score.1.refs_0_), channel_id=1, source_target_pairs={{0,3},{1,2},{2,1},{3,0},{4,7},{5,6},{6,5},{7,4},{8,11},{9,10},{10,... | collective-permute-start | bytes 12296 | tf_op jit(solution)/shard_map/ppermute | solution.py:284
  (6 other events, 13.6 us)

commit v6 on v5

--- a/solution.py
+++ b/solution.py
@@ -133,7 +133,7 @@
     )(me, held, lang.reshape(1, rows), *squares)
 
 
-def product_kernel(middle_ref, own_ref, raw_ref, far_ref, near_ref, o_ref, square_ref, grad_ref):
+def product_kernel(middle_ref, own_ref, end_ref, near_ref, o_ref, square_ref, grad_ref):
     middle = middle_ref[0] == 1
     rows = own_ref.shape[1] * 2 // 3
     seq = rows // UNIT
@@ -147,7 +147,7 @@
 
     def total(unit, start):
         block = (unit, pl.ds(start, seq), slice(None))
-        return own_ref[block] + raw_ref[block] + jnp.where(middle, near_ref[block], far_ref[block])
+        return own_ref[block] + end_ref[block] + jnp.where(middle, near_ref[block], 0.0)
 
     for unit in range(PIECE):
         for pair in range(UNIT // 2):
@@ -252,10 +252,6 @@
     o_ref[1] = two_ref[...]
 
 
-def route_kernel(middle_ref, raw_ref, got_ref, end_ref, o_ref):
-    o_ref[...] = jnp.where(middle_ref[0] == 1, raw_ref[...] + got_ref[...], end_ref[...])
-
-
 def join_kernel(middle_ref, pair_ref, inner_ref, outer_ref, o_ref):
     o_ref[:2] = pair_ref[...]
     o_ref[2:] = jnp.where(middle_ref[0] == 1, inner_ref[...], outer_ref[...])
@@ -307,9 +303,8 @@
     down_like = jax.ShapeDtypeStruct((width, 2 * rank_sketch.shape[0]), jnp.bfloat16)
     square_like = jax.ShapeDtypeStruct((held.shape[0], 1), jnp.float32)
     inward = [(0, 1), (3, 2)]
-    far_pairs = [(1, 3), (2, 0)]
-    round_pairs = inward + far_pairs
-    near_pairs = [(1, 2), (2, 1), (0, 0), (3, 3)]
+    outward = [(1, 0), (2, 3)]
+    inner = [(1, 2), (2, 1), (0, 0), (3, 3)]
     is_middle = middle.astype(jnp.int32).reshape(1)
 
     def onward(raw, got):
@@ -319,39 +314,43 @@
         first_kernel, me_feat, 0, 2, acts2, grads2, [adapter, rank_sketch, out_sketch, held], [down_like, square_like]
     )
     squares = [own_square] + [swap(own_square, "feat", mask) for mask in (1, 2, 3)]
-    got1 = [lax.ppermute(x, "feat", inward) for x in raw0]
+    got1 = [swap(x, "feat", 1) for x in raw0]
     raw1 = project(more_kernel, me_feat, 2, 2, acts2, grads2, [down, out_sketch], [])
 
     squares[1:] = [after(x, raw1[0]) for x in squares[1:]]
     other, *parts = lang_parts(me_ex, held, squares, perm % LANGS, n_ex)
     other = swap(other, "ex", 1)
     parts = [x + other[i] for i, x in enumerate(parts)]
+    scattered = [swap(parts[i], "ex", 2 * i) for i in range(1, n_ex // 2)]
     sent1 = [onward(after(raw0[0], parts[0]), got1[0])]
-    far = [lax.ppermute(sent1[0], "feat", far_pairs)]
-    scattered = [swap(parts[i], "ex", 2 * i) for i in range(1, n_ex // 2)]
+    far = [lax.ppermute(sent1[0], "feat", inner)]
     lang = after(parts[0], sent1[0]) + sum(scattered)
     other = swap(lang, "feat", 1)
     raw1 = [after(x, lang) for x in raw1]
-    sent1.append(small(route_kernel, raw1[0].shape, is_middle, [raw0[1], got1[1], after(raw1[0], other)]))
-    round_a = lax.ppermute(sent1[1], "feat", round_pairs)
-    pair = small(stack_kernel, (2, *lang.shape), is_middle, [after(lang, sent1[1]), other])
-    far_pair = [lax.ppermute(pair, "feat", pairs) for pairs in (near_pairs, far_pairs)]
-    got2 = [round_a, lax.ppermute(after(raw1[1], pair), "feat", inward)]
-    *raw2, own_a, own_b = project(
-        more_kernel, me_feat, 4, 4, acts2, grads2, [after(down, pair), out_sketch], []
-    )
-    got3 = [swap(raw2[0], "feat", 1)]
+    got2 = [swap(raw1[0], "feat", 1)]
+    pair = small(stack_kernel, (2, *lang.shape), is_middle, [lang, other])
+    far_pair = lax.ppermute(pair, "feat", inner)
+    sent1.append(onward(after(raw0[1], pair), got1[1]))
+    far.append(lax.ppermute(sent1[1], "feat", inner))
+    got2.append(lax.ppermute(after(raw1[1], pair), "feat", inward))
+    far_pair = after(far_pair, sent1[1])
+    outer_pair = lax.ppermute(far_pair, "feat", outward)
+    *raw2, own_a, own_b = project(more_kernel, me_feat, 4, 4, acts2, grads2, [after(down, far_pair), out_sketch], [])
     sent2 = [onward(after(raw1[0], own_a), got2[0])]
-    near = [lax.ppermute(sent2[0], "feat", near_pairs)]
-    langs = [small(join_kernel, (4, *lang.shape), is_middle, [after(pair, sent2[0]), *far_pair])]
+    near = [lax.ppermute(sent2[0], "feat", inner)]
+    sent3 = [onward(after(raw2[0], sent2[0]), far[0])]
+    got3 = [swap(sent3[0], "feat", 1)]
+    pair = after(pair, sent3[0])
+    langs = [small(join_kernel, (4, *lang.shape), is_middle, [pair, far_pair, outer_pair])]
     langs = langs + [swap(langs[0], "ex", mask) for mask in range(2, n_ex, 2)]
-    got3.append(swap(after(raw2[1], sent2[0]), "feat", 1))
-    sent2.append(onward(after(raw1[1], langs[0]), got2[1]))
-    near.append(lax.ppermute(sent2[1], "feat", near_pairs))
-    grad_a, square_a = product(is_middle, [after(own_a, sent2[1]), got3[0], far[0], near[0]])
+    sent3.append(onward(after(raw2[1], langs[0]), far[1]))
+    got3.append(swap(sent3[1], "feat", 1))
+    sent2.append(onward(after(raw1[1], sent3[1]), got2[1]))
+    near.append(lax.ppermute(sent2[1], "feat", inner))
+    grad_a, square_a = product(is_middle, [after(own_a, sent2[1]), got3[0], near[0]])
     langs[1:] = [after(x, square_a) for x in langs[1:]]
     langs = langs + [swap(x, "ex", 1) for x in langs]
-    grad_b, square_b = product(is_middle, [after(own_b, square_a), got3[1], round_a, near[1]])
+    grad_b, square_b = product(is_middle, [after(own_b, square_a), got3[1], near[1]])
     products = [(grad_a, square_a), (grad_b, square_b)]
     per_lang = perm.shape[0] * n_ex // LANGS
     scale = (KF * per_lang) ** 0.5 / per_lang

time: 96.9 us -> 98.1 us (1.012)
  waiting for transfers between devices: 41.6 us -> 46.1 us
  starting transfers between devices: 37.5 us -> 34 us
    ppermute x20 -> x23, waiting for transfers between devices: 20 us -> 35.3 us  [swap(): lax.ppermute(x, axis, [(i, i ^ mask) for i in range(lax.axis_size(axis))])]
    ppermute x9 -> x7, waiting for transfers between devices: 21.6 us -> 10.8 us  [the longest x1 10.8 us: ordered(): outer_pair = lax.ppermute(far_pair, 'feat', outward)]
    ppermute x9 -> x7, starting transfers between devices: 17 us -> 11.4 us  [the longest x1 6.7 us: ordered(): got2.append(lax.ppermute(after(raw1[1], pair), 'feat', inward))]
    ppermute x20 -> x23, starting transfers between devices: 20.5 us -> 22.6 us  [swap(): lax.ppermute(x, axis, [(i, i ^ mask) for i in range(lax.axis_size(axis))])]
  transfers between devices with their start and end apart: 29 -> 30, of which waited for: 13 -> 12; matrix products, arithmetic and copies ran while one was open for 0% -> 0% of each run, Pallas kernels for 11% -> 11%
where the time goes in v6:
time: 98.1 us; the launch traced here: 97.8 us
  waiting for transfers between devices  46.1 us (47%)
  starting transfers between devices  34 us (35%)
  Pallas kernels  17.3 us (18%)
    ppermute x23, waiting for transfers between devices, swap(): lax.ppermute(x, axis, [(i, i ^ mask) for i in range(lax.axis_size(axis))])  35.3 us
    ppermute x23, starting transfers between devices, swap(): lax.ppermute(x, axis, [(i, i ^ mask) for i in range(lax.axis_size(axis))])  22.6 us
    pallas_call x3, Pallas kernels, project(): pl.pallas_call(kernel, out_shape=[jax.ShapeDtypeStruct(piece, jnp.float32...  12.2 us
    ppermute x1, waiting for transfers between devices, ordered(): outer_pair = lax.ppermute(far_pair, 'feat', outward)  10.8 us
    ppermute x1, starting transfers between devices, ordered(): got2.append(lax.ppermute(after(raw1[1], pair), 'feat', inward))  6.7 us
  transfers between devices with their start and end apart: 30, of which 12 were waited for; matrix products, arithmetic and copies ran while one was open for 0% of the time, Pallas kernels for 11%

profile of v6, /device:TPU:0, one launch (start us, length us, event | category | flops | bytes accessed | tf_op | source)
XLA Modules:
  0.0 97.8 jit_solution(13172101014810204426)
XLA Ops:
  0.0 3.5 %project.3 = (f32[2,384,128]{2,1,0:T(8,128)S(1)}, f32[2,384,128]{2,1,0:T(8,128)S(1)}, bf16[1024,128]{1,0:T(8,128)(2,1)S(1)}, f32[32,1]{1,0:T(8,128)S(1)}) custom-call(s32[1]{0:T(128)} %bitcast.feat.feat_ref.me_ref, bf16[4096,1024]{1,0:T(8,128)(2,1)} %bitcast.24, bf16[4096,1024]{1,0:T(8,128)(2,1)} %bitcast.27, bf16[1024,128]{1,0:T(8,128)(2,1)} %adapter_ref.1, ...), custom_call_target="tpu_custom_call" | custom-call | flops 536870912 | bytes 4980736 | tf_op jit(solution)/shard_map/project/pallas_call | solution.py:81
  3.5 3.1 %collective-permute-start = (f32[32,1]{1,0:T(8,128)S(1)}, f32[32,1]{1,0:T(8,128)S(1)}, u32[]{:S(2)}, u32[]{:S(2)}) collective-permute-start(f32[32,1]{1,0:T(8,128)S(1)} %get-tuple-element.45.refs_0_), channel_id=1, source_target_pairs={{0,1},{1,0},{2,3},{3,2},{4,5},{5,4},{6,7},{7,6},{8,9},{9,8},{10,11... | collective-permute-start | bytes 392 | tf_op jit(solution)/shard_map/ppermute | solution.py:280
  6.7 2.6 %collective-permute-start.1 = (f32[32,1]{1,0:T(8,128)S(1)}, f32[32,1]{1,0:T(8,128)S(1)}, u32[]{:S(2)}, u32[]{:S(2)}) collective-permute-start(f32[32,1]{1,0:T(8,128)S(1)} %get-tuple-element.45.refs_0_), channel_id=1, source_target_pairs={{0,2},{1,3},{2,0},{3,1},{4,6},{5,7},{6,4},{7,5},{8,10},{9,11},{10,... | collective-permute-start | bytes 392 | tf_op jit(solution)/shard_map/ppermute | solution.py:280
  9.3 3.1 %project.4 = (f32[2,384,128]{2,1,0:T(8,128)S(1)}, f32[2,384,128]{2,1,0:T(8,128)S(1)}) custom-call(s32[1]{0:T(128)} %bitcast.feat.feat_ref.me_ref, bf16[4096,1024]{1,0:T(8,128)(2,1)} %bitcast.25, bf16[4096,1024]{1,0:T(8,128)(2,1)} %bitcast.28, bf16[1024,128]{1,0:T(8,128)(2,1)S(1)} %get-tuple-element.62.down_ref, bf16[1024,128]{1,0:T(8,128)(2,1)} %sketch_ref.5), custom_call_target="tpu_custom_call" | custom-call | flops 536870912 | bytes 4980736 | tf_op jit(solution)/shard_map/project/pallas_call | solution.py:81
  12.4 2.4 %collective-permute-done.2.refs_3_ = f32[32,1]{1,0:T(8,128)S(1)} collective-permute-done((f32[32,1]{1,0:T(8,128)S(1)}, f32[32,1]{1,0:T(8,128)S(1)}, u32[]{:S(2)}, u32[]{:S(2)}) %collective-permute-start.2) | collective-permute-done | bytes 160 | tf_op jit(solution)/shard_map/ppermute | solution.py:280
  14.8 1.6 %lang_parts.1 = (f32[4,64,256]{2,1,0:T(8,128)S(1)}, f32[64,256]{1,0:T(8,128)S(1)}, f32[64,256]{1,0:T(8,128)S(1)}, f32[64,256]{1,0:T(8,128)S(1)}, f32[64,256]{1,0:T(8,128)S(1)}) custom-call(s32[1]{0:T(128)} %bitcast.1.me_ref.ex_ref, f32[32,2048]{1,0:T(8,128)} %held_ref.3, s32[1,32]{1,0:T(1,128)S(1)} %fusion.4.lang_ref, ...), custom_call_target="tpu_custom_call" | custom-call | tf_op jit(solution)/shard_map/lang_parts/pallas_call | solution.py:125
  16.5 1.4 %collective-permute-done.3 = f32[4,64,256]{2,1,0:T(8,128)S(1)} collective-permute-done((f32[4,64,256]{2,1,0:T(8,128)S(1)}, f32[4,64,256]{2,1,0:T(8,128)S(1)}, u32[]{:S(2)}, u32[]{:S(2)}) %collective-permute-start.3) | collective-permute-done | bytes 262176 | tf_op jit(solution)/shard_map/ppermute | solution.py:280
  18.0 2.5 %collective-permute-start.7 = (f32[64,256]{1,0:T(8,128)S(1)}, f32[64,256]{1,0:T(8,128)S(1)}, u32[]{:S(2)}, u32[]{:S(2)}) collective-permute-start(f32[64,256]{1,0:T(8,128)S(1)} %get-tuple-element.86), channel_id=1, source_target_pairs={{0,24},{4,28},{8,16},{12,20},{16,8},{20,12},{24,0},{28,4},{1,25},{... | collective-permute-start | bytes 196616 | tf_op jit(solution)/shard_map/ppermute | solution.py:280
  22.1 6.4 %collective-permute-done.4.got_ref = f32[2,384,128]{2,1,0:T(8,128)S(1)} collective-permute-done((f32[2,384,128]{2,1,0:T(8,128)S(1)}, f32[2,384,128]{2,1,0:T(8,128)S(1)}, u32[]{:S(2)}, u32[]{:S(2)}) %collective-permute-start.4) | collective-permute-done | bytes 393248 | tf_op jit(solution)/shard_map/ppermute | solution.py:280
  29.4 3.9 %collective-permute-start.8 = (f32[64,256]{1,0:T(8,128)S(1)}, f32[64,256]{1,0:T(8,128)S(1)}, u32[]{:S(2)}, u32[]{:S(2)}) collective-permute-start(f32[64,256]{1,0:T(8,128)S(1)} %add_add_fusion.one_ref), channel_id=1, source_target_pairs={{0,1},{1,0},{2,3},{3,2},{4,5},{5,4},{6,7},{7,6},{8,9},{9,8},{10,11... | collective-permute-start | bytes 196616 | tf_op jit(solution)/shard_map/ppermute | solution.py:280
  33.3 13.0 %collective-permute-done.8.two_ref = f32[64,256]{1,0:T(8,128)S(1)} collective-permute-done((f32[64,256]{1,0:T(8,128)S(1)}, f32[64,256]{1,0:T(8,128)S(1)}, u32[]{:S(2)}, u32[]{:S(2)}) %collective-permute-start.8) | collective-permute-done | bytes 65568 | tf_op jit(solution)/shard_map/ppermute | solution.py:280
  47.7 6.7 %collective-permute-start.16 = (f32[2,384,128]{2,1,0:T(8,128)S(1)}, f32[2,384,128]{2,1,0:T(8,128)S(1)}, u32[]{:S(2)}, u32[]{:S(2)}) collective-permute-start(f32[2,384,128]{2,1,0:T(8,128)S(1)} %get-tuple-element.74.raw_ref), channel_id=1, source_target_pairs={{0,1},{3,2},{4,5},{7,6},{8,9},{11,10},{12,13},{15,14},{16,17},{19,... | collective-permute-start | bytes 1179656 | tf_op jit(solution)/shard_map/ppermute | solution.py:335
  54.4 5.6 %project.5 = (f32[2,384,128]{2,1,0:T(8,128)S(1)}, f32[2,384,128]{2,1,0:T(8,128)S(1)}, f32[2,384,128]{2,1,0:T(8,128)S(1)}, f32[2,384,128]{2,1,0:T(8,128)S(1)}) custom-call(s32[1]{0:T(128)} %bitcast.feat.feat_ref.me_ref, bf16[4096,1024]{1,0:T(8,128)(2,1)} %bitcast.26, bf16[4096,1024]{1,0:T(8,128)(2,1)} %bitcast.29, ...), custom_call_target="tpu_custom_call" | custom-call | flops 1073741824 | bytes 9961472 | tf_op jit(solution)/shard_map/project/pallas_call | solution.py:81
  60.2 1.3 %collective-permute-start.13 = (f32[2,64,256]{2,1,0:T(8,128)S(1)}, f32[2,64,256]{2,1,0:T(8,128)S(1)}, u32[]{:S(2)}, u32[]{:S(2)}) collective-permute-start(f32[2,64,256]{2,1,0:T(8,128)S(1)} %collective-permute-done.9.inner_ref), channel_id=1, source_target_pairs={{1,0},{2,3},{5,4},{6,7},{9,8},{10,11},{13,12},{14,15},{17,16},{18,... | collective-permute-start | bytes 393224 | tf_op jit(solution)/shard_map/ppermute | solution.py:337
  62.2 10.8 %collective-permute-done.13.outer_ref = f32[2,64,256]{2,1,0:T(8,128)S(1)} collective-permute-done((f32[2,64,256]{2,1,0:T(8,128)S(1)}, f32[2,64,256]{2,1,0:T(8,128)S(1)}, u32[]{:S(2)}, u32[]{:S(2)}) %collective-permute-start.13) | collective-permute-done | bytes 131104 | tf_op jit(solution)/shard_map/ppermute | solution.py:337
  73.2 1.6 %collective-permute-start.14 = (f32[4,64,256]{2,1,0:T(8,128)S(1)}, f32[4,64,256]{2,1,0:T(8,128)S(1)}, u32[]{:S(2)}, u32[]{:S(2)}) collective-permute-start(f32[4,64,256]{2,1,0:T(8,128)S(1)} %shard_map.78.refs_0_), channel_id=1, source_target_pairs={{0,8},{4,12},{8,0},{12,4},{16,24},{20,28},{24,16},{28,20},{1,9},{5... | collective-permute-start | bytes 786440 | tf_op jit(solution)/shard_map/ppermute | solution.py:280
  74.8 1.5 %collective-permute-start.19 = (f32[4,64,256]{2,1,0:T(8,128)S(1)}, f32[4,64,256]{2,1,0:T(8,128)S(1)}, u32[]{:S(2)}, u32[]{:S(2)}) collective-permute-start(f32[4,64,256]{2,1,0:T(8,128)S(1)} %shard_map.78.refs_0_), channel_id=1, source_target_pairs={{0,16},{4,20},{8,24},{12,28},{16,0},{20,4},{24,8},{28,12},{1,17},{... | collective-permute-start | bytes 786440 | tf_op jit(solution)/shard_map/ppermute | solution.py:280
  78.4 4.1 %collective-permute-done.14.refs_1_ = f32[4,64,256]{2,1,0:T(8,128)S(1)} collective-permute-done((f32[4,64,256]{2,1,0:T(8,128)S(1)}, f32[4,64,256]{2,1,0:T(8,128)S(1)}, u32[]{:S(2)}, u32[]{:S(2)}) %collective-permute-start.14) | collective-permute-done | bytes 262176 | tf_op jit(solution)/shard_map/ppermute | solution.py:280
  82.5 4.0 %collective-permute-done.19.refs_2_ = f32[4,64,256]{2,1,0:T(8,128)S(1)} collective-permute-done((f32[4,64,256]{2,1,0:T(8,128)S(1)}, f32[4,64,256]{2,1,0:T(8,128)S(1)}, u32[]{:S(2)}, u32[]{:S(2)}) %collective-permute-start.19) | collective-permute-done | bytes 262176 | tf_op jit(solution)/shard_map/ppermute | solution.py:280
  88.8 0.9 score.1.refs_0_
  89.7 1.7 %collective-permute-start.27 = (f32[16,64]{1,0:T(8,128)S(1)}, f32[16,64]{1,0:T(8,128)S(1)}, u32[]{:S(2)}, u32[]{:S(2)}) collective-permute-start(f32[16,64]{1,0:T(8,128)S(1)} %score.1.refs_0_), channel_id=1, source_target_pairs={{0,1},{1,0},{2,3},{3,2},{4,5},{5,4},{6,7},{7,6},{8,9},{9,8},{10,11... | collective-permute-start | bytes 12296 | tf_op jit(solution)/shard_map/ppermute | solution.py:280
  91.7 2.3 %collective-permute-start.29 = (f32[16,64]{1,0:T(8,128)S(1)}, f32[16,64]{1,0:T(8,128)S(1)}, u32[]{:S(2)}, u32[]{:S(2)}) collective-permute-start(f32[16,64]{1,0:T(8,128)S(1)} %score.1.refs_0_), channel_id=1, source_target_pairs={{0,3},{1,2},{2,1},{3,0},{4,7},{5,6},{6,5},{7,4},{8,11},{9,10},{10,... | collective-permute-start | bytes 12296 | tf_op jit(solution)/shard_map/ppermute | solution.py:280
  94.1 1.8 %collective-permute-done.28.refs_2_ = f32[16,64]{1,0:T(8,128)S(1)} collective-permute-done((f32[16,64]{1,0:T(8,128)S(1)}, f32[16,64]{1,0:T(8,128)S(1)}, u32[]{:S(2)}, u32[]{:S(2)}) %collective-permute-start.28) | collective-permute-done | bytes 4128 | tf_op jit(solution)/shard_map/ppermute | solution.py:280
  95.9 1.3 %collective-permute-done.29.refs_3_ = f32[16,64]{1,0:T(8,128)S(1)} collective-permute-done((f32[16,64]{1,0:T(8,128)S(1)}, f32[16,64]{1,0:T(8,128)S(1)}, u32[]{:S(2)}, u32[]{:S(2)}) %collective-permute-start.29) | collective-permute-done | bytes 4128 | tf_op jit(solution)/shard_map/ppermute | solution.py:280
  (57 shorter events, 10.4 us)
Async XLA Ops:
  3.5 8.9 %collective-permute-start = (f32[32,1]{1,0:T(8,128)S(1)}, f32[32,1]{1,0:T(8,128)S(1)}, u32[]{:S(2)}, u32[]{:S(2)}) collective-permute-start(f32[32,1]{1,0:T(8,128)S(1)} %get-tuple-element.45.refs_0_), channel_id=1, source_target_pairs={{0,1},{1,0},{2,3},{3,2},{4,5},{5,4},{6,7},{7,6},{8,9},{9,8},{10,11... | collective-permute-start | bytes 392 | tf_op jit(solution)/shard_map/ppermute | solution.py:280
  6.7 5.8 %collective-permute-start.1 = (f32[32,1]{1,0:T(8,128)S(1)}, f32[32,1]{1,0:T(8,128)S(1)}, u32[]{:S(2)}, u32[]{:S(2)}) collective-permute-start(f32[32,1]{1,0:T(8,128)S(1)} %get-tuple-element.45.refs_0_), channel_id=1, source_target_pairs={{0,2},{1,3},{2,0},{3,1},{4,6},{5,7},{6,4},{7,5},{8,10},{9,11},{10,... | collective-permute-start | bytes 392 | tf_op jit(solution)/shard_map/ppermute | solution.py:280
  9.2 5.5 %collective-permute-start.2 = (f32[32,1]{1,0:T(8,128)S(1)}, f32[32,1]{1,0:T(8,128)S(1)}, u32[]{:S(2)}, u32[]{:S(2)}) collective-permute-start(f32[32,1]{1,0:T(8,128)S(1)} %get-tuple-element.45.refs_0_), channel_id=1, source_target_pairs={{0,3},{1,2},{2,1},{3,0},{4,7},{5,6},{6,5},{7,4},{8,11},{9,10},{10,... | collective-permute-start | bytes 392 | tf_op jit(solution)/shard_map/ppermute | solution.py:280
  16.4 12.1 %collective-permute-start.4 = (f32[2,384,128]{2,1,0:T(8,128)S(1)}, f32[2,384,128]{2,1,0:T(8,128)S(1)}, u32[]{:S(2)}, u32[]{:S(2)}) collective-permute-start(f32[2,384,128]{2,1,0:T(8,128)S(1)} %get-tuple-element.54.raw_ref), channel_id=1, source_target_pairs={{0,1},{1,0},{2,3},{3,2},{4,5},{5,4},{6,7},{7,6},{8,9},{9,8},{10,11... | collective-permute-start | bytes 1179656 | tf_op jit(solution)/shard_map/ppermute | solution.py:280
  18.0 10.5 %collective-permute-start.7 = (f32[64,256]{1,0:T(8,128)S(1)}, f32[64,256]{1,0:T(8,128)S(1)}, u32[]{:S(2)}, u32[]{:S(2)}) collective-permute-start(f32[64,256]{1,0:T(8,128)S(1)} %get-tuple-element.86), channel_id=1, source_target_pairs={{0,24},{4,28},{8,16},{12,20},{16,8},{20,12},{24,0},{28,4},{1,25},{... | collective-permute-start | bytes 196616 | tf_op jit(solution)/shard_map/ppermute | solution.py:280
  20.5 8.0 %collective-permute-start.5 = (f32[64,256]{1,0:T(8,128)S(1)}, f32[64,256]{1,0:T(8,128)S(1)}, u32[]{:S(2)}, u32[]{:S(2)}) collective-permute-start(f32[64,256]{1,0:T(8,128)S(1)} %get-tuple-element.87), channel_id=1, source_target_pairs={{0,8},{4,12},{8,0},{12,4},{16,24},{20,28},{24,16},{28,20},{1,9},{5... | collective-permute-start | bytes 196616 | tf_op jit(solution)/shard_map/ppermute | solution.py:280
  21.1 7.5 %collective-permute-start.6 = (f32[64,256]{1,0:T(8,128)S(1)}, f32[64,256]{1,0:T(8,128)S(1)}, u32[]{:S(2)}, u32[]{:S(2)}) collective-permute-start(f32[64,256]{1,0:T(8,128)S(1)} %get-tuple-element.85), channel_id=1, source_target_pairs={{0,16},{4,20},{8,24},{12,28},{16,0},{20,4},{24,8},{28,12},{1,17},{... | collective-permute-start | bytes 196616 | tf_op jit(solution)/shard_map/ppermute | solution.py:280
  21.6 25.3 %collective-permute-start.10 = (f32[2,384,128]{2,1,0:T(8,128)S(1)}, f32[2,384,128]{2,1,0:T(8,128)S(1)}, u32[]{:S(2)}, u32[]{:S(2)}) collective-permute-start(f32[2,384,128]{2,1,0:T(8,128)S(1)} %get-tuple-element.60.raw_ref), channel_id=1, source_target_pairs={{0,1},{1,0},{2,3},{3,2},{4,5},{5,4},{6,7},{7,6},{8,9},{9,8},{10,11... | collective-permute-start | bytes 1179656 | tf_op jit(solution)/shard_map/ppermute | solution.py:280
  28.6 31.4 %collective-permute-start.11 = (f32[2,384,128]{2,1,0:T(8,128)S(1)}, f32[2,384,128]{2,1,0:T(8,128)S(1)}, u32[]{:S(2)}, u32[]{:S(2)}) collective-permute-start(f32[2,384,128]{2,1,0:T(8,128)S(1)} %get-tuple-element.66.raw_ref), channel_id=1, source_target_pairs={{0,1},{1,0},{2,3},{3,2},{4,5},{5,4},{6,7},{7,6},{8,9},{9,8},{10,11... | collective-permute-start | bytes 1179656 | tf_op jit(solution)/shard_map/ppermute | solution.py:280
  28.7 31.4 %collective-permute-start.12 = (f32[2,384,128]{2,1,0:T(8,128)S(1)}, f32[2,384,128]{2,1,0:T(8,128)S(1)}, u32[]{:S(2)}, u32[]{:S(2)}) collective-permute-start(f32[2,384,128]{2,1,0:T(8,128)S(1)} %shard_map.73), channel_id=1, source_target_pairs={{1,2},{2,1},{0,0},{3,3},{5,6},{6,5},{4,4},{7,7},{9,10},{10,9},{8,8... | collective-permute-start | bytes 1179656 | tf_op jit(solution)/shard_map/ppermute | solution.py:326
  29.4 16.8 %collective-permute-start.8 = (f32[64,256]{1,0:T(8,128)S(1)}, f32[64,256]{1,0:T(8,128)S(1)}, u32[]{:S(2)}, u32[]{:S(2)}) collective-permute-start(f32[64,256]{1,0:T(8,128)S(1)} %add_add_fusion.one_ref), channel_id=1, source_target_pairs={{0,1},{1,0},{2,3},{3,2},{4,5},{5,4},{6,7},{7,6},{8,9},{9,8},{10,11... | collective-permute-start | bytes 196616 | tf_op jit(solution)/shard_map/ppermute | solution.py:280
  46.2 8.2 %collective-permute-start.9 = (f32[2,64,256]{2,1,0:T(8,128)S(1)}, f32[2,64,256]{2,1,0:T(8,128)S(1)}, u32[]{:S(2)}, u32[]{:S(2)}) collective-permute-start(f32[2,64,256]{2,1,0:T(8,128)S(1)} %shard_map.74.pair_ref), channel_id=1, source_target_pairs={{1,2},{2,1},{0,0},{3,3},{5,6},{6,5},{4,4},{7,7},{9,10},{10,9},{8,8... | collective-permute-start | bytes 393224 | tf_op jit(solution)/shard_map/ppermute | solution.py:332
  47.0 26.1 %collective-permute-start.15 = (f32[2,384,128]{2,1,0:T(8,128)S(1)}, f32[2,384,128]{2,1,0:T(8,128)S(1)}, u32[]{:S(2)}, u32[]{:S(2)}) collective-permute-start(f32[2,384,128]{2,1,0:T(8,128)S(1)} %shard_map.75), channel_id=1, source_target_pairs={{1,2},{2,1},{0,0},{3,3},{5,6},{6,5},{4,4},{7,7},{9,10},{10,9},{8,8... | collective-permute-start | bytes 1179656 | tf_op jit(solution)/shard_map/ppermute | solution.py:334
  47.7 27.1 %collective-permute-start.16 = (f32[2,384,128]{2,1,0:T(8,128)S(1)}, f32[2,384,128]{2,1,0:T(8,128)S(1)}, u32[]{:S(2)}, u32[]{:S(2)}) collective-permute-start(f32[2,384,128]{2,1,0:T(8,128)S(1)} %get-tuple-element.74.raw_ref), channel_id=1, source_target_pairs={{0,1},{3,2},{4,5},{7,6},{8,9},{11,10},{12,13},{15,14},{16,17},{19,... | collective-permute-start | bytes 1179656 | tf_op jit(solution)/shard_map/ppermute | solution.py:335
  60.1 16.2 %collective-permute-start.17 = (f32[2,384,128]{2,1,0:T(8,128)S(1)}, f32[2,384,128]{2,1,0:T(8,128)S(1)}, u32[]{:S(2)}, u32[]{:S(2)}) collective-permute-start(f32[2,384,128]{2,1,0:T(8,128)S(1)} %shard_map.77), channel_id=1, source_target_pairs={{0,1},{1,0},{2,3},{3,2},{4,5},{5,4},{6,7},{7,6},{8,9},{9,8},{10,11... | collective-permute-start | bytes 1179656 | tf_op jit(solution)/shard_map/ppermute | solution.py:280
  60.2 12.8 %collective-permute-start.13 = (f32[2,64,256]{2,1,0:T(8,128)S(1)}, f32[2,64,256]{2,1,0:T(8,128)S(1)}, u32[]{:S(2)}, u32[]{:S(2)}) collective-permute-start(f32[2,64,256]{2,1,0:T(8,128)S(1)} %collective-permute-done.9.inner_ref), channel_id=1, source_target_pairs={{1,0},{2,3},{5,4},{6,7},{9,8},{10,11},{13,12},{14,15},{17,16},{18,... | collective-permute-start | bytes 393224 | tf_op jit(solution)/shard_map/ppermute | solution.py:337
  61.5 15.3 %collective-permute-start.18 = (f32[2,384,128]{2,1,0:T(8,128)S(1)}, f32[2,384,128]{2,1,0:T(8,128)S(1)}, u32[]{:S(2)}, u32[]{:S(2)}) collective-permute-start(f32[2,384,128]{2,1,0:T(8,128)S(1)} %shard_map.76), channel_id=1, source_target_pairs={{1,2},{2,1},{0,0},{3,3},{5,6},{6,5},{4,4},{7,7},{9,10},{10,9},{8,8... | collective-permute-start | bytes 1179656 | tf_op jit(solution)/shard_map/ppermute | solution.py:340
  73.1 13.9 %collective-permute-start.25 = (f32[2,384,128]{2,1,0:T(8,128)S(1)}, f32[2,384,128]{2,1,0:T(8,128)S(1)}, u32[]{:S(2)}, u32[]{:S(2)}) collective-permute-start(f32[2,384,128]{2,1,0:T(8,128)S(1)} %shard_map.79), channel_id=1, source_target_pairs={{0,1},{1,0},{2,3},{3,2},{4,5},{5,4},{6,7},{7,6},{8,9},{9,8},{10,11... | collective-permute-start | bytes 1179656 | tf_op jit(solution)/shard_map/ppermute | solution.py:280
  73.2 9.2 %collective-permute-start.14 = (f32[4,64,256]{2,1,0:T(8,128)S(1)}, f32[4,64,256]{2,1,0:T(8,128)S(1)}, u32[]{:S(2)}, u32[]{:S(2)}) collective-permute-start(f32[4,64,256]{2,1,0:T(8,128)S(1)} %shard_map.78.refs_0_), channel_id=1, source_target_pairs={{0,8},{4,12},{8,0},{12,4},{16,24},{20,28},{24,16},{28,20},{1,9},{5... | collective-permute-start | bytes 786440 | tf_op jit(solution)/shard_map/ppermute | solution.py:280
  74.8 11.7 %collective-permute-start.19 = (f32[4,64,256]{2,1,0:T(8,128)S(1)}, f32[4,64,256]{2,1,0:T(8,128)S(1)}, u32[]{:S(2)}, u32[]{:S(2)}) collective-permute-start(f32[4,64,256]{2,1,0:T(8,128)S(1)} %shard_map.78.refs_0_), channel_id=1, source_target_pairs={{0,16},{4,20},{8,24},{12,28},{16,0},{20,4},{24,8},{28,12},{1,17},{... | collective-permute-start | bytes 786440 | tf_op jit(solution)/shard_map/ppermute | solution.py:280
  76.3 10.2 %collective-permute-start.20 = (f32[4,64,256]{2,1,0:T(8,128)S(1)}, f32[4,64,256]{2,1,0:T(8,128)S(1)}, u32[]{:S(2)}, u32[]{:S(2)}) collective-permute-start(f32[4,64,256]{2,1,0:T(8,128)S(1)} %shard_map.78.refs_0_), channel_id=1, source_target_pairs={{0,24},{4,28},{8,16},{12,20},{16,8},{20,12},{24,0},{28,4},{1,25},{... | collective-permute-start | bytes 786440 | tf_op jit(solution)/shard_map/ppermute | solution.py:280
  76.9 10.2 %collective-permute-start.26 = (f32[2,384,128]{2,1,0:T(8,128)S(1)}, f32[2,384,128]{2,1,0:T(8,128)S(1)}, u32[]{:S(2)}, u32[]{:S(2)}) collective-permute-start(f32[2,384,128]{2,1,0:T(8,128)S(1)} %shard_map.80), channel_id=1, source_target_pairs={{1,2},{2,1},{0,0},{3,3},{5,6},{6,5},{4,4},{7,7},{9,10},{10,9},{8,8... | collective-permute-start | bytes 1179656 | tf_op jit(solution)/shard_map/ppermute | solution.py:349
  82.5 5.4 %collective-permute-start.21 = (f32[4,64,256]{2,1,0:T(8,128)S(1)}, f32[4,64,256]{2,1,0:T(8,128)S(1)}, u32[]{:S(2)}, u32[]{:S(2)}) collective-permute-start(f32[4,64,256]{2,1,0:T(8,128)S(1)} %shard_map.78.refs_0_), channel_id=1, source_target_pairs={{0,4},{4,0},{8,12},{12,8},{16,20},{20,16},{24,28},{28,24},{1,5},{5... | collective-permute-start | bytes 786440 | tf_op jit(solution)/shard_map/ppermute | solution.py:280
  91.7 5.4 %collective-permute-start.29 = (f32[16,64]{1,0:T(8,128)S(1)}, f32[16,64]{1,0:T(8,128)S(1)}, u32[]{:S(2)}, u32[]{:S(2)}) collective-permute-start(f32[16,64]{1,0:T(8,128)S(1)} %score.1.refs_0_), channel_id=1, source_target_pairs={{0,3},{1,2},{2,1},{3,0},{4,7},{5,6},{6,5},{7,4},{8,11},{9,10},{10,... | collective-permute-start | bytes 12296 | tf_op jit(solution)/shard_map/ppermute | solution.py:280
  (7 other events, 25.0 us)

commit v7 on v6

--- a/solution.py
+++ b/solution.py
@@ -105,13 +105,16 @@
     piece = width // (2 * count)
     hit = lang_ref[...] == lax.broadcasted_iota(jnp.int32, (LANGS, rows), 0)
     hit = jnp.where(hit, 1.0, 0.0)
+    hit = jnp.concatenate([hit, hit], axis=1).astype(jnp.bfloat16)
     inverse = lax.rsqrt(sum(ref[...] for ref in square_refs) + 1e-06)
 
     def sums(part):
         columns = pl.ds(pl.multiple_of(part * piece, piece), piece)
-        return jnp.dot(
-            hit, held_ref[:, columns] * inverse, precision=HIGHEST, preferred_element_type=jnp.float32
-        )
+        unit = held_ref[:, columns] * inverse
+        high = unit.astype(jnp.bfloat16)
+        rest = (unit - high.astype(jnp.float32)).astype(jnp.bfloat16)
+        both = jnp.concatenate([high, rest], axis=0)
+        return jnp.dot(hit, both, preferred_element_type=jnp.float32)
 
     for index in range(count):
         other_ref[index] = sums(me_ref[0] ^ 1 ^ (2 * index))
@@ -328,6 +331,8 @@
     other = swap(lang, "feat", 1)
     raw1 = [after(x, lang) for x in raw1]
     got2 = [swap(raw1[0], "feat", 1)]
+    raw2 = project(more_kernel, me_feat, 4, 2, acts2, grads2, [after(down, lang), out_sketch], [])
+    other = after(other, raw2[0])
     pair = small(stack_kernel, (2, *lang.shape), is_middle, [lang, other])
     far_pair = lax.ppermute(pair, "feat", inner)
     sent1.append(onward(after(raw0[1], pair), got1[1]))
@@ -335,8 +340,7 @@
     got2.append(lax.ppermute(after(raw1[1], pair), "feat", inward))
     far_pair = after(far_pair, sent1[1])
     outer_pair = lax.ppermute(far_pair, "feat", outward)
-    *raw2, own_a, own_b = project(more_kernel, me_feat, 4, 4, acts2, grads2, [after(down, far_pair), out_sketch], [])
-    sent2 = [onward(after(raw1[0], own_a), got2[0])]
+    sent2 = [onward(after(raw1[0], far_pair), got2[0])]
     near = [lax.ppermute(sent2[0], "feat", inner)]
     sent3 = [onward(after(raw2[0], sent2[0]), far[0])]
     got3 = [swap(sent3[0], "feat", 1)]
@@ -347,7 +351,8 @@
     got3.append(swap(sent3[1], "feat", 1))
     sent2.append(onward(after(raw1[1], sent3[1]), got2[1]))
     near.append(lax.ppermute(sent2[1], "feat", inner))
-    grad_a, square_a = product(is_middle, [after(own_a, sent2[1]), got3[0], near[0]])
+    own_a, own_b = project(more_kernel, me_feat, 6, 2, acts2, grads2, [after(down, sent2[1]), out_sketch], [])
+    grad_a, square_a = product(is_middle, [own_a, got3[0], near[0]])
     langs[1:] = [after(x, square_a) for x in langs[1:]]
     langs = langs + [swap(x, "ex", 1) for x in langs]
     grad_b, square_b = product(is_middle, [after(own_b, square_a), got3[1], near[1]])

time: 98.1 us -> 92.3 us (0.941)
  waiting for transfers between devices: 46.1 us -> 35.2 us
  starting transfers between devices: 34 us -> 38.9 us
    ppermute x23, waiting for transfers between devices: 35.3 us -> 24.3 us  [swap(): lax.ppermute(x, axis, [(i, i ^ mask) for i in range(lax.axis_size(axis))])]
    ppermute x23, starting transfers between devices: 22.6 us -> 27.2 us  [swap(): lax.ppermute(x, axis, [(i, i ^ mask) for i in range(lax.axis_size(axis))])]
    pallas_call x3 -> x4, Pallas kernels: 12.2 us -> 12.9 us  [project(): pl.pallas_call(kernel, out_shape=[jax.ShapeDtypeStruct(piece, jnp.float32...]
  transfers between devices with their start and end apart: 30 -> 30, of which waited for: 12 -> 13; matrix products, arithmetic and copies ran while one was open for 0% -> 0% of each run, Pallas kernels for 11% -> 12%
where the time goes in v7:
time: 92.3 us; the launch traced here: 92 us
  starting transfers between devices  38.9 us (42%)
  waiting for transfers between devices  35.2 us (38%)
  Pallas kernels  17.6 us (19%)
    ppermute x23, starting transfers between devices, swap(): lax.ppermute(x, axis, [(i, i ^ mask) for i in range(lax.axis_size(axis))])  27.2 us
    ppermute x23, waiting for transfers between devices, swap(): lax.ppermute(x, axis, [(i, i ^ mask) for i in range(lax.axis_size(axis))])  24.3 us
    pallas_call x4, Pallas kernels, project(): pl.pallas_call(kernel, out_shape=[jax.ShapeDtypeStruct(piece, jnp.float32...  12.9 us
    ppermute x1, waiting for transfers between devices, ordered(): outer_pair = lax.ppermute(far_pair, 'feat', outward)  10.8 us
    ppermute x1, starting transfers between devices, ordered(): got2.append(lax.ppermute(after(raw1[1], pair), 'feat', inward))  7 us
  transfers between devices with their start and end apart: 30, of which 13 were waited for; matrix products, arithmetic and copies ran while one was open for 0% of the time, Pallas kernels for 12%

profile of v7, /device:TPU:0, one launch (start us, length us, event | category | flops | bytes accessed | tf_op | source)
XLA Modules:
  0.0 92.0 jit_solution(9614427886995045147)
XLA Ops:
  0.0 3.5 %project.4 = (f32[2,384,128]{2,1,0:T(8,128)S(1)}, f32[2,384,128]{2,1,0:T(8,128)S(1)}, bf16[1024,128]{1,0:T(8,128)(2,1)S(1)}, f32[32,1]{1,0:T(8,128)S(1)}) custom-call(s32[1]{0:T(128)} %bitcast.feat.feat_ref.me_ref, bf16[4096,1024]{1,0:T(8,128)(2,1)} %bitcast.24, bf16[4096,1024]{1,0:T(8,128)(2,1)} %bitcast.28, bf16[1024,128]{1,0:T(8,128)(2,1)} %adapter_ref.1, ...), custom_call_target="tpu_custom_call" | custom-call | flops 536870912 | bytes 4980736 | tf_op jit(solution)/shard_map/project/pallas_call | solution.py:81
  3.5 5.2 %collective-permute-start.2 = (f32[32,1]{1,0:T(8,128)S(1)}, f32[32,1]{1,0:T(8,128)S(1)}, u32[]{:S(2)}, u32[]{:S(2)}) collective-permute-start(f32[32,1]{1,0:T(8,128)S(1)} %get-tuple-element.46.refs_0_), channel_id=1, source_target_pairs={{0,3},{1,2},{2,1},{3,0},{4,7},{5,6},{6,5},{7,4},{8,11},{9,10},{10,... | collective-permute-start | bytes 392 | tf_op jit(solution)/shard_map/ppermute | solution.py:283
  9.3 3.1 %project.5 = (f32[2,384,128]{2,1,0:T(8,128)S(1)}, f32[2,384,128]{2,1,0:T(8,128)S(1)}) custom-call(s32[1]{0:T(128)} %bitcast.feat.feat_ref.me_ref, bf16[4096,1024]{1,0:T(8,128)(2,1)} %bitcast.25, bf16[4096,1024]{1,0:T(8,128)(2,1)} %bitcast.29, bf16[1024,128]{1,0:T(8,128)(2,1)S(1)} %get-tuple-element.76.down_ref, bf16[1024,128]{1,0:T(8,128)(2,1)} %sketch_ref.7), custom_call_target="tpu_custom_call" | custom-call | flops 536870912 | bytes 4980736 | tf_op jit(solution)/shard_map/project/pallas_call | solution.py:81
  13.3 1.2 %lang_parts.1 = (f32[4,64,256]{2,1,0:T(8,128)S(1)}, f32[64,256]{1,0:T(8,128)S(1)}, f32[64,256]{1,0:T(8,128)S(1)}, f32[64,256]{1,0:T(8,128)S(1)}, f32[64,256]{1,0:T(8,128)S(1)}) custom-call(s32[1]{0:T(128)} %bitcast.1.me_ref.ex_ref, f32[32,2048]{1,0:T(8,128)} %held_ref.3, s32[1,32]{1,0:T(1,128)S(1)} %fusion.4.lang_ref, ...), custom_call_target="tpu_custom_call" | custom-call | tf_op jit(solution)/shard_map/lang_parts/pallas_call | solution.py:128
  15.3 0.9 collective-permute-done.3
  16.2 1.6 %collective-permute-start.6 = (f32[64,256]{1,0:T(8,128)S(1)}, f32[64,256]{1,0:T(8,128)S(1)}, u32[]{:S(2)}, u32[]{:S(2)}) collective-permute-start(f32[64,256]{1,0:T(8,128)S(1)} %get-tuple-element.87), channel_id=1, source_target_pairs={{0,16},{4,20},{8,24},{12,28},{16,0},{20,4},{24,8},{28,12},{1,17},{... | collective-permute-start | bytes 196616 | tf_op jit(solution)/shard_map/ppermute | solution.py:283
  17.8 1.4 %collective-permute-start.7 = (f32[64,256]{1,0:T(8,128)S(1)}, f32[64,256]{1,0:T(8,128)S(1)}, u32[]{:S(2)}, u32[]{:S(2)}) collective-permute-start(f32[64,256]{1,0:T(8,128)S(1)} %get-tuple-element.88), channel_id=1, source_target_pairs={{0,24},{4,28},{8,16},{12,20},{16,8},{20,12},{24,0},{28,4},{1,25},{... | collective-permute-start | bytes 196616 | tf_op jit(solution)/shard_map/ppermute | solution.py:283
  20.3 6.4 %collective-permute-done.4.got_ref = f32[2,384,128]{2,1,0:T(8,128)S(1)} collective-permute-done((f32[2,384,128]{2,1,0:T(8,128)S(1)}, f32[2,384,128]{2,1,0:T(8,128)S(1)}, u32[]{:S(2)}, u32[]{:S(2)}) %collective-permute-start.4) | collective-permute-done | bytes 393248 | tf_op jit(solution)/shard_map/ppermute | solution.py:283
  28.1 4.8 %collective-permute-start.8 = (f32[64,256]{1,0:T(8,128)S(1)}, f32[64,256]{1,0:T(8,128)S(1)}, u32[]{:S(2)}, u32[]{:S(2)}) collective-permute-start(f32[64,256]{1,0:T(8,128)S(1)} %add_add_fusion.one_ref), channel_id=1, source_target_pairs={{0,1},{1,0},{2,3},{3,2},{4,5},{5,4},{6,7},{7,6},{8,9},{9,8},{10,11... | collective-permute-start | bytes 196616 | tf_op jit(solution)/shard_map/ppermute | solution.py:283
  32.9 3.1 %project.6 = (f32[2,384,128]{2,1,0:T(8,128)S(1)}, f32[2,384,128]{2,1,0:T(8,128)S(1)}) custom-call(s32[1]{0:T(128)} %bitcast.feat.feat_ref.me_ref, bf16[4096,1024]{1,0:T(8,128)(2,1)} %bitcast.26, bf16[4096,1024]{1,0:T(8,128)(2,1)} %bitcast.30, bf16[1024,128]{1,0:T(8,128)(2,1)S(1)} %get-tuple-element.76.down_ref, bf16[1024,128]{1,0:T(8,128)(2,1)} %sketch_ref.7), custom_call_target="tpu_custom_call" | custom-call | flops 536870912 | bytes 4980736 | tf_op jit(solution)/shard_map/project/pallas_call | solution.py:81
  36.0 8.4 %collective-permute-done.8.two_ref = f32[64,256]{1,0:T(8,128)S(1)} collective-permute-done((f32[64,256]{1,0:T(8,128)S(1)}, f32[64,256]{1,0:T(8,128)S(1)}, u32[]{:S(2)}, u32[]{:S(2)}) %collective-permute-start.8) | collective-permute-done | bytes 65568 | tf_op jit(solution)/shard_map/ppermute | solution.py:283
  45.9 7.0 %collective-permute-start.16 = (f32[2,384,128]{2,1,0:T(8,128)S(1)}, f32[2,384,128]{2,1,0:T(8,128)S(1)}, u32[]{:S(2)}, u32[]{:S(2)}) collective-permute-start(f32[2,384,128]{2,1,0:T(8,128)S(1)} %get-tuple-element.75.raw_ref), channel_id=1, source_target_pairs={{0,1},{3,2},{4,5},{7,6},{8,9},{11,10},{12,13},{15,14},{16,17},{19,... | collective-permute-start | bytes 1179656 | tf_op jit(solution)/shard_map/ppermute | solution.py:340
  53.1 1.3 %collective-permute-start.13 = (f32[2,64,256]{2,1,0:T(8,128)S(1)}, f32[2,64,256]{2,1,0:T(8,128)S(1)}, u32[]{:S(2)}, u32[]{:S(2)}) collective-permute-start(f32[2,64,256]{2,1,0:T(8,128)S(1)} %collective-permute-done.9.inner_ref), channel_id=1, source_target_pairs={{1,0},{2,3},{5,4},{6,7},{9,8},{10,11},{13,12},{14,15},{17,16},{18,... | collective-permute-start | bytes 393224 | tf_op jit(solution)/shard_map/ppermute | solution.py:342
  55.1 10.8 %collective-permute-done.13.outer_ref = f32[2,64,256]{2,1,0:T(8,128)S(1)} collective-permute-done((f32[2,64,256]{2,1,0:T(8,128)S(1)}, f32[2,64,256]{2,1,0:T(8,128)S(1)}, u32[]{:S(2)}, u32[]{:S(2)}) %collective-permute-start.13) | collective-permute-done | bytes 131104 | tf_op jit(solution)/shard_map/ppermute | solution.py:342
  66.1 2.5 %collective-permute-start.20 = (f32[4,64,256]{2,1,0:T(8,128)S(1)}, f32[4,64,256]{2,1,0:T(8,128)S(1)}, u32[]{:S(2)}, u32[]{:S(2)}) collective-permute-start(f32[4,64,256]{2,1,0:T(8,128)S(1)} %shard_map.78.refs_0_), channel_id=1, source_target_pairs={{0,24},{4,28},{8,16},{12,20},{16,8},{20,12},{24,0},{28,4},{1,25},{... | collective-permute-start | bytes 786440 | tf_op jit(solution)/shard_map/ppermute | solution.py:283
  69.1 1.6 %collective-permute-done.17.end_ref = f32[2,384,128]{2,1,0:T(8,128)S(1)} collective-permute-done((f32[2,384,128]{2,1,0:T(8,128)S(1)}, f32[2,384,128]{2,1,0:T(8,128)S(1)}, u32[]{:S(2)}, u32[]{:S(2)}) %collective-permute-start.17) | collective-permute-done | bytes 393248 | tf_op jit(solution)/shard_map/ppermute | solution.py:283
  70.8 1.5 %collective-permute-start.14 = (f32[4,64,256]{2,1,0:T(8,128)S(1)}, f32[4,64,256]{2,1,0:T(8,128)S(1)}, u32[]{:S(2)}, u32[]{:S(2)}) collective-permute-start(f32[4,64,256]{2,1,0:T(8,128)S(1)} %shard_map.78.refs_0_), channel_id=1, source_target_pairs={{0,8},{4,12},{8,0},{12,4},{16,24},{20,28},{24,16},{28,20},{1,9},{5... | collective-permute-start | bytes 786440 | tf_op jit(solution)/shard_map/ppermute | solution.py:283
  73.0 3.1 %project.7 = (f32[2,384,128]{2,1,0:T(8,128)S(1)}, f32[2,384,128]{2,1,0:T(8,128)S(1)}) custom-call(s32[1]{0:T(128)} %bitcast.feat.feat_ref.me_ref, bf16[4096,1024]{1,0:T(8,128)(2,1)} %bitcast.27, bf16[4096,1024]{1,0:T(8,128)(2,1)} %bitcast.31, bf16[1024,128]{1,0:T(8,128)(2,1)S(1)} %get-tuple-element.76.down_ref, bf16[1024,128]{1,0:T(8,128)(2,1)} %sketch_ref.7), custom_call_target="tpu_custom_call" | custom-call | flops 536870912 | bytes 4980736 | tf_op jit(solution)/shard_map/project/pallas_call | solution.py:81
  77.0 2.0 %collective-permute-done.19.refs_2_ = f32[4,64,256]{2,1,0:T(8,128)S(1)} collective-permute-done((f32[4,64,256]{2,1,0:T(8,128)S(1)}, f32[4,64,256]{2,1,0:T(8,128)S(1)}, u32[]{:S(2)}, u32[]{:S(2)}) %collective-permute-start.19) | collective-permute-done | bytes 262176 | tf_op jit(solution)/shard_map/ppermute | solution.py:283
  81.5 0.9 score.1.refs_0_
  82.3 2.4 %collective-permute-start.29 = (f32[16,64]{1,0:T(8,128)S(1)}, f32[16,64]{1,0:T(8,128)S(1)}, u32[]{:S(2)}, u32[]{:S(2)}) collective-permute-start(f32[16,64]{1,0:T(8,128)S(1)} %score.1.refs_0_), channel_id=1, source_target_pairs={{0,3},{1,2},{2,1},{3,0},{4,7},{5,6},{6,5},{7,4},{8,11},{9,10},{10,... | collective-permute-start | bytes 12296 | tf_op jit(solution)/shard_map/ppermute | solution.py:283
  84.7 3.1 %collective-permute-start.28 = (f32[16,64]{1,0:T(8,128)S(1)}, f32[16,64]{1,0:T(8,128)S(1)}, u32[]{:S(2)}, u32[]{:S(2)}) collective-permute-start(f32[16,64]{1,0:T(8,128)S(1)} %score.1.refs_0_), channel_id=1, source_target_pairs={{0,2},{1,3},{2,0},{3,1},{4,6},{5,7},{6,4},{7,5},{8,10},{9,11},{10,... | collective-permute-start | bytes 12296 | tf_op jit(solution)/shard_map/ppermute | solution.py:283
  88.3 1.2 %collective-permute-done.28.refs_2_ = f32[16,64]{1,0:T(8,128)S(1)} collective-permute-done((f32[16,64]{1,0:T(8,128)S(1)}, f32[16,64]{1,0:T(8,128)S(1)}, u32[]{:S(2)}, u32[]{:S(2)}) %collective-permute-start.28) | collective-permute-done | bytes 4128 | tf_op jit(solution)/shard_map/ppermute | solution.py:283
  89.5 2.0 %collective-permute-done.27.refs_1_ = f32[16,64]{1,0:T(8,128)S(1)} collective-permute-done((f32[16,64]{1,0:T(8,128)S(1)}, f32[16,64]{1,0:T(8,128)S(1)}, u32[]{:S(2)}, u32[]{:S(2)}) %collective-permute-start.27) | collective-permute-done | bytes 4128 | tf_op jit(solution)/shard_map/ppermute | solution.py:283
  (58 shorter events, 12.8 us)
Async XLA Ops:
  3.5 9.0 %collective-permute-start.2 = (f32[32,1]{1,0:T(8,128)S(1)}, f32[32,1]{1,0:T(8,128)S(1)}, u32[]{:S(2)}, u32[]{:S(2)}) collective-permute-start(f32[32,1]{1,0:T(8,128)S(1)} %get-tuple-element.46.refs_0_), channel_id=1, source_target_pairs={{0,3},{1,2},{2,1},{3,0},{4,7},{5,6},{6,5},{7,4},{8,11},{9,10},{10,... | collective-permute-start | bytes 392 | tf_op jit(solution)/shard_map/ppermute | solution.py:283
  8.7 4.6 %collective-permute-start.1 = (f32[32,1]{1,0:T(8,128)S(1)}, f32[32,1]{1,0:T(8,128)S(1)}, u32[]{:S(2)}, u32[]{:S(2)}) collective-permute-start(f32[32,1]{1,0:T(8,128)S(1)} %get-tuple-element.46.refs_0_), channel_id=1, source_target_pairs={{0,2},{1,3},{2,0},{3,1},{4,6},{5,7},{6,4},{7,5},{8,10},{9,11},{10,... | collective-permute-start | bytes 392 | tf_op jit(solution)/shard_map/ppermute | solution.py:283
  8.7 4.6 %collective-permute-start = (f32[32,1]{1,0:T(8,128)S(1)}, f32[32,1]{1,0:T(8,128)S(1)}, u32[]{:S(2)}, u32[]{:S(2)}) collective-permute-start(f32[32,1]{1,0:T(8,128)S(1)} %get-tuple-element.46.refs_0_), channel_id=1, source_target_pairs={{0,1},{1,0},{2,3},{3,2},{4,5},{5,4},{6,7},{7,6},{8,9},{9,8},{10,11... | collective-permute-start | bytes 392 | tf_op jit(solution)/shard_map/ppermute | solution.py:283
  14.6 12.1 %collective-permute-start.4 = (f32[2,384,128]{2,1,0:T(8,128)S(1)}, f32[2,384,128]{2,1,0:T(8,128)S(1)}, u32[]{:S(2)}, u32[]{:S(2)}) collective-permute-start(f32[2,384,128]{2,1,0:T(8,128)S(1)} %get-tuple-element.55.raw_ref), channel_id=1, source_target_pairs={{0,1},{1,0},{2,3},{3,2},{4,5},{5,4},{6,7},{7,6},{8,9},{9,8},{10,11... | collective-permute-start | bytes 1179656 | tf_op jit(solution)/shard_map/ppermute | solution.py:283
  16.2 10.5 %collective-permute-start.6 = (f32[64,256]{1,0:T(8,128)S(1)}, f32[64,256]{1,0:T(8,128)S(1)}, u32[]{:S(2)}, u32[]{:S(2)}) collective-permute-start(f32[64,256]{1,0:T(8,128)S(1)} %get-tuple-element.87), channel_id=1, source_target_pairs={{0,16},{4,20},{8,24},{12,28},{16,0},{20,4},{24,8},{28,12},{1,17},{... | collective-permute-start | bytes 196616 | tf_op jit(solution)/shard_map/ppermute | solution.py:283
  17.8 9.0 %collective-permute-start.7 = (f32[64,256]{1,0:T(8,128)S(1)}, f32[64,256]{1,0:T(8,128)S(1)}, u32[]{:S(2)}, u32[]{:S(2)}) collective-permute-start(f32[64,256]{1,0:T(8,128)S(1)} %get-tuple-element.88), channel_id=1, source_target_pairs={{0,24},{4,28},{8,16},{12,20},{16,8},{20,12},{24,0},{28,4},{1,25},{... | collective-permute-start | bytes 196616 | tf_op jit(solution)/shard_map/ppermute | solution.py:283
  19.2 7.6 %collective-permute-start.5 = (f32[64,256]{1,0:T(8,128)S(1)}, f32[64,256]{1,0:T(8,128)S(1)}, u32[]{:S(2)}, u32[]{:S(2)}) collective-permute-start(f32[64,256]{1,0:T(8,128)S(1)} %get-tuple-element.89), channel_id=1, source_target_pairs={{0,8},{4,12},{8,0},{12,4},{16,24},{20,28},{24,16},{28,20},{1,9},{5... | collective-permute-start | bytes 196616 | tf_op jit(solution)/shard_map/ppermute | solution.py:283
  19.8 25.3 %collective-permute-start.10 = (f32[2,384,128]{2,1,0:T(8,128)S(1)}, f32[2,384,128]{2,1,0:T(8,128)S(1)}, u32[]{:S(2)}, u32[]{:S(2)}) collective-permute-start(f32[2,384,128]{2,1,0:T(8,128)S(1)} %get-tuple-element.65.raw_ref), channel_id=1, source_target_pairs={{0,1},{1,0},{2,3},{3,2},{4,5},{5,4},{6,7},{7,6},{8,9},{9,8},{10,11... | collective-permute-start | bytes 1179656 | tf_op jit(solution)/shard_map/ppermute | solution.py:283
  26.8 26.1 %collective-permute-start.11 = (f32[2,384,128]{2,1,0:T(8,128)S(1)}, f32[2,384,128]{2,1,0:T(8,128)S(1)}, u32[]{:S(2)}, u32[]{:S(2)}) collective-permute-start(f32[2,384,128]{2,1,0:T(8,128)S(1)} %get-tuple-element.67.raw_ref), channel_id=1, source_target_pairs={{0,1},{1,0},{2,3},{3,2},{4,5},{5,4},{6,7},{7,6},{8,9},{9,8},{10,11... | collective-permute-start | bytes 1179656 | tf_op jit(solution)/shard_map/ppermute | solution.py:283
  27.5 25.5 %collective-permute-start.12 = (f32[2,384,128]{2,1,0:T(8,128)S(1)}, f32[2,384,128]{2,1,0:T(8,128)S(1)}, u32[]{:S(2)}, u32[]{:S(2)}) collective-permute-start(f32[2,384,128]{2,1,0:T(8,128)S(1)} %shard_map.73), channel_id=1, source_target_pairs={{1,2},{2,1},{0,0},{3,3},{5,6},{6,5},{4,4},{7,7},{9,10},{10,9},{8,8... | collective-permute-start | bytes 1179656 | tf_op jit(solution)/shard_map/ppermute | solution.py:329
  28.1 16.3 %collective-permute-start.8 = (f32[64,256]{1,0:T(8,128)S(1)}, f32[64,256]{1,0:T(8,128)S(1)}, u32[]{:S(2)}, u32[]{:S(2)}) collective-permute-start(f32[64,256]{1,0:T(8,128)S(1)} %add_add_fusion.one_ref), channel_id=1, source_target_pairs={{0,1},{1,0},{2,3},{3,2},{4,5},{5,4},{6,7},{7,6},{8,9},{9,8},{10,11... | collective-permute-start | bytes 196616 | tf_op jit(solution)/shard_map/ppermute | solution.py:283
  44.4 8.5 %collective-permute-start.9 = (f32[2,64,256]{2,1,0:T(8,128)S(1)}, f32[2,64,256]{2,1,0:T(8,128)S(1)}, u32[]{:S(2)}, u32[]{:S(2)}) collective-permute-start(f32[2,64,256]{2,1,0:T(8,128)S(1)} %shard_map.74.pair_ref), channel_id=1, source_target_pairs={{1,2},{2,1},{0,0},{3,3},{5,6},{6,5},{4,4},{7,7},{9,10},{10,9},{8,8... | collective-permute-start | bytes 393224 | tf_op jit(solution)/shard_map/ppermute | solution.py:337
  45.2 20.8 %collective-permute-start.15 = (f32[2,384,128]{2,1,0:T(8,128)S(1)}, f32[2,384,128]{2,1,0:T(8,128)S(1)}, u32[]{:S(2)}, u32[]{:S(2)}) collective-permute-start(f32[2,384,128]{2,1,0:T(8,128)S(1)} %shard_map.75), channel_id=1, source_target_pairs={{1,2},{2,1},{0,0},{3,3},{5,6},{6,5},{4,4},{7,7},{9,10},{10,9},{8,8... | collective-permute-start | bytes 1179656 | tf_op jit(solution)/shard_map/ppermute | solution.py:339
  45.9 22.8 %collective-permute-start.16 = (f32[2,384,128]{2,1,0:T(8,128)S(1)}, f32[2,384,128]{2,1,0:T(8,128)S(1)}, u32[]{:S(2)}, u32[]{:S(2)}) collective-permute-start(f32[2,384,128]{2,1,0:T(8,128)S(1)} %get-tuple-element.75.raw_ref), channel_id=1, source_target_pairs={{0,1},{3,2},{4,5},{7,6},{8,9},{11,10},{12,13},{15,14},{16,17},{19,... | collective-permute-start | bytes 1179656 | tf_op jit(solution)/shard_map/ppermute | solution.py:340
  53.0 17.7 %collective-permute-start.17 = (f32[2,384,128]{2,1,0:T(8,128)S(1)}, f32[2,384,128]{2,1,0:T(8,128)S(1)}, u32[]{:S(2)}, u32[]{:S(2)}) collective-permute-start(f32[2,384,128]{2,1,0:T(8,128)S(1)} %shard_map.77), channel_id=1, source_target_pairs={{0,1},{1,0},{2,3},{3,2},{4,5},{5,4},{6,7},{7,6},{8,9},{9,8},{10,11... | collective-permute-start | bytes 1179656 | tf_op jit(solution)/shard_map/ppermute | solution.py:283
  53.1 12.8 %collective-permute-start.13 = (f32[2,64,256]{2,1,0:T(8,128)S(1)}, f32[2,64,256]{2,1,0:T(8,128)S(1)}, u32[]{:S(2)}, u32[]{:S(2)}) collective-permute-start(f32[2,64,256]{2,1,0:T(8,128)S(1)} %collective-permute-done.9.inner_ref), channel_id=1, source_target_pairs={{1,0},{2,3},{5,4},{6,7},{9,8},{10,11},{13,12},{14,15},{17,16},{18,... | collective-permute-start | bytes 393224 | tf_op jit(solution)/shard_map/ppermute | solution.py:342
  54.4 17.9 %collective-permute-start.18 = (f32[2,384,128]{2,1,0:T(8,128)S(1)}, f32[2,384,128]{2,1,0:T(8,128)S(1)}, u32[]{:S(2)}, u32[]{:S(2)}) collective-permute-start(f32[2,384,128]{2,1,0:T(8,128)S(1)} %shard_map.76), channel_id=1, source_target_pairs={{1,2},{2,1},{0,0},{3,3},{5,6},{6,5},{4,4},{7,7},{9,10},{10,9},{8,8... | collective-permute-start | bytes 1179656 | tf_op jit(solution)/shard_map/ppermute | solution.py:344
  66.0 13.6 %collective-permute-start.25 = (f32[2,384,128]{2,1,0:T(8,128)S(1)}, f32[2,384,128]{2,1,0:T(8,128)S(1)}, u32[]{:S(2)}, u32[]{:S(2)}) collective-permute-start(f32[2,384,128]{2,1,0:T(8,128)S(1)} %shard_map.79), channel_id=1, source_target_pairs={{0,1},{1,0},{2,3},{3,2},{4,5},{5,4},{6,7},{7,6},{8,9},{9,8},{10,11... | collective-permute-start | bytes 1179656 | tf_op jit(solution)/shard_map/ppermute | solution.py:283
  66.1 10.9 %collective-permute-start.20 = (f32[4,64,256]{2,1,0:T(8,128)S(1)}, f32[4,64,256]{2,1,0:T(8,128)S(1)}, u32[]{:S(2)}, u32[]{:S(2)}) collective-permute-start(f32[4,64,256]{2,1,0:T(8,128)S(1)} %shard_map.78.refs_0_), channel_id=1, source_target_pairs={{0,24},{4,28},{8,16},{12,20},{16,8},{20,12},{24,0},{28,4},{1,25},{... | collective-permute-start | bytes 786440 | tf_op jit(solution)/shard_map/ppermute | solution.py:283
  68.6 10.4 %collective-permute-start.19 = (f32[4,64,256]{2,1,0:T(8,128)S(1)}, f32[4,64,256]{2,1,0:T(8,128)S(1)}, u32[]{:S(2)}, u32[]{:S(2)}) collective-permute-start(f32[4,64,256]{2,1,0:T(8,128)S(1)} %shard_map.78.refs_0_), channel_id=1, source_target_pairs={{0,16},{4,20},{8,24},{12,28},{16,0},{20,4},{24,8},{28,12},{1,17},{... | collective-permute-start | bytes 786440 | tf_op jit(solution)/shard_map/ppermute | solution.py:283
  70.8 8.4 %collective-permute-start.14 = (f32[4,64,256]{2,1,0:T(8,128)S(1)}, f32[4,64,256]{2,1,0:T(8,128)S(1)}, u32[]{:S(2)}, u32[]{:S(2)}) collective-permute-start(f32[4,64,256]{2,1,0:T(8,128)S(1)} %shard_map.78.refs_0_), channel_id=1, source_target_pairs={{0,8},{4,12},{8,0},{12,4},{16,24},{20,28},{24,16},{28,20},{1,9},{5... | collective-permute-start | bytes 786440 | tf_op jit(solution)/shard_map/ppermute | solution.py:283
  72.3 7.4 %collective-permute-start.26 = (f32[2,384,128]{2,1,0:T(8,128)S(1)}, f32[2,384,128]{2,1,0:T(8,128)S(1)}, u32[]{:S(2)}, u32[]{:S(2)}) collective-permute-start(f32[2,384,128]{2,1,0:T(8,128)S(1)} %shard_map.80), channel_id=1, source_target_pairs={{1,2},{2,1},{0,0},{3,3},{5,6},{6,5},{4,4},{7,7},{9,10},{10,9},{8,8... | collective-permute-start | bytes 1179656 | tf_op jit(solution)/shard_map/ppermute | solution.py:353
  82.3 5.9 %collective-permute-start.29 = (f32[16,64]{1,0:T(8,128)S(1)}, f32[16,64]{1,0:T(8,128)S(1)}, u32[]{:S(2)}, u32[]{:S(2)}) collective-permute-start(f32[16,64]{1,0:T(8,128)S(1)} %score.1.refs_0_), channel_id=1, source_target_pairs={{0,3},{1,2},{2,1},{3,0},{4,7},{5,6},{6,5},{7,4},{8,11},{9,10},{10,... | collective-permute-start | bytes 12296 | tf_op jit(solution)/shard_map/ppermute | solution.py:283
  84.7 4.8 %collective-permute-start.28 = (f32[16,64]{1,0:T(8,128)S(1)}, f32[16,64]{1,0:T(8,128)S(1)}, u32[]{:S(2)}, u32[]{:S(2)}) collective-permute-start(f32[16,64]{1,0:T(8,128)S(1)} %score.1.refs_0_), channel_id=1, source_target_pairs={{0,2},{1,3},{2,0},{3,1},{4,6},{5,7},{6,4},{7,5},{8,10},{9,11},{10,... | collective-permute-start | bytes 12296 | tf_op jit(solution)/shard_map/ppermute | solution.py:283
  (7 other events, 23.3 us)

commit v8 on v7

--- a/solution.py
+++ b/solution.py
@@ -195,8 +195,10 @@
     )(middle, *parts)
 
 
-def score_kernel(feat_ref, ex_ref, *refs, scale, n_lang):
-    lang_refs, grad_refs, square_refs, o_ref = refs[:n_lang], refs[n_lang:-1:2], refs[n_lang + 1 : -1 : 2], refs[-1]
+def score_kernel(middle_ref, feat_ref, ex_ref, *refs, scale, n_lang):
+    lang_refs, (grad_a, square_a, *part_refs, o_ref, grad_b, square_b, grad_ref) = refs[:n_lang], refs[n_lang:]
+    product_kernel(middle_ref, *part_refs, grad_b, square_b, grad_ref)
+    grad_refs, square_refs = [grad_a, grad_b], [square_a, square_b]
     total = None
     feat, ex = feat_ref[0], ex_ref[0]
     middle = (feat == 1) | (feat == 2)
@@ -222,17 +224,23 @@
         o_ref[index * count : (index + 1) * count] = inner * (lax.rsqrt(square_ref[...] + 1e-06) * scale)
 
 
-def score(feat, ex, langs, products, scale):
-    flat = [x for pair in products for x in pair]
-    mine = sum(square.shape[0] for _, square in products)
+def score(middle, feat, ex, langs, first, parts, scale):
+    grad, square = first
+    operands = [*langs, *first, *parts]
+    wide = parts[0].shape[2]
     return pl.pallas_call(
         functools.partial(score_kernel, scale=scale, n_lang=len(langs)),
-        out_shape=jax.ShapeDtypeStruct((mine, LANGS), jnp.float32),
-        in_specs=[SMEM] * 2 + [VMEM] * (len(langs) + len(flat)),
+        out_shape=jax.ShapeDtypeStruct((2 * square.shape[0], LANGS), jnp.float32),
+        in_specs=[SMEM] * 3 + [VMEM] * len(operands),
         out_specs=VMEM,
+        scratch_shapes=[
+            pltpu.VMEM(grad.shape, grad.dtype),
+            pltpu.VMEM(square.shape, square.dtype),
+            pltpu.VMEM((square.shape[0], wide, wide), jnp.float32),
+        ],
         compiler_params=pltpu.CompilerParams(vmem_limit_bytes=SMALL),
         name="score",
-    )(feat, ex, *langs, *flat)
+    )(middle, feat, ex, *operands)
 
 
 def small(kernel, shape, middle, operands):
@@ -299,53 +307,49 @@
     me_ex = ex.astype(jnp.int32).reshape(1)
     me_feat = feat.astype(jnp.int32).reshape(1)
     acts2, grads2 = acts.reshape(-1, width), grads.reshape(-1, width)
-    adapter, rank_sketch, out_sketch, held, acts2, grads2 = (
+    adapter, rank_sketch, out_sketch, held_far, acts2, grads2 = (
         pltpu.with_memory_space_constraint(x, pltpu.HBM)
         for x in (adapter, rank_sketch.T, out_sketch, held, acts2, grads2)
     )
     down_like = jax.ShapeDtypeStruct((width, 2 * rank_sketch.shape[0]), jnp.bfloat16)
     square_like = jax.ShapeDtypeStruct((held.shape[0], 1), jnp.float32)
     inward = [(0, 1), (3, 2)]
-    outward = [(1, 0), (2, 3)]
     inner = [(1, 2), (2, 1), (0, 0), (3, 3)]
     is_middle = middle.astype(jnp.int32).reshape(1)
 
     def onward(raw, got):
         return small(onward_kernel, raw.shape, is_middle, [raw, got])
 
-    *raw0, down, own_square = project(
-        first_kernel, me_feat, 0, 2, acts2, grads2, [adapter, rank_sketch, out_sketch, held], [down_like, square_like]
+    raw0_a, down, own_square = project(
+        first_kernel, me_feat, 0, 1, acts2, grads2, [adapter, rank_sketch, out_sketch, held_far], [down_like, square_like]
     )
+    got1 = [swap(raw0_a, "feat", 1)]
     squares = [own_square] + [swap(own_square, "feat", mask) for mask in (1, 2, 3)]
-    got1 = [swap(x, "feat", 1) for x in raw0]
-    raw1 = project(more_kernel, me_feat, 2, 2, acts2, grads2, [down, out_sketch], [])
-
-    squares[1:] = [after(x, raw1[0]) for x in squares[1:]]
+    raw0_b, *raw1 = project(more_kernel, me_feat, 1, 3, acts2, grads2, [down, out_sketch], [])
+    got1.append(swap(raw0_b, "feat", 1))
+    got2 = [swap(raw1[0], "feat", 1)]
+    sent1 = [onward(after(raw0_a, raw1[1]), got1[0])]
+    far = [lax.ppermute(sent1[0], "feat", inner)]
+
+    squares[1:] = [after(x, sent1[0]) for x in squares[1:]]
     other, *parts = lang_parts(me_ex, held, squares, perm % LANGS, n_ex)
     other = swap(other, "ex", 1)
     parts = [x + other[i] for i, x in enumerate(parts)]
     scattered = [swap(parts[i], "ex", 2 * i) for i in range(1, n_ex // 2)]
-    sent1 = [onward(after(raw0[0], parts[0]), got1[0])]
-    far = [lax.ppermute(sent1[0], "feat", inner)]
-    lang = after(parts[0], sent1[0]) + sum(scattered)
+    sent1.append(onward(after(raw0_b, parts[0]), got1[1]))
+    far.append(lax.ppermute(sent1[1], "feat", inner))
+    lang = after(parts[0], sent1[1]) + sum(scattered)
     other = swap(lang, "feat", 1)
-    raw1 = [after(x, lang) for x in raw1]
-    got2 = [swap(raw1[0], "feat", 1)]
     raw2 = project(more_kernel, me_feat, 4, 2, acts2, grads2, [after(down, lang), out_sketch], [])
-    other = after(other, raw2[0])
-    pair = small(stack_kernel, (2, *lang.shape), is_middle, [lang, other])
-    far_pair = lax.ppermute(pair, "feat", inner)
-    sent1.append(onward(after(raw0[1], pair), got1[1]))
-    far.append(lax.ppermute(sent1[1], "feat", inner))
-    got2.append(lax.ppermute(after(raw1[1], pair), "feat", inward))
-    far_pair = after(far_pair, sent1[1])
-    outer_pair = lax.ppermute(far_pair, "feat", outward)
-    sent2 = [onward(after(raw1[0], far_pair), got2[0])]
+    got2.append(lax.ppermute(after(raw1[1], raw2[0]), "feat", inward))
+    pair = small(stack_kernel, (2, *lang.shape), is_middle, [lang, after(other, raw2[0])])
+    far_pair = [lax.ppermute(pair, "feat", pairs) for pairs in (inner, [(1, 3), (2, 0)])]
+    sent2 = [onward(after(raw1[0], pair), got2[0])]
     near = [lax.ppermute(sent2[0], "feat", inner)]
     sent3 = [onward(after(raw2[0], sent2[0]), far[0])]
     got3 = [swap(sent3[0], "feat", 1)]
     pair = after(pair, sent3[0])
-    langs = [small(join_kernel, (4, *lang.shape), is_middle, [pair, far_pair, outer_pair])]
+    langs = [small(join_kernel, (4, *lang.shape), is_middle, [pair, *far_pair])]
     langs = langs + [swap(langs[0], "ex", mask) for mask in range(2, n_ex, 2)]
     sent3.append(onward(after(raw2[1], langs[0]), far[1]))
     got3.append(swap(sent3[1], "feat", 1))
@@ -355,11 +359,9 @@
     grad_a, square_a = product(is_middle, [own_a, got3[0], near[0]])
     langs[1:] = [after(x, square_a) for x in langs[1:]]
     langs = langs + [swap(x, "ex", 1) for x in langs]
-    grad_b, square_b = product(is_middle, [after(own_b, square_a), got3[1], near[1]])
-    products = [(grad_a, square_a), (grad_b, square_b)]
     per_lang = perm.shape[0] * n_ex // LANGS
     scale = (KF * per_lang) ** 0.5 / per_lang
-    mine = score(me_feat, me_ex, langs, products, scale)
+    mine = score(is_middle, me_feat, me_ex, langs, [grad_a, square_a], [own_b, got3[1], near[1]], scale)
     return place(me_feat, [mine] + [swap(mine, "feat", mask) for mask in (1, 2, 3)])
 
 

time: 92.3 us -> 94.9 us (1.028)
  starting transfers between devices: 38.9 us -> 54.7 us
  waiting for transfers between devices: 35.2 us -> 22 us
    ppermute x23, starting transfers between devices: 27.2 us -> 45.6 us  [swap(): lax.ppermute(x, axis, [(i, i ^ mask) for i in range(lax.axis_size(axis))])]
    ppermute x3, waiting for transfers between devices: 10.8 us -> 0.95 us  [the longest x2 0.95 us: ordered(): lax.ppermute(pair, 'feat', pairs)]
    ppermute x23, waiting for transfers between devices: 24.3 us -> 21.1 us  [swap(): lax.ppermute(x, axis, [(i, i ^ mask) for i in range(lax.axis_size(axis))])]
    ppermute x3, starting transfers between devices: 8.96 us -> 6.43 us  [the longest x1 4.47 us: ordered(): got2.append(lax.ppermute(after(raw1[1], raw2[0]), 'feat', inward))]
  transfers between devices with their start and end apart: 30 -> 30, of which waited for: 13 -> 8; matrix products, arithmetic and copies ran while one was open for 0% -> 0% of each run, Pallas kernels for 12% -> 13%
where the time goes in v8:
time: 94.9 us; the launch traced here: 94.5 us
  starting transfers between devices  54.7 us (58%)
  waiting for transfers between devices  22 us (23%)
  Pallas kernels  17.4 us (18%)
    ppermute x23, starting transfers between devices, swap(): lax.ppermute(x, axis, [(i, i ^ mask) for i in range(lax.axis_size(axis))])  45.6 us
    ppermute x23, waiting for transfers between devices, swap(): lax.ppermute(x, axis, [(i, i ^ mask) for i in range(lax.axis_size(axis))])  21.1 us
    pallas_call x4, Pallas kernels, project(): pl.pallas_call(kernel, out_shape=[jax.ShapeDtypeStruct(piece, jnp.float32...  13.6 us
    ppermute x1, starting transfers between devices, ordered(): got2.append(lax.ppermute(after(raw1[1], raw2[0]), 'feat', inward))  4.47 us
    ppermute x2, starting transfers between devices, ordered(): lax.ppermute(pair, 'feat', pairs)  1.96 us
  transfers between devices with their start and end apart: 30, of which 8 were waited for; matrix products, arithmetic and copies ran while one was open for 0% of the time, Pallas kernels for 13%

profile of v8, /device:TPU:0, one launch (start us, length us, event | category | flops | bytes accessed | tf_op | source)
XLA Modules:
  0.0 94.5 jit_solution(15148845776221220514)
XLA Ops:
  0.0 2.7 %project.4 = (f32[2,384,128]{2,1,0:T(8,128)S(1)}, bf16[1024,128]{1,0:T(8,128)(2,1)S(1)}, f32[32,1]{1,0:T(8,128)S(1)}) custom-call(s32[1]{0:T(128)} %bitcast.feat.feat_ref.me_ref, bf16[4096,1024]{1,0:T(8,128)(2,1)} %bitcast.24, bf16[4096,1024]{1,0:T(8,128)(2,1)} %bitcast.28, bf16[1024,128]{1,0:T(8,128)(2,1)} %adapter_ref.1, bf16[64,128]{1,0:T(8,128)(2,1)} %bitcast.32, ...), custom_call_target="tpu_custom_call" | custom-call | flops 268435456 | bytes 2490368 | tf_op jit(solution)/shard_map/project/pallas_call | solution.py:81
  2.7 3.1 %collective-permute-start.1 = (f32[2,384,128]{2,1,0:T(8,128)S(1)}, f32[2,384,128]{2,1,0:T(8,128)S(1)}, u32[]{:S(2)}, u32[]{:S(2)}) collective-permute-start(f32[2,384,128]{2,1,0:T(8,128)S(1)} %get-tuple-element.44.raw_ref), channel_id=1, source_target_pairs={{0,1},{1,0},{2,3},{3,2},{4,5},{5,4},{6,7},{7,6},{8,9},{9,8},{10,11... | collective-permute-start | bytes 1179656 | tf_op jit(solution)/shard_map/ppermute | solution.py:291
  5.8 2.5 %collective-permute-start.3 = (f32[32,1]{1,0:T(8,128)S(1)}, f32[32,1]{1,0:T(8,128)S(1)}, u32[]{:S(2)}, u32[]{:S(2)}) collective-permute-start(f32[32,1]{1,0:T(8,128)S(1)} %get-tuple-element.40.refs_0_), channel_id=1, source_target_pairs={{0,3},{1,2},{2,1},{3,0},{4,7},{5,6},{6,5},{7,4},{8,11},{9,10},{10,... | collective-permute-start | bytes 392 | tf_op jit(solution)/shard_map/ppermute | solution.py:291
  8.4 1.8 %collective-permute-start = (f32[32,1]{1,0:T(8,128)S(1)}, f32[32,1]{1,0:T(8,128)S(1)}, u32[]{:S(2)}, u32[]{:S(2)}) collective-permute-start(f32[32,1]{1,0:T(8,128)S(1)} %get-tuple-element.40.refs_0_), channel_id=1, source_target_pairs={{0,1},{1,0},{2,3},{3,2},{4,5},{5,4},{6,7},{7,6},{8,9},{9,8},{10,11... | collective-permute-start | bytes 392 | tf_op jit(solution)/shard_map/ppermute | solution.py:291
  10.2 4.7 %project.5 = (f32[2,384,128]{2,1,0:T(8,128)S(1)}, f32[2,384,128]{2,1,0:T(8,128)S(1)}, f32[2,384,128]{2,1,0:T(8,128)S(1)}) custom-call(s32[1]{0:T(128)} %bitcast.feat.feat_ref.me_ref, bf16[4096,1024]{1,0:T(8,128)(2,1)} %bitcast.25, bf16[4096,1024]{1,0:T(8,128)(2,1)} %bitcast.29, bf16[1024,128]{1,0:T(8,128)(2,1)S(1)} %get-tuple-element.67.down_ref, ...), custom_call_target="tpu_custom_call" | custom-call | flops 805306368 | bytes 7471104 | tf_op jit(solution)/shard_map/project/pallas_call | solution.py:81
  15.5 2.3 %collective-permute-done.3.refs_3_ = f32[32,1]{1,0:T(8,128)S(1)} collective-permute-done((f32[32,1]{1,0:T(8,128)S(1)}, f32[32,1]{1,0:T(8,128)S(1)}, u32[]{:S(2)}, u32[]{:S(2)}) %collective-permute-start.3) | collective-permute-done | bytes 160 | tf_op jit(solution)/shard_map/ppermute | solution.py:291
  19.0 1.3 %collective-permute-start.10 = (f32[2,384,128]{2,1,0:T(8,128)S(1)}, f32[2,384,128]{2,1,0:T(8,128)S(1)}, u32[]{:S(2)}, u32[]{:S(2)}) collective-permute-start(f32[2,384,128]{2,1,0:T(8,128)S(1)} %get-tuple-element.60.raw_ref), channel_id=1, source_target_pairs={{0,1},{1,0},{2,3},{3,2},{4,5},{5,4},{6,7},{7,6},{8,9},{9,8},{10,11... | collective-permute-start | bytes 1179656 | tf_op jit(solution)/shard_map/ppermute | solution.py:291
  20.3 1.6 %collective-permute-start.6 = (f32[64,256]{1,0:T(8,128)S(1)}, f32[64,256]{1,0:T(8,128)S(1)}, u32[]{:S(2)}, u32[]{:S(2)}) collective-permute-start(f32[64,256]{1,0:T(8,128)S(1)} %get-tuple-element.77), channel_id=1, source_target_pairs={{0,8},{4,12},{8,0},{12,4},{16,24},{20,28},{24,16},{28,20},{1,9},{5... | collective-permute-start | bytes 196616 | tf_op jit(solution)/shard_map/ppermute | solution.py:291
  21.9 1.5 %collective-permute-start.7 = (f32[64,256]{1,0:T(8,128)S(1)}, f32[64,256]{1,0:T(8,128)S(1)}, u32[]{:S(2)}, u32[]{:S(2)}) collective-permute-start(f32[64,256]{1,0:T(8,128)S(1)} %get-tuple-element.75), channel_id=1, source_target_pairs={{0,16},{4,20},{8,24},{12,28},{16,0},{20,4},{24,8},{28,12},{1,17},{... | collective-permute-start | bytes 196616 | tf_op jit(solution)/shard_map/ppermute | solution.py:291
  23.9 6.4 %collective-permute-done.5.got_ref = f32[2,384,128]{2,1,0:T(8,128)S(1)} collective-permute-done((f32[2,384,128]{2,1,0:T(8,128)S(1)}, f32[2,384,128]{2,1,0:T(8,128)S(1)}, u32[]{:S(2)}, u32[]{:S(2)}) %collective-permute-start.5) | collective-permute-done | bytes 393248 | tf_op jit(solution)/shard_map/ppermute | solution.py:291
  31.1 2.8 %collective-permute-start.9 = (f32[64,256]{1,0:T(8,128)S(1)}, f32[64,256]{1,0:T(8,128)S(1)}, u32[]{:S(2)}, u32[]{:S(2)}) collective-permute-start(f32[64,256]{1,0:T(8,128)S(1)} %add_add_fusion.one_ref), channel_id=1, source_target_pairs={{0,1},{1,0},{2,3},{3,2},{4,5},{5,4},{6,7},{7,6},{8,9},{9,8},{10,11... | collective-permute-start | bytes 196616 | tf_op jit(solution)/shard_map/ppermute | solution.py:291
  34.5 3.1 %project.6 = (f32[2,384,128]{2,1,0:T(8,128)S(1)}, f32[2,384,128]{2,1,0:T(8,128)S(1)}) custom-call(s32[1]{0:T(128)} %bitcast.feat.feat_ref.me_ref, bf16[4096,1024]{1,0:T(8,128)(2,1)} %bitcast.26, bf16[4096,1024]{1,0:T(8,128)(2,1)} %bitcast.30, bf16[1024,128]{1,0:T(8,128)(2,1)S(1)} %get-tuple-element.67.down_ref, bf16[1024,128]{1,0:T(8,128)(2,1)} %sketch_ref.7), custom_call_target="tpu_custom_call" | custom-call | flops 536870912 | bytes 4980736 | tf_op jit(solution)/shard_map/project/pallas_call | solution.py:81
  37.6 4.5 %collective-permute-start.16 = (f32[2,384,128]{2,1,0:T(8,128)S(1)}, f32[2,384,128]{2,1,0:T(8,128)S(1)}, u32[]{:S(2)}, u32[]{:S(2)}) collective-permute-start(f32[2,384,128]{2,1,0:T(8,128)S(1)} %get-tuple-element.66.raw_ref), channel_id=1, source_target_pairs={{0,1},{3,2},{4,5},{7,6},{8,9},{11,10},{12,13},{15,14},{16,17},{19,... | collective-permute-start | bytes 1179656 | tf_op jit(solution)/shard_map/ppermute | solution.py:344
  43.6 1.3 %collective-permute-start.13 = (f32[2,64,256]{2,1,0:T(8,128)S(1)}, f32[2,64,256]{2,1,0:T(8,128)S(1)}, u32[]{:S(2)}, u32[]{:S(2)}) collective-permute-start(f32[2,64,256]{2,1,0:T(8,128)S(1)} %shard_map.75.pair_ref), channel_id=1, source_target_pairs={{1,3},{2,0},{5,7},{6,4},{9,11},{10,8},{13,15},{14,12},{17,19},{18,... | collective-permute-start | bytes 393224 | tf_op jit(solution)/shard_map/ppermute | solution.py:346
  45.0 19.0 %collective-permute-start.17 = (f32[2,384,128]{2,1,0:T(8,128)S(1)}, f32[2,384,128]{2,1,0:T(8,128)S(1)}, u32[]{:S(2)}, u32[]{:S(2)}) collective-permute-start(f32[2,384,128]{2,1,0:T(8,128)S(1)} %shard_map.77), channel_id=1, source_target_pairs={{0,1},{1,0},{2,3},{3,2},{4,5},{5,4},{6,7},{7,6},{8,9},{9,8},{10,11... | collective-permute-start | bytes 1179656 | tf_op jit(solution)/shard_map/ppermute | solution.py:291
  65.0 2.5 %collective-permute-start.20 = (f32[4,64,256]{2,1,0:T(8,128)S(1)}, f32[4,64,256]{2,1,0:T(8,128)S(1)}, u32[]{:S(2)}, u32[]{:S(2)}) collective-permute-start(f32[4,64,256]{2,1,0:T(8,128)S(1)} %shard_map.78.refs_0_), channel_id=1, source_target_pairs={{0,24},{4,28},{8,16},{12,20},{16,8},{20,12},{24,0},{28,4},{1,25},{... | collective-permute-start | bytes 786440 | tf_op jit(solution)/shard_map/ppermute | solution.py:291
  68.6 6.1 %collective-permute-done.20.refs_3_ = f32[4,64,256]{2,1,0:T(8,128)S(1)} collective-permute-done((f32[4,64,256]{2,1,0:T(8,128)S(1)}, f32[4,64,256]{2,1,0:T(8,128)S(1)}, u32[]{:S(2)}, u32[]{:S(2)}) %collective-permute-start.20) | collective-permute-done | bytes 262176 | tf_op jit(solution)/shard_map/ppermute | solution.py:291
  75.5 3.1 %project.7 = (f32[2,384,128]{2,1,0:T(8,128)S(1)}, f32[2,384,128]{2,1,0:T(8,128)S(1)}) custom-call(s32[1]{0:T(128)} %bitcast.feat.feat_ref.me_ref, bf16[4096,1024]{1,0:T(8,128)(2,1)} %bitcast.27, bf16[4096,1024]{1,0:T(8,128)(2,1)} %bitcast.31, bf16[1024,128]{1,0:T(8,128)(2,1)S(1)} %get-tuple-element.67.down_ref, bf16[1024,128]{1,0:T(8,128)(2,1)} %sketch_ref.7), custom_call_target="tpu_custom_call" | custom-call | flops 536870912 | bytes 4980736 | tf_op jit(solution)/shard_map/project/pallas_call | solution.py:81
  80.1 2.4 %collective-permute-done.25.refs_11_ = f32[2,384,128]{2,1,0:T(8,128)S(1)} collective-permute-done((f32[2,384,128]{2,1,0:T(8,128)S(1)}, f32[2,384,128]{2,1,0:T(8,128)S(1)}, u32[]{:S(2)}, u32[]{:S(2)}) %collective-permute-start.25) | collective-permute-done | bytes 393248 | tf_op jit(solution)/shard_map/ppermute | solution.py:291
  82.5 1.7 %score.1.refs_0_ = f32[16,64]{1,0:T(8,128)S(1)} custom-call(s32[1]{0:T(128)} %bitcast.1.middle_ref, s32[1]{0:T(128)} %bitcast.feat.feat_ref.me_ref, s32[1]{0:T(128)} %bitcast.2.me_ref.ex_ref, f32[4,64,256]{2,1,0:T(8,128)S(1)} %shard_map.78.refs_0_, f32[4,64,256]{2,1,0:T(8,128)S(1)} %collective-permute-done.14.refs_1_, ...), custom_call_target="tpu_custom_call" | custom-call | tf_op jit(solution)/shard_map/score/pallas_call | solution.py:231
  84.2 4.0 %collective-permute-start.27 = (f32[16,64]{1,0:T(8,128)S(1)}, f32[16,64]{1,0:T(8,128)S(1)}, u32[]{:S(2)}, u32[]{:S(2)}) collective-permute-start(f32[16,64]{1,0:T(8,128)S(1)} %score.1.refs_0_), channel_id=1, source_target_pairs={{0,1},{1,0},{2,3},{3,2},{4,5},{5,4},{6,7},{7,6},{8,9},{9,8},{10,11... | collective-permute-start | bytes 12296 | tf_op jit(solution)/shard_map/ppermute | solution.py:291
  88.5 2.2 %collective-permute-start.29 = (f32[16,64]{1,0:T(8,128)S(1)}, f32[16,64]{1,0:T(8,128)S(1)}, u32[]{:S(2)}, u32[]{:S(2)}) collective-permute-start(f32[16,64]{1,0:T(8,128)S(1)} %score.1.refs_0_), channel_id=1, source_target_pairs={{0,3},{1,2},{2,1},{3,0},{4,7},{5,6},{6,5},{7,4},{8,11},{9,10},{10,... | collective-permute-start | bytes 12296 | tf_op jit(solution)/shard_map/ppermute | solution.py:291
  90.7 2.1 %collective-permute-done.28.refs_2_ = f32[16,64]{1,0:T(8,128)S(1)} collective-permute-done((f32[16,64]{1,0:T(8,128)S(1)}, f32[16,64]{1,0:T(8,128)S(1)}, u32[]{:S(2)}, u32[]{:S(2)}) %collective-permute-start.28) | collective-permute-done | bytes 4128 | tf_op jit(solution)/shard_map/ppermute | solution.py:291
  92.8 1.1 %collective-permute-done.29.refs_3_ = f32[16,64]{1,0:T(8,128)S(1)} collective-permute-done((f32[16,64]{1,0:T(8,128)S(1)}, f32[16,64]{1,0:T(8,128)S(1)}, u32[]{:S(2)}, u32[]{:S(2)}) %collective-permute-start.29) | collective-permute-done | bytes 4128 | tf_op jit(solution)/shard_map/ppermute | solution.py:291
  (59 shorter events, 10.5 us)
Async XLA Ops:
  2.7 12.8 %collective-permute-start.1 = (f32[2,384,128]{2,1,0:T(8,128)S(1)}, f32[2,384,128]{2,1,0:T(8,128)S(1)}, u32[]{:S(2)}, u32[]{:S(2)}) collective-permute-start(f32[2,384,128]{2,1,0:T(8,128)S(1)} %get-tuple-element.44.raw_ref), channel_id=1, source_target_pairs={{0,1},{1,0},{2,3},{3,2},{4,5},{5,4},{6,7},{7,6},{8,9},{9,8},{10,11... | collective-permute-start | bytes 1179656 | tf_op jit(solution)/shard_map/ppermute | solution.py:291
  5.8 12.0 %collective-permute-start.3 = (f32[32,1]{1,0:T(8,128)S(1)}, f32[32,1]{1,0:T(8,128)S(1)}, u32[]{:S(2)}, u32[]{:S(2)}) collective-permute-start(f32[32,1]{1,0:T(8,128)S(1)} %get-tuple-element.40.refs_0_), channel_id=1, source_target_pairs={{0,3},{1,2},{2,1},{3,0},{4,7},{5,6},{6,5},{7,4},{8,11},{9,10},{10,... | collective-permute-start | bytes 392 | tf_op jit(solution)/shard_map/ppermute | solution.py:291
  8.3 9.5 %collective-permute-start.2 = (f32[32,1]{1,0:T(8,128)S(1)}, f32[32,1]{1,0:T(8,128)S(1)}, u32[]{:S(2)}, u32[]{:S(2)}) collective-permute-start(f32[32,1]{1,0:T(8,128)S(1)} %get-tuple-element.40.refs_0_), channel_id=1, source_target_pairs={{0,2},{1,3},{2,0},{3,1},{4,6},{5,7},{6,4},{7,5},{8,10},{9,11},{10,... | collective-permute-start | bytes 392 | tf_op jit(solution)/shard_map/ppermute | solution.py:291
  8.4 9.4 %collective-permute-start = (f32[32,1]{1,0:T(8,128)S(1)}, f32[32,1]{1,0:T(8,128)S(1)}, u32[]{:S(2)}, u32[]{:S(2)}) collective-permute-start(f32[32,1]{1,0:T(8,128)S(1)} %get-tuple-element.40.refs_0_), channel_id=1, source_target_pairs={{0,1},{1,0},{2,3},{3,2},{4,5},{5,4},{6,7},{7,6},{8,9},{9,8},{10,11... | collective-permute-start | bytes 392 | tf_op jit(solution)/shard_map/ppermute | solution.py:291
  18.2 12.1 %collective-permute-start.5 = (f32[2,384,128]{2,1,0:T(8,128)S(1)}, f32[2,384,128]{2,1,0:T(8,128)S(1)}, u32[]{:S(2)}, u32[]{:S(2)}) collective-permute-start(f32[2,384,128]{2,1,0:T(8,128)S(1)} %get-tuple-element.51.raw_ref), channel_id=1, source_target_pairs={{0,1},{1,0},{2,3},{3,2},{4,5},{5,4},{6,7},{7,6},{8,9},{9,8},{10,11... | collective-permute-start | bytes 1179656 | tf_op jit(solution)/shard_map/ppermute | solution.py:291
  19.0 23.1 %collective-permute-start.10 = (f32[2,384,128]{2,1,0:T(8,128)S(1)}, f32[2,384,128]{2,1,0:T(8,128)S(1)}, u32[]{:S(2)}, u32[]{:S(2)}) collective-permute-start(f32[2,384,128]{2,1,0:T(8,128)S(1)} %get-tuple-element.60.raw_ref), channel_id=1, source_target_pairs={{0,1},{1,0},{2,3},{3,2},{4,5},{5,4},{6,7},{7,6},{8,9},{9,8},{10,11... | collective-permute-start | bytes 1179656 | tf_op jit(solution)/shard_map/ppermute | solution.py:291
  20.3 10.7 %collective-permute-start.6 = (f32[64,256]{1,0:T(8,128)S(1)}, f32[64,256]{1,0:T(8,128)S(1)}, u32[]{:S(2)}, u32[]{:S(2)}) collective-permute-start(f32[64,256]{1,0:T(8,128)S(1)} %get-tuple-element.77), channel_id=1, source_target_pairs={{0,8},{4,12},{8,0},{12,4},{16,24},{20,28},{24,16},{28,20},{1,9},{5... | collective-permute-start | bytes 196616 | tf_op jit(solution)/shard_map/ppermute | solution.py:291
  21.9 9.1 %collective-permute-start.7 = (f32[64,256]{1,0:T(8,128)S(1)}, f32[64,256]{1,0:T(8,128)S(1)}, u32[]{:S(2)}, u32[]{:S(2)}) collective-permute-start(f32[64,256]{1,0:T(8,128)S(1)} %get-tuple-element.75), channel_id=1, source_target_pairs={{0,16},{4,20},{8,24},{12,28},{16,0},{20,4},{24,8},{28,12},{1,17},{... | collective-permute-start | bytes 196616 | tf_op jit(solution)/shard_map/ppermute | solution.py:291
  23.4 7.6 %collective-permute-start.8 = (f32[64,256]{1,0:T(8,128)S(1)}, f32[64,256]{1,0:T(8,128)S(1)}, u32[]{:S(2)}, u32[]{:S(2)}) collective-permute-start(f32[64,256]{1,0:T(8,128)S(1)} %get-tuple-element.76), channel_id=1, source_target_pairs={{0,24},{4,28},{8,16},{12,20},{16,8},{20,12},{24,0},{28,4},{1,25},{... | collective-permute-start | bytes 196616 | tf_op jit(solution)/shard_map/ppermute | solution.py:291
  30.3 13.3 %collective-permute-start.11 = (f32[2,384,128]{2,1,0:T(8,128)S(1)}, f32[2,384,128]{2,1,0:T(8,128)S(1)}, u32[]{:S(2)}, u32[]{:S(2)}) collective-permute-start(f32[2,384,128]{2,1,0:T(8,128)S(1)} %shard_map.73), channel_id=1, source_target_pairs={{1,2},{2,1},{0,0},{3,3},{5,6},{6,5},{4,4},{7,7},{9,10},{10,9},{8,8... | collective-permute-start | bytes 1179656 | tf_op jit(solution)/shard_map/ppermute | solution.py:332
  31.1 11.1 %collective-permute-start.9 = (f32[64,256]{1,0:T(8,128)S(1)}, f32[64,256]{1,0:T(8,128)S(1)}, u32[]{:S(2)}, u32[]{:S(2)}) collective-permute-start(f32[64,256]{1,0:T(8,128)S(1)} %add_add_fusion.one_ref), channel_id=1, source_target_pairs={{0,1},{1,0},{2,3},{3,2},{4,5},{5,4},{6,7},{7,6},{8,9},{9,8},{10,11... | collective-permute-start | bytes 196616 | tf_op jit(solution)/shard_map/ppermute | solution.py:291
  33.8 33.7 %collective-permute-start.15 = (f32[2,384,128]{2,1,0:T(8,128)S(1)}, f32[2,384,128]{2,1,0:T(8,128)S(1)}, u32[]{:S(2)}, u32[]{:S(2)}) collective-permute-start(f32[2,384,128]{2,1,0:T(8,128)S(1)} %shard_map.74), channel_id=1, source_target_pairs={{1,2},{2,1},{0,0},{3,3},{5,6},{6,5},{4,4},{7,7},{9,10},{10,9},{8,8... | collective-permute-start | bytes 1179656 | tf_op jit(solution)/shard_map/ppermute | solution.py:340
  37.6 30.3 %collective-permute-start.16 = (f32[2,384,128]{2,1,0:T(8,128)S(1)}, f32[2,384,128]{2,1,0:T(8,128)S(1)}, u32[]{:S(2)}, u32[]{:S(2)}) collective-permute-start(f32[2,384,128]{2,1,0:T(8,128)S(1)} %get-tuple-element.66.raw_ref), channel_id=1, source_target_pairs={{0,1},{3,2},{4,5},{7,6},{8,9},{11,10},{12,13},{15,14},{16,17},{19,... | collective-permute-start | bytes 1179656 | tf_op jit(solution)/shard_map/ppermute | solution.py:344
  42.2 26.3 %collective-permute-start.18 = (f32[2,384,128]{2,1,0:T(8,128)S(1)}, f32[2,384,128]{2,1,0:T(8,128)S(1)}, u32[]{:S(2)}, u32[]{:S(2)}) collective-permute-start(f32[2,384,128]{2,1,0:T(8,128)S(1)} %shard_map.76), channel_id=1, source_target_pairs={{1,2},{2,1},{0,0},{3,3},{5,6},{6,5},{4,4},{7,7},{9,10},{10,9},{8,8... | collective-permute-start | bytes 1179656 | tf_op jit(solution)/shard_map/ppermute | solution.py:348
  43.6 21.3 %collective-permute-start.13 = (f32[2,64,256]{2,1,0:T(8,128)S(1)}, f32[2,64,256]{2,1,0:T(8,128)S(1)}, u32[]{:S(2)}, u32[]{:S(2)}) collective-permute-start(f32[2,64,256]{2,1,0:T(8,128)S(1)} %shard_map.75.pair_ref), channel_id=1, source_target_pairs={{1,3},{2,0},{5,7},{6,4},{9,11},{10,8},{13,15},{14,12},{17,19},{18,... | collective-permute-start | bytes 393224 | tf_op jit(solution)/shard_map/ppermute | solution.py:346
  45.0 29.8 %collective-permute-start.17 = (f32[2,384,128]{2,1,0:T(8,128)S(1)}, f32[2,384,128]{2,1,0:T(8,128)S(1)}, u32[]{:S(2)}, u32[]{:S(2)}) collective-permute-start(f32[2,384,128]{2,1,0:T(8,128)S(1)} %shard_map.77), channel_id=1, source_target_pairs={{0,1},{1,0},{2,3},{3,2},{4,5},{5,4},{6,7},{7,6},{8,9},{9,8},{10,11... | collective-permute-start | bytes 1179656 | tf_op jit(solution)/shard_map/ppermute | solution.py:291
  65.0 9.8 %collective-permute-start.20 = (f32[4,64,256]{2,1,0:T(8,128)S(1)}, f32[4,64,256]{2,1,0:T(8,128)S(1)}, u32[]{:S(2)}, u32[]{:S(2)}) collective-permute-start(f32[4,64,256]{2,1,0:T(8,128)S(1)} %shard_map.78.refs_0_), channel_id=1, source_target_pairs={{0,24},{4,28},{8,16},{12,20},{16,8},{20,12},{24,0},{28,4},{1,25},{... | collective-permute-start | bytes 786440 | tf_op jit(solution)/shard_map/ppermute | solution.py:291
  67.5 12.0 %collective-permute-start.19 = (f32[4,64,256]{2,1,0:T(8,128)S(1)}, f32[4,64,256]{2,1,0:T(8,128)S(1)}, u32[]{:S(2)}, u32[]{:S(2)}) collective-permute-start(f32[4,64,256]{2,1,0:T(8,128)S(1)} %shard_map.78.refs_0_), channel_id=1, source_target_pairs={{0,16},{4,20},{8,24},{12,28},{16,0},{20,4},{24,8},{28,12},{1,17},{... | collective-permute-start | bytes 786440 | tf_op jit(solution)/shard_map/ppermute | solution.py:291
  68.0 11.5 %collective-permute-start.14 = (f32[4,64,256]{2,1,0:T(8,128)S(1)}, f32[4,64,256]{2,1,0:T(8,128)S(1)}, u32[]{:S(2)}, u32[]{:S(2)}) collective-permute-start(f32[4,64,256]{2,1,0:T(8,128)S(1)} %shard_map.78.refs_0_), channel_id=1, source_target_pairs={{0,8},{4,12},{8,0},{12,4},{16,24},{20,28},{24,16},{28,20},{1,9},{5... | collective-permute-start | bytes 786440 | tf_op jit(solution)/shard_map/ppermute | solution.py:291
  68.5 11.5 %collective-permute-start.21 = (f32[4,64,256]{2,1,0:T(8,128)S(1)}, f32[4,64,256]{2,1,0:T(8,128)S(1)}, u32[]{:S(2)}, u32[]{:S(2)}) collective-permute-start(f32[4,64,256]{2,1,0:T(8,128)S(1)} %shard_map.78.refs_0_), channel_id=1, source_target_pairs={{0,4},{4,0},{8,12},{12,8},{16,20},{20,16},{24,28},{28,24},{1,5},{5... | collective-permute-start | bytes 786440 | tf_op jit(solution)/shard_map/ppermute | solution.py:291
  74.7 7.8 %collective-permute-start.25 = (f32[2,384,128]{2,1,0:T(8,128)S(1)}, f32[2,384,128]{2,1,0:T(8,128)S(1)}, u32[]{:S(2)}, u32[]{:S(2)}) collective-permute-start(f32[2,384,128]{2,1,0:T(8,128)S(1)} %shard_map.79), channel_id=1, source_target_pairs={{0,1},{1,0},{2,3},{3,2},{4,5},{5,4},{6,7},{7,6},{8,9},{9,8},{10,11... | collective-permute-start | bytes 1179656 | tf_op jit(solution)/shard_map/ppermute | solution.py:291
  74.8 7.7 %collective-permute-start.26 = (f32[2,384,128]{2,1,0:T(8,128)S(1)}, f32[2,384,128]{2,1,0:T(8,128)S(1)}, u32[]{:S(2)}, u32[]{:S(2)}) collective-permute-start(f32[2,384,128]{2,1,0:T(8,128)S(1)} %shard_map.80), channel_id=1, source_target_pairs={{1,2},{2,1},{0,0},{3,3},{5,6},{6,5},{4,4},{7,7},{9,10},{10,9},{8,8... | collective-permute-start | bytes 1179656 | tf_op jit(solution)/shard_map/ppermute | solution.py:357
  84.2 6.5 %collective-permute-start.27 = (f32[16,64]{1,0:T(8,128)S(1)}, f32[16,64]{1,0:T(8,128)S(1)}, u32[]{:S(2)}, u32[]{:S(2)}) collective-permute-start(f32[16,64]{1,0:T(8,128)S(1)} %score.1.refs_0_), channel_id=1, source_target_pairs={{0,1},{1,0},{2,3},{3,2},{4,5},{5,4},{6,7},{7,6},{8,9},{9,8},{10,11... | collective-permute-start | bytes 12296 | tf_op jit(solution)/shard_map/ppermute | solution.py:291
  88.5 5.4 %collective-permute-start.29 = (f32[16,64]{1,0:T(8,128)S(1)}, f32[16,64]{1,0:T(8,128)S(1)}, u32[]{:S(2)}, u32[]{:S(2)}) collective-permute-start(f32[16,64]{1,0:T(8,128)S(1)} %score.1.refs_0_), channel_id=1, source_target_pairs={{0,3},{1,2},{2,1},{3,0},{4,7},{5,6},{6,5},{7,4},{8,11},{9,10},{10,... | collective-permute-start | bytes 12296 | tf_op jit(solution)/shard_map/ppermute | solution.py:291
  (8 other events, 29.7 us)

commit v9 on v8

--- a/solution.py
+++ b/solution.py
@@ -195,43 +195,59 @@
     )(middle, *parts)
 
 
-def score_kernel(middle_ref, feat_ref, ex_ref, *refs, scale, n_lang):
-    lang_refs, (grad_a, square_a, *part_refs, o_ref, grad_b, square_b, grad_ref) = refs[:n_lang], refs[n_lang:]
-    product_kernel(middle_ref, *part_refs, grad_b, square_b, grad_ref)
-    grad_refs, square_refs = [grad_a, grad_b], [square_a, square_b]
-    total = None
+def split_kernel(feat_ref, ex_ref, *refs):
+    *lang_refs, o_ref = refs
     feat, ex = feat_ref[0], ex_ref[0]
     middle = (feat == 1) | (feat == 2)
     second = feat ^ jnp.where(middle, 3, 2)
     rows_from = [feat, feat ^ 1, second, second ^ 1]
-    masks = [*range(0, n_lang, 2), *range(1, n_lang, 2)]
+    n_ex = len(lang_refs)
+    masks = [*range(0, n_ex, 2), *range(1, n_ex, 2)]
     for j, ref in enumerate(lang_refs):
         for m in range(4):
-            index = rows_from[m] * n_lang + (ex ^ masks[j])
             lang = ref[m]
             rest = lang - lang.astype(jnp.bfloat16).astype(jnp.float32)
-            lang = jnp.concatenate([lang, rest], axis=0).astype(jnp.bfloat16)
-            grad = jnp.concatenate([g[index] for g in grad_refs], axis=0)
-            term = lax.dot_general(
-                grad, lang, (((1,), (1,)), ((), ())), preferred_element_type=jnp.float32
-            )
-            total = term if total is None else total + term
+            o_ref[rows_from[m] * n_ex + (ex ^ masks[j])] = jnp.concatenate([lang, rest], axis=0).astype(jnp.bfloat16)
+
+
+def split(feat, ex, langs):
+    rows, count, piece = langs[0].shape
+    return pl.pallas_call(
+        split_kernel,
+        out_shape=jax.ShapeDtypeStruct((rows * len(langs), 2 * count, piece), jnp.bfloat16),
+        in_specs=[SMEM] * 2 + [VMEM] * len(langs),
+        out_specs=VMEM,
+        compiler_params=pltpu.CompilerParams(vmem_limit_bytes=SMALL),
+        name="split",
+    )(feat, ex, *langs)
+
+
+def score_kernel(middle_ref, lang_ref, grad_a, square_a, *refs, scale):
+    *part_refs, o_ref, grad_b, square_b, grad_ref = refs
+    product_kernel(middle_ref, *part_refs, grad_b, square_b, grad_ref)
+    total = None
+    for index in range(lang_ref.shape[0]):
+        grad = jnp.concatenate([grad_a[index], grad_b[index]], axis=0)
+        term = lax.dot_general(
+            grad, lang_ref[index], (((1,), (1,)), ((), ())), preferred_element_type=jnp.float32
+        )
+        total = term if total is None else total + term
     total = total + pltpu.roll(total, LANGS, 1)
-    count = square_refs[0].shape[0]
-    for index, square_ref in enumerate(square_refs):
+    count = square_a.shape[0]
+    for index, square_ref in enumerate([square_a, square_b]):
         start = 2 * count * index
         inner = total[start : start + count, :LANGS] + total[start + count : start + 2 * count, :LANGS]
         o_ref[index * count : (index + 1) * count] = inner * (lax.rsqrt(square_ref[...] + 1e-06) * scale)
 
 
-def score(middle, feat, ex, langs, first, parts, scale):
+def score(middle, langs, first, parts, scale):
     grad, square = first
-    operands = [*langs, *first, *parts]
+    operands = [langs, *first, *parts]
     wide = parts[0].shape[2]
     return pl.pallas_call(
-        functools.partial(score_kernel, scale=scale, n_lang=len(langs)),
+        functools.partial(score_kernel, scale=scale),
         out_shape=jax.ShapeDtypeStruct((2 * square.shape[0], LANGS), jnp.float32),
-        in_specs=[SMEM] * 3 + [VMEM] * len(operands),
+        in_specs=[SMEM] + [VMEM] * len(operands),
         out_specs=VMEM,
         scratch_shapes=[
             pltpu.VMEM(grad.shape, grad.dtype),
@@ -240,7 +256,7 @@
         ],
         compiler_params=pltpu.CompilerParams(vmem_limit_bytes=SMALL),
         name="score",
-    )(middle, feat, ex, *operands)
+    )(middle, *operands)
 
 
 def small(kernel, shape, middle, operands):
@@ -340,8 +356,8 @@
     far.append(lax.ppermute(sent1[1], "feat", inner))
     lang = after(parts[0], sent1[1]) + sum(scattered)
     other = swap(lang, "feat", 1)
+    got2.append(lax.ppermute(after(raw1[1], lang), "feat", inward))
     raw2 = project(more_kernel, me_feat, 4, 2, acts2, grads2, [after(down, lang), out_sketch], [])
-    got2.append(lax.ppermute(after(raw1[1], raw2[0]), "feat", inward))
     pair = small(stack_kernel, (2, *lang.shape), is_middle, [lang, after(other, raw2[0])])
     far_pair = [lax.ppermute(pair, "feat", pairs) for pairs in (inner, [(1, 3), (2, 0)])]
     sent2 = [onward(after(raw1[0], pair), got2[0])]
@@ -361,8 +377,13 @@
     langs = langs + [swap(x, "ex", 1) for x in langs]
     per_lang = perm.shape[0] * n_ex // LANGS
     scale = (KF * per_lang) ** 0.5 / per_lang
-    mine = score(is_middle, me_feat, me_ex, langs, [grad_a, square_a], [own_b, got3[1], near[1]], scale)
-    return place(me_feat, [mine] + [swap(mine, "feat", mask) for mask in (1, 2, 3)])
+    halves = split(me_feat, me_ex, langs)
+    late = [after(got3[1], halves), after(near[1], halves)]
+    mine = score(is_middle, halves, [grad_a, square_a], [own_b, *late], scale)
+    gathered = [mine]
+    for mask in (1, 2, 3):
+        gathered.append(swap(mine, "feat", mask))
+    return place(me_feat, gathered)
 
 
 def general(acts, grads, adapter, rank_sketch, out_sketch, held, perm):

time: 94.9 us -> 89.7 us (0.945)
  starting transfers between devices: 54.7 us -> 46.2 us
  waiting for transfers between devices: 22 us -> 25.3 us
    ppermute x2, waiting for transfers between devices: 0.95 us -> 10.7 us  [ordered(): lax.ppermute(pair, 'feat', pairs)]
    ppermute x23, starting transfers between devices: 45.6 us -> 37 us  [swap(): lax.ppermute(x, axis, [(i, i ^ mask) for i in range(lax.axis_size(axis))])]
    ppermute x23, waiting for transfers between devices: 21.1 us -> 14.6 us  [swap(): lax.ppermute(x, axis, [(i, i ^ mask) for i in range(lax.axis_size(axis))])]
  transfers between devices with their start and end apart: 30 -> 30, of which waited for: 8 -> 9; matrix products, arithmetic and copies ran while one was open for 0% -> 0% of each run, Pallas kernels for 13% -> 14%
where the time goes in v9:
time: 89.7 us; the launch traced here: 89.4 us
  starting transfers between devices  46.2 us (52%)
  waiting for transfers between devices  25.3 us (28%)
  Pallas kernels  17.5 us (20%)
    ppermute x23, starting transfers between devices, swap(): lax.ppermute(x, axis, [(i, i ^ mask) for i in range(lax.axis_size(axis))])  37 us
    ppermute x23, waiting for transfers between devices, swap(): lax.ppermute(x, axis, [(i, i ^ mask) for i in range(lax.axis_size(axis))])  14.6 us
    pallas_call x4, Pallas kernels, project(): pl.pallas_call(kernel, out_shape=[jax.ShapeDtypeStruct(piece, jnp.float32...  13.6 us
    ppermute x2, waiting for transfers between devices, ordered(): lax.ppermute(pair, 'feat', pairs)  10.7 us
    ppermute x1, starting transfers between devices, ordered(): got2.append(lax.ppermute(after(raw1[1], lang), 'feat', inward))  4.47 us
    ppermute x2, starting transfers between devices, ordered(): lax.ppermute(pair, 'feat', pairs)  1.96 us
  transfers between devices with their start and end apart: 30, of which 9 were waited for; matrix products, arithmetic and copies ran while one was open for 0% of the time, Pallas kernels for 14%

profile of v9, /device:TPU:0, one launch (start us, length us, event | category | flops | bytes accessed | tf_op | source)
XLA Modules:
  0.0 89.4 jit_solution(16871983878312488424)
XLA Ops:
  0.0 2.7 %project.4 = (f32[2,384,128]{2,1,0:T(8,128)S(1)}, bf16[1024,128]{1,0:T(8,128)(2,1)S(1)}, f32[32,1]{1,0:T(8,128)S(1)}) custom-call(s32[1]{0:T(128)} %bitcast.feat.feat_ref.me_ref, bf16[4096,1024]{1,0:T(8,128)(2,1)} %bitcast.24, bf16[4096,1024]{1,0:T(8,128)(2,1)} %bitcast.28, bf16[1024,128]{1,0:T(8,128)(2,1)} %adapter_ref.1, bf16[64,128]{1,0:T(8,128)(2,1)} %bitcast.32, ...), custom_call_target="tpu_custom_call" | custom-call | flops 268435456 | bytes 2490368 | tf_op jit(solution)/shard_map/project/pallas_call | solution.py:81
  2.7 3.1 %collective-permute-start.1 = (f32[2,384,128]{2,1,0:T(8,128)S(1)}, f32[2,384,128]{2,1,0:T(8,128)S(1)}, u32[]{:S(2)}, u32[]{:S(2)}) collective-permute-start(f32[2,384,128]{2,1,0:T(8,128)S(1)} %get-tuple-element.46.raw_ref), channel_id=1, source_target_pairs={{0,1},{1,0},{2,3},{3,2},{4,5},{5,4},{6,7},{7,6},{8,9},{9,8},{10,11... | collective-permute-start | bytes 1179656 | tf_op jit(solution)/shard_map/ppermute | solution.py:307
  5.8 2.5 %collective-permute-start.3 = (f32[32,1]{1,0:T(8,128)S(1)}, f32[32,1]{1,0:T(8,128)S(1)}, u32[]{:S(2)}, u32[]{:S(2)}) collective-permute-start(f32[32,1]{1,0:T(8,128)S(1)} %get-tuple-element.42.refs_0_), channel_id=1, source_target_pairs={{0,3},{1,2},{2,1},{3,0},{4,7},{5,6},{6,5},{7,4},{8,11},{9,10},{10,... | collective-permute-start | bytes 392 | tf_op jit(solution)/shard_map/ppermute | solution.py:307
  8.4 1.8 %collective-permute-start = (f32[32,1]{1,0:T(8,128)S(1)}, f32[32,1]{1,0:T(8,128)S(1)}, u32[]{:S(2)}, u32[]{:S(2)}) collective-permute-start(f32[32,1]{1,0:T(8,128)S(1)} %get-tuple-element.42.refs_0_), channel_id=1, source_target_pairs={{0,1},{1,0},{2,3},{3,2},{4,5},{5,4},{6,7},{7,6},{8,9},{9,8},{10,11... | collective-permute-start | bytes 392 | tf_op jit(solution)/shard_map/ppermute | solution.py:307
  10.2 4.7 %project.5 = (f32[2,384,128]{2,1,0:T(8,128)S(1)}, f32[2,384,128]{2,1,0:T(8,128)S(1)}, f32[2,384,128]{2,1,0:T(8,128)S(1)}) custom-call(s32[1]{0:T(128)} %bitcast.feat.feat_ref.me_ref, bf16[4096,1024]{1,0:T(8,128)(2,1)} %bitcast.25, bf16[4096,1024]{1,0:T(8,128)(2,1)} %bitcast.29, bf16[1024,128]{1,0:T(8,128)(2,1)S(1)} %get-tuple-element.69.down_ref, ...), custom_call_target="tpu_custom_call" | custom-call | flops 805306368 | bytes 7471104 | tf_op jit(solution)/shard_map/project/pallas_call | solution.py:81
  15.5 2.3 %collective-permute-done.3.refs_3_ = f32[32,1]{1,0:T(8,128)S(1)} collective-permute-done((f32[32,1]{1,0:T(8,128)S(1)}, f32[32,1]{1,0:T(8,128)S(1)}, u32[]{:S(2)}, u32[]{:S(2)}) %collective-permute-start.3) | collective-permute-done | bytes 160 | tf_op jit(solution)/shard_map/ppermute | solution.py:307
  19.0 1.3 %collective-permute-start.10 = (f32[2,384,128]{2,1,0:T(8,128)S(1)}, f32[2,384,128]{2,1,0:T(8,128)S(1)}, u32[]{:S(2)}, u32[]{:S(2)}) collective-permute-start(f32[2,384,128]{2,1,0:T(8,128)S(1)} %get-tuple-element.62.raw_ref), channel_id=1, source_target_pairs={{0,1},{1,0},{2,3},{3,2},{4,5},{5,4},{6,7},{7,6},{8,9},{9,8},{10,11... | collective-permute-start | bytes 1179656 | tf_op jit(solution)/shard_map/ppermute | solution.py:307
  20.3 1.6 %collective-permute-start.7 = (f32[64,256]{1,0:T(8,128)S(1)}, f32[64,256]{1,0:T(8,128)S(1)}, u32[]{:S(2)}, u32[]{:S(2)}) collective-permute-start(f32[64,256]{1,0:T(8,128)S(1)} %get-tuple-element.79), channel_id=1, source_target_pairs={{0,16},{4,20},{8,24},{12,28},{16,0},{20,4},{24,8},{28,12},{1,17},{... | collective-permute-start | bytes 196616 | tf_op jit(solution)/shard_map/ppermute | solution.py:307
  21.9 1.4 %collective-permute-start.8 = (f32[64,256]{1,0:T(8,128)S(1)}, f32[64,256]{1,0:T(8,128)S(1)}, u32[]{:S(2)}, u32[]{:S(2)}) collective-permute-start(f32[64,256]{1,0:T(8,128)S(1)} %get-tuple-element.80), channel_id=1, source_target_pairs={{0,24},{4,28},{8,16},{12,20},{16,8},{20,12},{24,0},{28,4},{1,25},{... | collective-permute-start | bytes 196616 | tf_op jit(solution)/shard_map/ppermute | solution.py:307
  23.9 6.4 %collective-permute-done.5.got_ref = f32[2,384,128]{2,1,0:T(8,128)S(1)} collective-permute-done((f32[2,384,128]{2,1,0:T(8,128)S(1)}, f32[2,384,128]{2,1,0:T(8,128)S(1)}, u32[]{:S(2)}, u32[]{:S(2)}) %collective-permute-start.5) | collective-permute-done | bytes 393248 | tf_op jit(solution)/shard_map/ppermute | solution.py:307
  31.1 2.8 %collective-permute-start.9 = (f32[64,256]{1,0:T(8,128)S(1)}, f32[64,256]{1,0:T(8,128)S(1)}, u32[]{:S(2)}, u32[]{:S(2)}) collective-permute-start(f32[64,256]{1,0:T(8,128)S(1)} %add_add_fusion.one_ref), channel_id=1, source_target_pairs={{0,1},{1,0},{2,3},{3,2},{4,5},{5,4},{6,7},{7,6},{8,9},{9,8},{10,11... | collective-permute-start | bytes 196616 | tf_op jit(solution)/shard_map/ppermute | solution.py:307
  34.5 4.5 %collective-permute-start.16 = (f32[2,384,128]{2,1,0:T(8,128)S(1)}, f32[2,384,128]{2,1,0:T(8,128)S(1)}, u32[]{:S(2)}, u32[]{:S(2)}) collective-permute-start(f32[2,384,128]{2,1,0:T(8,128)S(1)} %get-tuple-element.68.raw_ref), channel_id=1, source_target_pairs={{0,1},{3,2},{4,5},{7,6},{8,9},{11,10},{12,13},{15,14},{16,17},{19,... | collective-permute-start | bytes 1179656 | tf_op jit(solution)/shard_map/ppermute | solution.py:359
  39.0 3.1 %project.6 = (f32[2,384,128]{2,1,0:T(8,128)S(1)}, f32[2,384,128]{2,1,0:T(8,128)S(1)}) custom-call(s32[1]{0:T(128)} %bitcast.feat.feat_ref.me_ref, bf16[4096,1024]{1,0:T(8,128)(2,1)} %bitcast.26, bf16[4096,1024]{1,0:T(8,128)(2,1)} %bitcast.30, bf16[1024,128]{1,0:T(8,128)(2,1)S(1)} %get-tuple-element.69.down_ref, bf16[1024,128]{1,0:T(8,128)(2,1)} %sketch_ref.7), custom_call_target="tpu_custom_call" | custom-call | flops 536870912 | bytes 4980736 | tf_op jit(solution)/shard_map/project/pallas_call | solution.py:81
  42.1 1.3 %collective-permute-start.13 = (f32[2,64,256]{2,1,0:T(8,128)S(1)}, f32[2,64,256]{2,1,0:T(8,128)S(1)}, u32[]{:S(2)}, u32[]{:S(2)}) collective-permute-start(f32[2,64,256]{2,1,0:T(8,128)S(1)} %shard_map.75.pair_ref), channel_id=1, source_target_pairs={{1,3},{2,0},{5,7},{6,4},{9,11},{10,8},{13,15},{14,12},{17,19},{18,... | collective-permute-start | bytes 393224 | tf_op jit(solution)/shard_map/ppermute | solution.py:362
  44.3 10.7 %collective-permute-done.13.outer_ref = f32[2,64,256]{2,1,0:T(8,128)S(1)} collective-permute-done((f32[2,64,256]{2,1,0:T(8,128)S(1)}, f32[2,64,256]{2,1,0:T(8,128)S(1)}, u32[]{:S(2)}, u32[]{:S(2)}) %collective-permute-start.13) | collective-permute-done | bytes 131104 | tf_op jit(solution)/shard_map/ppermute | solution.py:362
  55.0 2.5 %collective-permute-start.20 = (f32[4,64,256]{2,1,0:T(8,128)S(1)}, f32[4,64,256]{2,1,0:T(8,128)S(1)}, u32[]{:S(2)}, u32[]{:S(2)}) collective-permute-start(f32[4,64,256]{2,1,0:T(8,128)S(1)} %shard_map.78.refs_0_), channel_id=1, source_target_pairs={{0,24},{4,28},{8,16},{12,20},{16,8},{20,12},{24,0},{28,4},{1,25},{... | collective-permute-start | bytes 786440 | tf_op jit(solution)/shard_map/ppermute | solution.py:307
  58.2 4.0 %collective-permute-start.17 = (f32[2,384,128]{2,1,0:T(8,128)S(1)}, f32[2,384,128]{2,1,0:T(8,128)S(1)}, u32[]{:S(2)}, u32[]{:S(2)}) collective-permute-start(f32[2,384,128]{2,1,0:T(8,128)S(1)} %shard_map.77), channel_id=1, source_target_pairs={{0,1},{1,0},{2,3},{3,2},{4,5},{5,4},{6,7},{7,6},{8,9},{9,8},{10,11... | collective-permute-start | bytes 1179656 | tf_op jit(solution)/shard_map/ppermute | solution.py:307
  63.3 6.7 %collective-permute-start.25 = (f32[2,384,128]{2,1,0:T(8,128)S(1)}, f32[2,384,128]{2,1,0:T(8,128)S(1)}, u32[]{:S(2)}, u32[]{:S(2)}) collective-permute-start(f32[2,384,128]{2,1,0:T(8,128)S(1)} %shard_map.79), channel_id=1, source_target_pairs={{0,1},{1,0},{2,3},{3,2},{4,5},{5,4},{6,7},{7,6},{8,9},{9,8},{10,11... | collective-permute-start | bytes 1179656 | tf_op jit(solution)/shard_map/ppermute | solution.py:307
  70.8 3.1 %project.7 = (f32[2,384,128]{2,1,0:T(8,128)S(1)}, f32[2,384,128]{2,1,0:T(8,128)S(1)}) custom-call(s32[1]{0:T(128)} %bitcast.feat.feat_ref.me_ref, bf16[4096,1024]{1,0:T(8,128)(2,1)} %bitcast.27, bf16[4096,1024]{1,0:T(8,128)(2,1)} %bitcast.31, bf16[1024,128]{1,0:T(8,128)(2,1)S(1)} %get-tuple-element.69.down_ref, bf16[1024,128]{1,0:T(8,128)(2,1)} %sketch_ref.7), custom_call_target="tpu_custom_call" | custom-call | flops 536870912 | bytes 4980736 | tf_op jit(solution)/shard_map/project/pallas_call | solution.py:81
  77.3 1.5 %score.1.refs_0_ = f32[16,64]{1,0:T(8,128)S(1)} custom-call(s32[1]{0:T(128)} %bitcast.1.middle_ref, bf16[32,128,256]{2,1,0:T(8,128)(2,1)S(1)} %split.1.lang_ref, bf16[32,16,256]{2,1,0:T(8,128)(2,1)S(1)} %get-tuple-element.75.grad_a, f32[8,1]{1,0:T(8,128)S(1)} %get-tuple-element.71.square_a, f32[2,384,128]{2,1,0:T(8,128)S(1)} %get-tuple-element.76.refs_0_, ...), custom_call_target="tpu_custom_call" | custom-call | tf_op jit(solution)/shard_map/score/pallas_call | solution.py:247
  78.9 2.7 %collective-permute-start.29 = (f32[16,64]{1,0:T(8,128)S(1)}, f32[16,64]{1,0:T(8,128)S(1)}, u32[]{:S(2)}, u32[]{:S(2)}) collective-permute-start(f32[16,64]{1,0:T(8,128)S(1)} %score.1.refs_0_), channel_id=1, source_target_pairs={{0,3},{1,2},{2,1},{3,0},{4,7},{5,6},{6,5},{7,4},{8,11},{9,10},{10,... | collective-permute-start | bytes 12296 | tf_op jit(solution)/shard_map/ppermute | solution.py:307
  81.6 3.5 %collective-permute-start.28 = (f32[16,64]{1,0:T(8,128)S(1)}, f32[16,64]{1,0:T(8,128)S(1)}, u32[]{:S(2)}, u32[]{:S(2)}) collective-permute-start(f32[16,64]{1,0:T(8,128)S(1)} %score.1.refs_0_), channel_id=1, source_target_pairs={{0,2},{1,3},{2,0},{3,1},{4,6},{5,7},{6,4},{7,5},{8,10},{9,11},{10,... | collective-permute-start | bytes 12296 | tf_op jit(solution)/shard_map/ppermute | solution.py:307
  85.1 1.7 %collective-permute-done.28.refs_2_ = f32[16,64]{1,0:T(8,128)S(1)} collective-permute-done((f32[16,64]{1,0:T(8,128)S(1)}, f32[16,64]{1,0:T(8,128)S(1)}, u32[]{:S(2)}, u32[]{:S(2)}) %collective-permute-start.28) | collective-permute-done | bytes 4128 | tf_op jit(solution)/shard_map/ppermute | solution.py:307
  86.8 1.9 %collective-permute-done.27.refs_1_ = f32[16,64]{1,0:T(8,128)S(1)} collective-permute-done((f32[16,64]{1,0:T(8,128)S(1)}, f32[16,64]{1,0:T(8,128)S(1)}, u32[]{:S(2)}, u32[]{:S(2)}) %collective-permute-start.27) | collective-permute-done | bytes 4128 | tf_op jit(solution)/shard_map/ppermute | solution.py:307
  (60 shorter events, 11.3 us)
Async XLA Ops:
  2.7 12.8 %collective-permute-start.1 = (f32[2,384,128]{2,1,0:T(8,128)S(1)}, f32[2,384,128]{2,1,0:T(8,128)S(1)}, u32[]{:S(2)}, u32[]{:S(2)}) collective-permute-start(f32[2,384,128]{2,1,0:T(8,128)S(1)} %get-tuple-element.46.raw_ref), channel_id=1, source_target_pairs={{0,1},{1,0},{2,3},{3,2},{4,5},{5,4},{6,7},{7,6},{8,9},{9,8},{10,11... | collective-permute-start | bytes 1179656 | tf_op jit(solution)/shard_map/ppermute | solution.py:307
  5.8 12.0 %collective-permute-start.3 = (f32[32,1]{1,0:T(8,128)S(1)}, f32[32,1]{1,0:T(8,128)S(1)}, u32[]{:S(2)}, u32[]{:S(2)}) collective-permute-start(f32[32,1]{1,0:T(8,128)S(1)} %get-tuple-element.42.refs_0_), channel_id=1, source_target_pairs={{0,3},{1,2},{2,1},{3,0},{4,7},{5,6},{6,5},{7,4},{8,11},{9,10},{10,... | collective-permute-start | bytes 392 | tf_op jit(solution)/shard_map/ppermute | solution.py:307
  8.3 9.5 %collective-permute-start.2 = (f32[32,1]{1,0:T(8,128)S(1)}, f32[32,1]{1,0:T(8,128)S(1)}, u32[]{:S(2)}, u32[]{:S(2)}) collective-permute-start(f32[32,1]{1,0:T(8,128)S(1)} %get-tuple-element.42.refs_0_), channel_id=1, source_target_pairs={{0,2},{1,3},{2,0},{3,1},{4,6},{5,7},{6,4},{7,5},{8,10},{9,11},{10,... | collective-permute-start | bytes 392 | tf_op jit(solution)/shard_map/ppermute | solution.py:307
  8.4 9.4 %collective-permute-start = (f32[32,1]{1,0:T(8,128)S(1)}, f32[32,1]{1,0:T(8,128)S(1)}, u32[]{:S(2)}, u32[]{:S(2)}) collective-permute-start(f32[32,1]{1,0:T(8,128)S(1)} %get-tuple-element.42.refs_0_), channel_id=1, source_target_pairs={{0,1},{1,0},{2,3},{3,2},{4,5},{5,4},{6,7},{7,6},{8,9},{9,8},{10,11... | collective-permute-start | bytes 392 | tf_op jit(solution)/shard_map/ppermute | solution.py:307
  18.2 12.1 %collective-permute-start.5 = (f32[2,384,128]{2,1,0:T(8,128)S(1)}, f32[2,384,128]{2,1,0:T(8,128)S(1)}, u32[]{:S(2)}, u32[]{:S(2)}) collective-permute-start(f32[2,384,128]{2,1,0:T(8,128)S(1)} %get-tuple-element.53.raw_ref), channel_id=1, source_target_pairs={{0,1},{1,0},{2,3},{3,2},{4,5},{5,4},{6,7},{7,6},{8,9},{9,8},{10,11... | collective-permute-start | bytes 1179656 | tf_op jit(solution)/shard_map/ppermute | solution.py:307
  19.0 24.4 %collective-permute-start.10 = (f32[2,384,128]{2,1,0:T(8,128)S(1)}, f32[2,384,128]{2,1,0:T(8,128)S(1)}, u32[]{:S(2)}, u32[]{:S(2)}) collective-permute-start(f32[2,384,128]{2,1,0:T(8,128)S(1)} %get-tuple-element.62.raw_ref), channel_id=1, source_target_pairs={{0,1},{1,0},{2,3},{3,2},{4,5},{5,4},{6,7},{7,6},{8,9},{9,8},{10,11... | collective-permute-start | bytes 1179656 | tf_op jit(solution)/shard_map/ppermute | solution.py:307
  20.3 10.7 %collective-permute-start.7 = (f32[64,256]{1,0:T(8,128)S(1)}, f32[64,256]{1,0:T(8,128)S(1)}, u32[]{:S(2)}, u32[]{:S(2)}) collective-permute-start(f32[64,256]{1,0:T(8,128)S(1)} %get-tuple-element.79), channel_id=1, source_target_pairs={{0,16},{4,20},{8,24},{12,28},{16,0},{20,4},{24,8},{28,12},{1,17},{... | collective-permute-start | bytes 196616 | tf_op jit(solution)/shard_map/ppermute | solution.py:307
  21.9 9.1 %collective-permute-start.8 = (f32[64,256]{1,0:T(8,128)S(1)}, f32[64,256]{1,0:T(8,128)S(1)}, u32[]{:S(2)}, u32[]{:S(2)}) collective-permute-start(f32[64,256]{1,0:T(8,128)S(1)} %get-tuple-element.80), channel_id=1, source_target_pairs={{0,24},{4,28},{8,16},{12,20},{16,8},{20,12},{24,0},{28,4},{1,25},{... | collective-permute-start | bytes 196616 | tf_op jit(solution)/shard_map/ppermute | solution.py:307
  23.4 7.7 %collective-permute-start.6 = (f32[64,256]{1,0:T(8,128)S(1)}, f32[64,256]{1,0:T(8,128)S(1)}, u32[]{:S(2)}, u32[]{:S(2)}) collective-permute-start(f32[64,256]{1,0:T(8,128)S(1)} %get-tuple-element.81), channel_id=1, source_target_pairs={{0,8},{4,12},{8,0},{12,4},{16,24},{20,28},{24,16},{28,20},{1,9},{5... | collective-permute-start | bytes 196616 | tf_op jit(solution)/shard_map/ppermute | solution.py:307
  30.3 13.9 %collective-permute-start.11 = (f32[2,384,128]{2,1,0:T(8,128)S(1)}, f32[2,384,128]{2,1,0:T(8,128)S(1)}, u32[]{:S(2)}, u32[]{:S(2)}) collective-permute-start(f32[2,384,128]{2,1,0:T(8,128)S(1)} %shard_map.73), channel_id=1, source_target_pairs={{1,2},{2,1},{0,0},{3,3},{5,6},{6,5},{4,4},{7,7},{9,10},{10,9},{8,8... | collective-permute-start | bytes 1179656 | tf_op jit(solution)/shard_map/ppermute | solution.py:348
  31.1 11.1 %collective-permute-start.9 = (f32[64,256]{1,0:T(8,128)S(1)}, f32[64,256]{1,0:T(8,128)S(1)}, u32[]{:S(2)}, u32[]{:S(2)}) collective-permute-start(f32[64,256]{1,0:T(8,128)S(1)} %add_add_fusion.one_ref), channel_id=1, source_target_pairs={{0,1},{1,0},{2,3},{3,2},{4,5},{5,4},{6,7},{7,6},{8,9},{9,8},{10,11... | collective-permute-start | bytes 196616 | tf_op jit(solution)/shard_map/ppermute | solution.py:307
  33.8 28.4 %collective-permute-start.15 = (f32[2,384,128]{2,1,0:T(8,128)S(1)}, f32[2,384,128]{2,1,0:T(8,128)S(1)}, u32[]{:S(2)}, u32[]{:S(2)}) collective-permute-start(f32[2,384,128]{2,1,0:T(8,128)S(1)} %shard_map.74), channel_id=1, source_target_pairs={{1,2},{2,1},{0,0},{3,3},{5,6},{6,5},{4,4},{7,7},{9,10},{10,9},{8,8... | collective-permute-start | bytes 1179656 | tf_op jit(solution)/shard_map/ppermute | solution.py:356
  34.5 28.2 %collective-permute-start.16 = (f32[2,384,128]{2,1,0:T(8,128)S(1)}, f32[2,384,128]{2,1,0:T(8,128)S(1)}, u32[]{:S(2)}, u32[]{:S(2)}) collective-permute-start(f32[2,384,128]{2,1,0:T(8,128)S(1)} %get-tuple-element.68.raw_ref), channel_id=1, source_target_pairs={{0,1},{3,2},{4,5},{7,6},{8,9},{11,10},{12,13},{15,14},{16,17},{19,... | collective-permute-start | bytes 1179656 | tf_op jit(solution)/shard_map/ppermute | solution.py:359
  42.1 12.9 %collective-permute-start.13 = (f32[2,64,256]{2,1,0:T(8,128)S(1)}, f32[2,64,256]{2,1,0:T(8,128)S(1)}, u32[]{:S(2)}, u32[]{:S(2)}) collective-permute-start(f32[2,64,256]{2,1,0:T(8,128)S(1)} %shard_map.75.pair_ref), channel_id=1, source_target_pairs={{1,3},{2,0},{5,7},{6,4},{9,11},{10,8},{13,15},{14,12},{17,19},{18,... | collective-permute-start | bytes 393224 | tf_op jit(solution)/shard_map/ppermute | solution.py:362
  43.5 11.6 %collective-permute-start.12 = (f32[2,64,256]{2,1,0:T(8,128)S(1)}, f32[2,64,256]{2,1,0:T(8,128)S(1)}, u32[]{:S(2)}, u32[]{:S(2)}) collective-permute-start(f32[2,64,256]{2,1,0:T(8,128)S(1)} %shard_map.75.pair_ref), channel_id=1, source_target_pairs={{1,2},{2,1},{0,0},{3,3},{5,6},{6,5},{4,4},{7,7},{9,10},{10,9},{8,8... | collective-permute-start | bytes 393224 | tf_op jit(solution)/shard_map/ppermute | solution.py:362
  55.0 8.2 %collective-permute-start.20 = (f32[4,64,256]{2,1,0:T(8,128)S(1)}, f32[4,64,256]{2,1,0:T(8,128)S(1)}, u32[]{:S(2)}, u32[]{:S(2)}) collective-permute-start(f32[4,64,256]{2,1,0:T(8,128)S(1)} %shard_map.78.refs_0_), channel_id=1, source_target_pairs={{0,24},{4,28},{8,16},{12,20},{16,8},{20,12},{24,0},{28,4},{1,25},{... | collective-permute-start | bytes 786440 | tf_op jit(solution)/shard_map/ppermute | solution.py:307
  57.5 5.8 %collective-permute-start.18 = (f32[2,384,128]{2,1,0:T(8,128)S(1)}, f32[2,384,128]{2,1,0:T(8,128)S(1)}, u32[]{:S(2)}, u32[]{:S(2)}) collective-permute-start(f32[2,384,128]{2,1,0:T(8,128)S(1)} %shard_map.76), channel_id=1, source_target_pairs={{1,2},{2,1},{0,0},{3,3},{5,6},{6,5},{4,4},{7,7},{9,10},{10,9},{8,8... | collective-permute-start | bytes 1179656 | tf_op jit(solution)/shard_map/ppermute | solution.py:364
  58.2 11.8 %collective-permute-start.17 = (f32[2,384,128]{2,1,0:T(8,128)S(1)}, f32[2,384,128]{2,1,0:T(8,128)S(1)}, u32[]{:S(2)}, u32[]{:S(2)}) collective-permute-start(f32[2,384,128]{2,1,0:T(8,128)S(1)} %shard_map.77), channel_id=1, source_target_pairs={{0,1},{1,0},{2,3},{3,2},{4,5},{5,4},{6,7},{7,6},{8,9},{9,8},{10,11... | collective-permute-start | bytes 1179656 | tf_op jit(solution)/shard_map/ppermute | solution.py:307
  62.2 12.5 %collective-permute-start.19 = (f32[4,64,256]{2,1,0:T(8,128)S(1)}, f32[4,64,256]{2,1,0:T(8,128)S(1)}, u32[]{:S(2)}, u32[]{:S(2)}) collective-permute-start(f32[4,64,256]{2,1,0:T(8,128)S(1)} %shard_map.78.refs_0_), channel_id=1, source_target_pairs={{0,16},{4,20},{8,24},{12,28},{16,0},{20,4},{24,8},{28,12},{1,17},{... | collective-permute-start | bytes 786440 | tf_op jit(solution)/shard_map/ppermute | solution.py:307
  62.7 12.0 %collective-permute-start.14 = (f32[4,64,256]{2,1,0:T(8,128)S(1)}, f32[4,64,256]{2,1,0:T(8,128)S(1)}, u32[]{:S(2)}, u32[]{:S(2)}) collective-permute-start(f32[4,64,256]{2,1,0:T(8,128)S(1)} %shard_map.78.refs_0_), channel_id=1, source_target_pairs={{0,8},{4,12},{8,0},{12,4},{16,24},{20,28},{24,16},{28,20},{1,9},{5... | collective-permute-start | bytes 786440 | tf_op jit(solution)/shard_map/ppermute | solution.py:307
  63.3 12.0 %collective-permute-start.21 = (f32[4,64,256]{2,1,0:T(8,128)S(1)}, f32[4,64,256]{2,1,0:T(8,128)S(1)}, u32[]{:S(2)}, u32[]{:S(2)}) collective-permute-start(f32[4,64,256]{2,1,0:T(8,128)S(1)} %shard_map.78.refs_0_), channel_id=1, source_target_pairs={{0,4},{4,0},{8,12},{12,8},{16,20},{20,16},{24,28},{28,24},{1,5},{5... | collective-permute-start | bytes 786440 | tf_op jit(solution)/shard_map/ppermute | solution.py:307
  63.3 14.0 %collective-permute-start.25 = (f32[2,384,128]{2,1,0:T(8,128)S(1)}, f32[2,384,128]{2,1,0:T(8,128)S(1)}, u32[]{:S(2)}, u32[]{:S(2)}) collective-permute-start(f32[2,384,128]{2,1,0:T(8,128)S(1)} %shard_map.79), channel_id=1, source_target_pairs={{0,1},{1,0},{2,3},{3,2},{4,5},{5,4},{6,7},{7,6},{8,9},{9,8},{10,11... | collective-permute-start | bytes 1179656 | tf_op jit(solution)/shard_map/ppermute | solution.py:307
  70.1 7.2 %collective-permute-start.26 = (f32[2,384,128]{2,1,0:T(8,128)S(1)}, f32[2,384,128]{2,1,0:T(8,128)S(1)}, u32[]{:S(2)}, u32[]{:S(2)}) collective-permute-start(f32[2,384,128]{2,1,0:T(8,128)S(1)} %shard_map.80), channel_id=1, source_target_pairs={{1,2},{2,1},{0,0},{3,3},{5,6},{6,5},{4,4},{7,7},{9,10},{10,9},{8,8... | collective-permute-start | bytes 1179656 | tf_op jit(solution)/shard_map/ppermute | solution.py:373
  78.9 6.3 %collective-permute-start.29 = (f32[16,64]{1,0:T(8,128)S(1)}, f32[16,64]{1,0:T(8,128)S(1)}, u32[]{:S(2)}, u32[]{:S(2)}) collective-permute-start(f32[16,64]{1,0:T(8,128)S(1)} %score.1.refs_0_), channel_id=1, source_target_pairs={{0,3},{1,2},{2,1},{3,0},{4,7},{5,6},{6,5},{7,4},{8,11},{9,10},{10,... | collective-permute-start | bytes 12296 | tf_op jit(solution)/shard_map/ppermute | solution.py:307
  (8 other events, 28.6 us)

commit v10 on v9

--- a/solution.py
+++ b/solution.py
@@ -352,19 +352,19 @@
     other = swap(other, "ex", 1)
     parts = [x + other[i] for i, x in enumerate(parts)]
     scattered = [swap(parts[i], "ex", 2 * i) for i in range(1, n_ex // 2)]
-    sent1.append(onward(after(raw0_b, parts[0]), got1[1]))
+    raw2 = project(more_kernel, me_feat, 4, 2, acts2, grads2, [after(down, parts[0]), out_sketch], [])
+    sent1.append(onward(after(raw0_b, raw2[0]), got1[1]))
     far.append(lax.ppermute(sent1[1], "feat", inner))
     lang = after(parts[0], sent1[1]) + sum(scattered)
     other = swap(lang, "feat", 1)
     got2.append(lax.ppermute(after(raw1[1], lang), "feat", inward))
-    raw2 = project(more_kernel, me_feat, 4, 2, acts2, grads2, [after(down, lang), out_sketch], [])
-    pair = small(stack_kernel, (2, *lang.shape), is_middle, [lang, after(other, raw2[0])])
+    sent3 = [onward(after(raw2[0], lang), far[0])]
+    got3 = [swap(sent3[0], "feat", 1)]
+    pair = small(stack_kernel, (2, *lang.shape), is_middle, [lang, after(other, sent3[0])])
     far_pair = [lax.ppermute(pair, "feat", pairs) for pairs in (inner, [(1, 3), (2, 0)])]
     sent2 = [onward(after(raw1[0], pair), got2[0])]
     near = [lax.ppermute(sent2[0], "feat", inner)]
-    sent3 = [onward(after(raw2[0], sent2[0]), far[0])]
-    got3 = [swap(sent3[0], "feat", 1)]
-    pair = after(pair, sent3[0])
+    pair = after(pair, sent2[0])
     langs = [small(join_kernel, (4, *lang.shape), is_middle, [pair, *far_pair])]
     langs = langs + [swap(langs[0], "ex", mask) for mask in range(2, n_ex, 2)]
     sent3.append(onward(after(raw2[1], langs[0]), far[1]))

time: 89.7 us -> 85.6 us (0.954)
  waiting for transfers between devices: 25.3 us -> 22.9 us
  starting transfers between devices: 46.2 us -> 44.6 us
    ppermute x2, waiting for transfers between devices: 10.7 us -> 6.71 us  [ordered(): lax.ppermute(pair, 'feat', pairs)]
    ppermute x23, starting transfers between devices: 37 us -> 35.3 us  [swap(): lax.ppermute(x, axis, [(i, i ^ mask) for i in range(lax.axis_size(axis))])]
    ppermute x23, waiting for transfers between devices: 14.6 us -> 16.2 us  [swap(): lax.ppermute(x, axis, [(i, i ^ mask) for i in range(lax.axis_size(axis))])]
  transfers between devices with their start and end apart: 30 -> 30, of which waited for: 9 -> 12; matrix products, arithmetic and copies ran while one was open for 0% -> 0% of each run, Pallas kernels for 14% -> 14%
where the time goes in v10:
time: 85.6 us; the launch traced here: 85.3 us
  starting transfers between devices  44.6 us (52%)
  waiting for transfers between devices  22.9 us (27%)
  Pallas kernels  17.5 us (20%)
    ppermute x23, starting transfers between devices, swap(): lax.ppermute(x, axis, [(i, i ^ mask) for i in range(lax.axis_size(axis))])  35.3 us
    ppermute x23, waiting for transfers between devices, swap(): lax.ppermute(x, axis, [(i, i ^ mask) for i in range(lax.axis_size(axis))])  16.2 us
    pallas_call x4, Pallas kernels, project(): pl.pallas_call(kernel, out_shape=[jax.ShapeDtypeStruct(piece, jnp.float32...  13.6 us
    ppermute x2, waiting for transfers between devices, ordered(): lax.ppermute(pair, 'feat', pairs)  6.71 us
    ppermute x1, starting transfers between devices, ordered(): got2.append(lax.ppermute(after(raw1[1], lang), 'feat', inward))  4.62 us
    ppermute x2, starting transfers between devices, ordered(): lax.ppermute(pair, 'feat', pairs)  1.96 us
  transfers between devices with their start and end apart: 30, of which 12 were waited for; matrix products, arithmetic and copies ran while one was open for 0% of the time, Pallas kernels for 14%

profile of v10, /device:TPU:0, one launch (start us, length us, event | category | flops | bytes accessed | tf_op | source)
XLA Modules:
  0.0 85.3 jit_solution(7520900318324632791)
XLA Ops:
  0.0 2.7 %project.4 = (f32[2,384,128]{2,1,0:T(8,128)S(1)}, bf16[1024,128]{1,0:T(8,128)(2,1)S(1)}, f32[32,1]{1,0:T(8,128)S(1)}) custom-call(s32[1]{0:T(128)} %bitcast.feat.feat_ref.me_ref, bf16[4096,1024]{1,0:T(8,128)(2,1)} %bitcast.24, bf16[4096,1024]{1,0:T(8,128)(2,1)} %bitcast.28, bf16[1024,128]{1,0:T(8,128)(2,1)} %adapter_ref.1, bf16[64,128]{1,0:T(8,128)(2,1)} %bitcast.32, ...), custom_call_target="tpu_custom_call" | custom-call | flops 268435456 | bytes 2490368 | tf_op jit(solution)/shard_map/project/pallas_call | solution.py:81
  2.7 3.1 %collective-permute-start.1 = (f32[2,384,128]{2,1,0:T(8,128)S(1)}, f32[2,384,128]{2,1,0:T(8,128)S(1)}, u32[]{:S(2)}, u32[]{:S(2)}) collective-permute-start(f32[2,384,128]{2,1,0:T(8,128)S(1)} %get-tuple-element.46.raw_ref), channel_id=1, source_target_pairs={{0,1},{1,0},{2,3},{3,2},{4,5},{5,4},{6,7},{7,6},{8,9},{9,8},{10,11... | collective-permute-start | bytes 1179656 | tf_op jit(solution)/shard_map/ppermute | solution.py:307
  5.8 2.5 %collective-permute-start.3 = (f32[32,1]{1,0:T(8,128)S(1)}, f32[32,1]{1,0:T(8,128)S(1)}, u32[]{:S(2)}, u32[]{:S(2)}) collective-permute-start(f32[32,1]{1,0:T(8,128)S(1)} %get-tuple-element.42.refs_0_), channel_id=1, source_target_pairs={{0,3},{1,2},{2,1},{3,0},{4,7},{5,6},{6,5},{7,4},{8,11},{9,10},{10,... | collective-permute-start | bytes 392 | tf_op jit(solution)/shard_map/ppermute | solution.py:307
  8.4 1.8 %collective-permute-start = (f32[32,1]{1,0:T(8,128)S(1)}, f32[32,1]{1,0:T(8,128)S(1)}, u32[]{:S(2)}, u32[]{:S(2)}) collective-permute-start(f32[32,1]{1,0:T(8,128)S(1)} %get-tuple-element.42.refs_0_), channel_id=1, source_target_pairs={{0,1},{1,0},{2,3},{3,2},{4,5},{5,4},{6,7},{7,6},{8,9},{9,8},{10,11... | collective-permute-start | bytes 392 | tf_op jit(solution)/shard_map/ppermute | solution.py:307
  10.2 4.7 %project.5 = (f32[2,384,128]{2,1,0:T(8,128)S(1)}, f32[2,384,128]{2,1,0:T(8,128)S(1)}, f32[2,384,128]{2,1,0:T(8,128)S(1)}) custom-call(s32[1]{0:T(128)} %bitcast.feat.feat_ref.me_ref, bf16[4096,1024]{1,0:T(8,128)(2,1)} %bitcast.25, bf16[4096,1024]{1,0:T(8,128)(2,1)} %bitcast.29, bf16[1024,128]{1,0:T(8,128)(2,1)S(1)} %get-tuple-element.69.down_ref, ...), custom_call_target="tpu_custom_call" | custom-call | flops 805306368 | bytes 7471104 | tf_op jit(solution)/shard_map/project/pallas_call | solution.py:81
  15.5 2.3 %collective-permute-done.3.refs_3_ = f32[32,1]{1,0:T(8,128)S(1)} collective-permute-done((f32[32,1]{1,0:T(8,128)S(1)}, f32[32,1]{1,0:T(8,128)S(1)}, u32[]{:S(2)}, u32[]{:S(2)}) %collective-permute-start.3) | collective-permute-done | bytes 160 | tf_op jit(solution)/shard_map/ppermute | solution.py:307
  19.8 1.6 %collective-permute-start.7 = (f32[64,256]{1,0:T(8,128)S(1)}, f32[64,256]{1,0:T(8,128)S(1)}, u32[]{:S(2)}, u32[]{:S(2)}) collective-permute-start(f32[64,256]{1,0:T(8,128)S(1)} %get-tuple-element.79), channel_id=1, source_target_pairs={{0,16},{4,20},{8,24},{12,28},{16,0},{20,4},{24,8},{28,12},{1,17},{... | collective-permute-start | bytes 196616 | tf_op jit(solution)/shard_map/ppermute | solution.py:307
  21.4 1.4 %collective-permute-start.8 = (f32[64,256]{1,0:T(8,128)S(1)}, f32[64,256]{1,0:T(8,128)S(1)}, u32[]{:S(2)}, u32[]{:S(2)}) collective-permute-start(f32[64,256]{1,0:T(8,128)S(1)} %get-tuple-element.80), channel_id=1, source_target_pairs={{0,24},{4,28},{8,16},{12,20},{16,8},{20,12},{24,0},{28,4},{1,25},{... | collective-permute-start | bytes 196616 | tf_op jit(solution)/shard_map/ppermute | solution.py:307
  23.3 3.1 %project.6 = (f32[2,384,128]{2,1,0:T(8,128)S(1)}, f32[2,384,128]{2,1,0:T(8,128)S(1)}) custom-call(s32[1]{0:T(128)} %bitcast.feat.feat_ref.me_ref, bf16[4096,1024]{1,0:T(8,128)(2,1)} %bitcast.26, bf16[4096,1024]{1,0:T(8,128)(2,1)} %bitcast.30, bf16[1024,128]{1,0:T(8,128)(2,1)S(1)} %get-tuple-element.69.down_ref, bf16[1024,128]{1,0:T(8,128)(2,1)} %sketch_ref.7), custom_call_target="tpu_custom_call" | custom-call | flops 536870912 | bytes 4980736 | tf_op jit(solution)/shard_map/project/pallas_call | solution.py:81
  26.4 3.3 %collective-permute-done.5.got_ref = f32[2,384,128]{2,1,0:T(8,128)S(1)} collective-permute-done((f32[2,384,128]{2,1,0:T(8,128)S(1)}, f32[2,384,128]{2,1,0:T(8,128)S(1)}, u32[]{:S(2)}, u32[]{:S(2)}) %collective-permute-start.5) | collective-permute-done | bytes 393248 | tf_op jit(solution)/shard_map/ppermute | solution.py:307
  30.6 1.4 %collective-permute-start.9 = (f32[64,256]{1,0:T(8,128)S(1)}, f32[64,256]{1,0:T(8,128)S(1)}, u32[]{:S(2)}, u32[]{:S(2)}) collective-permute-start(f32[64,256]{1,0:T(8,128)S(1)} %add_add_fusion.one_ref), channel_id=1, source_target_pairs={{0,1},{1,0},{2,3},{3,2},{4,5},{5,4},{6,7},{7,6},{8,9},{9,8},{10,11... | collective-permute-start | bytes 196616 | tf_op jit(solution)/shard_map/ppermute | solution.py:307
  32.6 4.6 %collective-permute-start.16 = (f32[2,384,128]{2,1,0:T(8,128)S(1)}, f32[2,384,128]{2,1,0:T(8,128)S(1)}, u32[]{:S(2)}, u32[]{:S(2)}) collective-permute-start(f32[2,384,128]{2,1,0:T(8,128)S(1)} %get-tuple-element.68.raw_ref), channel_id=1, source_target_pairs={{0,1},{3,2},{4,5},{7,6},{8,9},{11,10},{12,13},{15,14},{16,17},{19,... | collective-permute-start | bytes 1179656 | tf_op jit(solution)/shard_map/ppermute | solution.py:360
  37.3 4.4 %collective-permute-done.9.two_ref = f32[64,256]{1,0:T(8,128)S(1)} collective-permute-done((f32[64,256]{1,0:T(8,128)S(1)}, f32[64,256]{1,0:T(8,128)S(1)}, u32[]{:S(2)}, u32[]{:S(2)}) %collective-permute-start.9) | collective-permute-done | bytes 65568 | tf_op jit(solution)/shard_map/ppermute | solution.py:307
  41.7 1.3 %collective-permute-start.13 = (f32[2,64,256]{2,1,0:T(8,128)S(1)}, f32[2,64,256]{2,1,0:T(8,128)S(1)}, u32[]{:S(2)}, u32[]{:S(2)}) collective-permute-start(f32[2,64,256]{2,1,0:T(8,128)S(1)} %shard_map.76.pair_ref), channel_id=1, source_target_pairs={{1,3},{2,0},{5,7},{6,4},{9,11},{10,8},{13,15},{14,12},{17,19},{18,... | collective-permute-start | bytes 393224 | tf_op jit(solution)/shard_map/ppermute | solution.py:364
  43.8 6.7 %collective-permute-done.13.outer_ref = f32[2,64,256]{2,1,0:T(8,128)S(1)} collective-permute-done((f32[2,64,256]{2,1,0:T(8,128)S(1)}, f32[2,64,256]{2,1,0:T(8,128)S(1)}, u32[]{:S(2)}, u32[]{:S(2)}) %collective-permute-start.13) | collective-permute-done | bytes 131104 | tf_op jit(solution)/shard_map/ppermute | solution.py:364
  50.5 2.5 %collective-permute-start.20 = (f32[4,64,256]{2,1,0:T(8,128)S(1)}, f32[4,64,256]{2,1,0:T(8,128)S(1)}, u32[]{:S(2)}, u32[]{:S(2)}) collective-permute-start(f32[4,64,256]{2,1,0:T(8,128)S(1)} %shard_map.78.refs_0_), channel_id=1, source_target_pairs={{0,24},{4,28},{8,16},{12,20},{16,8},{20,12},{24,0},{28,4},{1,25},{... | collective-permute-start | bytes 786440 | tf_op jit(solution)/shard_map/ppermute | solution.py:307
  53.7 4.8 %collective-permute-start.17 = (f32[2,384,128]{2,1,0:T(8,128)S(1)}, f32[2,384,128]{2,1,0:T(8,128)S(1)}, u32[]{:S(2)}, u32[]{:S(2)}) collective-permute-start(f32[2,384,128]{2,1,0:T(8,128)S(1)} %shard_map.75), channel_id=1, source_target_pairs={{0,1},{1,0},{2,3},{3,2},{4,5},{5,4},{6,7},{7,6},{8,9},{9,8},{10,11... | collective-permute-start | bytes 1179656 | tf_op jit(solution)/shard_map/ppermute | solution.py:307
  59.6 6.8 %collective-permute-start.25 = (f32[2,384,128]{2,1,0:T(8,128)S(1)}, f32[2,384,128]{2,1,0:T(8,128)S(1)}, u32[]{:S(2)}, u32[]{:S(2)}) collective-permute-start(f32[2,384,128]{2,1,0:T(8,128)S(1)} %shard_map.79), channel_id=1, source_target_pairs={{0,1},{1,0},{2,3},{3,2},{4,5},{5,4},{6,7},{7,6},{8,9},{9,8},{10,11... | collective-permute-start | bytes 1179656 | tf_op jit(solution)/shard_map/ppermute | solution.py:307
  67.3 3.1 %project.7 = (f32[2,384,128]{2,1,0:T(8,128)S(1)}, f32[2,384,128]{2,1,0:T(8,128)S(1)}) custom-call(s32[1]{0:T(128)} %bitcast.feat.feat_ref.me_ref, bf16[4096,1024]{1,0:T(8,128)(2,1)} %bitcast.27, bf16[4096,1024]{1,0:T(8,128)(2,1)} %bitcast.31, bf16[1024,128]{1,0:T(8,128)(2,1)S(1)} %get-tuple-element.69.down_ref, bf16[1024,128]{1,0:T(8,128)(2,1)} %sketch_ref.7), custom_call_target="tpu_custom_call" | custom-call | flops 536870912 | bytes 4980736 | tf_op jit(solution)/shard_map/project/pallas_call | solution.py:81
  74.0 1.5 %score.1.refs_0_ = f32[16,64]{1,0:T(8,128)S(1)} custom-call(s32[1]{0:T(128)} %bitcast.1.middle_ref, bf16[32,128,256]{2,1,0:T(8,128)(2,1)S(1)} %split.1.lang_ref, bf16[32,16,256]{2,1,0:T(8,128)(2,1)S(1)} %get-tuple-element.75.grad_a, f32[8,1]{1,0:T(8,128)S(1)} %get-tuple-element.71.square_a, f32[2,384,128]{2,1,0:T(8,128)S(1)} %get-tuple-element.76.refs_0_, ...), custom_call_target="tpu_custom_call" | custom-call | tf_op jit(solution)/shard_map/score/pallas_call | solution.py:247
  75.5 2.0 %collective-permute-start.29 = (f32[16,64]{1,0:T(8,128)S(1)}, f32[16,64]{1,0:T(8,128)S(1)}, u32[]{:S(2)}, u32[]{:S(2)}) collective-permute-start(f32[16,64]{1,0:T(8,128)S(1)} %score.1.refs_0_), channel_id=1, source_target_pairs={{0,3},{1,2},{2,1},{3,0},{4,7},{5,6},{6,5},{7,4},{8,11},{9,10},{10,... | collective-permute-start | bytes 12296 | tf_op jit(solution)/shard_map/ppermute | solution.py:307
  77.4 3.6 %collective-permute-start.28 = (f32[16,64]{1,0:T(8,128)S(1)}, f32[16,64]{1,0:T(8,128)S(1)}, u32[]{:S(2)}, u32[]{:S(2)}) collective-permute-start(f32[16,64]{1,0:T(8,128)S(1)} %score.1.refs_0_), channel_id=1, source_target_pairs={{0,2},{1,3},{2,0},{3,1},{4,6},{5,7},{6,4},{7,5},{8,10},{9,11},{10,... | collective-permute-start | bytes 12296 | tf_op jit(solution)/shard_map/ppermute | solution.py:307
  81.0 1.7 %collective-permute-done.28.refs_2_ = f32[16,64]{1,0:T(8,128)S(1)} collective-permute-done((f32[16,64]{1,0:T(8,128)S(1)}, f32[16,64]{1,0:T(8,128)S(1)}, u32[]{:S(2)}, u32[]{:S(2)}) %collective-permute-start.28) | collective-permute-done | bytes 4128 | tf_op jit(solution)/shard_map/ppermute | solution.py:307
  82.8 1.9 %collective-permute-done.27.refs_1_ = f32[16,64]{1,0:T(8,128)S(1)} collective-permute-done((f32[16,64]{1,0:T(8,128)S(1)}, f32[16,64]{1,0:T(8,128)S(1)}, u32[]{:S(2)}, u32[]{:S(2)}) %collective-permute-start.27) | collective-permute-done | bytes 4128 | tf_op jit(solution)/shard_map/ppermute | solution.py:307
  (60 shorter events, 12.2 us)
Async XLA Ops:
  2.7 12.8 %collective-permute-start.1 = (f32[2,384,128]{2,1,0:T(8,128)S(1)}, f32[2,384,128]{2,1,0:T(8,128)S(1)}, u32[]{:S(2)}, u32[]{:S(2)}) collective-permute-start(f32[2,384,128]{2,1,0:T(8,128)S(1)} %get-tuple-element.46.raw_ref), channel_id=1, source_target_pairs={{0,1},{1,0},{2,3},{3,2},{4,5},{5,4},{6,7},{7,6},{8,9},{9,8},{10,11... | collective-permute-start | bytes 1179656 | tf_op jit(solution)/shard_map/ppermute | solution.py:307
  5.8 12.0 %collective-permute-start.3 = (f32[32,1]{1,0:T(8,128)S(1)}, f32[32,1]{1,0:T(8,128)S(1)}, u32[]{:S(2)}, u32[]{:S(2)}) collective-permute-start(f32[32,1]{1,0:T(8,128)S(1)} %get-tuple-element.42.refs_0_), channel_id=1, source_target_pairs={{0,3},{1,2},{2,1},{3,0},{4,7},{5,6},{6,5},{7,4},{8,11},{9,10},{10,... | collective-permute-start | bytes 392 | tf_op jit(solution)/shard_map/ppermute | solution.py:307
  8.3 9.5 %collective-permute-start.2 = (f32[32,1]{1,0:T(8,128)S(1)}, f32[32,1]{1,0:T(8,128)S(1)}, u32[]{:S(2)}, u32[]{:S(2)}) collective-permute-start(f32[32,1]{1,0:T(8,128)S(1)} %get-tuple-element.42.refs_0_), channel_id=1, source_target_pairs={{0,2},{1,3},{2,0},{3,1},{4,6},{5,7},{6,4},{7,5},{8,10},{9,11},{10,... | collective-permute-start | bytes 392 | tf_op jit(solution)/shard_map/ppermute | solution.py:307
  8.4 9.4 %collective-permute-start = (f32[32,1]{1,0:T(8,128)S(1)}, f32[32,1]{1,0:T(8,128)S(1)}, u32[]{:S(2)}, u32[]{:S(2)}) collective-permute-start(f32[32,1]{1,0:T(8,128)S(1)} %get-tuple-element.42.refs_0_), channel_id=1, source_target_pairs={{0,1},{1,0},{2,3},{3,2},{4,5},{5,4},{6,7},{7,6},{8,9},{9,8},{10,11... | collective-permute-start | bytes 392 | tf_op jit(solution)/shard_map/ppermute | solution.py:307
  18.2 11.5 %collective-permute-start.5 = (f32[2,384,128]{2,1,0:T(8,128)S(1)}, f32[2,384,128]{2,1,0:T(8,128)S(1)}, u32[]{:S(2)}, u32[]{:S(2)}) collective-permute-start(f32[2,384,128]{2,1,0:T(8,128)S(1)} %get-tuple-element.55.raw_ref), channel_id=1, source_target_pairs={{0,1},{1,0},{2,3},{3,2},{4,5},{5,4},{6,7},{7,6},{8,9},{9,8},{10,11... | collective-permute-start | bytes 1179656 | tf_op jit(solution)/shard_map/ppermute | solution.py:307
  19.0 18.2 %collective-permute-start.10 = (f32[2,384,128]{2,1,0:T(8,128)S(1)}, f32[2,384,128]{2,1,0:T(8,128)S(1)}, u32[]{:S(2)}, u32[]{:S(2)}) collective-permute-start(f32[2,384,128]{2,1,0:T(8,128)S(1)} %shard_map.73), channel_id=1, source_target_pairs={{1,2},{2,1},{0,0},{3,3},{5,6},{6,5},{4,4},{7,7},{9,10},{10,9},{8,8... | collective-permute-start | bytes 1179656 | tf_op jit(solution)/shard_map/ppermute | solution.py:348
  19.8 10.7 %collective-permute-start.7 = (f32[64,256]{1,0:T(8,128)S(1)}, f32[64,256]{1,0:T(8,128)S(1)}, u32[]{:S(2)}, u32[]{:S(2)}) collective-permute-start(f32[64,256]{1,0:T(8,128)S(1)} %get-tuple-element.79), channel_id=1, source_target_pairs={{0,16},{4,20},{8,24},{12,28},{16,0},{20,4},{24,8},{28,12},{1,17},{... | collective-permute-start | bytes 196616 | tf_op jit(solution)/shard_map/ppermute | solution.py:307
  21.4 9.2 %collective-permute-start.8 = (f32[64,256]{1,0:T(8,128)S(1)}, f32[64,256]{1,0:T(8,128)S(1)}, u32[]{:S(2)}, u32[]{:S(2)}) collective-permute-start(f32[64,256]{1,0:T(8,128)S(1)} %get-tuple-element.80), channel_id=1, source_target_pairs={{0,24},{4,28},{8,16},{12,20},{16,8},{20,12},{24,0},{28,4},{1,25},{... | collective-permute-start | bytes 196616 | tf_op jit(solution)/shard_map/ppermute | solution.py:307
  22.8 7.7 %collective-permute-start.6 = (f32[64,256]{1,0:T(8,128)S(1)}, f32[64,256]{1,0:T(8,128)S(1)}, u32[]{:S(2)}, u32[]{:S(2)}) collective-permute-start(f32[64,256]{1,0:T(8,128)S(1)} %get-tuple-element.81), channel_id=1, source_target_pairs={{0,8},{4,12},{8,0},{12,4},{16,24},{20,28},{24,16},{28,20},{1,9},{5... | collective-permute-start | bytes 196616 | tf_op jit(solution)/shard_map/ppermute | solution.py:307
  29.7 14.0 %collective-permute-start.11 = (f32[2,384,128]{2,1,0:T(8,128)S(1)}, f32[2,384,128]{2,1,0:T(8,128)S(1)}, u32[]{:S(2)}, u32[]{:S(2)}) collective-permute-start(f32[2,384,128]{2,1,0:T(8,128)S(1)} %get-tuple-element.63.raw_ref), channel_id=1, source_target_pairs={{0,1},{1,0},{2,3},{3,2},{4,5},{5,4},{6,7},{7,6},{8,9},{9,8},{10,11... | collective-permute-start | bytes 1179656 | tf_op jit(solution)/shard_map/ppermute | solution.py:307
  30.6 11.2 %collective-permute-start.9 = (f32[64,256]{1,0:T(8,128)S(1)}, f32[64,256]{1,0:T(8,128)S(1)}, u32[]{:S(2)}, u32[]{:S(2)}) collective-permute-start(f32[64,256]{1,0:T(8,128)S(1)} %add_add_fusion.one_ref), channel_id=1, source_target_pairs={{0,1},{1,0},{2,3},{3,2},{4,5},{5,4},{6,7},{7,6},{8,9},{9,8},{10,11... | collective-permute-start | bytes 196616 | tf_op jit(solution)/shard_map/ppermute | solution.py:307
  31.9 26.6 %collective-permute-start.15 = (f32[2,384,128]{2,1,0:T(8,128)S(1)}, f32[2,384,128]{2,1,0:T(8,128)S(1)}, u32[]{:S(2)}, u32[]{:S(2)}) collective-permute-start(f32[2,384,128]{2,1,0:T(8,128)S(1)} %shard_map.74), channel_id=1, source_target_pairs={{1,2},{2,1},{0,0},{3,3},{5,6},{6,5},{4,4},{7,7},{9,10},{10,9},{8,8... | collective-permute-start | bytes 1179656 | tf_op jit(solution)/shard_map/ppermute | solution.py:357
  32.6 26.4 %collective-permute-start.16 = (f32[2,384,128]{2,1,0:T(8,128)S(1)}, f32[2,384,128]{2,1,0:T(8,128)S(1)}, u32[]{:S(2)}, u32[]{:S(2)}) collective-permute-start(f32[2,384,128]{2,1,0:T(8,128)S(1)} %get-tuple-element.68.raw_ref), channel_id=1, source_target_pairs={{0,1},{3,2},{4,5},{7,6},{8,9},{11,10},{12,13},{15,14},{16,17},{19,... | collective-permute-start | bytes 1179656 | tf_op jit(solution)/shard_map/ppermute | solution.py:360
  41.7 8.8 %collective-permute-start.13 = (f32[2,64,256]{2,1,0:T(8,128)S(1)}, f32[2,64,256]{2,1,0:T(8,128)S(1)}, u32[]{:S(2)}, u32[]{:S(2)}) collective-permute-start(f32[2,64,256]{2,1,0:T(8,128)S(1)} %shard_map.76.pair_ref), channel_id=1, source_target_pairs={{1,3},{2,0},{5,7},{6,4},{9,11},{10,8},{13,15},{14,12},{17,19},{18,... | collective-permute-start | bytes 393224 | tf_op jit(solution)/shard_map/ppermute | solution.py:364
  43.0 7.5 %collective-permute-start.12 = (f32[2,64,256]{2,1,0:T(8,128)S(1)}, f32[2,64,256]{2,1,0:T(8,128)S(1)}, u32[]{:S(2)}, u32[]{:S(2)}) collective-permute-start(f32[2,64,256]{2,1,0:T(8,128)S(1)} %shard_map.76.pair_ref), channel_id=1, source_target_pairs={{1,2},{2,1},{0,0},{3,3},{5,6},{6,5},{4,4},{7,7},{9,10},{10,9},{8,8... | collective-permute-start | bytes 393224 | tf_op jit(solution)/shard_map/ppermute | solution.py:364
  50.5 9.0 %collective-permute-start.20 = (f32[4,64,256]{2,1,0:T(8,128)S(1)}, f32[4,64,256]{2,1,0:T(8,128)S(1)}, u32[]{:S(2)}, u32[]{:S(2)}) collective-permute-start(f32[4,64,256]{2,1,0:T(8,128)S(1)} %shard_map.78.refs_0_), channel_id=1, source_target_pairs={{0,24},{4,28},{8,16},{12,20},{16,8},{20,12},{24,0},{28,4},{1,25},{... | collective-permute-start | bytes 786440 | tf_op jit(solution)/shard_map/ppermute | solution.py:307
  53.0 6.6 %collective-permute-start.18 = (f32[2,384,128]{2,1,0:T(8,128)S(1)}, f32[2,384,128]{2,1,0:T(8,128)S(1)}, u32[]{:S(2)}, u32[]{:S(2)}) collective-permute-start(f32[2,384,128]{2,1,0:T(8,128)S(1)} %shard_map.77), channel_id=1, source_target_pairs={{1,2},{2,1},{0,0},{3,3},{5,6},{6,5},{4,4},{7,7},{9,10},{10,9},{8,8... | collective-permute-start | bytes 1179656 | tf_op jit(solution)/shard_map/ppermute | solution.py:366
  53.7 12.9 %collective-permute-start.17 = (f32[2,384,128]{2,1,0:T(8,128)S(1)}, f32[2,384,128]{2,1,0:T(8,128)S(1)}, u32[]{:S(2)}, u32[]{:S(2)}) collective-permute-start(f32[2,384,128]{2,1,0:T(8,128)S(1)} %shard_map.75), channel_id=1, source_target_pairs={{0,1},{1,0},{2,3},{3,2},{4,5},{5,4},{6,7},{7,6},{8,9},{9,8},{10,11... | collective-permute-start | bytes 1179656 | tf_op jit(solution)/shard_map/ppermute | solution.py:307
  58.5 12.8 %collective-permute-start.19 = (f32[4,64,256]{2,1,0:T(8,128)S(1)}, f32[4,64,256]{2,1,0:T(8,128)S(1)}, u32[]{:S(2)}, u32[]{:S(2)}) collective-permute-start(f32[4,64,256]{2,1,0:T(8,128)S(1)} %shard_map.78.refs_0_), channel_id=1, source_target_pairs={{0,16},{4,20},{8,24},{12,28},{16,0},{20,4},{24,8},{28,12},{1,17},{... | collective-permute-start | bytes 786440 | tf_op jit(solution)/shard_map/ppermute | solution.py:307
  59.0 12.2 %collective-permute-start.14 = (f32[4,64,256]{2,1,0:T(8,128)S(1)}, f32[4,64,256]{2,1,0:T(8,128)S(1)}, u32[]{:S(2)}, u32[]{:S(2)}) collective-permute-start(f32[4,64,256]{2,1,0:T(8,128)S(1)} %shard_map.78.refs_0_), channel_id=1, source_target_pairs={{0,8},{4,12},{8,0},{12,4},{16,24},{20,28},{24,16},{28,20},{1,9},{5... | collective-permute-start | bytes 786440 | tf_op jit(solution)/shard_map/ppermute | solution.py:307
  59.6 12.2 %collective-permute-start.21 = (f32[4,64,256]{2,1,0:T(8,128)S(1)}, f32[4,64,256]{2,1,0:T(8,128)S(1)}, u32[]{:S(2)}, u32[]{:S(2)}) collective-permute-start(f32[4,64,256]{2,1,0:T(8,128)S(1)} %shard_map.78.refs_0_), channel_id=1, source_target_pairs={{0,4},{4,0},{8,12},{12,8},{16,20},{20,16},{24,28},{28,24},{1,5},{5... | collective-permute-start | bytes 786440 | tf_op jit(solution)/shard_map/ppermute | solution.py:307
  59.6 14.3 %collective-permute-start.25 = (f32[2,384,128]{2,1,0:T(8,128)S(1)}, f32[2,384,128]{2,1,0:T(8,128)S(1)}, u32[]{:S(2)}, u32[]{:S(2)}) collective-permute-start(f32[2,384,128]{2,1,0:T(8,128)S(1)} %shard_map.79), channel_id=1, source_target_pairs={{0,1},{1,0},{2,3},{3,2},{4,5},{5,4},{6,7},{7,6},{8,9},{9,8},{10,11... | collective-permute-start | bytes 1179656 | tf_op jit(solution)/shard_map/ppermute | solution.py:307
  66.6 7.4 %collective-permute-start.26 = (f32[2,384,128]{2,1,0:T(8,128)S(1)}, f32[2,384,128]{2,1,0:T(8,128)S(1)}, u32[]{:S(2)}, u32[]{:S(2)}) collective-permute-start(f32[2,384,128]{2,1,0:T(8,128)S(1)} %shard_map.80), channel_id=1, source_target_pairs={{1,2},{2,1},{0,0},{3,3},{5,6},{6,5},{4,4},{7,7},{9,10},{10,9},{8,8... | collective-permute-start | bytes 1179656 | tf_op jit(solution)/shard_map/ppermute | solution.py:373
  75.5 5.6 %collective-permute-start.29 = (f32[16,64]{1,0:T(8,128)S(1)}, f32[16,64]{1,0:T(8,128)S(1)}, u32[]{:S(2)}, u32[]{:S(2)}) collective-permute-start(f32[16,64]{1,0:T(8,128)S(1)} %score.1.refs_0_), channel_id=1, source_target_pairs={{0,3},{1,2},{2,1},{3,0},{4,7},{5,6},{6,5},{7,4},{8,11},{9,10},{10,... | collective-permute-start | bytes 12296 | tf_op jit(solution)/shard_map/ppermute | solution.py:307
  (8 other events, 28.1 us)

commit v11 on v10

--- a/solution.py
+++ b/solution.py
@@ -352,16 +352,17 @@
     other = swap(other, "ex", 1)
     parts = [x + other[i] for i, x in enumerate(parts)]
     scattered = [swap(parts[i], "ex", 2 * i) for i in range(1, n_ex // 2)]
-    raw2 = project(more_kernel, me_feat, 4, 2, acts2, grads2, [after(down, parts[0]), out_sketch], [])
-    sent1.append(onward(after(raw0_b, raw2[0]), got1[1]))
+    sent1.append(onward(after(raw0_b, parts[0]), got1[1]))
     far.append(lax.ppermute(sent1[1], "feat", inner))
     lang = after(parts[0], sent1[1]) + sum(scattered)
     other = swap(lang, "feat", 1)
     got2.append(lax.ppermute(after(raw1[1], lang), "feat", inward))
-    sent3 = [onward(after(raw2[0], lang), far[0])]
+    raw2 = project(more_kernel, me_feat, 4, 2, acts2, grads2, [after(down, lang), out_sketch], [])
+    sent3 = [onward(raw2[0], far[0])]
     got3 = [swap(sent3[0], "feat", 1)]
     pair = small(stack_kernel, (2, *lang.shape), is_middle, [lang, after(other, sent3[0])])
-    far_pair = [lax.ppermute(pair, "feat", pairs) for pairs in (inner, [(1, 3), (2, 0)])]
+    far_pair = [lax.ppermute(pair, "feat", inner)]
+    far_pair.append(lax.ppermute(pair, "feat", [(1, 3), (2, 0)]))
     sent2 = [onward(after(raw1[0], pair), got2[0])]
     near = [lax.ppermute(sent2[0], "feat", inner)]
     pair = after(pair, sent2[0])

time: 85.6 us -> 85.6 us (level)
  transfers between devices with their start and end apart: 30 -> 30, of which waited for: 12 -> 12; matrix products, arithmetic and copies ran while one was open for 0% -> 0% of each run, Pallas kernels for 14% -> 15%
where the time goes in v11:
time: 85.6 us; the launch traced here: 85.3 us
  starting transfers between devices  44.6 us (52%)
  waiting for transfers between devices  22.9 us (27%)
  Pallas kernels  17.5 us (20%)
    ppermute x23, starting transfers between devices, swap(): lax.ppermute(x, axis, [(i, i ^ mask) for i in range(lax.axis_size(axis))])  35.4 us
    ppermute x23, waiting for transfers between devices, swap(): lax.ppermute(x, axis, [(i, i ^ mask) for i in range(lax.axis_size(axis))])  16.2 us
    pallas_call x4, Pallas kernels, project(): pl.pallas_call(kernel, out_shape=[jax.ShapeDtypeStruct(piece, jnp.float32...  13.6 us
    ppermute x1, waiting for transfers between devices, ordered(): far_pair.append(lax.ppermute(pair, 'feat', [(1, 3), (2, 0)]))  6.71 us
    ppermute x1, starting transfers between devices, ordered(): got2.append(lax.ppermute(after(raw1[1], lang), 'feat', inward))  4.58 us
  transfers between devices with their start and end apart: 30, of which 12 were waited for; matrix products, arithmetic and copies ran while one was open for 0% of the time, Pallas kernels for 15%

profile of v11, /device:TPU:0, one launch (start us, length us, event | category | flops | bytes accessed | tf_op | source)
XLA Modules:
  0.0 85.3 jit_solution(17483188531537570369)
XLA Ops:
  0.0 2.7 %project.4 = (f32[2,384,128]{2,1,0:T(8,128)S(1)}, bf16[1024,128]{1,0:T(8,128)(2,1)S(1)}, f32[32,1]{1,0:T(8,128)S(1)}) custom-call(s32[1]{0:T(128)} %bitcast.feat.feat_ref.me_ref, bf16[4096,1024]{1,0:T(8,128)(2,1)} %bitcast.24, bf16[4096,1024]{1,0:T(8,128)(2,1)} %bitcast.28, bf16[1024,128]{1,0:T(8,128)(2,1)} %adapter_ref.1, bf16[64,128]{1,0:T(8,128)(2,1)} %bitcast.32, ...), custom_call_target="tpu_custom_call" | custom-call | flops 268435456 | bytes 2490368 | tf_op jit(solution)/shard_map/project/pallas_call | solution.py:81
  2.7 3.1 %collective-permute-start.1 = (f32[2,384,128]{2,1,0:T(8,128)S(1)}, f32[2,384,128]{2,1,0:T(8,128)S(1)}, u32[]{:S(2)}, u32[]{:S(2)}) collective-permute-start(f32[2,384,128]{2,1,0:T(8,128)S(1)} %get-tuple-element.45.raw_ref), channel_id=1, source_target_pairs={{0,1},{1,0},{2,3},{3,2},{4,5},{5,4},{6,7},{7,6},{8,9},{9,8},{10,11... | collective-permute-start | bytes 1179656 | tf_op jit(solution)/shard_map/ppermute | solution.py:307
  5.8 2.5 %collective-permute-start.3 = (f32[32,1]{1,0:T(8,128)S(1)}, f32[32,1]{1,0:T(8,128)S(1)}, u32[]{:S(2)}, u32[]{:S(2)}) collective-permute-start(f32[32,1]{1,0:T(8,128)S(1)} %get-tuple-element.41.refs_0_), channel_id=1, source_target_pairs={{0,3},{1,2},{2,1},{3,0},{4,7},{5,6},{6,5},{7,4},{8,11},{9,10},{10,... | collective-permute-start | bytes 392 | tf_op jit(solution)/shard_map/ppermute | solution.py:307
  8.4 1.8 %collective-permute-start = (f32[32,1]{1,0:T(8,128)S(1)}, f32[32,1]{1,0:T(8,128)S(1)}, u32[]{:S(2)}, u32[]{:S(2)}) collective-permute-start(f32[32,1]{1,0:T(8,128)S(1)} %get-tuple-element.41.refs_0_), channel_id=1, source_target_pairs={{0,1},{1,0},{2,3},{3,2},{4,5},{5,4},{6,7},{7,6},{8,9},{9,8},{10,11... | collective-permute-start | bytes 392 | tf_op jit(solution)/shard_map/ppermute | solution.py:307
  10.2 4.7 %project.5 = (f32[2,384,128]{2,1,0:T(8,128)S(1)}, f32[2,384,128]{2,1,0:T(8,128)S(1)}, f32[2,384,128]{2,1,0:T(8,128)S(1)}) custom-call(s32[1]{0:T(128)} %bitcast.feat.feat_ref.me_ref, bf16[4096,1024]{1,0:T(8,128)(2,1)} %bitcast.25, bf16[4096,1024]{1,0:T(8,128)(2,1)} %bitcast.29, bf16[1024,128]{1,0:T(8,128)(2,1)S(1)} %get-tuple-element.67.down_ref, ...), custom_call_target="tpu_custom_call" | custom-call | flops 805306368 | bytes 7471104 | tf_op jit(solution)/shard_map/project/pallas_call | solution.py:81
  15.5 2.3 %collective-permute-done.3.refs_3_ = f32[32,1]{1,0:T(8,128)S(1)} collective-permute-done((f32[32,1]{1,0:T(8,128)S(1)}, f32[32,1]{1,0:T(8,128)S(1)}, u32[]{:S(2)}, u32[]{:S(2)}) %collective-permute-start.3) | collective-permute-done | bytes 160 | tf_op jit(solution)/shard_map/ppermute | solution.py:307
  19.8 1.6 %collective-permute-start.7 = (f32[64,256]{1,0:T(8,128)S(1)}, f32[64,256]{1,0:T(8,128)S(1)}, u32[]{:S(2)}, u32[]{:S(2)}) collective-permute-start(f32[64,256]{1,0:T(8,128)S(1)} %get-tuple-element.77), channel_id=1, source_target_pairs={{0,16},{4,20},{8,24},{12,28},{16,0},{20,4},{24,8},{28,12},{1,17},{... | collective-permute-start | bytes 196616 | tf_op jit(solution)/shard_map/ppermute | solution.py:307
  21.3 1.4 %collective-permute-start.8 = (f32[64,256]{1,0:T(8,128)S(1)}, f32[64,256]{1,0:T(8,128)S(1)}, u32[]{:S(2)}, u32[]{:S(2)}) collective-permute-start(f32[64,256]{1,0:T(8,128)S(1)} %get-tuple-element.78), channel_id=1, source_target_pairs={{0,24},{4,28},{8,16},{12,20},{16,8},{20,12},{24,0},{28,4},{1,25},{... | collective-permute-start | bytes 196616 | tf_op jit(solution)/shard_map/ppermute | solution.py:307
  23.3 6.4 %collective-permute-done.5.got_ref = f32[2,384,128]{2,1,0:T(8,128)S(1)} collective-permute-done((f32[2,384,128]{2,1,0:T(8,128)S(1)}, f32[2,384,128]{2,1,0:T(8,128)S(1)}, u32[]{:S(2)}, u32[]{:S(2)}) %collective-permute-start.5) | collective-permute-done | bytes 393248 | tf_op jit(solution)/shard_map/ppermute | solution.py:307
  30.6 1.4 %collective-permute-start.9 = (f32[64,256]{1,0:T(8,128)S(1)}, f32[64,256]{1,0:T(8,128)S(1)}, u32[]{:S(2)}, u32[]{:S(2)}) collective-permute-start(f32[64,256]{1,0:T(8,128)S(1)} %add_add_fusion.one_ref), channel_id=1, source_target_pairs={{0,1},{1,0},{2,3},{3,2},{4,5},{5,4},{6,7},{7,6},{8,9},{9,8},{10,11... | collective-permute-start | bytes 196616 | tf_op jit(solution)/shard_map/ppermute | solution.py:307
  32.6 4.6 %collective-permute-start.16 = (f32[2,384,128]{2,1,0:T(8,128)S(1)}, f32[2,384,128]{2,1,0:T(8,128)S(1)}, u32[]{:S(2)}, u32[]{:S(2)}) collective-permute-start(f32[2,384,128]{2,1,0:T(8,128)S(1)} %get-tuple-element.66.raw_ref), channel_id=1, source_target_pairs={{0,1},{3,2},{4,5},{7,6},{8,9},{11,10},{12,13},{15,14},{16,17},{19,... | collective-permute-start | bytes 1179656 | tf_op jit(solution)/shard_map/ppermute | solution.py:359
  37.2 3.1 %project.6 = (f32[2,384,128]{2,1,0:T(8,128)S(1)}, f32[2,384,128]{2,1,0:T(8,128)S(1)}) custom-call(s32[1]{0:T(128)} %bitcast.feat.feat_ref.me_ref, bf16[4096,1024]{1,0:T(8,128)(2,1)} %bitcast.26, bf16[4096,1024]{1,0:T(8,128)(2,1)} %bitcast.30, bf16[1024,128]{1,0:T(8,128)(2,1)S(1)} %get-tuple-element.67.down_ref, bf16[1024,128]{1,0:T(8,128)(2,1)} %sketch_ref.7), custom_call_target="tpu_custom_call" | custom-call | flops 536870912 | bytes 4980736 | tf_op jit(solution)/shard_map/project/pallas_call | solution.py:81
  40.4 1.3 %collective-permute-done.9.two_ref = f32[64,256]{1,0:T(8,128)S(1)} collective-permute-done((f32[64,256]{1,0:T(8,128)S(1)}, f32[64,256]{1,0:T(8,128)S(1)}, u32[]{:S(2)}, u32[]{:S(2)}) %collective-permute-start.9) | collective-permute-done | bytes 65568 | tf_op jit(solution)/shard_map/ppermute | solution.py:307
  41.7 1.3 %collective-permute-start.13 = (f32[2,64,256]{2,1,0:T(8,128)S(1)}, f32[2,64,256]{2,1,0:T(8,128)S(1)}, u32[]{:S(2)}, u32[]{:S(2)}) collective-permute-start(f32[2,64,256]{2,1,0:T(8,128)S(1)} %shard_map.76.pair_ref), channel_id=1, source_target_pairs={{1,3},{2,0},{5,7},{6,4},{9,11},{10,8},{13,15},{14,12},{17,19},{18,... | collective-permute-start | bytes 393224 | tf_op jit(solution)/shard_map/ppermute | solution.py:365
  43.8 6.7 %collective-permute-done.13.outer_ref = f32[2,64,256]{2,1,0:T(8,128)S(1)} collective-permute-done((f32[2,64,256]{2,1,0:T(8,128)S(1)}, f32[2,64,256]{2,1,0:T(8,128)S(1)}, u32[]{:S(2)}, u32[]{:S(2)}) %collective-permute-start.13) | collective-permute-done | bytes 131104 | tf_op jit(solution)/shard_map/ppermute | solution.py:365
  50.5 2.5 %collective-permute-start.20 = (f32[4,64,256]{2,1,0:T(8,128)S(1)}, f32[4,64,256]{2,1,0:T(8,128)S(1)}, u32[]{:S(2)}, u32[]{:S(2)}) collective-permute-start(f32[4,64,256]{2,1,0:T(8,128)S(1)} %shard_map.78.refs_0_), channel_id=1, source_target_pairs={{0,24},{4,28},{8,16},{12,20},{16,8},{20,12},{24,0},{28,4},{1,25},{... | collective-permute-start | bytes 786440 | tf_op jit(solution)/shard_map/ppermute | solution.py:307
  53.7 4.8 %collective-permute-start.17 = (f32[2,384,128]{2,1,0:T(8,128)S(1)}, f32[2,384,128]{2,1,0:T(8,128)S(1)}, u32[]{:S(2)}, u32[]{:S(2)}) collective-permute-start(f32[2,384,128]{2,1,0:T(8,128)S(1)} %shard_map.75), channel_id=1, source_target_pairs={{0,1},{1,0},{2,3},{3,2},{4,5},{5,4},{6,7},{7,6},{8,9},{9,8},{10,11... | collective-permute-start | bytes 1179656 | tf_op jit(solution)/shard_map/ppermute | solution.py:307
  59.6 6.8 %collective-permute-start.25 = (f32[2,384,128]{2,1,0:T(8,128)S(1)}, f32[2,384,128]{2,1,0:T(8,128)S(1)}, u32[]{:S(2)}, u32[]{:S(2)}) collective-permute-start(f32[2,384,128]{2,1,0:T(8,128)S(1)} %shard_map.79), channel_id=1, source_target_pairs={{0,1},{1,0},{2,3},{3,2},{4,5},{5,4},{6,7},{7,6},{8,9},{9,8},{10,11... | collective-permute-start | bytes 1179656 | tf_op jit(solution)/shard_map/ppermute | solution.py:307
  67.3 3.1 %project.7 = (f32[2,384,128]{2,1,0:T(8,128)S(1)}, f32[2,384,128]{2,1,0:T(8,128)S(1)}) custom-call(s32[1]{0:T(128)} %bitcast.feat.feat_ref.me_ref, bf16[4096,1024]{1,0:T(8,128)(2,1)} %bitcast.27, bf16[4096,1024]{1,0:T(8,128)(2,1)} %bitcast.31, bf16[1024,128]{1,0:T(8,128)(2,1)S(1)} %get-tuple-element.67.down_ref, bf16[1024,128]{1,0:T(8,128)(2,1)} %sketch_ref.7), custom_call_target="tpu_custom_call" | custom-call | flops 536870912 | bytes 4980736 | tf_op jit(solution)/shard_map/project/pallas_call | solution.py:81
  74.0 1.5 %score.1.refs_0_ = f32[16,64]{1,0:T(8,128)S(1)} custom-call(s32[1]{0:T(128)} %bitcast.1.middle_ref, bf16[32,128,256]{2,1,0:T(8,128)(2,1)S(1)} %split.1.lang_ref, bf16[32,16,256]{2,1,0:T(8,128)(2,1)S(1)} %get-tuple-element.73.grad_a, f32[8,1]{1,0:T(8,128)S(1)} %get-tuple-element.69.square_a, f32[2,384,128]{2,1,0:T(8,128)S(1)} %get-tuple-element.74.refs_0_, ...), custom_call_target="tpu_custom_call" | custom-call | tf_op jit(solution)/shard_map/score/pallas_call | solution.py:247
  75.5 2.0 %collective-permute-start.29 = (f32[16,64]{1,0:T(8,128)S(1)}, f32[16,64]{1,0:T(8,128)S(1)}, u32[]{:S(2)}, u32[]{:S(2)}) collective-permute-start(f32[16,64]{1,0:T(8,128)S(1)} %score.1.refs_0_), channel_id=1, source_target_pairs={{0,3},{1,2},{2,1},{3,0},{4,7},{5,6},{6,5},{7,4},{8,11},{9,10},{10,... | collective-permute-start | bytes 12296 | tf_op jit(solution)/shard_map/ppermute | solution.py:307
  77.4 3.6 %collective-permute-start.28 = (f32[16,64]{1,0:T(8,128)S(1)}, f32[16,64]{1,0:T(8,128)S(1)}, u32[]{:S(2)}, u32[]{:S(2)}) collective-permute-start(f32[16,64]{1,0:T(8,128)S(1)} %score.1.refs_0_), channel_id=1, source_target_pairs={{0,2},{1,3},{2,0},{3,1},{4,6},{5,7},{6,4},{7,5},{8,10},{9,11},{10,... | collective-permute-start | bytes 12296 | tf_op jit(solution)/shard_map/ppermute | solution.py:307
  81.0 1.7 %collective-permute-done.28.refs_2_ = f32[16,64]{1,0:T(8,128)S(1)} collective-permute-done((f32[16,64]{1,0:T(8,128)S(1)}, f32[16,64]{1,0:T(8,128)S(1)}, u32[]{:S(2)}, u32[]{:S(2)}) %collective-permute-start.28) | collective-permute-done | bytes 4128 | tf_op jit(solution)/shard_map/ppermute | solution.py:307
  82.8 1.9 %collective-permute-done.27.refs_1_ = f32[16,64]{1,0:T(8,128)S(1)} collective-permute-done((f32[16,64]{1,0:T(8,128)S(1)}, f32[16,64]{1,0:T(8,128)S(1)}, u32[]{:S(2)}, u32[]{:S(2)}) %collective-permute-start.27) | collective-permute-done | bytes 4128 | tf_op jit(solution)/shard_map/ppermute | solution.py:307
  (60 shorter events, 12.2 us)
Async XLA Ops:
  2.7 12.8 %collective-permute-start.1 = (f32[2,384,128]{2,1,0:T(8,128)S(1)}, f32[2,384,128]{2,1,0:T(8,128)S(1)}, u32[]{:S(2)}, u32[]{:S(2)}) collective-permute-start(f32[2,384,128]{2,1,0:T(8,128)S(1)} %get-tuple-element.45.raw_ref), channel_id=1, source_target_pairs={{0,1},{1,0},{2,3},{3,2},{4,5},{5,4},{6,7},{7,6},{8,9},{9,8},{10,11... | collective-permute-start | bytes 1179656 | tf_op jit(solution)/shard_map/ppermute | solution.py:307
  5.8 12.0 %collective-permute-start.3 = (f32[32,1]{1,0:T(8,128)S(1)}, f32[32,1]{1,0:T(8,128)S(1)}, u32[]{:S(2)}, u32[]{:S(2)}) collective-permute-start(f32[32,1]{1,0:T(8,128)S(1)} %get-tuple-element.41.refs_0_), channel_id=1, source_target_pairs={{0,3},{1,2},{2,1},{3,0},{4,7},{5,6},{6,5},{7,4},{8,11},{9,10},{10,... | collective-permute-start | bytes 392 | tf_op jit(solution)/shard_map/ppermute | solution.py:307
  8.3 9.5 %collective-permute-start.2 = (f32[32,1]{1,0:T(8,128)S(1)}, f32[32,1]{1,0:T(8,128)S(1)}, u32[]{:S(2)}, u32[]{:S(2)}) collective-permute-start(f32[32,1]{1,0:T(8,128)S(1)} %get-tuple-element.41.refs_0_), channel_id=1, source_target_pairs={{0,2},{1,3},{2,0},{3,1},{4,6},{5,7},{6,4},{7,5},{8,10},{9,11},{10,... | collective-permute-start | bytes 392 | tf_op jit(solution)/shard_map/ppermute | solution.py:307
  8.4 9.4 %collective-permute-start = (f32[32,1]{1,0:T(8,128)S(1)}, f32[32,1]{1,0:T(8,128)S(1)}, u32[]{:S(2)}, u32[]{:S(2)}) collective-permute-start(f32[32,1]{1,0:T(8,128)S(1)} %get-tuple-element.41.refs_0_), channel_id=1, source_target_pairs={{0,1},{1,0},{2,3},{3,2},{4,5},{5,4},{6,7},{7,6},{8,9},{9,8},{10,11... | collective-permute-start | bytes 392 | tf_op jit(solution)/shard_map/ppermute | solution.py:307
  18.2 11.5 %collective-permute-start.5 = (f32[2,384,128]{2,1,0:T(8,128)S(1)}, f32[2,384,128]{2,1,0:T(8,128)S(1)}, u32[]{:S(2)}, u32[]{:S(2)}) collective-permute-start(f32[2,384,128]{2,1,0:T(8,128)S(1)} %get-tuple-element.52.raw_ref), channel_id=1, source_target_pairs={{0,1},{1,0},{2,3},{3,2},{4,5},{5,4},{6,7},{7,6},{8,9},{9,8},{10,11... | collective-permute-start | bytes 1179656 | tf_op jit(solution)/shard_map/ppermute | solution.py:307
  19.0 21.4 %collective-permute-start.10 = (f32[2,384,128]{2,1,0:T(8,128)S(1)}, f32[2,384,128]{2,1,0:T(8,128)S(1)}, u32[]{:S(2)}, u32[]{:S(2)}) collective-permute-start(f32[2,384,128]{2,1,0:T(8,128)S(1)} %shard_map.73), channel_id=1, source_target_pairs={{1,2},{2,1},{0,0},{3,3},{5,6},{6,5},{4,4},{7,7},{9,10},{10,9},{8,8... | collective-permute-start | bytes 1179656 | tf_op jit(solution)/shard_map/ppermute | solution.py:348
  19.8 10.7 %collective-permute-start.7 = (f32[64,256]{1,0:T(8,128)S(1)}, f32[64,256]{1,0:T(8,128)S(1)}, u32[]{:S(2)}, u32[]{:S(2)}) collective-permute-start(f32[64,256]{1,0:T(8,128)S(1)} %get-tuple-element.77), channel_id=1, source_target_pairs={{0,16},{4,20},{8,24},{12,28},{16,0},{20,4},{24,8},{28,12},{1,17},{... | collective-permute-start | bytes 196616 | tf_op jit(solution)/shard_map/ppermute | solution.py:307
  21.3 9.2 %collective-permute-start.8 = (f32[64,256]{1,0:T(8,128)S(1)}, f32[64,256]{1,0:T(8,128)S(1)}, u32[]{:S(2)}, u32[]{:S(2)}) collective-permute-start(f32[64,256]{1,0:T(8,128)S(1)} %get-tuple-element.78), channel_id=1, source_target_pairs={{0,24},{4,28},{8,16},{12,20},{16,8},{20,12},{24,0},{28,4},{1,25},{... | collective-permute-start | bytes 196616 | tf_op jit(solution)/shard_map/ppermute | solution.py:307
  22.8 7.7 %collective-permute-start.6 = (f32[64,256]{1,0:T(8,128)S(1)}, f32[64,256]{1,0:T(8,128)S(1)}, u32[]{:S(2)}, u32[]{:S(2)}) collective-permute-start(f32[64,256]{1,0:T(8,128)S(1)} %get-tuple-element.79), channel_id=1, source_target_pairs={{0,8},{4,12},{8,0},{12,4},{16,24},{20,28},{24,16},{28,20},{1,9},{5... | collective-permute-start | bytes 196616 | tf_op jit(solution)/shard_map/ppermute | solution.py:307
  29.7 14.0 %collective-permute-start.11 = (f32[2,384,128]{2,1,0:T(8,128)S(1)}, f32[2,384,128]{2,1,0:T(8,128)S(1)}, u32[]{:S(2)}, u32[]{:S(2)}) collective-permute-start(f32[2,384,128]{2,1,0:T(8,128)S(1)} %get-tuple-element.61.raw_ref), channel_id=1, source_target_pairs={{0,1},{1,0},{2,3},{3,2},{4,5},{5,4},{6,7},{7,6},{8,9},{9,8},{10,11... | collective-permute-start | bytes 1179656 | tf_op jit(solution)/shard_map/ppermute | solution.py:307
  30.6 11.2 %collective-permute-start.9 = (f32[64,256]{1,0:T(8,128)S(1)}, f32[64,256]{1,0:T(8,128)S(1)}, u32[]{:S(2)}, u32[]{:S(2)}) collective-permute-start(f32[64,256]{1,0:T(8,128)S(1)} %add_add_fusion.one_ref), channel_id=1, source_target_pairs={{0,1},{1,0},{2,3},{3,2},{4,5},{5,4},{6,7},{7,6},{8,9},{9,8},{10,11... | collective-permute-start | bytes 196616 | tf_op jit(solution)/shard_map/ppermute | solution.py:307
  32.0 26.5 %collective-permute-start.15 = (f32[2,384,128]{2,1,0:T(8,128)S(1)}, f32[2,384,128]{2,1,0:T(8,128)S(1)}, u32[]{:S(2)}, u32[]{:S(2)}) collective-permute-start(f32[2,384,128]{2,1,0:T(8,128)S(1)} %shard_map.74), channel_id=1, source_target_pairs={{1,2},{2,1},{0,0},{3,3},{5,6},{6,5},{4,4},{7,7},{9,10},{10,9},{8,8... | collective-permute-start | bytes 1179656 | tf_op jit(solution)/shard_map/ppermute | solution.py:356
  32.6 26.4 %collective-permute-start.16 = (f32[2,384,128]{2,1,0:T(8,128)S(1)}, f32[2,384,128]{2,1,0:T(8,128)S(1)}, u32[]{:S(2)}, u32[]{:S(2)}) collective-permute-start(f32[2,384,128]{2,1,0:T(8,128)S(1)} %get-tuple-element.66.raw_ref), channel_id=1, source_target_pairs={{0,1},{3,2},{4,5},{7,6},{8,9},{11,10},{12,13},{15,14},{16,17},{19,... | collective-permute-start | bytes 1179656 | tf_op jit(solution)/shard_map/ppermute | solution.py:359
  41.7 8.8 %collective-permute-start.13 = (f32[2,64,256]{2,1,0:T(8,128)S(1)}, f32[2,64,256]{2,1,0:T(8,128)S(1)}, u32[]{:S(2)}, u32[]{:S(2)}) collective-permute-start(f32[2,64,256]{2,1,0:T(8,128)S(1)} %shard_map.76.pair_ref), channel_id=1, source_target_pairs={{1,3},{2,0},{5,7},{6,4},{9,11},{10,8},{13,15},{14,12},{17,19},{18,... | collective-permute-start | bytes 393224 | tf_op jit(solution)/shard_map/ppermute | solution.py:365
  43.0 7.5 %collective-permute-start.12 = (f32[2,64,256]{2,1,0:T(8,128)S(1)}, f32[2,64,256]{2,1,0:T(8,128)S(1)}, u32[]{:S(2)}, u32[]{:S(2)}) collective-permute-start(f32[2,64,256]{2,1,0:T(8,128)S(1)} %shard_map.76.pair_ref), channel_id=1, source_target_pairs={{1,2},{2,1},{0,0},{3,3},{5,6},{6,5},{4,4},{7,7},{9,10},{10,9},{8,8... | collective-permute-start | bytes 393224 | tf_op jit(solution)/shard_map/ppermute | solution.py:364
  50.5 9.0 %collective-permute-start.20 = (f32[4,64,256]{2,1,0:T(8,128)S(1)}, f32[4,64,256]{2,1,0:T(8,128)S(1)}, u32[]{:S(2)}, u32[]{:S(2)}) collective-permute-start(f32[4,64,256]{2,1,0:T(8,128)S(1)} %shard_map.78.refs_0_), channel_id=1, source_target_pairs={{0,24},{4,28},{8,16},{12,20},{16,8},{20,12},{24,0},{28,4},{1,25},{... | collective-permute-start | bytes 786440 | tf_op jit(solution)/shard_map/ppermute | solution.py:307
  53.0 6.6 %collective-permute-start.18 = (f32[2,384,128]{2,1,0:T(8,128)S(1)}, f32[2,384,128]{2,1,0:T(8,128)S(1)}, u32[]{:S(2)}, u32[]{:S(2)}) collective-permute-start(f32[2,384,128]{2,1,0:T(8,128)S(1)} %shard_map.77), channel_id=1, source_target_pairs={{1,2},{2,1},{0,0},{3,3},{5,6},{6,5},{4,4},{7,7},{9,10},{10,9},{8,8... | collective-permute-start | bytes 1179656 | tf_op jit(solution)/shard_map/ppermute | solution.py:367
  53.7 12.9 %collective-permute-start.17 = (f32[2,384,128]{2,1,0:T(8,128)S(1)}, f32[2,384,128]{2,1,0:T(8,128)S(1)}, u32[]{:S(2)}, u32[]{:S(2)}) collective-permute-start(f32[2,384,128]{2,1,0:T(8,128)S(1)} %shard_map.75), channel_id=1, source_target_pairs={{0,1},{1,0},{2,3},{3,2},{4,5},{5,4},{6,7},{7,6},{8,9},{9,8},{10,11... | collective-permute-start | bytes 1179656 | tf_op jit(solution)/shard_map/ppermute | solution.py:307
  58.5 12.8 %collective-permute-start.19 = (f32[4,64,256]{2,1,0:T(8,128)S(1)}, f32[4,64,256]{2,1,0:T(8,128)S(1)}, u32[]{:S(2)}, u32[]{:S(2)}) collective-permute-start(f32[4,64,256]{2,1,0:T(8,128)S(1)} %shard_map.78.refs_0_), channel_id=1, source_target_pairs={{0,16},{4,20},{8,24},{12,28},{16,0},{20,4},{24,8},{28,12},{1,17},{... | collective-permute-start | bytes 786440 | tf_op jit(solution)/shard_map/ppermute | solution.py:307
  59.0 12.2 %collective-permute-start.14 = (f32[4,64,256]{2,1,0:T(8,128)S(1)}, f32[4,64,256]{2,1,0:T(8,128)S(1)}, u32[]{:S(2)}, u32[]{:S(2)}) collective-permute-start(f32[4,64,256]{2,1,0:T(8,128)S(1)} %shard_map.78.refs_0_), channel_id=1, source_target_pairs={{0,8},{4,12},{8,0},{12,4},{16,24},{20,28},{24,16},{28,20},{1,9},{5... | collective-permute-start | bytes 786440 | tf_op jit(solution)/shard_map/ppermute | solution.py:307
  59.6 12.2 %collective-permute-start.21 = (f32[4,64,256]{2,1,0:T(8,128)S(1)}, f32[4,64,256]{2,1,0:T(8,128)S(1)}, u32[]{:S(2)}, u32[]{:S(2)}) collective-permute-start(f32[4,64,256]{2,1,0:T(8,128)S(1)} %shard_map.78.refs_0_), channel_id=1, source_target_pairs={{0,4},{4,0},{8,12},{12,8},{16,20},{20,16},{24,28},{28,24},{1,5},{5... | collective-permute-start | bytes 786440 | tf_op jit(solution)/shard_map/ppermute | solution.py:307
  59.6 14.3 %collective-permute-start.25 = (f32[2,384,128]{2,1,0:T(8,128)S(1)}, f32[2,384,128]{2,1,0:T(8,128)S(1)}, u32[]{:S(2)}, u32[]{:S(2)}) collective-permute-start(f32[2,384,128]{2,1,0:T(8,128)S(1)} %shard_map.79), channel_id=1, source_target_pairs={{0,1},{1,0},{2,3},{3,2},{4,5},{5,4},{6,7},{7,6},{8,9},{9,8},{10,11... | collective-permute-start | bytes 1179656 | tf_op jit(solution)/shard_map/ppermute | solution.py:307
  66.6 7.4 %collective-permute-start.26 = (f32[2,384,128]{2,1,0:T(8,128)S(1)}, f32[2,384,128]{2,1,0:T(8,128)S(1)}, u32[]{:S(2)}, u32[]{:S(2)}) collective-permute-start(f32[2,384,128]{2,1,0:T(8,128)S(1)} %shard_map.80), channel_id=1, source_target_pairs={{1,2},{2,1},{0,0},{3,3},{5,6},{6,5},{4,4},{7,7},{9,10},{10,9},{8,8... | collective-permute-start | bytes 1179656 | tf_op jit(solution)/shard_map/ppermute | solution.py:374
  75.5 5.6 %collective-permute-start.29 = (f32[16,64]{1,0:T(8,128)S(1)}, f32[16,64]{1,0:T(8,128)S(1)}, u32[]{:S(2)}, u32[]{:S(2)}) collective-permute-start(f32[16,64]{1,0:T(8,128)S(1)} %score.1.refs_0_), channel_id=1, source_target_pairs={{0,3},{1,2},{2,1},{3,0},{4,7},{5,6},{6,5},{7,4},{8,11},{9,10},{10,... | collective-permute-start | bytes 12296 | tf_op jit(solution)/shard_map/ppermute | solution.py:307
  (8 other events, 28.1 us)

commit v12 on v11

--- a/solution.py
+++ b/solution.py
@@ -358,12 +358,12 @@
     other = swap(lang, "feat", 1)
     got2.append(lax.ppermute(after(raw1[1], lang), "feat", inward))
     raw2 = project(more_kernel, me_feat, 4, 2, acts2, grads2, [after(down, lang), out_sketch], [])
-    sent3 = [onward(raw2[0], far[0])]
-    got3 = [swap(sent3[0], "feat", 1)]
-    pair = small(stack_kernel, (2, *lang.shape), is_middle, [lang, after(other, sent3[0])])
+    pair = small(stack_kernel, (2, *lang.shape), is_middle, [lang, after(other, raw2[0])])
     far_pair = [lax.ppermute(pair, "feat", inner)]
     far_pair.append(lax.ppermute(pair, "feat", [(1, 3), (2, 0)]))
-    sent2 = [onward(after(raw1[0], pair), got2[0])]
+    sent3 = [onward(after(raw2[0], pair), far[0])]
+    got3 = [swap(sent3[0], "feat", 1)]
+    sent2 = [onward(after(raw1[0], sent3[0]), got2[0])]
     near = [lax.ppermute(sent2[0], "feat", inner)]
     pair = after(pair, sent2[0])
     langs = [small(join_kernel, (4, *lang.shape), is_middle, [pair, *far_pair])]

time: 85.6 us -> 85.6 us (level)
  no operation moved by 1% of the time
where the time goes in v12:
time: 85.6 us; the launch traced here: 85.3 us
  starting transfers between devices  44.6 us (52%)
  waiting for transfers between devices  22.9 us (27%)
  Pallas kernels  17.5 us (20%)
    ppermute x23, starting transfers between devices, swap(): lax.ppermute(x, axis, [(i, i ^ mask) for i in range(lax.axis_size(axis))])  35.4 us
    ppermute x23, waiting for transfers between devices, swap(): lax.ppermute(x, axis, [(i, i ^ mask) for i in range(lax.axis_size(axis))])  16.2 us
    pallas_call x4, Pallas kernels, project(): pl.pallas_call(kernel, out_shape=[jax.ShapeDtypeStruct(piece, jnp.float32...  13.6 us
    ppermute x1, waiting for transfers between devices, ordered(): far_pair.append(lax.ppermute(pair, 'feat', [(1, 3), (2, 0)]))  6.62 us
    ppermute x1, starting transfers between devices, ordered(): got2.append(lax.ppermute(after(raw1[1], lang), 'feat', inward))  4.62 us
  transfers between devices with their start and end apart: 30, of which 12 were waited for; matrix products, arithmetic and copies ran while one was open for 0% of the time, Pallas kernels for 15%

profile of v12, /device:TPU:0, one launch (start us, length us, event | category | flops | bytes accessed | tf_op | source)
XLA Modules:
  0.0 85.3 jit_solution(7040739166865515200)
XLA Ops:
  0.0 2.7 %project.4 = (f32[2,384,128]{2,1,0:T(8,128)S(1)}, bf16[1024,128]{1,0:T(8,128)(2,1)S(1)}, f32[32,1]{1,0:T(8,128)S(1)}) custom-call(s32[1]{0:T(128)} %bitcast.feat.feat_ref.me_ref, bf16[4096,1024]{1,0:T(8,128)(2,1)} %bitcast.24, bf16[4096,1024]{1,0:T(8,128)(2,1)} %bitcast.28, bf16[1024,128]{1,0:T(8,128)(2,1)} %adapter_ref.1, bf16[64,128]{1,0:T(8,128)(2,1)} %bitcast.32, ...), custom_call_target="tpu_custom_call" | custom-call | flops 268435456 | bytes 2490368 | tf_op jit(solution)/shard_map/project/pallas_call | solution.py:81
  2.7 3.1 %collective-permute-start.1 = (f32[2,384,128]{2,1,0:T(8,128)S(1)}, f32[2,384,128]{2,1,0:T(8,128)S(1)}, u32[]{:S(2)}, u32[]{:S(2)}) collective-permute-start(f32[2,384,128]{2,1,0:T(8,128)S(1)} %get-tuple-element.46.raw_ref), channel_id=1, source_target_pairs={{0,1},{1,0},{2,3},{3,2},{4,5},{5,4},{6,7},{7,6},{8,9},{9,8},{10,11... | collective-permute-start | bytes 1179656 | tf_op jit(solution)/shard_map/ppermute | solution.py:307
  5.8 2.5 %collective-permute-start.3 = (f32[32,1]{1,0:T(8,128)S(1)}, f32[32,1]{1,0:T(8,128)S(1)}, u32[]{:S(2)}, u32[]{:S(2)}) collective-permute-start(f32[32,1]{1,0:T(8,128)S(1)} %get-tuple-element.42.refs_0_), channel_id=1, source_target_pairs={{0,3},{1,2},{2,1},{3,0},{4,7},{5,6},{6,5},{7,4},{8,11},{9,10},{10,... | collective-permute-start | bytes 392 | tf_op jit(solution)/shard_map/ppermute | solution.py:307
  8.4 1.8 %collective-permute-start = (f32[32,1]{1,0:T(8,128)S(1)}, f32[32,1]{1,0:T(8,128)S(1)}, u32[]{:S(2)}, u32[]{:S(2)}) collective-permute-start(f32[32,1]{1,0:T(8,128)S(1)} %get-tuple-element.42.refs_0_), channel_id=1, source_target_pairs={{0,1},{1,0},{2,3},{3,2},{4,5},{5,4},{6,7},{7,6},{8,9},{9,8},{10,11... | collective-permute-start | bytes 392 | tf_op jit(solution)/shard_map/ppermute | solution.py:307
  10.2 4.7 %project.5 = (f32[2,384,128]{2,1,0:T(8,128)S(1)}, f32[2,384,128]{2,1,0:T(8,128)S(1)}, f32[2,384,128]{2,1,0:T(8,128)S(1)}) custom-call(s32[1]{0:T(128)} %bitcast.feat.feat_ref.me_ref, bf16[4096,1024]{1,0:T(8,128)(2,1)} %bitcast.25, bf16[4096,1024]{1,0:T(8,128)(2,1)} %bitcast.29, bf16[1024,128]{1,0:T(8,128)(2,1)S(1)} %get-tuple-element.69.down_ref, ...), custom_call_target="tpu_custom_call" | custom-call | flops 805306368 | bytes 7471104 | tf_op jit(solution)/shard_map/project/pallas_call | solution.py:81
  15.5 2.3 %collective-permute-done.3.refs_3_ = f32[32,1]{1,0:T(8,128)S(1)} collective-permute-done((f32[32,1]{1,0:T(8,128)S(1)}, f32[32,1]{1,0:T(8,128)S(1)}, u32[]{:S(2)}, u32[]{:S(2)}) %collective-permute-start.3) | collective-permute-done | bytes 160 | tf_op jit(solution)/shard_map/ppermute | solution.py:307
  19.8 1.6 %collective-permute-start.7 = (f32[64,256]{1,0:T(8,128)S(1)}, f32[64,256]{1,0:T(8,128)S(1)}, u32[]{:S(2)}, u32[]{:S(2)}) collective-permute-start(f32[64,256]{1,0:T(8,128)S(1)} %get-tuple-element.79), channel_id=1, source_target_pairs={{0,16},{4,20},{8,24},{12,28},{16,0},{20,4},{24,8},{28,12},{1,17},{... | collective-permute-start | bytes 196616 | tf_op jit(solution)/shard_map/ppermute | solution.py:307
  21.4 1.4 %collective-permute-start.8 = (f32[64,256]{1,0:T(8,128)S(1)}, f32[64,256]{1,0:T(8,128)S(1)}, u32[]{:S(2)}, u32[]{:S(2)}) collective-permute-start(f32[64,256]{1,0:T(8,128)S(1)} %get-tuple-element.80), channel_id=1, source_target_pairs={{0,24},{4,28},{8,16},{12,20},{16,8},{20,12},{24,0},{28,4},{1,25},{... | collective-permute-start | bytes 196616 | tf_op jit(solution)/shard_map/ppermute | solution.py:307
  23.3 6.4 %collective-permute-done.5.got_ref = f32[2,384,128]{2,1,0:T(8,128)S(1)} collective-permute-done((f32[2,384,128]{2,1,0:T(8,128)S(1)}, f32[2,384,128]{2,1,0:T(8,128)S(1)}, u32[]{:S(2)}, u32[]{:S(2)}) %collective-permute-start.5) | collective-permute-done | bytes 393248 | tf_op jit(solution)/shard_map/ppermute | solution.py:307
  30.6 1.4 %collective-permute-start.9 = (f32[64,256]{1,0:T(8,128)S(1)}, f32[64,256]{1,0:T(8,128)S(1)}, u32[]{:S(2)}, u32[]{:S(2)}) collective-permute-start(f32[64,256]{1,0:T(8,128)S(1)} %add_add_fusion.one_ref), channel_id=1, source_target_pairs={{0,1},{1,0},{2,3},{3,2},{4,5},{5,4},{6,7},{7,6},{8,9},{9,8},{10,11... | collective-permute-start | bytes 196616 | tf_op jit(solution)/shard_map/ppermute | solution.py:307
  32.6 4.6 %collective-permute-start.16 = (f32[2,384,128]{2,1,0:T(8,128)S(1)}, f32[2,384,128]{2,1,0:T(8,128)S(1)}, u32[]{:S(2)}, u32[]{:S(2)}) collective-permute-start(f32[2,384,128]{2,1,0:T(8,128)S(1)} %get-tuple-element.68.raw_ref), channel_id=1, source_target_pairs={{0,1},{3,2},{4,5},{7,6},{8,9},{11,10},{12,13},{15,14},{16,17},{19,... | collective-permute-start | bytes 1179656 | tf_op jit(solution)/shard_map/ppermute | solution.py:359
  37.2 3.1 %project.6 = (f32[2,384,128]{2,1,0:T(8,128)S(1)}, f32[2,384,128]{2,1,0:T(8,128)S(1)}) custom-call(s32[1]{0:T(128)} %bitcast.feat.feat_ref.me_ref, bf16[4096,1024]{1,0:T(8,128)(2,1)} %bitcast.26, bf16[4096,1024]{1,0:T(8,128)(2,1)} %bitcast.30, bf16[1024,128]{1,0:T(8,128)(2,1)S(1)} %get-tuple-element.69.down_ref, bf16[1024,128]{1,0:T(8,128)(2,1)} %sketch_ref.7), custom_call_target="tpu_custom_call" | custom-call | flops 536870912 | bytes 4980736 | tf_op jit(solution)/shard_map/project/pallas_call | solution.py:81
  40.4 1.3 %collective-permute-done.9.two_ref = f32[64,256]{1,0:T(8,128)S(1)} collective-permute-done((f32[64,256]{1,0:T(8,128)S(1)}, f32[64,256]{1,0:T(8,128)S(1)}, u32[]{:S(2)}, u32[]{:S(2)}) %collective-permute-start.9) | collective-permute-done | bytes 65568 | tf_op jit(solution)/shard_map/ppermute | solution.py:307
  41.7 1.3 %collective-permute-start.13 = (f32[2,64,256]{2,1,0:T(8,128)S(1)}, f32[2,64,256]{2,1,0:T(8,128)S(1)}, u32[]{:S(2)}, u32[]{:S(2)}) collective-permute-start(f32[2,64,256]{2,1,0:T(8,128)S(1)} %shard_map.75.pair_ref), channel_id=1, source_target_pairs={{1,3},{2,0},{5,7},{6,4},{9,11},{10,8},{13,15},{14,12},{17,19},{18,... | collective-permute-start | bytes 393224 | tf_op jit(solution)/shard_map/ppermute | solution.py:363
  43.9 6.6 %collective-permute-done.13.outer_ref = f32[2,64,256]{2,1,0:T(8,128)S(1)} collective-permute-done((f32[2,64,256]{2,1,0:T(8,128)S(1)}, f32[2,64,256]{2,1,0:T(8,128)S(1)}, u32[]{:S(2)}, u32[]{:S(2)}) %collective-permute-start.13) | collective-permute-done | bytes 131104 | tf_op jit(solution)/shard_map/ppermute | solution.py:363
  50.5 2.5 %collective-permute-start.20 = (f32[4,64,256]{2,1,0:T(8,128)S(1)}, f32[4,64,256]{2,1,0:T(8,128)S(1)}, u32[]{:S(2)}, u32[]{:S(2)}) collective-permute-start(f32[4,64,256]{2,1,0:T(8,128)S(1)} %shard_map.78.refs_0_), channel_id=1, source_target_pairs={{0,24},{4,28},{8,16},{12,20},{16,8},{20,12},{24,0},{28,4},{1,25},{... | collective-permute-start | bytes 786440 | tf_op jit(solution)/shard_map/ppermute | solution.py:307
  53.7 4.8 %collective-permute-start.17 = (f32[2,384,128]{2,1,0:T(8,128)S(1)}, f32[2,384,128]{2,1,0:T(8,128)S(1)}, u32[]{:S(2)}, u32[]{:S(2)}) collective-permute-start(f32[2,384,128]{2,1,0:T(8,128)S(1)} %shard_map.76), channel_id=1, source_target_pairs={{0,1},{1,0},{2,3},{3,2},{4,5},{5,4},{6,7},{7,6},{8,9},{9,8},{10,11... | collective-permute-start | bytes 1179656 | tf_op jit(solution)/shard_map/ppermute | solution.py:307
  59.6 6.8 %collective-permute-start.25 = (f32[2,384,128]{2,1,0:T(8,128)S(1)}, f32[2,384,128]{2,1,0:T(8,128)S(1)}, u32[]{:S(2)}, u32[]{:S(2)}) collective-permute-start(f32[2,384,128]{2,1,0:T(8,128)S(1)} %shard_map.79), channel_id=1, source_target_pairs={{0,1},{1,0},{2,3},{3,2},{4,5},{5,4},{6,7},{7,6},{8,9},{9,8},{10,11... | collective-permute-start | bytes 1179656 | tf_op jit(solution)/shard_map/ppermute | solution.py:307
  67.3 3.1 %project.7 = (f32[2,384,128]{2,1,0:T(8,128)S(1)}, f32[2,384,128]{2,1,0:T(8,128)S(1)}) custom-call(s32[1]{0:T(128)} %bitcast.feat.feat_ref.me_ref, bf16[4096,1024]{1,0:T(8,128)(2,1)} %bitcast.27, bf16[4096,1024]{1,0:T(8,128)(2,1)} %bitcast.31, bf16[1024,128]{1,0:T(8,128)(2,1)S(1)} %get-tuple-element.69.down_ref, bf16[1024,128]{1,0:T(8,128)(2,1)} %sketch_ref.7), custom_call_target="tpu_custom_call" | custom-call | flops 536870912 | bytes 4980736 | tf_op jit(solution)/shard_map/project/pallas_call | solution.py:81
  74.0 1.5 %score.1.refs_0_ = f32[16,64]{1,0:T(8,128)S(1)} custom-call(s32[1]{0:T(128)} %bitcast.1.middle_ref, bf16[32,128,256]{2,1,0:T(8,128)(2,1)S(1)} %split.1.lang_ref, bf16[32,16,256]{2,1,0:T(8,128)(2,1)S(1)} %get-tuple-element.75.grad_a, f32[8,1]{1,0:T(8,128)S(1)} %get-tuple-element.71.square_a, f32[2,384,128]{2,1,0:T(8,128)S(1)} %get-tuple-element.76.refs_0_, ...), custom_call_target="tpu_custom_call" | custom-call | tf_op jit(solution)/shard_map/score/pallas_call | solution.py:247
  75.5 2.0 %collective-permute-start.29 = (f32[16,64]{1,0:T(8,128)S(1)}, f32[16,64]{1,0:T(8,128)S(1)}, u32[]{:S(2)}, u32[]{:S(2)}) collective-permute-start(f32[16,64]{1,0:T(8,128)S(1)} %score.1.refs_0_), channel_id=1, source_target_pairs={{0,3},{1,2},{2,1},{3,0},{4,7},{5,6},{6,5},{7,4},{8,11},{9,10},{10,... | collective-permute-start | bytes 12296 | tf_op jit(solution)/shard_map/ppermute | solution.py:307
  77.4 3.6 %collective-permute-start.28 = (f32[16,64]{1,0:T(8,128)S(1)}, f32[16,64]{1,0:T(8,128)S(1)}, u32[]{:S(2)}, u32[]{:S(2)}) collective-permute-start(f32[16,64]{1,0:T(8,128)S(1)} %score.1.refs_0_), channel_id=1, source_target_pairs={{0,2},{1,3},{2,0},{3,1},{4,6},{5,7},{6,4},{7,5},{8,10},{9,11},{10,... | collective-permute-start | bytes 12296 | tf_op jit(solution)/shard_map/ppermute | solution.py:307
  81.1 1.7 %collective-permute-done.28.refs_2_ = f32[16,64]{1,0:T(8,128)S(1)} collective-permute-done((f32[16,64]{1,0:T(8,128)S(1)}, f32[16,64]{1,0:T(8,128)S(1)}, u32[]{:S(2)}, u32[]{:S(2)}) %collective-permute-start.28) | collective-permute-done | bytes 4128 | tf_op jit(solution)/shard_map/ppermute | solution.py:307
  82.8 1.9 %collective-permute-done.27.refs_1_ = f32[16,64]{1,0:T(8,128)S(1)} collective-permute-done((f32[16,64]{1,0:T(8,128)S(1)}, f32[16,64]{1,0:T(8,128)S(1)}, u32[]{:S(2)}, u32[]{:S(2)}) %collective-permute-start.27) | collective-permute-done | bytes 4128 | tf_op jit(solution)/shard_map/ppermute | solution.py:307
  (60 shorter events, 12.2 us)
Async XLA Ops:
  2.7 12.8 %collective-permute-start.1 = (f32[2,384,128]{2,1,0:T(8,128)S(1)}, f32[2,384,128]{2,1,0:T(8,128)S(1)}, u32[]{:S(2)}, u32[]{:S(2)}) collective-permute-start(f32[2,384,128]{2,1,0:T(8,128)S(1)} %get-tuple-element.46.raw_ref), channel_id=1, source_target_pairs={{0,1},{1,0},{2,3},{3,2},{4,5},{5,4},{6,7},{7,6},{8,9},{9,8},{10,11... | collective-permute-start | bytes 1179656 | tf_op jit(solution)/shard_map/ppermute | solution.py:307
  5.8 12.0 %collective-permute-start.3 = (f32[32,1]{1,0:T(8,128)S(1)}, f32[32,1]{1,0:T(8,128)S(1)}, u32[]{:S(2)}, u32[]{:S(2)}) collective-permute-start(f32[32,1]{1,0:T(8,128)S(1)} %get-tuple-element.42.refs_0_), channel_id=1, source_target_pairs={{0,3},{1,2},{2,1},{3,0},{4,7},{5,6},{6,5},{7,4},{8,11},{9,10},{10,... | collective-permute-start | bytes 392 | tf_op jit(solution)/shard_map/ppermute | solution.py:307
  8.3 9.5 %collective-permute-start.2 = (f32[32,1]{1,0:T(8,128)S(1)}, f32[32,1]{1,0:T(8,128)S(1)}, u32[]{:S(2)}, u32[]{:S(2)}) collective-permute-start(f32[32,1]{1,0:T(8,128)S(1)} %get-tuple-element.42.refs_0_), channel_id=1, source_target_pairs={{0,2},{1,3},{2,0},{3,1},{4,6},{5,7},{6,4},{7,5},{8,10},{9,11},{10,... | collective-permute-start | bytes 392 | tf_op jit(solution)/shard_map/ppermute | solution.py:307
  8.4 9.4 %collective-permute-start = (f32[32,1]{1,0:T(8,128)S(1)}, f32[32,1]{1,0:T(8,128)S(1)}, u32[]{:S(2)}, u32[]{:S(2)}) collective-permute-start(f32[32,1]{1,0:T(8,128)S(1)} %get-tuple-element.42.refs_0_), channel_id=1, source_target_pairs={{0,1},{1,0},{2,3},{3,2},{4,5},{5,4},{6,7},{7,6},{8,9},{9,8},{10,11... | collective-permute-start | bytes 392 | tf_op jit(solution)/shard_map/ppermute | solution.py:307
  18.2 11.5 %collective-permute-start.5 = (f32[2,384,128]{2,1,0:T(8,128)S(1)}, f32[2,384,128]{2,1,0:T(8,128)S(1)}, u32[]{:S(2)}, u32[]{:S(2)}) collective-permute-start(f32[2,384,128]{2,1,0:T(8,128)S(1)} %get-tuple-element.53.raw_ref), channel_id=1, source_target_pairs={{0,1},{1,0},{2,3},{3,2},{4,5},{5,4},{6,7},{7,6},{8,9},{9,8},{10,11... | collective-permute-start | bytes 1179656 | tf_op jit(solution)/shard_map/ppermute | solution.py:307
  19.0 24.0 %collective-permute-start.10 = (f32[2,384,128]{2,1,0:T(8,128)S(1)}, f32[2,384,128]{2,1,0:T(8,128)S(1)}, u32[]{:S(2)}, u32[]{:S(2)}) collective-permute-start(f32[2,384,128]{2,1,0:T(8,128)S(1)} %shard_map.73), channel_id=1, source_target_pairs={{1,2},{2,1},{0,0},{3,3},{5,6},{6,5},{4,4},{7,7},{9,10},{10,9},{8,8... | collective-permute-start | bytes 1179656 | tf_op jit(solution)/shard_map/ppermute | solution.py:348
  19.8 10.7 %collective-permute-start.7 = (f32[64,256]{1,0:T(8,128)S(1)}, f32[64,256]{1,0:T(8,128)S(1)}, u32[]{:S(2)}, u32[]{:S(2)}) collective-permute-start(f32[64,256]{1,0:T(8,128)S(1)} %get-tuple-element.79), channel_id=1, source_target_pairs={{0,16},{4,20},{8,24},{12,28},{16,0},{20,4},{24,8},{28,12},{1,17},{... | collective-permute-start | bytes 196616 | tf_op jit(solution)/shard_map/ppermute | solution.py:307
  21.4 9.2 %collective-permute-start.8 = (f32[64,256]{1,0:T(8,128)S(1)}, f32[64,256]{1,0:T(8,128)S(1)}, u32[]{:S(2)}, u32[]{:S(2)}) collective-permute-start(f32[64,256]{1,0:T(8,128)S(1)} %get-tuple-element.80), channel_id=1, source_target_pairs={{0,24},{4,28},{8,16},{12,20},{16,8},{20,12},{24,0},{28,4},{1,25},{... | collective-permute-start | bytes 196616 | tf_op jit(solution)/shard_map/ppermute | solution.py:307
  22.8 7.7 %collective-permute-start.6 = (f32[64,256]{1,0:T(8,128)S(1)}, f32[64,256]{1,0:T(8,128)S(1)}, u32[]{:S(2)}, u32[]{:S(2)}) collective-permute-start(f32[64,256]{1,0:T(8,128)S(1)} %get-tuple-element.81), channel_id=1, source_target_pairs={{0,8},{4,12},{8,0},{12,4},{16,24},{20,28},{24,16},{28,20},{1,9},{5... | collective-permute-start | bytes 196616 | tf_op jit(solution)/shard_map/ppermute | solution.py:307
  29.7 14.1 %collective-permute-start.11 = (f32[2,384,128]{2,1,0:T(8,128)S(1)}, f32[2,384,128]{2,1,0:T(8,128)S(1)}, u32[]{:S(2)}, u32[]{:S(2)}) collective-permute-start(f32[2,384,128]{2,1,0:T(8,128)S(1)} %get-tuple-element.63.raw_ref), channel_id=1, source_target_pairs={{0,1},{1,0},{2,3},{3,2},{4,5},{5,4},{6,7},{7,6},{8,9},{9,8},{10,11... | collective-permute-start | bytes 1179656 | tf_op jit(solution)/shard_map/ppermute | solution.py:307
  30.6 11.2 %collective-permute-start.9 = (f32[64,256]{1,0:T(8,128)S(1)}, f32[64,256]{1,0:T(8,128)S(1)}, u32[]{:S(2)}, u32[]{:S(2)}) collective-permute-start(f32[64,256]{1,0:T(8,128)S(1)} %add_add_fusion.one_ref), channel_id=1, source_target_pairs={{0,1},{1,0},{2,3},{3,2},{4,5},{5,4},{6,7},{7,6},{8,9},{9,8},{10,11... | collective-permute-start | bytes 196616 | tf_op jit(solution)/shard_map/ppermute | solution.py:307
  31.9 26.6 %collective-permute-start.15 = (f32[2,384,128]{2,1,0:T(8,128)S(1)}, f32[2,384,128]{2,1,0:T(8,128)S(1)}, u32[]{:S(2)}, u32[]{:S(2)}) collective-permute-start(f32[2,384,128]{2,1,0:T(8,128)S(1)} %shard_map.74), channel_id=1, source_target_pairs={{1,2},{2,1},{0,0},{3,3},{5,6},{6,5},{4,4},{7,7},{9,10},{10,9},{8,8... | collective-permute-start | bytes 1179656 | tf_op jit(solution)/shard_map/ppermute | solution.py:356
  32.6 26.4 %collective-permute-start.16 = (f32[2,384,128]{2,1,0:T(8,128)S(1)}, f32[2,384,128]{2,1,0:T(8,128)S(1)}, u32[]{:S(2)}, u32[]{:S(2)}) collective-permute-start(f32[2,384,128]{2,1,0:T(8,128)S(1)} %get-tuple-element.68.raw_ref), channel_id=1, source_target_pairs={{0,1},{3,2},{4,5},{7,6},{8,9},{11,10},{12,13},{15,14},{16,17},{19,... | collective-permute-start | bytes 1179656 | tf_op jit(solution)/shard_map/ppermute | solution.py:359
  41.7 8.7 %collective-permute-start.13 = (f32[2,64,256]{2,1,0:T(8,128)S(1)}, f32[2,64,256]{2,1,0:T(8,128)S(1)}, u32[]{:S(2)}, u32[]{:S(2)}) collective-permute-start(f32[2,64,256]{2,1,0:T(8,128)S(1)} %shard_map.75.pair_ref), channel_id=1, source_target_pairs={{1,3},{2,0},{5,7},{6,4},{9,11},{10,8},{13,15},{14,12},{17,19},{18,... | collective-permute-start | bytes 393224 | tf_op jit(solution)/shard_map/ppermute | solution.py:363
  43.0 7.4 %collective-permute-start.12 = (f32[2,64,256]{2,1,0:T(8,128)S(1)}, f32[2,64,256]{2,1,0:T(8,128)S(1)}, u32[]{:S(2)}, u32[]{:S(2)}) collective-permute-start(f32[2,64,256]{2,1,0:T(8,128)S(1)} %shard_map.75.pair_ref), channel_id=1, source_target_pairs={{1,2},{2,1},{0,0},{3,3},{5,6},{6,5},{4,4},{7,7},{9,10},{10,9},{8,8... | collective-permute-start | bytes 393224 | tf_op jit(solution)/shard_map/ppermute | solution.py:362
  50.5 9.1 %collective-permute-start.20 = (f32[4,64,256]{2,1,0:T(8,128)S(1)}, f32[4,64,256]{2,1,0:T(8,128)S(1)}, u32[]{:S(2)}, u32[]{:S(2)}) collective-permute-start(f32[4,64,256]{2,1,0:T(8,128)S(1)} %shard_map.78.refs_0_), channel_id=1, source_target_pairs={{0,24},{4,28},{8,16},{12,20},{16,8},{20,12},{24,0},{28,4},{1,25},{... | collective-permute-start | bytes 786440 | tf_op jit(solution)/shard_map/ppermute | solution.py:307
  53.0 6.6 %collective-permute-start.18 = (f32[2,384,128]{2,1,0:T(8,128)S(1)}, f32[2,384,128]{2,1,0:T(8,128)S(1)}, u32[]{:S(2)}, u32[]{:S(2)}) collective-permute-start(f32[2,384,128]{2,1,0:T(8,128)S(1)} %shard_map.77), channel_id=1, source_target_pairs={{1,2},{2,1},{0,0},{3,3},{5,6},{6,5},{4,4},{7,7},{9,10},{10,9},{8,8... | collective-permute-start | bytes 1179656 | tf_op jit(solution)/shard_map/ppermute | solution.py:367
  53.7 12.9 %collective-permute-start.17 = (f32[2,384,128]{2,1,0:T(8,128)S(1)}, f32[2,384,128]{2,1,0:T(8,128)S(1)}, u32[]{:S(2)}, u32[]{:S(2)}) collective-permute-start(f32[2,384,128]{2,1,0:T(8,128)S(1)} %shard_map.76), channel_id=1, source_target_pairs={{0,1},{1,0},{2,3},{3,2},{4,5},{5,4},{6,7},{7,6},{8,9},{9,8},{10,11... | collective-permute-start | bytes 1179656 | tf_op jit(solution)/shard_map/ppermute | solution.py:307
  58.5 12.7 %collective-permute-start.19 = (f32[4,64,256]{2,1,0:T(8,128)S(1)}, f32[4,64,256]{2,1,0:T(8,128)S(1)}, u32[]{:S(2)}, u32[]{:S(2)}) collective-permute-start(f32[4,64,256]{2,1,0:T(8,128)S(1)} %shard_map.78.refs_0_), channel_id=1, source_target_pairs={{0,16},{4,20},{8,24},{12,28},{16,0},{20,4},{24,8},{28,12},{1,17},{... | collective-permute-start | bytes 786440 | tf_op jit(solution)/shard_map/ppermute | solution.py:307
  59.0 12.2 %collective-permute-start.14 = (f32[4,64,256]{2,1,0:T(8,128)S(1)}, f32[4,64,256]{2,1,0:T(8,128)S(1)}, u32[]{:S(2)}, u32[]{:S(2)}) collective-permute-start(f32[4,64,256]{2,1,0:T(8,128)S(1)} %shard_map.78.refs_0_), channel_id=1, source_target_pairs={{0,8},{4,12},{8,0},{12,4},{16,24},{20,28},{24,16},{28,20},{1,9},{5... | collective-permute-start | bytes 786440 | tf_op jit(solution)/shard_map/ppermute | solution.py:307
  59.6 12.2 %collective-permute-start.21 = (f32[4,64,256]{2,1,0:T(8,128)S(1)}, f32[4,64,256]{2,1,0:T(8,128)S(1)}, u32[]{:S(2)}, u32[]{:S(2)}) collective-permute-start(f32[4,64,256]{2,1,0:T(8,128)S(1)} %shard_map.78.refs_0_), channel_id=1, source_target_pairs={{0,4},{4,0},{8,12},{12,8},{16,20},{20,16},{24,28},{28,24},{1,5},{5... | collective-permute-start | bytes 786440 | tf_op jit(solution)/shard_map/ppermute | solution.py:307
  59.6 14.3 %collective-permute-start.25 = (f32[2,384,128]{2,1,0:T(8,128)S(1)}, f32[2,384,128]{2,1,0:T(8,128)S(1)}, u32[]{:S(2)}, u32[]{:S(2)}) collective-permute-start(f32[2,384,128]{2,1,0:T(8,128)S(1)} %shard_map.79), channel_id=1, source_target_pairs={{0,1},{1,0},{2,3},{3,2},{4,5},{5,4},{6,7},{7,6},{8,9},{9,8},{10,11... | collective-permute-start | bytes 1179656 | tf_op jit(solution)/shard_map/ppermute | solution.py:307
  66.6 7.3 %collective-permute-start.26 = (f32[2,384,128]{2,1,0:T(8,128)S(1)}, f32[2,384,128]{2,1,0:T(8,128)S(1)}, u32[]{:S(2)}, u32[]{:S(2)}) collective-permute-start(f32[2,384,128]{2,1,0:T(8,128)S(1)} %shard_map.80), channel_id=1, source_target_pairs={{1,2},{2,1},{0,0},{3,3},{5,6},{6,5},{4,4},{7,7},{9,10},{10,9},{8,8... | collective-permute-start | bytes 1179656 | tf_op jit(solution)/shard_map/ppermute | solution.py:374
  75.5 5.6 %collective-permute-start.29 = (f32[16,64]{1,0:T(8,128)S(1)}, f32[16,64]{1,0:T(8,128)S(1)}, u32[]{:S(2)}, u32[]{:S(2)}) collective-permute-start(f32[16,64]{1,0:T(8,128)S(1)} %score.1.refs_0_), channel_id=1, source_target_pairs={{0,3},{1,2},{2,1},{3,0},{4,7},{5,6},{6,5},{7,4},{8,11},{9,10},{10,... | collective-permute-start | bytes 12296 | tf_op jit(solution)/shard_map/ppermute | solution.py:307
  (8 other events, 28.1 us)

commit v13 on v12

--- a/solution.py
+++ b/solution.py
@@ -341,8 +341,9 @@
     )
     got1 = [swap(raw0_a, "feat", 1)]
     squares = [own_square] + [swap(own_square, "feat", mask) for mask in (1, 2, 3)]
-    raw0_b, *raw1 = project(more_kernel, me_feat, 1, 3, acts2, grads2, [down, out_sketch], [])
+    [raw0_b] = project(more_kernel, me_feat, 1, 1, acts2, grads2, [down, out_sketch], [])
     got1.append(swap(raw0_b, "feat", 1))
+    raw1 = project(more_kernel, me_feat, 2, 2, acts2, grads2, [after(down, raw0_b), out_sketch], [])
     got2 = [swap(raw1[0], "feat", 1)]
     sent1 = [onward(after(raw0_a, raw1[1]), got1[0])]
     far = [lax.ppermute(sent1[0], "feat", inner)]
@@ -357,7 +358,9 @@
     lang = after(parts[0], sent1[1]) + sum(scattered)
     other = swap(lang, "feat", 1)
     got2.append(lax.ppermute(after(raw1[1], lang), "feat", inward))
-    raw2 = project(more_kernel, me_feat, 4, 2, acts2, grads2, [after(down, lang), out_sketch], [])
+    *raw2, own_a, own_b = project(
+        more_kernel, me_feat, 4, 4, acts2, grads2, [after(down, lang), out_sketch], []
+    )
     pair = small(stack_kernel, (2, *lang.shape), is_middle, [lang, after(other, raw2[0])])
     far_pair = [lax.ppermute(pair, "feat", inner)]
     far_pair.append(lax.ppermute(pair, "feat", [(1, 3), (2, 0)]))
@@ -372,8 +375,7 @@
     got3.append(swap(sent3[1], "feat", 1))
     sent2.append(onward(after(raw1[1], sent3[1]), got2[1]))
     near.append(lax.ppermute(sent2[1], "feat", inner))
-    own_a, own_b = project(more_kernel, me_feat, 6, 2, acts2, grads2, [after(down, sent2[1]), out_sketch], [])
-    grad_a, square_a = product(is_middle, [own_a, got3[0], near[0]])
+    grad_a, square_a = product(is_middle, [after(own_a, sent2[1]), got3[0], near[0]])
     langs[1:] = [after(x, square_a) for x in langs[1:]]
     langs = langs + [swap(x, "ex", 1) for x in langs]
     per_lang = perm.shape[0] * n_ex // LANGS

time: 85.6 us -> 86.4 us (level)
  waiting for transfers between devices: 22.9 us -> 23.8 us
    ppermute x1, starting transfers between devices: 4.62 us -> 1.94 us  [ordered(): got2.append(lax.ppermute(after(raw1[1], lang), 'feat', inward))]
    ppermute x23, starting transfers between devices: 35.4 us -> 37.6 us  [swap(): lax.ppermute(x, axis, [(i, i ^ mask) for i in range(lax.axis_size(axis))])]
    ppermute x23, waiting for transfers between devices: 16.2 us -> 17.2 us  [swap(): lax.ppermute(x, axis, [(i, i ^ mask) for i in range(lax.axis_size(axis))])]
  transfers between devices with their start and end apart: 30 -> 30, of which waited for: 12 -> 11; matrix products, arithmetic and copies ran while one was open for 0% -> 0% of each run, Pallas kernels for 15% -> 15%
where the time goes in v13:
time: 86.4 us; the launch traced here: 86 us
  starting transfers between devices  44.2 us (51%)
  waiting for transfers between devices  23.8 us (28%)
  Pallas kernels  17.6 us (20%)
    ppermute x23, starting transfers between devices, swap(): lax.ppermute(x, axis, [(i, i ^ mask) for i in range(lax.axis_size(axis))])  37.6 us
    ppermute x23, waiting for transfers between devices, swap(): lax.ppermute(x, axis, [(i, i ^ mask) for i in range(lax.axis_size(axis))])  17.2 us
    pallas_call x4, Pallas kernels, project(): pl.pallas_call(kernel, out_shape=[jax.ShapeDtypeStruct(piece, jnp.float32...  13.7 us
    ppermute x1, waiting for transfers between devices, ordered(): far_pair.append(lax.ppermute(pair, 'feat', [(1, 3), (2, 0)]))  6.61 us
    ppermute x1, starting transfers between devices, ordered(): got2.append(lax.ppermute(after(raw1[1], lang), 'feat', inward))  1.94 us
  transfers between devices with their start and end apart: 30, of which 11 were waited for; matrix products, arithmetic and copies ran while one was open for 0% of the time, Pallas kernels for 15%

profile of v13, /device:TPU:0, one launch (start us, length us, event | category | flops | bytes accessed | tf_op | source)
XLA Modules:
  0.0 86.0 jit_solution(7848528848524364641)
XLA Ops:
  0.0 2.7 %project.4 = (f32[2,384,128]{2,1,0:T(8,128)S(1)}, bf16[1024,128]{1,0:T(8,128)(2,1)S(1)}, f32[32,1]{1,0:T(8,128)S(1)}) custom-call(s32[1]{0:T(128)} %bitcast.feat.feat_ref.me_ref, bf16[4096,1024]{1,0:T(8,128)(2,1)} %bitcast.24, bf16[4096,1024]{1,0:T(8,128)(2,1)} %bitcast.28, bf16[1024,128]{1,0:T(8,128)(2,1)} %adapter_ref.1, bf16[64,128]{1,0:T(8,128)(2,1)} %bitcast.32, ...), custom_call_target="tpu_custom_call" | custom-call | flops 268435456 | bytes 2490368 | tf_op jit(solution)/shard_map/project/pallas_call | solution.py:81
  2.7 3.1 %collective-permute-start.1 = (f32[2,384,128]{2,1,0:T(8,128)S(1)}, f32[2,384,128]{2,1,0:T(8,128)S(1)}, u32[]{:S(2)}, u32[]{:S(2)}) collective-permute-start(f32[2,384,128]{2,1,0:T(8,128)S(1)} %get-tuple-element.47.raw_ref), channel_id=1, source_target_pairs={{0,1},{1,0},{2,3},{3,2},{4,5},{5,4},{6,7},{7,6},{8,9},{9,8},{10,11... | collective-permute-start | bytes 1179656 | tf_op jit(solution)/shard_map/ppermute | solution.py:307
  5.8 2.5 %collective-permute-start.3 = (f32[32,1]{1,0:T(8,128)S(1)}, f32[32,1]{1,0:T(8,128)S(1)}, u32[]{:S(2)}, u32[]{:S(2)}) collective-permute-start(f32[32,1]{1,0:T(8,128)S(1)} %get-tuple-element.42.refs_0_), channel_id=1, source_target_pairs={{0,3},{1,2},{2,1},{3,0},{4,7},{5,6},{6,5},{7,4},{8,11},{9,10},{10,... | collective-permute-start | bytes 392 | tf_op jit(solution)/shard_map/ppermute | solution.py:307
  8.4 1.8 %collective-permute-start = (f32[32,1]{1,0:T(8,128)S(1)}, f32[32,1]{1,0:T(8,128)S(1)}, u32[]{:S(2)}, u32[]{:S(2)}) collective-permute-start(f32[32,1]{1,0:T(8,128)S(1)} %get-tuple-element.42.refs_0_), channel_id=1, source_target_pairs={{0,1},{1,0},{2,3},{3,2},{4,5},{5,4},{6,7},{7,6},{8,9},{9,8},{10,11... | collective-permute-start | bytes 392 | tf_op jit(solution)/shard_map/ppermute | solution.py:307
  10.2 2.3 %project.5.raw_ref = f32[2,384,128]{2,1,0:T(8,128)S(1)} custom-call(s32[1]{0:T(128)} %bitcast.feat.feat_ref.me_ref, bf16[4096,1024]{1,0:T(8,128)(2,1)} %bitcast.25, bf16[4096,1024]{1,0:T(8,128)(2,1)} %bitcast.29, bf16[1024,128]{1,0:T(8,128)(2,1)S(1)} %get-tuple-element.58.down_ref, bf16[1024,128]{1,0:T(8,128)(2,1)} %sketch_ref.7), custom_call_target="tpu_custom_call" | custom-call | flops 268435456 | bytes 2490368 | tf_op jit(solution)/shard_map/project/pallas_call | solution.py:81
  12.5 3.2 %project.6 = (f32[2,384,128]{2,1,0:T(8,128)S(1)}, f32[2,384,128]{2,1,0:T(8,128)S(1)}) custom-call(s32[1]{0:T(128)} %bitcast.feat.feat_ref.me_ref, bf16[4096,1024]{1,0:T(8,128)(2,1)} %bitcast.26, bf16[4096,1024]{1,0:T(8,128)(2,1)} %bitcast.30, bf16[1024,128]{1,0:T(8,128)(2,1)S(1)} %get-tuple-element.58.down_ref, bf16[1024,128]{1,0:T(8,128)(2,1)} %sketch_ref.7), custom_call_target="tpu_custom_call" | custom-call | flops 536870912 | bytes 4980736 | tf_op jit(solution)/shard_map/project/pallas_call | solution.py:81
  15.8 2.0 %collective-permute-done.3.refs_3_ = f32[32,1]{1,0:T(8,128)S(1)} collective-permute-done((f32[32,1]{1,0:T(8,128)S(1)}, f32[32,1]{1,0:T(8,128)S(1)}, u32[]{:S(2)}, u32[]{:S(2)}) %collective-permute-start.3) | collective-permute-done | bytes 160 | tf_op jit(solution)/shard_map/ppermute | solution.py:307
  19.8 1.6 %collective-permute-start.7 = (f32[64,256]{1,0:T(8,128)S(1)}, f32[64,256]{1,0:T(8,128)S(1)}, u32[]{:S(2)}, u32[]{:S(2)}) collective-permute-start(f32[64,256]{1,0:T(8,128)S(1)} %get-tuple-element.79), channel_id=1, source_target_pairs={{0,16},{4,20},{8,24},{12,28},{16,0},{20,4},{24,8},{28,12},{1,17},{... | collective-permute-start | bytes 196616 | tf_op jit(solution)/shard_map/ppermute | solution.py:307
  21.4 1.4 %collective-permute-start.8 = (f32[64,256]{1,0:T(8,128)S(1)}, f32[64,256]{1,0:T(8,128)S(1)}, u32[]{:S(2)}, u32[]{:S(2)}) collective-permute-start(f32[64,256]{1,0:T(8,128)S(1)} %get-tuple-element.80), channel_id=1, source_target_pairs={{0,24},{4,28},{8,16},{12,20},{16,8},{20,12},{24,0},{28,4},{1,25},{... | collective-permute-start | bytes 196616 | tf_op jit(solution)/shard_map/ppermute | solution.py:307
  24.0 5.7 %collective-permute-done.5.got_ref = f32[2,384,128]{2,1,0:T(8,128)S(1)} collective-permute-done((f32[2,384,128]{2,1,0:T(8,128)S(1)}, f32[2,384,128]{2,1,0:T(8,128)S(1)}, u32[]{:S(2)}, u32[]{:S(2)}) %collective-permute-start.5) | collective-permute-done | bytes 393248 | tf_op jit(solution)/shard_map/ppermute | solution.py:307
  31.3 3.6 %collective-permute-start.9 = (f32[64,256]{1,0:T(8,128)S(1)}, f32[64,256]{1,0:T(8,128)S(1)}, u32[]{:S(2)}, u32[]{:S(2)}) collective-permute-start(f32[64,256]{1,0:T(8,128)S(1)} %add_add_fusion.one_ref), channel_id=1, source_target_pairs={{0,1},{1,0},{2,3},{3,2},{4,5},{5,4},{6,7},{7,6},{8,9},{9,8},{10,11... | collective-permute-start | bytes 196616 | tf_op jit(solution)/shard_map/ppermute | solution.py:307
  34.9 1.9 %collective-permute-start.16 = (f32[2,384,128]{2,1,0:T(8,128)S(1)}, f32[2,384,128]{2,1,0:T(8,128)S(1)}, u32[]{:S(2)}, u32[]{:S(2)}) collective-permute-start(f32[2,384,128]{2,1,0:T(8,128)S(1)} %get-tuple-element.69.raw_ref), channel_id=1, source_target_pairs={{0,1},{3,2},{4,5},{7,6},{8,9},{11,10},{12,13},{15,14},{16,17},{19,... | collective-permute-start | bytes 1179656 | tf_op jit(solution)/shard_map/ppermute | solution.py:360
  36.8 5.6 %project.7 = (f32[2,384,128]{2,1,0:T(8,128)S(1)}, f32[2,384,128]{2,1,0:T(8,128)S(1)}, f32[2,384,128]{2,1,0:T(8,128)S(1)}, f32[2,384,128]{2,1,0:T(8,128)S(1)}) custom-call(s32[1]{0:T(128)} %bitcast.feat.feat_ref.me_ref, bf16[4096,1024]{1,0:T(8,128)(2,1)} %bitcast.27, bf16[4096,1024]{1,0:T(8,128)(2,1)} %bitcast.31, ...), custom_call_target="tpu_custom_call" | custom-call | flops 1073741824 | bytes 9961472 | tf_op jit(solution)/shard_map/project/pallas_call | solution.py:81
  42.4 1.3 %collective-permute-start.13 = (f32[2,64,256]{2,1,0:T(8,128)S(1)}, f32[2,64,256]{2,1,0:T(8,128)S(1)}, u32[]{:S(2)}, u32[]{:S(2)}) collective-permute-start(f32[2,64,256]{2,1,0:T(8,128)S(1)} %shard_map.75.pair_ref), channel_id=1, source_target_pairs={{1,3},{2,0},{5,7},{6,4},{9,11},{10,8},{13,15},{14,12},{17,19},{18,... | collective-permute-start | bytes 393224 | tf_op jit(solution)/shard_map/ppermute | solution.py:366
  44.6 6.6 %collective-permute-done.13.outer_ref = f32[2,64,256]{2,1,0:T(8,128)S(1)} collective-permute-done((f32[2,64,256]{2,1,0:T(8,128)S(1)}, f32[2,64,256]{2,1,0:T(8,128)S(1)}, u32[]{:S(2)}, u32[]{:S(2)}) %collective-permute-start.13) | collective-permute-done | bytes 131104 | tf_op jit(solution)/shard_map/ppermute | solution.py:366
  51.2 2.5 %collective-permute-start.20 = (f32[4,64,256]{2,1,0:T(8,128)S(1)}, f32[4,64,256]{2,1,0:T(8,128)S(1)}, u32[]{:S(2)}, u32[]{:S(2)}) collective-permute-start(f32[4,64,256]{2,1,0:T(8,128)S(1)} %shard_map.78.refs_0_), channel_id=1, source_target_pairs={{0,24},{4,28},{8,16},{12,20},{16,8},{20,12},{24,0},{28,4},{1,25},{... | collective-permute-start | bytes 786440 | tf_op jit(solution)/shard_map/ppermute | solution.py:307
  54.4 4.8 %collective-permute-start.17 = (f32[2,384,128]{2,1,0:T(8,128)S(1)}, f32[2,384,128]{2,1,0:T(8,128)S(1)}, u32[]{:S(2)}, u32[]{:S(2)}) collective-permute-start(f32[2,384,128]{2,1,0:T(8,128)S(1)} %shard_map.76), channel_id=1, source_target_pairs={{0,1},{1,0},{2,3},{3,2},{4,5},{5,4},{6,7},{7,6},{8,9},{9,8},{10,11... | collective-permute-start | bytes 1179656 | tf_op jit(solution)/shard_map/ppermute | solution.py:307
  60.4 6.8 %collective-permute-start.25 = (f32[2,384,128]{2,1,0:T(8,128)S(1)}, f32[2,384,128]{2,1,0:T(8,128)S(1)}, u32[]{:S(2)}, u32[]{:S(2)}) collective-permute-start(f32[2,384,128]{2,1,0:T(8,128)S(1)} %shard_map.79), channel_id=1, source_target_pairs={{0,1},{1,0},{2,3},{3,2},{4,5},{5,4},{6,7},{7,6},{8,9},{9,8},{10,11... | collective-permute-start | bytes 1179656 | tf_op jit(solution)/shard_map/ppermute | solution.py:307
  71.4 3.3 %collective-permute-done.25.refs_1_ = f32[2,384,128]{2,1,0:T(8,128)S(1)} collective-permute-done((f32[2,384,128]{2,1,0:T(8,128)S(1)}, f32[2,384,128]{2,1,0:T(8,128)S(1)}, u32[]{:S(2)}, u32[]{:S(2)}) %collective-permute-start.25) | collective-permute-done | bytes 393248 | tf_op jit(solution)/shard_map/ppermute | solution.py:307
  74.7 1.5 %score.1.refs_0_ = f32[16,64]{1,0:T(8,128)S(1)} custom-call(s32[1]{0:T(128)} %bitcast.1.middle_ref, bf16[32,128,256]{2,1,0:T(8,128)(2,1)S(1)} %split.1.lang_ref, bf16[32,16,256]{2,1,0:T(8,128)(2,1)S(1)} %get-tuple-element.75.grad_a, f32[8,1]{1,0:T(8,128)S(1)} %get-tuple-element.71.square_a, f32[2,384,128]{2,1,0:T(8,128)S(1)} %get-tuple-element.76.refs_0_, ...), custom_call_target="tpu_custom_call" | custom-call | tf_op jit(solution)/shard_map/score/pallas_call | solution.py:247
  76.2 2.0 %collective-permute-start.29 = (f32[16,64]{1,0:T(8,128)S(1)}, f32[16,64]{1,0:T(8,128)S(1)}, u32[]{:S(2)}, u32[]{:S(2)}) collective-permute-start(f32[16,64]{1,0:T(8,128)S(1)} %score.1.refs_0_), channel_id=1, source_target_pairs={{0,3},{1,2},{2,1},{3,0},{4,7},{5,6},{6,5},{7,4},{8,11},{9,10},{10,... | collective-permute-start | bytes 12296 | tf_op jit(solution)/shard_map/ppermute | solution.py:307
  78.1 3.6 %collective-permute-start.28 = (f32[16,64]{1,0:T(8,128)S(1)}, f32[16,64]{1,0:T(8,128)S(1)}, u32[]{:S(2)}, u32[]{:S(2)}) collective-permute-start(f32[16,64]{1,0:T(8,128)S(1)} %score.1.refs_0_), channel_id=1, source_target_pairs={{0,2},{1,3},{2,0},{3,1},{4,6},{5,7},{6,4},{7,5},{8,10},{9,11},{10,... | collective-permute-start | bytes 12296 | tf_op jit(solution)/shard_map/ppermute | solution.py:307
  81.8 1.7 %collective-permute-done.28.refs_2_ = f32[16,64]{1,0:T(8,128)S(1)} collective-permute-done((f32[16,64]{1,0:T(8,128)S(1)}, f32[16,64]{1,0:T(8,128)S(1)}, u32[]{:S(2)}, u32[]{:S(2)}) %collective-permute-start.28) | collective-permute-done | bytes 4128 | tf_op jit(solution)/shard_map/ppermute | solution.py:307
  83.5 1.9 %collective-permute-done.27.refs_1_ = f32[16,64]{1,0:T(8,128)S(1)} collective-permute-done((f32[16,64]{1,0:T(8,128)S(1)}, f32[16,64]{1,0:T(8,128)S(1)}, u32[]{:S(2)}, u32[]{:S(2)}) %collective-permute-start.27) | collective-permute-done | bytes 4128 | tf_op jit(solution)/shard_map/ppermute | solution.py:307
  (60 shorter events, 12.3 us)
Async XLA Ops:
  2.7 13.0 %collective-permute-start.1 = (f32[2,384,128]{2,1,0:T(8,128)S(1)}, f32[2,384,128]{2,1,0:T(8,128)S(1)}, u32[]{:S(2)}, u32[]{:S(2)}) collective-permute-start(f32[2,384,128]{2,1,0:T(8,128)S(1)} %get-tuple-element.47.raw_ref), channel_id=1, source_target_pairs={{0,1},{1,0},{2,3},{3,2},{4,5},{5,4},{6,7},{7,6},{8,9},{9,8},{10,11... | collective-permute-start | bytes 1179656 | tf_op jit(solution)/shard_map/ppermute | solution.py:307
  5.8 12.0 %collective-permute-start.3 = (f32[32,1]{1,0:T(8,128)S(1)}, f32[32,1]{1,0:T(8,128)S(1)}, u32[]{:S(2)}, u32[]{:S(2)}) collective-permute-start(f32[32,1]{1,0:T(8,128)S(1)} %get-tuple-element.42.refs_0_), channel_id=1, source_target_pairs={{0,3},{1,2},{2,1},{3,0},{4,7},{5,6},{6,5},{7,4},{8,11},{9,10},{10,... | collective-permute-start | bytes 392 | tf_op jit(solution)/shard_map/ppermute | solution.py:307
  8.3 9.5 %collective-permute-start.2 = (f32[32,1]{1,0:T(8,128)S(1)}, f32[32,1]{1,0:T(8,128)S(1)}, u32[]{:S(2)}, u32[]{:S(2)}) collective-permute-start(f32[32,1]{1,0:T(8,128)S(1)} %get-tuple-element.42.refs_0_), channel_id=1, source_target_pairs={{0,2},{1,3},{2,0},{3,1},{4,6},{5,7},{6,4},{7,5},{8,10},{9,11},{10,... | collective-permute-start | bytes 392 | tf_op jit(solution)/shard_map/ppermute | solution.py:307
  8.4 9.4 %collective-permute-start = (f32[32,1]{1,0:T(8,128)S(1)}, f32[32,1]{1,0:T(8,128)S(1)}, u32[]{:S(2)}, u32[]{:S(2)}) collective-permute-start(f32[32,1]{1,0:T(8,128)S(1)} %get-tuple-element.42.refs_0_), channel_id=1, source_target_pairs={{0,1},{1,0},{2,3},{3,2},{4,5},{5,4},{6,7},{7,6},{8,9},{9,8},{10,11... | collective-permute-start | bytes 392 | tf_op jit(solution)/shard_map/ppermute | solution.py:307
  18.2 11.5 %collective-permute-start.5 = (f32[2,384,128]{2,1,0:T(8,128)S(1)}, f32[2,384,128]{2,1,0:T(8,128)S(1)}, u32[]{:S(2)}, u32[]{:S(2)}) collective-permute-start(f32[2,384,128]{2,1,0:T(8,128)S(1)} %project.5.raw_ref), channel_id=1, source_target_pairs={{0,1},{1,0},{2,3},{3,2},{4,5},{5,4},{6,7},{7,6},{8,9},{9,8},{10,11... | collective-permute-start | bytes 1179656 | tf_op jit(solution)/shard_map/ppermute | solution.py:307
  19.8 10.7 %collective-permute-start.7 = (f32[64,256]{1,0:T(8,128)S(1)}, f32[64,256]{1,0:T(8,128)S(1)}, u32[]{:S(2)}, u32[]{:S(2)}) collective-permute-start(f32[64,256]{1,0:T(8,128)S(1)} %get-tuple-element.79), channel_id=1, source_target_pairs={{0,16},{4,20},{8,24},{12,28},{16,0},{20,4},{24,8},{28,12},{1,17},{... | collective-permute-start | bytes 196616 | tf_op jit(solution)/shard_map/ppermute | solution.py:307
  21.4 9.9 %collective-permute-start.8 = (f32[64,256]{1,0:T(8,128)S(1)}, f32[64,256]{1,0:T(8,128)S(1)}, u32[]{:S(2)}, u32[]{:S(2)}) collective-permute-start(f32[64,256]{1,0:T(8,128)S(1)} %get-tuple-element.80), channel_id=1, source_target_pairs={{0,24},{4,28},{8,16},{12,20},{16,8},{20,12},{24,0},{28,4},{1,25},{... | collective-permute-start | bytes 196616 | tf_op jit(solution)/shard_map/ppermute | solution.py:307
  22.8 8.4 %collective-permute-start.6 = (f32[64,256]{1,0:T(8,128)S(1)}, f32[64,256]{1,0:T(8,128)S(1)}, u32[]{:S(2)}, u32[]{:S(2)}) collective-permute-start(f32[64,256]{1,0:T(8,128)S(1)} %get-tuple-element.81), channel_id=1, source_target_pairs={{0,8},{4,12},{8,0},{12,4},{16,24},{20,28},{24,16},{28,20},{1,9},{5... | collective-permute-start | bytes 196616 | tf_op jit(solution)/shard_map/ppermute | solution.py:307
  23.3 20.4 %collective-permute-start.10 = (f32[2,384,128]{2,1,0:T(8,128)S(1)}, f32[2,384,128]{2,1,0:T(8,128)S(1)}, u32[]{:S(2)}, u32[]{:S(2)}) collective-permute-start(f32[2,384,128]{2,1,0:T(8,128)S(1)} %shard_map.73), channel_id=1, source_target_pairs={{1,2},{2,1},{0,0},{3,3},{5,6},{6,5},{4,4},{7,7},{9,10},{10,9},{8,8... | collective-permute-start | bytes 1179656 | tf_op jit(solution)/shard_map/ppermute | solution.py:349
  29.7 14.8 %collective-permute-start.11 = (f32[2,384,128]{2,1,0:T(8,128)S(1)}, f32[2,384,128]{2,1,0:T(8,128)S(1)}, u32[]{:S(2)}, u32[]{:S(2)}) collective-permute-start(f32[2,384,128]{2,1,0:T(8,128)S(1)} %get-tuple-element.63.raw_ref), channel_id=1, source_target_pairs={{0,1},{1,0},{2,3},{3,2},{4,5},{5,4},{6,7},{7,6},{8,9},{9,8},{10,11... | collective-permute-start | bytes 1179656 | tf_op jit(solution)/shard_map/ppermute | solution.py:307
  30.5 28.7 %collective-permute-start.15 = (f32[2,384,128]{2,1,0:T(8,128)S(1)}, f32[2,384,128]{2,1,0:T(8,128)S(1)}, u32[]{:S(2)}, u32[]{:S(2)}) collective-permute-start(f32[2,384,128]{2,1,0:T(8,128)S(1)} %shard_map.74), channel_id=1, source_target_pairs={{1,2},{2,1},{0,0},{3,3},{5,6},{6,5},{4,4},{7,7},{9,10},{10,9},{8,8... | collective-permute-start | bytes 1179656 | tf_op jit(solution)/shard_map/ppermute | solution.py:357
  31.3 11.2 %collective-permute-start.9 = (f32[64,256]{1,0:T(8,128)S(1)}, f32[64,256]{1,0:T(8,128)S(1)}, u32[]{:S(2)}, u32[]{:S(2)}) collective-permute-start(f32[64,256]{1,0:T(8,128)S(1)} %add_add_fusion.one_ref), channel_id=1, source_target_pairs={{0,1},{1,0},{2,3},{3,2},{4,5},{5,4},{6,7},{7,6},{8,9},{9,8},{10,11... | collective-permute-start | bytes 196616 | tf_op jit(solution)/shard_map/ppermute | solution.py:307
  34.9 24.9 %collective-permute-start.16 = (f32[2,384,128]{2,1,0:T(8,128)S(1)}, f32[2,384,128]{2,1,0:T(8,128)S(1)}, u32[]{:S(2)}, u32[]{:S(2)}) collective-permute-start(f32[2,384,128]{2,1,0:T(8,128)S(1)} %get-tuple-element.69.raw_ref), channel_id=1, source_target_pairs={{0,1},{3,2},{4,5},{7,6},{8,9},{11,10},{12,13},{15,14},{16,17},{19,... | collective-permute-start | bytes 1179656 | tf_op jit(solution)/shard_map/ppermute | solution.py:360
  42.4 8.7 %collective-permute-start.13 = (f32[2,64,256]{2,1,0:T(8,128)S(1)}, f32[2,64,256]{2,1,0:T(8,128)S(1)}, u32[]{:S(2)}, u32[]{:S(2)}) collective-permute-start(f32[2,64,256]{2,1,0:T(8,128)S(1)} %shard_map.75.pair_ref), channel_id=1, source_target_pairs={{1,3},{2,0},{5,7},{6,4},{9,11},{10,8},{13,15},{14,12},{17,19},{18,... | collective-permute-start | bytes 393224 | tf_op jit(solution)/shard_map/ppermute | solution.py:366
  43.7 7.4 %collective-permute-start.12 = (f32[2,64,256]{2,1,0:T(8,128)S(1)}, f32[2,64,256]{2,1,0:T(8,128)S(1)}, u32[]{:S(2)}, u32[]{:S(2)}) collective-permute-start(f32[2,64,256]{2,1,0:T(8,128)S(1)} %shard_map.75.pair_ref), channel_id=1, source_target_pairs={{1,2},{2,1},{0,0},{3,3},{5,6},{6,5},{4,4},{7,7},{9,10},{10,9},{8,8... | collective-permute-start | bytes 393224 | tf_op jit(solution)/shard_map/ppermute | solution.py:365
  51.2 9.1 %collective-permute-start.20 = (f32[4,64,256]{2,1,0:T(8,128)S(1)}, f32[4,64,256]{2,1,0:T(8,128)S(1)}, u32[]{:S(2)}, u32[]{:S(2)}) collective-permute-start(f32[4,64,256]{2,1,0:T(8,128)S(1)} %shard_map.78.refs_0_), channel_id=1, source_target_pairs={{0,24},{4,28},{8,16},{12,20},{16,8},{20,12},{24,0},{28,4},{1,25},{... | collective-permute-start | bytes 786440 | tf_op jit(solution)/shard_map/ppermute | solution.py:307
  53.7 6.6 %collective-permute-start.18 = (f32[2,384,128]{2,1,0:T(8,128)S(1)}, f32[2,384,128]{2,1,0:T(8,128)S(1)}, u32[]{:S(2)}, u32[]{:S(2)}) collective-permute-start(f32[2,384,128]{2,1,0:T(8,128)S(1)} %shard_map.77), channel_id=1, source_target_pairs={{1,2},{2,1},{0,0},{3,3},{5,6},{6,5},{4,4},{7,7},{9,10},{10,9},{8,8... | collective-permute-start | bytes 1179656 | tf_op jit(solution)/shard_map/ppermute | solution.py:370
  54.4 12.9 %collective-permute-start.17 = (f32[2,384,128]{2,1,0:T(8,128)S(1)}, f32[2,384,128]{2,1,0:T(8,128)S(1)}, u32[]{:S(2)}, u32[]{:S(2)}) collective-permute-start(f32[2,384,128]{2,1,0:T(8,128)S(1)} %shard_map.76), channel_id=1, source_target_pairs={{0,1},{1,0},{2,3},{3,2},{4,5},{5,4},{6,7},{7,6},{8,9},{9,8},{10,11... | collective-permute-start | bytes 1179656 | tf_op jit(solution)/shard_map/ppermute | solution.py:307
  59.2 9.6 %collective-permute-start.19 = (f32[4,64,256]{2,1,0:T(8,128)S(1)}, f32[4,64,256]{2,1,0:T(8,128)S(1)}, u32[]{:S(2)}, u32[]{:S(2)}) collective-permute-start(f32[4,64,256]{2,1,0:T(8,128)S(1)} %shard_map.78.refs_0_), channel_id=1, source_target_pairs={{0,16},{4,20},{8,24},{12,28},{16,0},{20,4},{24,8},{28,12},{1,17},{... | collective-permute-start | bytes 786440 | tf_op jit(solution)/shard_map/ppermute | solution.py:307
  59.7 9.1 %collective-permute-start.14 = (f32[4,64,256]{2,1,0:T(8,128)S(1)}, f32[4,64,256]{2,1,0:T(8,128)S(1)}, u32[]{:S(2)}, u32[]{:S(2)}) collective-permute-start(f32[4,64,256]{2,1,0:T(8,128)S(1)} %shard_map.78.refs_0_), channel_id=1, source_target_pairs={{0,8},{4,12},{8,0},{12,4},{16,24},{20,28},{24,16},{28,20},{1,9},{5... | collective-permute-start | bytes 786440 | tf_op jit(solution)/shard_map/ppermute | solution.py:307
  60.3 9.1 %collective-permute-start.21 = (f32[4,64,256]{2,1,0:T(8,128)S(1)}, f32[4,64,256]{2,1,0:T(8,128)S(1)}, u32[]{:S(2)}, u32[]{:S(2)}) collective-permute-start(f32[4,64,256]{2,1,0:T(8,128)S(1)} %shard_map.78.refs_0_), channel_id=1, source_target_pairs={{0,4},{4,0},{8,12},{12,8},{16,20},{20,16},{24,28},{28,24},{1,5},{5... | collective-permute-start | bytes 786440 | tf_op jit(solution)/shard_map/ppermute | solution.py:307
  60.4 14.3 %collective-permute-start.25 = (f32[2,384,128]{2,1,0:T(8,128)S(1)}, f32[2,384,128]{2,1,0:T(8,128)S(1)}, u32[]{:S(2)}, u32[]{:S(2)}) collective-permute-start(f32[2,384,128]{2,1,0:T(8,128)S(1)} %shard_map.79), channel_id=1, source_target_pairs={{0,1},{1,0},{2,3},{3,2},{4,5},{5,4},{6,7},{7,6},{8,9},{9,8},{10,11... | collective-permute-start | bytes 1179656 | tf_op jit(solution)/shard_map/ppermute | solution.py:307
  67.3 7.3 %collective-permute-start.26 = (f32[2,384,128]{2,1,0:T(8,128)S(1)}, f32[2,384,128]{2,1,0:T(8,128)S(1)}, u32[]{:S(2)}, u32[]{:S(2)}) collective-permute-start(f32[2,384,128]{2,1,0:T(8,128)S(1)} %shard_map.80), channel_id=1, source_target_pairs={{1,2},{2,1},{0,0},{3,3},{5,6},{6,5},{4,4},{7,7},{9,10},{10,9},{8,8... | collective-permute-start | bytes 1179656 | tf_op jit(solution)/shard_map/ppermute | solution.py:377
  76.2 5.6 %collective-permute-start.29 = (f32[16,64]{1,0:T(8,128)S(1)}, f32[16,64]{1,0:T(8,128)S(1)}, u32[]{:S(2)}, u32[]{:S(2)}) collective-permute-start(f32[16,64]{1,0:T(8,128)S(1)} %score.1.refs_0_), channel_id=1, source_target_pairs={{0,3},{1,2},{2,1},{3,0},{4,7},{5,6},{6,5},{7,4},{8,11},{9,10},{10,... | collective-permute-start | bytes 12296 | tf_op jit(solution)/shard_map/ppermute | solution.py:307
  (8 other events, 24.3 us)

commit v14 on v12

--- a/solution.py
+++ b/solution.py
@@ -341,8 +341,9 @@
     )
     got1 = [swap(raw0_a, "feat", 1)]
     squares = [own_square] + [swap(own_square, "feat", mask) for mask in (1, 2, 3)]
-    raw0_b, *raw1 = project(more_kernel, me_feat, 1, 3, acts2, grads2, [down, out_sketch], [])
+    [raw0_b] = project(more_kernel, me_feat, 1, 1, acts2, grads2, [down, out_sketch], [])
     got1.append(swap(raw0_b, "feat", 1))
+    raw1 = project(more_kernel, me_feat, 2, 2, acts2, grads2, [after(down, raw0_b), out_sketch], [])
     got2 = [swap(raw1[0], "feat", 1)]
     sent1 = [onward(after(raw0_a, raw1[1]), got1[0])]
     far = [lax.ppermute(sent1[0], "feat", inner)]
@@ -368,11 +369,11 @@
     pair = after(pair, sent2[0])
     langs = [small(join_kernel, (4, *lang.shape), is_middle, [pair, *far_pair])]
     langs = langs + [swap(langs[0], "ex", mask) for mask in range(2, n_ex, 2)]
-    sent3.append(onward(after(raw2[1], langs[0]), far[1]))
+    sent2.append(onward(after(raw1[1], langs[0]), got2[1]))
+    near.append(lax.ppermute(sent2[1], "feat", inner))
+    sent3.append(onward(after(raw2[1], sent2[1]), far[1]))
     got3.append(swap(sent3[1], "feat", 1))
-    sent2.append(onward(after(raw1[1], sent3[1]), got2[1]))
-    near.append(lax.ppermute(sent2[1], "feat", inner))
-    own_a, own_b = project(more_kernel, me_feat, 6, 2, acts2, grads2, [after(down, sent2[1]), out_sketch], [])
+    own_a, own_b = project(more_kernel, me_feat, 6, 2, acts2, grads2, [after(down, sent3[1]), out_sketch], [])
     grad_a, square_a = product(is_middle, [own_a, got3[0], near[0]])
     langs[1:] = [after(x, square_a) for x in langs[1:]]
     langs = langs + [swap(x, "ex", 1) for x in langs]

time: 85.6 us -> 85.1 us (level)
  starting transfers between devices: 44.6 us -> 40.7 us
  waiting for transfers between devices: 22.9 us -> 25.4 us
    ppermute x23, starting transfers between devices: 35.4 us -> 31.4 us  [swap(): lax.ppermute(x, axis, [(i, i ^ mask) for i in range(lax.axis_size(axis))])]
    ppermute x23, waiting for transfers between devices: 16.2 us -> 18.8 us  [swap(): lax.ppermute(x, axis, [(i, i ^ mask) for i in range(lax.axis_size(axis))])]
    pallas_call x4 -> x5, Pallas kernels: 13.6 us -> 14.4 us  [project(): pl.pallas_call(kernel, out_shape=[jax.ShapeDtypeStruct(piece, jnp.float32...]
  transfers between devices with their start and end apart: 30 -> 30, of which waited for: 12 -> 11; matrix products, arithmetic and copies ran while one was open for 0% -> 0% of each run, Pallas kernels for 15% -> 15%
where the time goes in v14:
time: 85.1 us; the launch traced here: 84.8 us
  starting transfers between devices  40.7 us (48%)
  waiting for transfers between devices  25.4 us (30%)
  Pallas kernels  18.2 us (21%)
    ppermute x23, starting transfers between devices, swap(): lax.ppermute(x, axis, [(i, i ^ mask) for i in range(lax.axis_size(axis))])  31.4 us
    ppermute x23, waiting for transfers between devices, swap(): lax.ppermute(x, axis, [(i, i ^ mask) for i in range(lax.axis_size(axis))])  18.8 us
    pallas_call x5, Pallas kernels, project(): pl.pallas_call(kernel, out_shape=[jax.ShapeDtypeStruct(piece, jnp.float32...  14.4 us
    ppermute x1, waiting for transfers between devices, ordered(): far_pair.append(lax.ppermute(pair, 'feat', [(1, 3), (2, 0)]))  6.62 us
    ppermute x1, starting transfers between devices, ordered(): got2.append(lax.ppermute(after(raw1[1], lang), 'feat', inward))  4.62 us
  transfers between devices with their start and end apart: 30, of which 11 were waited for; matrix products, arithmetic and copies ran while one was open for 0% of the time, Pallas kernels for 15%

profile of v14, /device:TPU:0, one launch (start us, length us, event | category | flops | bytes accessed | tf_op | source)
XLA Modules:
  0.0 84.8 jit_solution(4526350428406289859)
XLA Ops:
  0.0 2.7 %project.5 = (f32[2,384,128]{2,1,0:T(8,128)S(1)}, bf16[1024,128]{1,0:T(8,128)(2,1)S(1)}, f32[32,1]{1,0:T(8,128)S(1)}) custom-call(s32[1]{0:T(128)} %bitcast.feat.feat_ref.me_ref, bf16[4096,1024]{1,0:T(8,128)(2,1)} %bitcast.24, bf16[4096,1024]{1,0:T(8,128)(2,1)} %bitcast.29, bf16[1024,128]{1,0:T(8,128)(2,1)} %adapter_ref.1, bf16[64,128]{1,0:T(8,128)(2,1)} %bitcast.34, ...), custom_call_target="tpu_custom_call" | custom-call | flops 268435456 | bytes 2490368 | tf_op jit(solution)/shard_map/project/pallas_call | solution.py:81
  2.7 3.1 %collective-permute-start.1 = (f32[2,384,128]{2,1,0:T(8,128)S(1)}, f32[2,384,128]{2,1,0:T(8,128)S(1)}, u32[]{:S(2)}, u32[]{:S(2)}) collective-permute-start(f32[2,384,128]{2,1,0:T(8,128)S(1)} %get-tuple-element.47.raw_ref), channel_id=1, source_target_pairs={{0,1},{1,0},{2,3},{3,2},{4,5},{5,4},{6,7},{7,6},{8,9},{9,8},{10,11... | collective-permute-start | bytes 1179656 | tf_op jit(solution)/shard_map/ppermute | solution.py:307
  5.8 2.5 %collective-permute-start.3 = (f32[32,1]{1,0:T(8,128)S(1)}, f32[32,1]{1,0:T(8,128)S(1)}, u32[]{:S(2)}, u32[]{:S(2)}) collective-permute-start(f32[32,1]{1,0:T(8,128)S(1)} %get-tuple-element.42.refs_0_), channel_id=1, source_target_pairs={{0,3},{1,2},{2,1},{3,0},{4,7},{5,6},{6,5},{7,4},{8,11},{9,10},{10,... | collective-permute-start | bytes 392 | tf_op jit(solution)/shard_map/ppermute | solution.py:307
  8.4 1.8 %collective-permute-start = (f32[32,1]{1,0:T(8,128)S(1)}, f32[32,1]{1,0:T(8,128)S(1)}, u32[]{:S(2)}, u32[]{:S(2)}) collective-permute-start(f32[32,1]{1,0:T(8,128)S(1)} %get-tuple-element.42.refs_0_), channel_id=1, source_target_pairs={{0,1},{1,0},{2,3},{3,2},{4,5},{5,4},{6,7},{7,6},{8,9},{9,8},{10,11... | collective-permute-start | bytes 392 | tf_op jit(solution)/shard_map/ppermute | solution.py:307
  10.2 2.3 %project.6.raw_ref = f32[2,384,128]{2,1,0:T(8,128)S(1)} custom-call(s32[1]{0:T(128)} %bitcast.feat.feat_ref.me_ref, bf16[4096,1024]{1,0:T(8,128)(2,1)} %bitcast.25, bf16[4096,1024]{1,0:T(8,128)(2,1)} %bitcast.30, bf16[1024,128]{1,0:T(8,128)(2,1)S(1)} %get-tuple-element.69.down_ref, bf16[1024,128]{1,0:T(8,128)(2,1)} %sketch_ref.9), custom_call_target="tpu_custom_call" | custom-call | flops 268435456 | bytes 2490368 | tf_op jit(solution)/shard_map/project/pallas_call | solution.py:81
  12.5 3.2 %project.7 = (f32[2,384,128]{2,1,0:T(8,128)S(1)}, f32[2,384,128]{2,1,0:T(8,128)S(1)}) custom-call(s32[1]{0:T(128)} %bitcast.feat.feat_ref.me_ref, bf16[4096,1024]{1,0:T(8,128)(2,1)} %bitcast.26, bf16[4096,1024]{1,0:T(8,128)(2,1)} %bitcast.31, bf16[1024,128]{1,0:T(8,128)(2,1)S(1)} %get-tuple-element.69.down_ref, bf16[1024,128]{1,0:T(8,128)(2,1)} %sketch_ref.9), custom_call_target="tpu_custom_call" | custom-call | flops 536870912 | bytes 4980736 | tf_op jit(solution)/shard_map/project/pallas_call | solution.py:81
  15.8 2.0 %collective-permute-done.3.refs_3_ = f32[32,1]{1,0:T(8,128)S(1)} collective-permute-done((f32[32,1]{1,0:T(8,128)S(1)}, f32[32,1]{1,0:T(8,128)S(1)}, u32[]{:S(2)}, u32[]{:S(2)}) %collective-permute-start.3) | collective-permute-done | bytes 160 | tf_op jit(solution)/shard_map/ppermute | solution.py:307
  19.8 1.6 %collective-permute-start.7 = (f32[64,256]{1,0:T(8,128)S(1)}, f32[64,256]{1,0:T(8,128)S(1)}, u32[]{:S(2)}, u32[]{:S(2)}) collective-permute-start(f32[64,256]{1,0:T(8,128)S(1)} %get-tuple-element.79), channel_id=1, source_target_pairs={{0,16},{4,20},{8,24},{12,28},{16,0},{20,4},{24,8},{28,12},{1,17},{... | collective-permute-start | bytes 196616 | tf_op jit(solution)/shard_map/ppermute | solution.py:307
  21.4 1.4 %collective-permute-start.8 = (f32[64,256]{1,0:T(8,128)S(1)}, f32[64,256]{1,0:T(8,128)S(1)}, u32[]{:S(2)}, u32[]{:S(2)}) collective-permute-start(f32[64,256]{1,0:T(8,128)S(1)} %get-tuple-element.80), channel_id=1, source_target_pairs={{0,24},{4,28},{8,16},{12,20},{16,8},{20,12},{24,0},{28,4},{1,25},{... | collective-permute-start | bytes 196616 | tf_op jit(solution)/shard_map/ppermute | solution.py:307
  23.3 6.4 %collective-permute-done.5.got_ref = f32[2,384,128]{2,1,0:T(8,128)S(1)} collective-permute-done((f32[2,384,128]{2,1,0:T(8,128)S(1)}, f32[2,384,128]{2,1,0:T(8,128)S(1)}, u32[]{:S(2)}, u32[]{:S(2)}) %collective-permute-start.5) | collective-permute-done | bytes 393248 | tf_op jit(solution)/shard_map/ppermute | solution.py:307
  30.6 1.4 %collective-permute-start.9 = (f32[64,256]{1,0:T(8,128)S(1)}, f32[64,256]{1,0:T(8,128)S(1)}, u32[]{:S(2)}, u32[]{:S(2)}) collective-permute-start(f32[64,256]{1,0:T(8,128)S(1)} %add_add_fusion.one_ref), channel_id=1, source_target_pairs={{0,1},{1,0},{2,3},{3,2},{4,5},{5,4},{6,7},{7,6},{8,9},{9,8},{10,11... | collective-permute-start | bytes 196616 | tf_op jit(solution)/shard_map/ppermute | solution.py:307
  32.6 4.6 %collective-permute-start.15 = (f32[2,384,128]{2,1,0:T(8,128)S(1)}, f32[2,384,128]{2,1,0:T(8,128)S(1)}, u32[]{:S(2)}, u32[]{:S(2)}) collective-permute-start(f32[2,384,128]{2,1,0:T(8,128)S(1)} %get-tuple-element.67.raw_ref), channel_id=1, source_target_pairs={{0,1},{3,2},{4,5},{7,6},{8,9},{11,10},{12,13},{15,14},{16,17},{19,... | collective-permute-start | bytes 1179656 | tf_op jit(solution)/shard_map/ppermute | solution.py:360
  37.2 3.1 %project.8 = (f32[2,384,128]{2,1,0:T(8,128)S(1)}, f32[2,384,128]{2,1,0:T(8,128)S(1)}) custom-call(s32[1]{0:T(128)} %bitcast.feat.feat_ref.me_ref, bf16[4096,1024]{1,0:T(8,128)(2,1)} %bitcast.27, bf16[4096,1024]{1,0:T(8,128)(2,1)} %bitcast.32, bf16[1024,128]{1,0:T(8,128)(2,1)S(1)} %get-tuple-element.69.down_ref, bf16[1024,128]{1,0:T(8,128)(2,1)} %sketch_ref.9), custom_call_target="tpu_custom_call" | custom-call | flops 536870912 | bytes 4980736 | tf_op jit(solution)/shard_map/project/pallas_call | solution.py:81
  40.4 1.3 %collective-permute-done.9.two_ref = f32[64,256]{1,0:T(8,128)S(1)} collective-permute-done((f32[64,256]{1,0:T(8,128)S(1)}, f32[64,256]{1,0:T(8,128)S(1)}, u32[]{:S(2)}, u32[]{:S(2)}) %collective-permute-start.9) | collective-permute-done | bytes 65568 | tf_op jit(solution)/shard_map/ppermute | solution.py:307
  41.7 1.3 %collective-permute-start.13 = (f32[2,64,256]{2,1,0:T(8,128)S(1)}, f32[2,64,256]{2,1,0:T(8,128)S(1)}, u32[]{:S(2)}, u32[]{:S(2)}) collective-permute-start(f32[2,64,256]{2,1,0:T(8,128)S(1)} %shard_map.75.pair_ref), channel_id=1, source_target_pairs={{1,3},{2,0},{5,7},{6,4},{9,11},{10,8},{13,15},{14,12},{17,19},{18,... | collective-permute-start | bytes 393224 | tf_op jit(solution)/shard_map/ppermute | solution.py:364
  43.9 6.6 %collective-permute-done.13.outer_ref = f32[2,64,256]{2,1,0:T(8,128)S(1)} collective-permute-done((f32[2,64,256]{2,1,0:T(8,128)S(1)}, f32[2,64,256]{2,1,0:T(8,128)S(1)}, u32[]{:S(2)}, u32[]{:S(2)}) %collective-permute-start.13) | collective-permute-done | bytes 131104 | tf_op jit(solution)/shard_map/ppermute | solution.py:364
  50.5 2.5 %collective-permute-start.20 = (f32[4,64,256]{2,1,0:T(8,128)S(1)}, f32[4,64,256]{2,1,0:T(8,128)S(1)}, u32[]{:S(2)}, u32[]{:S(2)}) collective-permute-start(f32[4,64,256]{2,1,0:T(8,128)S(1)} %shard_map.78.refs_0_), channel_id=1, source_target_pairs={{0,24},{4,28},{8,16},{12,20},{16,8},{20,12},{24,0},{28,4},{1,25},{... | collective-permute-start | bytes 786440 | tf_op jit(solution)/shard_map/ppermute | solution.py:307
  53.7 4.8 %collective-permute-start.17 = (f32[2,384,128]{2,1,0:T(8,128)S(1)}, f32[2,384,128]{2,1,0:T(8,128)S(1)}, u32[]{:S(2)}, u32[]{:S(2)}) collective-permute-start(f32[2,384,128]{2,1,0:T(8,128)S(1)} %shard_map.76), channel_id=1, source_target_pairs={{0,1},{1,0},{2,3},{3,2},{4,5},{5,4},{6,7},{7,6},{8,9},{9,8},{10,11... | collective-permute-start | bytes 1179656 | tf_op jit(solution)/shard_map/ppermute | solution.py:307
  60.4 5.1 %collective-permute-done.17.end_ref = f32[2,384,128]{2,1,0:T(8,128)S(1)} collective-permute-done((f32[2,384,128]{2,1,0:T(8,128)S(1)}, f32[2,384,128]{2,1,0:T(8,128)S(1)}, u32[]{:S(2)}, u32[]{:S(2)}) %collective-permute-start.17) | collective-permute-done | bytes 393248 | tf_op jit(solution)/shard_map/ppermute | solution.py:307
  65.5 4.0 %collective-permute-start.25 = (f32[2,384,128]{2,1,0:T(8,128)S(1)}, f32[2,384,128]{2,1,0:T(8,128)S(1)}, u32[]{:S(2)}, u32[]{:S(2)}) collective-permute-start(f32[2,384,128]{2,1,0:T(8,128)S(1)} %shard_map.80), channel_id=1, source_target_pairs={{0,1},{1,0},{2,3},{3,2},{4,5},{5,4},{6,7},{7,6},{8,9},{9,8},{10,11... | collective-permute-start | bytes 1179656 | tf_op jit(solution)/shard_map/ppermute | solution.py:307
  69.5 3.1 %project.9 = (f32[2,384,128]{2,1,0:T(8,128)S(1)}, f32[2,384,128]{2,1,0:T(8,128)S(1)}) custom-call(s32[1]{0:T(128)} %bitcast.feat.feat_ref.me_ref, bf16[4096,1024]{1,0:T(8,128)(2,1)} %bitcast.28, bf16[4096,1024]{1,0:T(8,128)(2,1)} %bitcast.33, bf16[1024,128]{1,0:T(8,128)(2,1)S(1)} %get-tuple-element.69.down_ref, bf16[1024,128]{1,0:T(8,128)(2,1)} %sketch_ref.9), custom_call_target="tpu_custom_call" | custom-call | flops 536870912 | bytes 4980736 | tf_op jit(solution)/shard_map/project/pallas_call | solution.py:81
  76.1 1.5 %score.1.refs_0_ = f32[16,64]{1,0:T(8,128)S(1)} custom-call(s32[1]{0:T(128)} %bitcast.1.middle_ref, bf16[32,128,256]{2,1,0:T(8,128)(2,1)S(1)} %split.1.lang_ref, bf16[32,16,256]{2,1,0:T(8,128)(2,1)S(1)} %get-tuple-element.75.grad_a, f32[8,1]{1,0:T(8,128)S(1)} %get-tuple-element.71.square_a, f32[2,384,128]{2,1,0:T(8,128)S(1)} %get-tuple-element.76.refs_0_, ...), custom_call_target="tpu_custom_call" | custom-call | tf_op jit(solution)/shard_map/score/pallas_call | solution.py:247
  77.6 2.0 %collective-permute-start.29 = (f32[16,64]{1,0:T(8,128)S(1)}, f32[16,64]{1,0:T(8,128)S(1)}, u32[]{:S(2)}, u32[]{:S(2)}) collective-permute-start(f32[16,64]{1,0:T(8,128)S(1)} %score.1.refs_0_), channel_id=1, source_target_pairs={{0,3},{1,2},{2,1},{3,0},{4,7},{5,6},{6,5},{7,4},{8,11},{9,10},{10,... | collective-permute-start | bytes 12296 | tf_op jit(solution)/shard_map/ppermute | solution.py:307
  80.5 1.6 %collective-permute-start.27 = (f32[16,64]{1,0:T(8,128)S(1)}, f32[16,64]{1,0:T(8,128)S(1)}, u32[]{:S(2)}, u32[]{:S(2)}) collective-permute-start(f32[16,64]{1,0:T(8,128)S(1)} %score.1.refs_0_), channel_id=1, source_target_pairs={{0,1},{1,0},{2,3},{3,2},{4,5},{5,4},{6,7},{7,6},{8,9},{9,8},{10,11... | collective-permute-start | bytes 12296 | tf_op jit(solution)/shard_map/ppermute | solution.py:307
  (61 shorter events, 14.6 us)
Async XLA Ops:
  2.7 13.0 %collective-permute-start.1 = (f32[2,384,128]{2,1,0:T(8,128)S(1)}, f32[2,384,128]{2,1,0:T(8,128)S(1)}, u32[]{:S(2)}, u32[]{:S(2)}) collective-permute-start(f32[2,384,128]{2,1,0:T(8,128)S(1)} %get-tuple-element.47.raw_ref), channel_id=1, source_target_pairs={{0,1},{1,0},{2,3},{3,2},{4,5},{5,4},{6,7},{7,6},{8,9},{9,8},{10,11... | collective-permute-start | bytes 1179656 | tf_op jit(solution)/shard_map/ppermute | solution.py:307
  5.8 12.0 %collective-permute-start.3 = (f32[32,1]{1,0:T(8,128)S(1)}, f32[32,1]{1,0:T(8,128)S(1)}, u32[]{:S(2)}, u32[]{:S(2)}) collective-permute-start(f32[32,1]{1,0:T(8,128)S(1)} %get-tuple-element.42.refs_0_), channel_id=1, source_target_pairs={{0,3},{1,2},{2,1},{3,0},{4,7},{5,6},{6,5},{7,4},{8,11},{9,10},{10,... | collective-permute-start | bytes 392 | tf_op jit(solution)/shard_map/ppermute | solution.py:307
  8.3 9.5 %collective-permute-start.2 = (f32[32,1]{1,0:T(8,128)S(1)}, f32[32,1]{1,0:T(8,128)S(1)}, u32[]{:S(2)}, u32[]{:S(2)}) collective-permute-start(f32[32,1]{1,0:T(8,128)S(1)} %get-tuple-element.42.refs_0_), channel_id=1, source_target_pairs={{0,2},{1,3},{2,0},{3,1},{4,6},{5,7},{6,4},{7,5},{8,10},{9,11},{10,... | collective-permute-start | bytes 392 | tf_op jit(solution)/shard_map/ppermute | solution.py:307
  8.4 9.4 %collective-permute-start = (f32[32,1]{1,0:T(8,128)S(1)}, f32[32,1]{1,0:T(8,128)S(1)}, u32[]{:S(2)}, u32[]{:S(2)}) collective-permute-start(f32[32,1]{1,0:T(8,128)S(1)} %get-tuple-element.42.refs_0_), channel_id=1, source_target_pairs={{0,1},{1,0},{2,3},{3,2},{4,5},{5,4},{6,7},{7,6},{8,9},{9,8},{10,11... | collective-permute-start | bytes 392 | tf_op jit(solution)/shard_map/ppermute | solution.py:307
  18.2 11.5 %collective-permute-start.5 = (f32[2,384,128]{2,1,0:T(8,128)S(1)}, f32[2,384,128]{2,1,0:T(8,128)S(1)}, u32[]{:S(2)}, u32[]{:S(2)}) collective-permute-start(f32[2,384,128]{2,1,0:T(8,128)S(1)} %project.6.raw_ref), channel_id=1, source_target_pairs={{0,1},{1,0},{2,3},{3,2},{4,5},{5,4},{6,7},{7,6},{8,9},{9,8},{10,11... | collective-permute-start | bytes 1179656 | tf_op jit(solution)/shard_map/ppermute | solution.py:307
  19.0 24.0 %collective-permute-start.10 = (f32[2,384,128]{2,1,0:T(8,128)S(1)}, f32[2,384,128]{2,1,0:T(8,128)S(1)}, u32[]{:S(2)}, u32[]{:S(2)}) collective-permute-start(f32[2,384,128]{2,1,0:T(8,128)S(1)} %shard_map.73), channel_id=1, source_target_pairs={{1,2},{2,1},{0,0},{3,3},{5,6},{6,5},{4,4},{7,7},{9,10},{10,9},{8,8... | collective-permute-start | bytes 1179656 | tf_op jit(solution)/shard_map/ppermute | solution.py:349
  19.8 10.7 %collective-permute-start.7 = (f32[64,256]{1,0:T(8,128)S(1)}, f32[64,256]{1,0:T(8,128)S(1)}, u32[]{:S(2)}, u32[]{:S(2)}) collective-permute-start(f32[64,256]{1,0:T(8,128)S(1)} %get-tuple-element.79), channel_id=1, source_target_pairs={{0,16},{4,20},{8,24},{12,28},{16,0},{20,4},{24,8},{28,12},{1,17},{... | collective-permute-start | bytes 196616 | tf_op jit(solution)/shard_map/ppermute | solution.py:307
  21.4 9.2 %collective-permute-start.8 = (f32[64,256]{1,0:T(8,128)S(1)}, f32[64,256]{1,0:T(8,128)S(1)}, u32[]{:S(2)}, u32[]{:S(2)}) collective-permute-start(f32[64,256]{1,0:T(8,128)S(1)} %get-tuple-element.80), channel_id=1, source_target_pairs={{0,24},{4,28},{8,16},{12,20},{16,8},{20,12},{24,0},{28,4},{1,25},{... | collective-permute-start | bytes 196616 | tf_op jit(solution)/shard_map/ppermute | solution.py:307
  22.8 7.7 %collective-permute-start.6 = (f32[64,256]{1,0:T(8,128)S(1)}, f32[64,256]{1,0:T(8,128)S(1)}, u32[]{:S(2)}, u32[]{:S(2)}) collective-permute-start(f32[64,256]{1,0:T(8,128)S(1)} %get-tuple-element.81), channel_id=1, source_target_pairs={{0,8},{4,12},{8,0},{12,4},{16,24},{20,28},{24,16},{28,20},{1,9},{5... | collective-permute-start | bytes 196616 | tf_op jit(solution)/shard_map/ppermute | solution.py:307
  29.7 14.1 %collective-permute-start.11 = (f32[2,384,128]{2,1,0:T(8,128)S(1)}, f32[2,384,128]{2,1,0:T(8,128)S(1)}, u32[]{:S(2)}, u32[]{:S(2)}) collective-permute-start(f32[2,384,128]{2,1,0:T(8,128)S(1)} %get-tuple-element.63.raw_ref), channel_id=1, source_target_pairs={{0,1},{1,0},{2,3},{3,2},{4,5},{5,4},{6,7},{7,6},{8,9},{9,8},{10,11... | collective-permute-start | bytes 1179656 | tf_op jit(solution)/shard_map/ppermute | solution.py:307
  30.6 11.2 %collective-permute-start.9 = (f32[64,256]{1,0:T(8,128)S(1)}, f32[64,256]{1,0:T(8,128)S(1)}, u32[]{:S(2)}, u32[]{:S(2)}) collective-permute-start(f32[64,256]{1,0:T(8,128)S(1)} %add_add_fusion.one_ref), channel_id=1, source_target_pairs={{0,1},{1,0},{2,3},{3,2},{4,5},{5,4},{6,7},{7,6},{8,9},{9,8},{10,11... | collective-permute-start | bytes 196616 | tf_op jit(solution)/shard_map/ppermute | solution.py:307
  31.9 26.6 %collective-permute-start.16 = (f32[2,384,128]{2,1,0:T(8,128)S(1)}, f32[2,384,128]{2,1,0:T(8,128)S(1)}, u32[]{:S(2)}, u32[]{:S(2)}) collective-permute-start(f32[2,384,128]{2,1,0:T(8,128)S(1)} %shard_map.74), channel_id=1, source_target_pairs={{1,2},{2,1},{0,0},{3,3},{5,6},{6,5},{4,4},{7,7},{9,10},{10,9},{8,8... | collective-permute-start | bytes 1179656 | tf_op jit(solution)/shard_map/ppermute | solution.py:357
  32.6 26.4 %collective-permute-start.15 = (f32[2,384,128]{2,1,0:T(8,128)S(1)}, f32[2,384,128]{2,1,0:T(8,128)S(1)}, u32[]{:S(2)}, u32[]{:S(2)}) collective-permute-start(f32[2,384,128]{2,1,0:T(8,128)S(1)} %get-tuple-element.67.raw_ref), channel_id=1, source_target_pairs={{0,1},{3,2},{4,5},{7,6},{8,9},{11,10},{12,13},{15,14},{16,17},{19,... | collective-permute-start | bytes 1179656 | tf_op jit(solution)/shard_map/ppermute | solution.py:360
  41.7 8.7 %collective-permute-start.13 = (f32[2,64,256]{2,1,0:T(8,128)S(1)}, f32[2,64,256]{2,1,0:T(8,128)S(1)}, u32[]{:S(2)}, u32[]{:S(2)}) collective-permute-start(f32[2,64,256]{2,1,0:T(8,128)S(1)} %shard_map.75.pair_ref), channel_id=1, source_target_pairs={{1,3},{2,0},{5,7},{6,4},{9,11},{10,8},{13,15},{14,12},{17,19},{18,... | collective-permute-start | bytes 393224 | tf_op jit(solution)/shard_map/ppermute | solution.py:364
  43.0 7.4 %collective-permute-start.12 = (f32[2,64,256]{2,1,0:T(8,128)S(1)}, f32[2,64,256]{2,1,0:T(8,128)S(1)}, u32[]{:S(2)}, u32[]{:S(2)}) collective-permute-start(f32[2,64,256]{2,1,0:T(8,128)S(1)} %shard_map.75.pair_ref), channel_id=1, source_target_pairs={{1,2},{2,1},{0,0},{3,3},{5,6},{6,5},{4,4},{7,7},{9,10},{10,9},{8,8... | collective-permute-start | bytes 393224 | tf_op jit(solution)/shard_map/ppermute | solution.py:363
  50.5 9.1 %collective-permute-start.20 = (f32[4,64,256]{2,1,0:T(8,128)S(1)}, f32[4,64,256]{2,1,0:T(8,128)S(1)}, u32[]{:S(2)}, u32[]{:S(2)}) collective-permute-start(f32[4,64,256]{2,1,0:T(8,128)S(1)} %shard_map.78.refs_0_), channel_id=1, source_target_pairs={{0,24},{4,28},{8,16},{12,20},{16,8},{20,12},{24,0},{28,4},{1,25},{... | collective-permute-start | bytes 786440 | tf_op jit(solution)/shard_map/ppermute | solution.py:307
  53.0 6.6 %collective-permute-start.18 = (f32[2,384,128]{2,1,0:T(8,128)S(1)}, f32[2,384,128]{2,1,0:T(8,128)S(1)}, u32[]{:S(2)}, u32[]{:S(2)}) collective-permute-start(f32[2,384,128]{2,1,0:T(8,128)S(1)} %shard_map.77), channel_id=1, source_target_pairs={{1,2},{2,1},{0,0},{3,3},{5,6},{6,5},{4,4},{7,7},{9,10},{10,9},{8,8... | collective-permute-start | bytes 1179656 | tf_op jit(solution)/shard_map/ppermute | solution.py:368
  53.7 11.8 %collective-permute-start.17 = (f32[2,384,128]{2,1,0:T(8,128)S(1)}, f32[2,384,128]{2,1,0:T(8,128)S(1)}, u32[]{:S(2)}, u32[]{:S(2)}) collective-permute-start(f32[2,384,128]{2,1,0:T(8,128)S(1)} %shard_map.76), channel_id=1, source_target_pairs={{0,1},{1,0},{2,3},{3,2},{4,5},{5,4},{6,7},{7,6},{8,9},{9,8},{10,11... | collective-permute-start | bytes 1179656 | tf_op jit(solution)/shard_map/ppermute | solution.py:307
  58.5 15.0 %collective-permute-start.19 = (f32[4,64,256]{2,1,0:T(8,128)S(1)}, f32[4,64,256]{2,1,0:T(8,128)S(1)}, u32[]{:S(2)}, u32[]{:S(2)}) collective-permute-start(f32[4,64,256]{2,1,0:T(8,128)S(1)} %shard_map.78.refs_0_), channel_id=1, source_target_pairs={{0,16},{4,20},{8,24},{12,28},{16,0},{20,4},{24,8},{28,12},{1,17},{... | collective-permute-start | bytes 786440 | tf_op jit(solution)/shard_map/ppermute | solution.py:307
  59.0 14.4 %collective-permute-start.14 = (f32[4,64,256]{2,1,0:T(8,128)S(1)}, f32[4,64,256]{2,1,0:T(8,128)S(1)}, u32[]{:S(2)}, u32[]{:S(2)}) collective-permute-start(f32[4,64,256]{2,1,0:T(8,128)S(1)} %shard_map.78.refs_0_), channel_id=1, source_target_pairs={{0,8},{4,12},{8,0},{12,4},{16,24},{20,28},{24,16},{28,20},{1,9},{5... | collective-permute-start | bytes 786440 | tf_op jit(solution)/shard_map/ppermute | solution.py:307
  59.6 14.4 %collective-permute-start.21 = (f32[4,64,256]{2,1,0:T(8,128)S(1)}, f32[4,64,256]{2,1,0:T(8,128)S(1)}, u32[]{:S(2)}, u32[]{:S(2)}) collective-permute-start(f32[4,64,256]{2,1,0:T(8,128)S(1)} %shard_map.78.refs_0_), channel_id=1, source_target_pairs={{0,4},{4,0},{8,12},{12,8},{16,20},{20,16},{24,28},{28,24},{1,5},{5... | collective-permute-start | bytes 786440 | tf_op jit(solution)/shard_map/ppermute | solution.py:307
  59.6 16.4 %collective-permute-start.26 = (f32[2,384,128]{2,1,0:T(8,128)S(1)}, f32[2,384,128]{2,1,0:T(8,128)S(1)}, u32[]{:S(2)}, u32[]{:S(2)}) collective-permute-start(f32[2,384,128]{2,1,0:T(8,128)S(1)} %shard_map.79), channel_id=1, source_target_pairs={{1,2},{2,1},{0,0},{3,3},{5,6},{6,5},{4,4},{7,7},{9,10},{10,9},{8,8... | collective-permute-start | bytes 1179656 | tf_op jit(solution)/shard_map/ppermute | solution.py:373
  65.5 10.5 %collective-permute-start.25 = (f32[2,384,128]{2,1,0:T(8,128)S(1)}, f32[2,384,128]{2,1,0:T(8,128)S(1)}, u32[]{:S(2)}, u32[]{:S(2)}) collective-permute-start(f32[2,384,128]{2,1,0:T(8,128)S(1)} %shard_map.80), channel_id=1, source_target_pairs={{0,1},{1,0},{2,3},{3,2},{4,5},{5,4},{6,7},{7,6},{8,9},{9,8},{10,11... | collective-permute-start | bytes 1179656 | tf_op jit(solution)/shard_map/ppermute | solution.py:307
  77.6 5.5 %collective-permute-start.29 = (f32[16,64]{1,0:T(8,128)S(1)}, f32[16,64]{1,0:T(8,128)S(1)}, u32[]{:S(2)}, u32[]{:S(2)}) collective-permute-start(f32[16,64]{1,0:T(8,128)S(1)} %score.1.refs_0_), channel_id=1, source_target_pairs={{0,3},{1,2},{2,1},{3,0},{4,7},{5,6},{6,5},{7,4},{8,11},{9,10},{10,... | collective-permute-start | bytes 12296 | tf_op jit(solution)/shard_map/ppermute | solution.py:307
  (8 other events, 23.6 us)
